TPU v7x, 128 devices: a whole 4x4x4 slice. The times are simulated.
128 devices in a mesh: seq: 16 (over y, z_lo, core), tp: 8 (over z_hi, x).
Axes of the slice: x: 4, y: 4, z: 4 (z_hi: 2, z_lo: 2; z = z_hi * 2 + z_lo), core: 2. Of those that a mesh axis runs over, the one named last changes fastest.
Arguments:
- tokens: bfloat16 [8192, 2048], P('seq'), may hold values from -6 to 6
- w_zx: float32 [2048, 8192], P(('seq', 'tp')), may hold values from -0.125 to 0.125
- w_dt: float32 [2048, 64], P(('seq', 'tp')), may hold values from -0.26516503 to 0.26516503
- w_bc: float32 [2048, 256], P(('seq', 'tp')), may hold values from -0.125 to 0.125
- conv_x_weight: float32 [4, 4096], P(None, 'tp'), may hold values from -3 to 3
- conv_x_bias: float32 [4096], P('tp'), may hold values from -1.8 to 1.8
- conv_bc_weight: float32 [4, 256], replicated, may hold values from -3 to 3
- conv_bc_bias: float32 [256], replicated, may hold values from -1.8 to 1.8
- dt_bias: float32 [64], P('tp'), may hold values from -11 to -2
- a_log: float32 [64], P('tp'), may hold values from 0 to 2.77
- skip: float32 [64], P('tp'), may hold values from 0.5 to 2
- norm_weight: float32 [4096], P('tp'), may hold values from 0.1 to 1.9
- w_out: float32 [4096, 2048], P('tp', 'seq'), may hold values from -0.09375 to 0.09375
- lengths: int32 [8], replicated, may hold values from 1 to 4096, 8192 in all
- request_group: int32 [32], replicated, may hold values from 0 to 31
Outputs:
- mixed: bfloat16 [8192, 2048], P(('seq', 'tp'))
- request_states: float32 [32, 64, 64, 128], P('seq', 'tp')
Inputs may be any that keep to these rules, and one draw needn't show every extreme that they name: 8 prompts packed end to end in this order; the lengths sum to 8192 and the longest is exactly 4096.
All inputs are finite; a program needn't handle non-finite values.
Results may differ from a plain program's by a relative error of at most 0.011.
Values may be sent and summed in bfloat16 or wider, within the bound.
A program may use at most 128 MiB of HBM per device.

v0:
```python
import jax
import jax.numpy as jnp
from jax import lax
from jax.sharding import PartitionSpec as P

INNER = 4096
GROUP = 256


epsilon = 1e-05


def from_behind(x, axis, by):
    count = lax.axis_size(axis)
    pairs = [(i, i + by) for i in range(count) if 0 <= i + by < count]
    return lax.ppermute(x, axis, pairs)


def prefix(part, axis, combine, identity):
    place = lax.axis_index(axis)
    gathered = jax.tree.map(lambda a: lax.all_gather(a, axis), part)
    state = jax.tree.map(lambda a, e: jnp.zeros_like(a) + jnp.asarray(e, a.dtype), part, identity)

    def one(step, state):
        return combine(
            state, jax.tree.map(lambda a: lax.dynamic_index_in_dim(a, step, 0, False), gathered)
        )

    return lax.fori_loop(0, place, one, state)


def segment_of(position, lengths):
    prompt_ends = jnp.cumsum(lengths)
    return jnp.sum((position[:, None] >= prompt_ends[None, :]).astype(jnp.int32), axis=1)


def on_device(
    tokens,
    w_zx,
    w_dt,
    w_bc,
    conv_x_weight,
    conv_x_bias,
    conv_bc_weight,
    conv_bc_bias,
    dt_bias,
    a_log,
    skip,
    norm_weight,
    w_out,
    lengths,
    request_group,
):
    tp_count = lax.axis_size("tp")
    tok_dev = tokens.shape[0]
    local_rows = w_zx.shape[0]
    inner_local = conv_x_weight.shape[1]
    heads_local = dt_bias.shape[0]
    head_width = inner_local // heads_local
    state_width = conv_bc_weight.shape[1] // 2
    taps = conv_x_weight.shape[0]
    groups_dev = tok_dev // GROUP
    zx_shard = w_zx.astype(jnp.bfloat16).reshape(local_rows, 2, tp_count, inner_local)
    zx_shard = zx_shard.transpose(0, 2, 1, 3).reshape(local_rows, tp_count * 2 * inner_local)
    dt_shard = w_dt.astype(jnp.bfloat16)
    zx_block, dt_block = (
        lax.all_to_all(zx_shard, "tp", split_axis=1, concat_axis=0, tiled=True),
        lax.all_to_all(dt_shard, "tp", split_axis=1, concat_axis=0, tiled=True),
    )
    columns = tokens
    zx_sum = jnp.dot(
        columns,
        lax.all_gather(zx_block, "seq", axis=0, tiled=True),
        preferred_element_type=jnp.float32,
    )
    dt_pre = jnp.dot(
        columns,
        lax.all_gather(dt_block, "seq", axis=0, tiled=True),
        preferred_element_type=jnp.float32,
    )
    zx_low = zx_sum.astype(jnp.bfloat16)
    gate_z = zx_low[:, :inner_local]
    x_raw = zx_low[:, inner_local:]
    columns = tokens
    bc_sum = jnp.dot(
        columns,
        lax.all_gather(w_bc.astype(jnp.bfloat16), ("seq", "tp"), axis=0, tiled=True),
        preferred_element_type=jnp.float32,
    )
    bc_raw = bc_sum.astype(jnp.bfloat16)
    raw_mix = jnp.concatenate([x_raw, bc_raw], axis=1)
    conv_weight = jnp.concatenate([conv_x_weight, conv_bc_weight], axis=1)
    conv_bias = jnp.concatenate([conv_x_bias, conv_bc_bias], axis=0)
    rim_rows = from_behind(raw_mix[tok_dev - (taps - 1) :], "seq", 1)
    padded = jnp.concatenate([rim_rows, raw_mix], axis=0)
    offset = lax.axis_index("seq") * tok_dev
    seg_pad = segment_of(
        offset - (taps - 1) + jnp.arange(tok_dev + taps - 1, dtype=jnp.int32), lengths
    )
    seg_tok = seg_pad[taps - 1 :]
    conv_sum = jnp.zeros((tok_dev, raw_mix.shape[1]), jnp.float32) + conv_bias[None, :]
    for offset_tap in range(taps):
        rows_wide = padded[offset_tap : offset_tap + tok_dev].astype(jnp.float32)
        keep_tap = seg_pad[offset_tap : offset_tap + tok_dev] == seg_tok
        conv_sum = conv_sum + jnp.where(
            keep_tap[:, None], rows_wide * conv_weight[offset_tap][None, :], 0.0
        )
    convolved = jax.nn.silu(conv_sum).astype(jnp.bfloat16)
    inputs = convolved[:, :inner_local].reshape(groups_dev, GROUP, heads_local, head_width)
    b_matrix = convolved[:, inner_local : inner_local + state_width].reshape(
        groups_dev, GROUP, state_width
    )
    c_matrix = convolved[:, inner_local + state_width :].reshape(groups_dev, GROUP, state_width)
    step_size = jax.nn.softplus(dt_pre + dt_bias[None, :]).reshape(groups_dev, GROUP, heads_local)
    step_heads = step_size.transpose(0, 2, 1)
    decay_rate = -jnp.exp(a_log)
    cumul_heads = jnp.cumsum(step_size * decay_rate[None, None, :], axis=1).transpose(0, 2, 1)
    segments = seg_tok.reshape(groups_dev, GROUP)
    seg_before = segment_of(offset + jnp.arange(groups_dev, dtype=jnp.int32) * GROUP - 1, lengths)
    within = jnp.arange(GROUP, dtype=jnp.int32)
    same_prompt = (segments[:, :, None] == segments[:, None, :]) & (
        within[:, None] >= within[None, :]
    )[None]
    log_decay = cumul_heads[:, :, :, None] - cumul_heads[:, :, None, :]
    decay_matrix = jnp.where(
        same_prompt[:, None], jnp.exp(jnp.where(same_prompt[:, None], log_decay, 0.0)), 0.0
    )
    scores = jnp.einsum("cin,cjn->cij", c_matrix, b_matrix, preferred_element_type=jnp.float32)
    mix_weights = (decay_matrix * scores[:, None] * step_heads[:, :, None, :]).astype(jnp.bfloat16)
    diag_out = jnp.einsum(
        "chij,cjhp->cihp", mix_weights, inputs, preferred_element_type=jnp.float32
    )
    last_segment = segments[:, -1]
    tail_weight = (
        jnp.where(
            (segments == last_segment[:, None])[:, None, :],
            jnp.exp(cumul_heads[:, :, -1:] - cumul_heads),
            0.0,
        )
        * step_heads
    )
    b_weighted = (b_matrix.astype(jnp.float32)[:, None] * tail_weight[:, :, :, None]).astype(
        jnp.bfloat16
    )
    contrib = jnp.einsum("cjhp,chjn->chpn", inputs, b_weighted, preferred_element_type=jnp.float32)
    pass_gate = jnp.where(
        (last_segment == seg_before)[:, None], jnp.exp(cumul_heads[:, :, -1]), 0.0
    )

    def local_step(carry_state, group_item):
        factor, source = group_item
        next_state = factor[:, None, None] * carry_state + source
        return (next_state, (carry_state, next_state))

    zero_state = jnp.zeros((heads_local, head_width, state_width), jnp.float32)
    dev_state, (local_in, local_end) = lax.scan(local_step, zero_state, (pass_gate, contrib))
    through_group = jnp.cumprod(pass_gate, axis=0)
    before_group = jnp.concatenate(
        [jnp.ones((1, heads_local), jnp.float32), through_group[:-1]], axis=0
    )
    dev_decay = through_group[-1]

    def combine(earlier, later_one):
        return (earlier[0] * later_one[0], later_one[0][:, None, None] * earlier[1] + later_one[1])

    identity = (jnp.ones((heads_local,), jnp.float32), zero_state)
    _, carried = prefix((dev_decay, dev_state), "seq", combine, identity)
    group_in = before_group[:, :, None, None] * carried[None] + local_in
    group_end = through_group[:, :, None, None] * carried[None] + local_end
    state_low = group_in.astype(jnp.bfloat16)
    carry_keep = jnp.where((segments == seg_before[:, None])[:, None, :], jnp.exp(cumul_heads), 0.0)
    carry_out = jnp.einsum(
        "cin,chpn->cihp", c_matrix, state_low, preferred_element_type=jnp.float32
    )
    carry_out = carry_out * carry_keep.transpose(0, 2, 1)[:, :, :, None]
    y_local = diag_out + carry_out + skip[None, None, :, None] * inputs.astype(jnp.float32)
    y_local = y_local.reshape(tok_dev, inner_local)
    gated = y_local * jax.nn.silu(gate_z.astype(jnp.float32))
    square_sum = lax.psum(jnp.sum(gated * gated, axis=1), "tp")
    normed = (
        gated * lax.rsqrt(square_sum / INNER + epsilon)[:, None] * norm_weight[None, :]
    ).astype(jnp.bfloat16)
    out_shard = w_out.astype(jnp.bfloat16)
    out_block = lax.all_gather(out_shard, "seq", axis=1, tiled=True)
    mixed = lax.psum_scatter(
        jnp.dot(normed, out_block, preferred_element_type=jnp.float32),
        "tp",
        scatter_dimension=0,
        tiled=True,
    ).astype(jnp.bfloat16)
    group_ids = lax.axis_index("seq") * groups_dev + jnp.arange(groups_dev, dtype=jnp.int32)
    selector = (request_group[:, None] == group_ids[None, :]).astype(jnp.float32)
    flat_end = group_end.reshape(groups_dev, heads_local * head_width * state_width)
    picked = jnp.dot(
        selector, flat_end, precision=lax.Precision.HIGHEST, preferred_element_type=jnp.float32
    )
    picked = picked.reshape(request_group.shape[0], heads_local, head_width, state_width)
    request_states = lax.psum_scatter(
        picked.astype(jnp.bfloat16), "seq", scatter_dimension=0, tiled=True
    ).astype(jnp.float32)
    return (mixed, request_states)


def solution(mesh):
    return jax.shard_map(
        on_device,
        mesh=mesh,
        in_specs=(
            P("seq", None),
            P(("seq", "tp"), None),
            P(("seq", "tp"), None),
            P(("seq", "tp"), None),
            P(None, "tp"),
            P("tp"),
            P(),
            P(),
            P("tp"),
            P("tp"),
            P("tp"),
            P("tp"),
            P("tp", "seq"),
            P(),
            P(),
        ),
        out_specs=(P(("seq", "tp"), None), P("seq", "tp", None, None)),
        check_vma=False,
    )
```

profile of v0, /device:TPU:1, one launch (start us, length us, event | category | flops | bytes accessed | tf_op | source)
XLA Modules:
  0.0 622.3 jit_solution(9006918756835963903)
XLA Ops:
  7.3 1.5 convert_element_type.77
  8.9 1.1 convert_element_type.75
  10.4 15.9 %all_to_all.38 = bf16[16,8,1024]{2,0,1:T(8,128)(2,1)} all-to-all(bf16[16,8,1024]{2,0,1:T(8,128)(2,1)S(1)} %all_to_all.28), channel_id=1, replica_groups=mesh['seq'=16,'tp'=8] {'tp'}, dimensions={1} | all-to-all | bytes 524288 | tf_op jit(solution)/shard_map/all_to_all | solution.py:67
  26.3 0.7 copy.78
  27.0 3.3 all-to-all-start.1
  31.8 5.1 all-to-all-done.1
  37.0 22.4 %all_gather.23 = bf16[2048,8]{0,1:T(8,128)(2,1)S(1)} all-gather(bf16[128,8]{0,1:T(8,128)(2,1)S(1)} %all_to_all.35), channel_id=1, replica_groups=mesh['seq'=16,'tp'=8] {'seq'}, dimensions={0}, use_global_device_ids=true | all-gather | bytes 34816 | tf_op jit(solution)/shard_map/all_gather | solution.py:78
  60.1 1.1 reduce-window.19
  61.4 0.7 select_bitcast_fusion
  62.2 0.7 select_multiply_fusion
  62.9 243.8 %all-gather.9.cloned.1.call-done = bf16[2048,256]{1,0:T(8,128)(2,1)} async-done(((bf16[16,256]{1,0:T(8,128)(2,1)}), bf16[2048,256]{1,0:T(8,128)(2,1)}) %all-gather.9.cloned.1.call-update) | async-done | bytes 1048592 | tf_op jit(solution)/shard_map/all_gather | solution.py:87
  306.8 1.9 convolution_convert_fusion.2
  308.7 37.0 %all-gather.7.cloned.1.call-done = bf16[2048,1024]{1,0:T(8,128)(2,1)} async-done(((bf16[128,1024]{1,0:T(8,128)(2,1)}), bf16[2048,1024]{1,0:T(8,128)(2,1)}) %all-gather.7.cloned.1.call-update) | async-done | bytes 4194320 | tf_op jit(solution)/shard_map/all_gather | solution.py:73
  345.7 4.5 convolution_convert_fusion.1
  350.3 3.2 collective-permute-start
  354.4 1.7 multiply_convert_fusion.3
  356.2 0.7 convert_element_type.87
  357.0 1.5 reshape.198
  358.5 1.7 copy.80
  360.2 1.9 fusion.15
  362.2 3.0 while.28
  362.8 0.8 bitcast_dynamic-update-slice_fusion.3
  364.3 0.8 bitcast_dynamic-update-slice_fusion.3
  365.1 0.7 copy-done.1
  365.9 1.6 convert_element_type.93
  367.7 0.9 compare_and_fusion
  368.6 0.7 reduce_window.9
  369.9 19.7 %all-gather.1 = f32[16,1,8]{2,1,0:T(1,128)} all-gather(f32[1,1,8]{2,1,0:T(1,128)S(1)} %get-tuple-element.175), channel_id=1, replica_groups=mesh['seq'=16,'tp'=8] {'seq'}, dimensions={0}, use_global_device_ids=true | all-gather | bytes 544 | tf_op jit(solution)/shard_map/all_gather | solution.py:21
  389.6 1.1 fusion.33
  390.7 3.2 fusion.8
  393.9 11.5 %all-gather.13.cloned.1.call-done = f32[128,64,128]{2,1,0:T(8,128)} async-done(((f32[8,64,128]{2,1,0:T(8,128)}), f32[128,64,128]{2,1,0:T(8,128)}) %all-gather.13.cloned.1.call-update) | async-done | bytes 4194320 | tf_op jit(solution)/shard_map/all_gather | solution.py:21
  405.5 1.8 while.27
  405.5 0.7 dynamic-slice_bitcast_fusion.2
  406.2 1.1 bitcast_add_fusion.4
  407.3 2.6 fusion.10
  409.9 3.2 copy.93
  413.1 1.9 reshape.197
  415.0 1.5 multiply_reduce_fusion
  416.5 20.8 %psum.7 = f32[512]{0:T(512)S(1)} all-reduce(f32[512]{0:T(512)S(1)} %multiply_reduce_fusion), channel_id=1, replica_groups=mesh['seq'=16,'tp'=8] {'tp'}, use_global_device_ids=true, to_apply=%region_11.12 | all-reduce | flops 512 | bytes 4096 | tf_op jit(solution)/shard_map/psum | solution.py:179
  437.3 7.1 %all-gather.11.cloned.1.call-done = bf16[512,2048]{1,0:T(8,128)(2,1)} async-done(((bf16[512,128]{1,0:T(8,128)(2,1)}), bf16[512,2048]{1,0:T(8,128)(2,1)}) %all-gather.11.cloned.1.call-update) | async-done | bytes 2097168 | tf_op jit(solution)/shard_map/all_gather | solution.py:184
  444.4 5.2 fusion.18
  449.7 0.9 copy-done.4
  451.2 4.0 convolution_convert_fusion
  455.2 3.6 copy.88
  458.8 88.6 %reduce-scatter.3.cloned.1.call-done = f32[64,2048]{1,0:T(8,128)} async-done(((f32[512,2048]{1,0:T(8,128)}), f32[64,2048]{1,0:T(8,128)}) %reduce-scatter.3.cloned.1.call-update) | async-done | bytes 524304 | tf_op jit(solution)/shard_map/reduce_scatter | solution.py:185
  547.4 1.8 convert_element_type.94
  549.2 64.5 %reduce-scatter.5.cloned.1.call-done = bf16[2,8,64,128]{3,2,1,0:T(8,128)(2,1)} async-done(((bf16[32,8,64,128]{3,2,1,0:T(8,128)(2,1)}), bf16[2,8,64,128]{3,2,1,0:T(8,128)(2,1)}) %reduce-scatter.5.cloned.1.call-update) | async-done | bytes 262160 | tf_op jit(solution)/shard_map/reduce_scatter | solution.py:198
  613.7 1.8 convert_element_type.96
  (100 shorter events, 6.8 us)
Async XLA Ops:
  7.2 52.2 %copy-start = (bf16[512,2048]{1,0:T(8,128)(2,1)S(1)}, bf16[512,2048]{1,0:T(8,128)(2,1)}, u32[]{:S(2)}) copy-start(bf16[512,2048]{1,0:T(8,128)(2,1)} %param.19) | copy-start | bytes 6291460
  7.2 19.1 %copy-start.11 = (f32[16,64]{1,0:T(8,128)S(1)}, f32[16,64]{1,0:T(8,128)}, u32[]{:S(2)}) copy-start(f32[16,64]{1,0:T(8,128)} %param.21) | copy-start | bytes 12292
  7.2 23.2 %copy-start.19 = (s32[8]{0:T(128)S(1)}, s32[8]{0:T(128)}, u32[]{:S(2)}) copy-start(s32[8]{0:T(128)} %param.32) | copy-start | bytes 100
  7.2 24.1 %copy-start.12 = (f32[4,512]{1,0:T(4,128)S(1)}, f32[4,512]{1,0:T(4,128)}, u32[]{:S(2)}) copy-start(f32[4,512]{1,0:T(4,128)} %param.23) | copy-start | bytes 24580
  7.2 24.1 %copy-start.13 = (f32[4,256]{1,0:T(4,128)S(1)}, f32[4,256]{1,0:T(4,128)}, u32[]{:S(2)}) copy-start(f32[4,256]{1,0:T(4,128)} %param.25) | copy-start | bytes 12292
  7.2 24.3 %copy-start.20 = (f32[8]{0:T(128)S(1)}, f32[8]{0:T(128)}, u32[]{:S(2)}) copy-start(f32[8]{0:T(128)} %param.28) | copy-start | bytes 100
  7.2 24.5 %copy-start.15 = (f32[256]{0:T(256)S(1)}, f32[256]{0:T(256)}, u32[]{:S(2)}) copy-start(f32[256]{0:T(256)} %param.26) | copy-start | bytes 3076
  7.2 24.5 %copy-start.14 = (f32[512]{0:T(512)S(1)}, f32[512]{0:T(512)}, u32[]{:S(2)}) copy-start(f32[512]{0:T(512)} %param.24) | copy-start | bytes 6148
  7.3 52.1 %copy-start.16 = (f32[8]{0:T(128)S(1)}, f32[8]{0:T(128)}, u32[]{:S(2)}) copy-start(f32[8]{0:T(128)} %param.27) | copy-start | bytes 100
  7.3 299.5 %all-gather.9.cloned.1.call-start = ((), (), s32[]{:S(2)}) async-start(), calls=%async_computation.5 | async-start | bytes 1056768 | tf_op jit(solution)/shard_map/all_gather | solution.py:87
  8.8 336.9 %all-gather.7.cloned.1.call-start = ((), (), s32[]{:S(2)}) async-start(), calls=%async_computation.4 | async-start | bytes 4456448 | tf_op jit(solution)/shard_map/all_gather | solution.py:73
  27.0 9.8 %all-to-all-start.1 = ((bf16[16,8,8]{0,2,1:T(8,128)(2,1)}), bf16[16,8,8]{0,2,1:T(8,128)(2,1)S(1)}, u32[]{:S(2)}, u32[]{:S(2)}) async-start(bf16[16,8,8]{0,2,1:T(8,128)(2,1)} %bitcast.67), calls=%async_computation.1 | async-start | bytes 32768 | tf_op jit(solution)/shard_map/all_to_all | solution.py:68
  30.4 375.1 %all-gather.13.cloned.1.call-start = ((), (), s32[]{:S(2)}) async-start(), calls=%async_computation.9 | async-start | bytes 4456448 | tf_op jit(solution)/shard_map/all_gather | solution.py:21
  31.1 0.6 copy-start.8
  62.1 0.8 copy-start.6
  350.2 5.9 copy-start.3
  350.3 4.0 collective-permute-start
  356.2 0.8 copy-start.2
  365.1 0.7 copy-start.1
  365.9 78.6 %all-gather.11.cloned.1.call-start = ((), (), s32[]{:S(2)}) async-start(), calls=%async_computation.6 | async-start | bytes 2228224 | tf_op jit(solution)/shard_map/all_gather | solution.py:184
  367.6 179.8 %reduce-scatter.3.cloned.1.call-start = ((), (), s32[]{:S(2)}) async-start(), calls=%async_computation.7 | async-start | bytes 4718592 | tf_op jit(solution)/shard_map/reduce_scatter | solution.py:185
  369.3 24.6 %copy-start.9 = (f32[2,8]{1,0:T(2,128)}, f32[2,8]{1,0:T(2,128)S(1)}, u32[]{:S(2)}) copy-start(f32[2,8]{1,0:T(2,128)S(1)} %reduce_window.9) | copy-start | bytes 196
  405.4 1.8 copy-start.5
  405.5 1.8 copy-start.7
  413.1 31.3 %copy-start.18 = (f32[512]{0:T(512)S(1)}, f32[512]{0:T(512)}, u32[]{:S(2)}) copy-start(f32[512]{0:T(512)} %param.30) | copy-start | bytes 6148
  449.6 1.0 copy-start.4
  449.6 1.0 copy-start.10
  449.6 1.5 copy-start.17
  449.6 164.0 %reduce-scatter.5.cloned.1.call-start = ((), (), s32[]{:S(2)}) async-start(), calls=%async_computation.8 | async-start | bytes 4456448 | tf_op jit(solution)/shard_map/reduce_scatter | solution.py:198
Sparse Core Ops, SparseCore 0:
  9.8 296.9 all-gather.8
  308.5 37.1 all-gather.6
  366.0 39.3 all-gather.12
  406.9 37.4 all-gather.10
  449.7 97.6 reduce-scatter.2
  549.6 63.9 reduce-scatter.4
where the time goes:
time: 627 us; the launch traced here: 622 us
  waiting for transfers between devices  458 us (73%)
  blocking collectives  78.7 us (13%)
  matrix products  25.1 us (4%)
  other arithmetic  20.3 us (3%)
  local copies, waits for them, and re-layouts  18.8 us (3%)
  between operations  14.6 us (2%)
  starting transfers between devices  6.78 us (1%)
    all_gather x1, waiting for transfers between devices, on_device(): lax.all_gather(w_bc.astype(jnp.bfloat16), ('seq', 'tp'), axis=0, tiled=True)  244 us
    reduce_scatter x1, waiting for transfers between devices, on_device(): lax.psum_scatter(jnp.dot(normed, out_block, preferred_element_type=jnp.fl...  88.6 us
    reduce_scatter x1, waiting for transfers between devices, on_device(): lax.psum_scatter(picked.astype(jnp.bfloat16), 'seq', scatter_dimension=0,...  64.5 us
    all_gather x1, waiting for transfers between devices, on_device(): lax.all_gather(zx_block, 'seq', axis=0, tiled=True)  37 us
    all_gather x1, blocking collectives, on_device(): lax.all_gather(dt_block, 'seq', axis=0, tiled=True)  22.4 us
    psum x1, blocking collectives, on_device(): square_sum = lax.psum(jnp.sum(gated * gated, axis=1), 'tp')  20.8 us
    all_gather x1, blocking collectives, prefix(): gathered = jax.tree.map(lambda a: lax.all_gather(a, axis), part)  19.7 us
    all_to_all x1, blocking collectives, on_device(): lax.all_to_all(zx_shard, 'tp', split_axis=1, concat_axis=0, tiled=True)  15.9 us
  transfers between devices with their start and end apart: 8, of which 8 were waited for; matrix products, arithmetic and copies ran while one was open for 6% of the time, Pallas kernels for 0%

commit v1 on v0

--- a/solution.py
+++ b/solution.py
@@ -16,22 +16,13 @@
     return lax.ppermute(x, axis, pairs)
 
 
-def prefix(part, axis, combine, identity):
-    place = lax.axis_index(axis)
-    gathered = jax.tree.map(lambda a: lax.all_gather(a, axis), part)
-    state = jax.tree.map(lambda a, e: jnp.zeros_like(a) + jnp.asarray(e, a.dtype), part, identity)
-
-    def one(step, state):
-        return combine(
-            state, jax.tree.map(lambda a: lax.dynamic_index_in_dim(a, step, 0, False), gathered)
-        )
-
-    return lax.fori_loop(0, place, one, state)
-
-
 def segment_of(position, lengths):
     prompt_ends = jnp.cumsum(lengths)
     return jnp.sum((position[:, None] >= prompt_ends[None, :]).astype(jnp.int32), axis=1)
+
+
+def round_up(n, m):
+    return (n + m - 1) // m * m
 
 
 def on_device(
@@ -52,48 +43,44 @@
     request_group,
 ):
     tp_count = lax.axis_size("tp")
+    seq_count = lax.axis_size("seq")
+    seq_index = lax.axis_index("seq")
     tok_dev = tokens.shape[0]
     local_rows = w_zx.shape[0]
     inner_local = conv_x_weight.shape[1]
     heads_local = dt_bias.shape[0]
     head_width = inner_local // heads_local
-    state_width = conv_bc_weight.shape[1] // 2
+    bc_width = conv_bc_weight.shape[1]
+    state_width = bc_width // 2
     taps = conv_x_weight.shape[0]
     groups_dev = tok_dev // GROUP
-    zx_shard = w_zx.astype(jnp.bfloat16).reshape(local_rows, 2, tp_count, inner_local)
-    zx_shard = zx_shard.transpose(0, 2, 1, 3).reshape(local_rows, tp_count * 2 * inner_local)
-    dt_shard = w_dt.astype(jnp.bfloat16)
-    zx_block, dt_block = (
-        lax.all_to_all(zx_shard, "tp", split_axis=1, concat_axis=0, tiled=True),
-        lax.all_to_all(dt_shard, "tp", split_axis=1, concat_axis=0, tiled=True),
-    )
-    columns = tokens
-    zx_sum = jnp.dot(
-        columns,
-        lax.all_gather(zx_block, "seq", axis=0, tiled=True),
-        preferred_element_type=jnp.float32,
-    )
-    dt_pre = jnp.dot(
-        columns,
-        lax.all_gather(dt_block, "seq", axis=0, tiled=True),
-        preferred_element_type=jnp.float32,
-    )
-    zx_low = zx_sum.astype(jnp.bfloat16)
+
+    zx_part = w_zx.astype(jnp.bfloat16).reshape(local_rows, 2, tp_count, inner_local)
+    zx_part = zx_part.transpose(0, 2, 1, 3).reshape(local_rows, tp_count, 2 * inner_local)
+    bc_part = jnp.broadcast_to(
+        w_bc.astype(jnp.bfloat16)[:, None, :], (local_rows, tp_count, bc_width)
+    )
+    dt_part = w_dt.astype(jnp.bfloat16).reshape(local_rows, tp_count, heads_local)
+    used = 2 * inner_local + bc_width + heads_local
+    width = round_up(used, 128)
+    pad_part = jnp.zeros((local_rows, tp_count, width - used), jnp.bfloat16)
+    packed = jnp.concatenate([zx_part, bc_part, dt_part, pad_part], axis=2)
+    packed = packed.reshape(local_rows, tp_count * width)
+    block = lax.all_to_all(packed, "tp", split_axis=1, concat_axis=0, tiled=True)
+    weights = lax.all_gather(block, "seq", axis=0, tiled=True)
+    proj = jnp.dot(tokens, weights, preferred_element_type=jnp.float32)
+    zx_low = proj[:, : 2 * inner_local].astype(jnp.bfloat16)
     gate_z = zx_low[:, :inner_local]
     x_raw = zx_low[:, inner_local:]
-    columns = tokens
-    bc_sum = jnp.dot(
-        columns,
-        lax.all_gather(w_bc.astype(jnp.bfloat16), ("seq", "tp"), axis=0, tiled=True),
-        preferred_element_type=jnp.float32,
-    )
-    bc_raw = bc_sum.astype(jnp.bfloat16)
+    bc_raw = proj[:, 2 * inner_local : 2 * inner_local + bc_width].astype(jnp.bfloat16)
+    dt_pre = proj[:, 2 * inner_local + bc_width : used]
+
     raw_mix = jnp.concatenate([x_raw, bc_raw], axis=1)
     conv_weight = jnp.concatenate([conv_x_weight, conv_bc_weight], axis=1)
     conv_bias = jnp.concatenate([conv_x_bias, conv_bc_bias], axis=0)
     rim_rows = from_behind(raw_mix[tok_dev - (taps - 1) :], "seq", 1)
     padded = jnp.concatenate([rim_rows, raw_mix], axis=0)
-    offset = lax.axis_index("seq") * tok_dev
+    offset = seq_index * tok_dev
     seg_pad = segment_of(
         offset - (taps - 1) + jnp.arange(tok_dev + taps - 1, dtype=jnp.int32), lengths
     )
@@ -153,20 +140,41 @@
         return (next_state, (carry_state, next_state))
 
     zero_state = jnp.zeros((heads_local, head_width, state_width), jnp.float32)
-    dev_state, (local_in, local_end) = lax.scan(local_step, zero_state, (pass_gate, contrib))
+    _, (local_in, local_end) = lax.scan(local_step, zero_state, (pass_gate, contrib))
     through_group = jnp.cumprod(pass_gate, axis=0)
     before_group = jnp.concatenate(
         [jnp.ones((1, heads_local), jnp.float32), through_group[:-1]], axis=0
     )
-    dev_decay = through_group[-1]
-
-    def combine(earlier, later_one):
-        return (earlier[0] * later_one[0], later_one[0][:, None, None] * earlier[1] + later_one[1])
-
-    identity = (jnp.ones((heads_local,), jnp.float32), zero_state)
-    _, carried = prefix((dev_decay, dev_state), "seq", combine, identity)
+
+    gate_hi = through_group.astype(jnp.bfloat16)
+    gate_lo = (through_group - gate_hi.astype(jnp.float32)).astype(jnp.bfloat16)
+    extra = jnp.zeros((groups_dev, heads_local, 8, state_width), jnp.bfloat16)
+    extra = extra.at[:, :, 0, :].set(jnp.broadcast_to(gate_hi[:, :, None], gate_hi.shape + (state_width,)))
+    extra = extra.at[:, :, 1, :].set(jnp.broadcast_to(gate_lo[:, :, None], gate_lo.shape + (state_width,)))
+    sendable = jnp.concatenate([local_end.astype(jnp.bfloat16), extra], axis=2)
+    every = lax.all_gather(sendable, "seq", axis=0, tiled=False)
+    every_end = every[:, :, :, :head_width].astype(jnp.float32)
+    every_gate = (
+        every[:, :, :, head_width, 0].astype(jnp.float32)
+        + every[:, :, :, head_width + 1, 0].astype(jnp.float32)
+    )
+    dev_gate = every_gate[:, -1]
+    dev_ids = jnp.arange(seq_count, dtype=jnp.int32)
+
+    def carry_weights(k):
+        between = (dev_ids[:, None] < dev_ids[None, :]) & (dev_ids[None, :] < k)
+        factors = jnp.where(between[:, :, None], dev_gate[None, :, :], 1.0)
+        return jnp.where((dev_ids < k)[:, None], jnp.prod(factors, axis=1), 0.0)
+
+    own_weights = carry_weights(seq_index)
+    slot_ids = jnp.arange(groups_dev, dtype=jnp.int32)
+    last_slot = (slot_ids == groups_dev - 1).astype(jnp.float32)
+    own_coef = own_weights[:, None, :] * last_slot[None, :, None]
+    carried = jnp.einsum(
+        "jch,jchpn->hpn", own_coef, every_end, precision=lax.Precision.HIGHEST,
+        preferred_element_type=jnp.float32,
+    )
     group_in = before_group[:, :, None, None] * carried[None] + local_in
-    group_end = through_group[:, :, None, None] * carried[None] + local_end
     state_low = group_in.astype(jnp.bfloat16)
     carry_keep = jnp.where((segments == seg_before[:, None])[:, None, :], jnp.exp(cumul_heads), 0.0)
     carry_out = jnp.einsum(
@@ -176,29 +184,35 @@
     y_local = diag_out + carry_out + skip[None, None, :, None] * inputs.astype(jnp.float32)
     y_local = y_local.reshape(tok_dev, inner_local)
     gated = y_local * jax.nn.silu(gate_z.astype(jnp.float32))
-    square_sum = lax.psum(jnp.sum(gated * gated, axis=1), "tp")
-    normed = (
-        gated * lax.rsqrt(square_sum / INNER + epsilon)[:, None] * norm_weight[None, :]
-    ).astype(jnp.bfloat16)
+    square_sum = jnp.sum(gated * gated, axis=1)
+    scaled = (gated * norm_weight[None, :]).astype(jnp.bfloat16)
     out_shard = w_out.astype(jnp.bfloat16)
     out_block = lax.all_gather(out_shard, "seq", axis=1, tiled=True)
-    mixed = lax.psum_scatter(
-        jnp.dot(normed, out_block, preferred_element_type=jnp.float32),
-        "tp",
-        scatter_dimension=0,
-        tiled=True,
-    ).astype(jnp.bfloat16)
-    group_ids = lax.axis_index("seq") * groups_dev + jnp.arange(groups_dev, dtype=jnp.int32)
-    selector = (request_group[:, None] == group_ids[None, :]).astype(jnp.float32)
-    flat_end = group_end.reshape(groups_dev, heads_local * head_width * state_width)
-    picked = jnp.dot(
-        selector, flat_end, precision=lax.Precision.HIGHEST, preferred_element_type=jnp.float32
-    )
-    picked = picked.reshape(request_group.shape[0], heads_local, head_width, state_width)
-    request_states = lax.psum_scatter(
-        picked.astype(jnp.bfloat16), "seq", scatter_dimension=0, tiled=True
-    ).astype(jnp.float32)
-    return (mixed, request_states)
+    partial = jnp.dot(scaled, out_block, preferred_element_type=jnp.float32)
+    side = jnp.zeros((tok_dev, 128), jnp.float32).at[:, 0].set(square_sum)
+    summed = lax.psum_scatter(
+        jnp.concatenate([partial, side], axis=1), "tp", scatter_dimension=0, tiled=True
+    )
+    d_model = out_block.shape[1]
+    mean_square = summed[:, d_model] / INNER
+    mixed = (summed[:, :d_model] * lax.rsqrt(mean_square + epsilon)[:, None]).astype(jnp.bfloat16)
+
+    req_dev = request_group.shape[0] // seq_count
+    mine = lax.dynamic_slice_in_dim(request_group, seq_index * req_dev, req_dev)
+    req_k = mine // groups_dev
+    req_c = mine % groups_dev
+    req_w = jax.vmap(carry_weights)(req_k)
+    req_gate = every_gate[req_k, req_c]
+    coef = req_gate[:, None, None, :] * req_w[:, :, None, :] * last_slot[None, None, :, None]
+    hit = (dev_ids[None, :, None] == req_k[:, None, None]) & (
+        slot_ids[None, None, :] == req_c[:, None, None]
+    )
+    coef = coef + hit[:, :, :, None].astype(jnp.float32)
+    request_states = jnp.einsum(
+        "rjch,jchpn->rhpn", coef, every_end, precision=lax.Precision.HIGHEST,
+        preferred_element_type=jnp.float32,
+    )
+    return (mixed.astype(jnp.bfloat16), request_states)
 
 
 def solution(mesh):

time: 627 us -> 280 us (0.45)
  waiting for transfers between devices: 458 us -> 166 us
  blocking collectives: 78.7 us -> 17.1 us
    all_gather x3 -> x2, waiting for transfers between devices: 292 us -> 67.8 us  [the longest x1 36.8 us: on_device(): weights = lax.all_gather(block, 'seq', axis=0, tiled=True)]
    reduce_scatter x2 -> x1, waiting for transfers between devices: 153 us -> 76.7 us  [on_device(): lax.psum_scatter(jnp.concatenate([partial, side], axis=1), 'tp', scatter_...]
    all_gather x2 -> x0, blocking collectives: 42.1 us -> none  [the longest x1 22.4 us: on_device(): lax.all_gather(dt_block, 'seq', axis=0, tiled=True)]
    psum x1 -> x0, blocking collectives: 20.8 us -> none  [on_device(): square_sum = lax.psum(jnp.sum(gated * gated, axis=1), 'tp')]
    all_gather x1, waiting for transfers between devices: 7.11 us -> 21.8 us  [on_device(): out_block = lax.all_gather(out_shard, 'seq', axis=1, tiled=True)]
    slice x3 -> x4, local copies, waits for them, and re-layouts: 0.21 us -> 8.94 us  [the longest x1 5.76 us: on_device(): every_end = every[:, :, :, :head_width].astype(jnp.float32)]
    dot_general x5 -> x4, matrix products: 16.3 us -> 22.1 us  [the longest x1 6.92 us: on_device(): proj = jnp.dot(tokens, weights, preferred_element_type=jnp.float32)]
  transfers between devices with their start and end apart: 8 -> 5, of which waited for: 8 -> 4; matrix products, arithmetic and copies ran while one was open for 6% -> 15% of each run, Pallas kernels for 0% -> 0%
where the time goes in v1:
time: 280 us; the launch traced here: 278 us
  waiting for transfers between devices  166 us (59%)
  matrix products  28.2 us (10%)
  other arithmetic  25.1 us (9%)
  local copies, waits for them, and re-layouts  24.3 us (9%)
  blocking collectives  17.1 us (6%)
  between operations  14.3 us (5%)
  starting transfers between devices  3.01 us (1%)
    reduce_scatter x1, waiting for transfers between devices, on_device(): lax.psum_scatter(jnp.concatenate([partial, side], axis=1), 'tp', scatter_...  76.7 us
    all_gather x1, waiting for transfers between devices, on_device(): weights = lax.all_gather(block, 'seq', axis=0, tiled=True)  36.8 us
    all_gather x1, waiting for transfers between devices, on_device(): every = lax.all_gather(sendable, 'seq', axis=0, tiled=False)  31 us
    all_gather x1, waiting for transfers between devices, on_device(): out_block = lax.all_gather(out_shard, 'seq', axis=1, tiled=True)  21.8 us
    all_to_all x1, blocking collectives, on_device(): lax.all_to_all(packed, 'tp', split_axis=1, concat_axis=0, tiled=True)  17.1 us
    dot_general x1, matrix products, on_device(): proj = jnp.dot(tokens, weights, preferred_element_type=jnp.float32)  6.92 us
    dot_general x1, matrix products, on_device(): jnp.einsum('jch,jchpn->hpn', own_coef, every_end, precision=lax.Precision...  6.27 us
    dot_general x1, matrix products, on_device(): jnp.einsum('rjch,jchpn->rhpn', coef, every_end, precision=lax.Precision.H...  5.76 us
  transfers between devices with their start and end apart: 5, of which 4 were waited for; matrix products, arithmetic and copies ran while one was open for 15% of the time, Pallas kernels for 0%

profile of v1, /device:TPU:1, one launch (start us, length us, event | category | flops | bytes accessed | tf_op | source)
XLA Modules:
  0.0 278.2 jit_solution(9809869660556258186)
XLA Ops:
  7.3 1.2 convert_element_type.121
  9.3 17.1 %all_to_all.16 = bf16[16,8,1408]{2,0,1:T(8,128)(2,1)} all-to-all(bf16[16,8,1408]{2,0,1:T(8,128)(2,1)S(1)} %concatenate.34), channel_id=1, replica_groups=mesh['seq'=16,'tp'=8] {'tp'}, dimensions={1} | all-to-all | bytes 720896 | tf_op jit(solution)/shard_map/all_to_all | solution.py:69
  28.2 0.6 slice_reduce_fusion.5
  28.9 0.7 slice_compare_fusion.2
  29.6 36.8 %all-gather.5.cloned.1.call-done = bf16[2048,1408]{1,0:T(8,128)(2,1)} async-done(((bf16[128,1408]{1,0:T(8,128)(2,1)}), bf16[2048,1408]{1,0:T(8,128)(2,1)}) %all-gather.5.cloned.1.call-update) | async-done | bytes 5767184 | tf_op jit(solution)/shard_map/all_gather | solution.py:70
  66.4 6.9 %fusion.59 = (bf16[512,1408]{0,1:T(8,128)(2,1)}, f32[512,1408]{0,1:T(8,128)S(1)}) fusion(bf16[2048,1408]{1,0:T(8,128)(2,1)} %all-gather.5.cloned.1.call-done, bf16[512,2048]{1,0:T(8,128)(2,1)S(1)} %copy-done), kind=kOutput, calls=%fused_computation.139 | convolution fusion | flops 2953510912 | bytes 12189696 | tf_op jit(solution)/shard_map/dot_general | solution.py:71
  73.5 1.1 reduce-window.19
  74.8 0.7 select_bitcast_fusion
  75.7 1.0 slice.194
  76.7 2.8 %collective-permute-start = (bf16[3,768]{0,1:T(8,128)(2,1)S(1)}, bf16[3,768]{0,1:T(8,128)(2,1)S(1)}, u32[]{:S(2)}, u32[]{:S(2)}) collective-permute-start(bf16[3,768]{0,1:T(8,128)(2,1)S(1)} %slice.194), channel_id=1, source_target_pairs={{0,8},{8,16},{16,24},{24,32},{32,40},{40,48},{48,56},{56,64},{64,7... | collective-permute-start | bytes 13832 | tf_op jit(solution)/shard_map/ppermute | solution.py:16
  79.6 0.7 select_multiply_fusion.1
  80.9 1.2 slice.195
  82.2 0.6 scatter.10
  82.8 0.7 broadcast.361
  83.5 1.4 scatter.11
  84.9 2.9 %multiply_convert_fusion.3 = bf16[512,768]{0,1:T(8,128)(2,1)S(1)} fusion(bf16[512,768]{0,1:T(8,128)(2,1)S(1)} %slice.195, bf16[3,768]{0,1:T(8,128)(2,1)S(1)} %collective-permute-done, f32[768]{0:T(1024)} %get-tuple-element.107, f32[768]{0:T(1024)} %get-tuple-element.108, f32[768]{0:T(1024)} %get-tuple-element.109, f32[768]{0:T(1024)} %get-tuple-element.106, ...), kind=kLoop, calls=%fused_computation.22 | loop fusion | flops 11403264 | bytes 1594368 | tf_op jit(solution)/shard_map/convert_element_type | solution.py:95
  87.9 0.7 fusion.58
  88.7 0.9 reshape.461
  89.6 0.8 copy.120
  90.4 2.0 fusion.22
  92.4 5.0 %while.18 = (s32[]{:T(128)}, f32[8,64,128]{2,1,0:T(8,128)S(1)}, f32[2,8,64,128]{3,2,1,0:T(8,128)}, bf16[2,8,64,128]{3,2,1,0:T(8,128)(2,1)}, f32[2,8]{1,0:T(2,128...) while((s32[]{:T(128)}, f32[8,64,128]{2,1,0:T(8,128)S(1)}, ...), condition=%wide.region_7.8_spmd.clone, body=%wide.region_6.7_spmd.clone.sunk | while | flops 196611 | bytes 1311907 | solution.py:143
  92.4 1.2 fusion.65
  93.5 1.3 bitcast_dynamic-update-slice_fusion.3
  94.9 1.1 fusion.65
  96.0 1.3 bitcast_dynamic-update-slice_fusion.3
  97.4 1.7 pad_maximum_fusion.1
  99.2 1.6 convert_element_type.144
  100.9 0.6 compare_reduce_fusion
  101.6 0.9 compare_and_fusion
  102.5 0.7 slice.182
  103.2 1.2 fusion.34
  104.4 2.5 fusion.12
  106.9 31.0 %all-gather.9.cloned.1.call-done = bf16[32,8,72,128]{3,2,1,0:T(8,128)(2,1)} async-done(((bf16[2,8,72,128]{3,2,1,0:T(8,128)(2,1)}), bf16[32,8,72,128]{3,2,1,0:T(8,128)(2,1)}) %all-gather.9.cloned.1.call-update) | async-done | bytes 4718608 | tf_op jit(solution)/shard_map/all_gather | solution.py:155
  137.9 5.8 %slice.215 = bf16[16,2,8,64,128]{4,3,2,1,0:T(8,128)(2,1)} slice(bf16[16,2,8,72,128]{4,3,2,1,0:T(8,128)(2,1)} %bitcast.91), slice={[0:16], [0:2], [0:8], [0:64], [0:128]} | slice | bytes 8388608 | tf_op jit(solution)/shard_map/slice | solution.py:156
  143.6 1.5 fusion.57
  146.1 6.3 %fusion.3 = f32[8,1,64,128,1]{3,1,4,2,0:T(1,128)S(1)} fusion(f32[16,2,8,1,1]{0,3,1,4,2:T(1,128)S(1)} %copy.133, bf16[16,2,8,64,128]{4,3,2,1,0:T(8,128)(2,1)} %slice.215), kind=kOutput, calls=%fused_computation.11 | convolution fusion | flops 25165824 | bytes 4457472 | tf_op jit(solution)/shard_map/jch,jchpn->hpn/dot_general | solution.py:173
  152.8 0.8 copy.127
  153.7 1.4 multiply_reduce_fusion
  155.9 21.8 %all-gather.7.cloned.1.call-done = bf16[512,2048]{1,0:T(8,128)(2,1)} async-done(((bf16[512,128]{1,0:T(8,128)(2,1)}), bf16[512,2048]{1,0:T(8,128)(2,1)}) %all-gather.7.cloned.1.call-update) | async-done | bytes 2097168 | tf_op jit(solution)/shard_map/all_gather | solution.py:190
  177.6 3.2 %fusion.27 = f32[512,2048]{1,0:T(8,128)S(1)} fusion(bf16[512,2048]{1,0:T(8,128)(2,1)} %all-gather.7.cloned.1.call-done, f32[512]{0:T(512)S(1)} %copy-done.18, f32[512,512]{0,1:T(8,128)S(1)} %bitcast.94, bf16[512,1408]{0,1:T(8,128)(2,1)} %get-tuple-element.143), kind=kOutput, calls=%fused_computation.46 | convolution fusion | flops 1075838976 | bytes 7866368 | tf_op jit(solution)/shard_map/dot_general | solution.py:191
  180.8 2.4 select_maximum_fusion
  183.2 0.6 copy-done.17
  184.8 0.6 select_reduce_fusion
  185.6 5.8 %fusion.15 = f32[2,8,64,128]{3,0,2,1:T(2,128)S(1)} fusion(bf16[16,2,8,64,128]{4,3,2,1,0:T(8,128)(2,1)} %slice.215, f32[2,16,2]{1,0,2:T(2,128)S(1)} %and_convert_fusion, f32[2,16,8]{1,0,2:T(2,128)S(1)} %copy.130, f32[2]{0:T(128)S(1)} %compare_convert_fusion), kind=kOutput, calls=%fused_computation.31 | convolution fusion | flops 50332672 | bytes 4719880 | tf_op jit(solution)/shard_map/rjch,jchpn->rhpn/dot_general | solution.py:211
  191.4 0.9 copy.131
  192.2 76.7 %reduce-scatter.2.cloned.1.call-done = f32[64,2176]{1,0:T(8,128)} async-done(((f32[512,2176]{1,0:T(8,128)}), f32[64,2176]{1,0:T(8,128)}) %reduce-scatter.2.cloned.1.call-update) | async-done | bytes 557072 | tf_op jit(solution)/shard_map/reduce_scatter | solution.py:193
  268.9 0.9 fusion.42
  269.8 1.9 fusion.28
  (117 shorter events, 7.5 us)
Async XLA Ops:
  7.2 59.2 %copy-start = (bf16[512,2048]{1,0:T(8,128)(2,1)S(1)}, bf16[512,2048]{1,0:T(8,128)(2,1)}, u32[]{:S(2)}) copy-start(bf16[512,2048]{1,0:T(8,128)(2,1)} %param.23) | copy-start | bytes 6291460
  7.2 1.8 copy-start.7
  7.2 1.8 copy-start.8
  7.2 19.3 %copy-start.19 = (s32[8]{0:T(128)S(1)}, s32[8]{0:T(128)}, u32[]{:S(2)}) copy-start(s32[8]{0:T(128)} %param.36) | copy-start | bytes 100
  7.2 20.2 %copy-start.9 = (f32[4,512]{1,0:T(4,128)S(1)}, f32[4,512]{1,0:T(4,128)}, u32[]{:S(2)}) copy-start(f32[4,512]{1,0:T(4,128)} %param.27) | copy-start | bytes 24580
  7.2 20.2 %copy-start.10 = (f32[4,256]{1,0:T(4,128)S(1)}, f32[4,256]{1,0:T(4,128)}, u32[]{:S(2)}) copy-start(f32[4,256]{1,0:T(4,128)} %param.29) | copy-start | bytes 12292
  7.2 20.2 %copy-start.13 = (f32[512]{0:T(512)S(1)}, f32[512]{0:T(512)}, u32[]{:S(2)}) copy-start(f32[512]{0:T(512)} %param.28) | copy-start | bytes 6148
  7.2 20.2 %copy-start.14 = (f32[256]{0:T(256)S(1)}, f32[256]{0:T(256)}, u32[]{:S(2)}) copy-start(f32[256]{0:T(256)} %param.30) | copy-start | bytes 3076
  7.3 21.6 %copy-start.20 = (f32[8]{0:T(128)S(1)}, f32[8]{0:T(128)}, u32[]{:S(2)}) copy-start(f32[8]{0:T(128)} %param.32) | copy-start | bytes 100
  7.3 59.1 %all-gather.5.cloned.1.call-start = ((), (), s32[]{:S(2)}) async-start(), calls=%async_computation.2 | async-start | bytes 6127616 | tf_op jit(solution)/shard_map/all_gather | solution.py:70
  26.5 111.4 %all-gather.9.cloned.1.call-start = ((), (), s32[]{:S(2)}) async-start(), calls=%async_computation.5 | async-start | bytes 5013504 | tf_op jit(solution)/shard_map/all_gather | solution.py:155
  26.9 46.4 %copy-start.6 = (s32[2,256]{1,0:T(2,128)}, s32[2,256]{1,0:T(2,128)S(1)}, u32[]{:S(2)}) copy-start(s32[2,256]{1,0:T(2,128)S(1)} %eq.111) | copy-start | bytes 6148
  29.6 43.7 %copy-start.15 = (f32[8]{0:T(128)S(1)}, f32[8]{0:T(128)}, u32[]{:S(2)}) copy-start(f32[8]{0:T(128)} %param.31) | copy-start | bytes 100
  75.5 4.9 %copy-start.3 = (f32[2,8,256]{2,1,0:T(8,128)}, f32[2,8,256]{2,1,0:T(8,128)S(1)}, u32[]{:S(2)}) copy-start(f32[2,8,256]{2,1,0:T(8,128)S(1)} %get-tuple-element.130) | copy-start | bytes 49156
  76.7 8.2 %collective-permute-start = (bf16[3,768]{0,1:T(8,128)(2,1)S(1)}, bf16[3,768]{0,1:T(8,128)(2,1)S(1)}, u32[]{:S(2)}, u32[]{:S(2)}) collective-permute-start(bf16[3,768]{0,1:T(8,128)(2,1)S(1)} %slice.194), channel_id=1, source_target_pairs={{0,8},{8,16},{16,24},{24,32},{32,40},{40,48},{48,56},{56,64},{64,7... | collective-permute-start | bytes 13832 | tf_op jit(solution)/shard_map/ppermute | solution.py:16
  79.6 0.7 copy-start.12
  80.4 0.6 copy-start.11
  97.4 7.0 %copy-start.4 = (f32[2,8,256]{2,1,0:T(8,128)S(1)}, f32[2,8,256]{2,1,0:T(8,128)}, u32[]{:S(2)}) copy-start(f32[2,8,256]{2,1,0:T(8,128)} %copy-done.3) | copy-start | bytes 49156
  99.1 78.5 %all-gather.7.cloned.1.call-start = ((), (), s32[]{:S(2)}) async-start(), calls=%async_computation.3 | async-start | bytes 2228224 | tf_op jit(solution)/shard_map/all_gather | solution.py:190
  100.8 168.1 %reduce-scatter.2.cloned.1.call-start = ((), (), s32[]{:S(2)}) async-start(), calls=%async_computation.4 | async-start | bytes 5013504 | tf_op jit(solution)/shard_map/reduce_scatter | solution.py:193
  146.1 6.3 %copy-start.1 = (f32[2,256,8,64]{1,3,2,0:T(8,128)S(1)}, f32[2,256,8,64]{1,3,2,0:T(8,128)}, u32[]{:S(2)}) copy-start(f32[2,256,8,64]{1,3,2,0:T(8,128)} %fusion.12) | copy-start | bytes 3145732
  146.1 6.3 %copy-start.2 = (f32[2,8,64,128]{3,2,1,0:T(8,128)S(1)}, f32[2,8,64,128]{3,2,1,0:T(8,128)}, u32[]{:S(2)}) copy-start(f32[2,8,64,128]{3,2,1,0:T(8,128)} %get-tuple-element.72) | copy-start | bytes 1572868
  146.1 6.3 %copy-start.5 = (f32[2,256,8]{1,2,0:T(8,128)S(1)}, f32[2,256,8]{1,2,0:T(8,128)}, u32[]{:S(2)}) copy-start(f32[2,256,8]{1,2,0:T(8,128)} %get-tuple-element.129) | copy-start | bytes 49156
  146.1 6.3 %copy-start.16 = (f32[8]{0:T(128)S(1)}, f32[8]{0:T(128)}, u32[]{:S(2)}) copy-start(f32[8]{0:T(128)} %param.33) | copy-start | bytes 100
  153.6 24.0 %copy-start.18 = (f32[512]{0:T(512)S(1)}, f32[512]{0:T(512)}, u32[]{:S(2)}) copy-start(f32[512]{0:T(512)} %param.34) | copy-start | bytes 6148
  183.2 0.7 copy-start.17
Sparse Core Ops, SparseCore 0:
  26.6 39.7 all-gather.4
  99.2 38.5 all-gather.8
  140.1 37.5 all-gather.6
  183.4 85.5 reduce-scatter.1

commit v2 on v1

--- a/solution.py
+++ b/solution.py
@@ -67,7 +67,15 @@
     packed = jnp.concatenate([zx_part, bc_part, dt_part, pad_part], axis=2)
     packed = packed.reshape(local_rows, tp_count * width)
     block = lax.all_to_all(packed, "tp", split_axis=1, concat_axis=0, tiled=True)
-    weights = lax.all_gather(block, "seq", axis=0, tiled=True)
+    out_rows, out_cols = w_out.shape
+    block_rows = block.shape[0]
+    out_piece = w_out.astype(jnp.bfloat16).reshape(block_rows, out_rows * out_cols // block_rows)
+    gathered = lax.all_gather(
+        jnp.concatenate([block, out_piece], axis=1), "seq", axis=0, tiled=True
+    )
+    weights = gathered[:, :width]
+    out_block = gathered[:, width:].reshape(seq_count, out_rows, out_cols)
+    out_block = out_block.transpose(1, 0, 2).reshape(out_rows, seq_count * out_cols)
     proj = jnp.dot(tokens, weights, preferred_element_type=jnp.float32)
     zx_low = proj[:, : 2 * inner_local].astype(jnp.bfloat16)
     gate_z = zx_low[:, :inner_local]
@@ -186,13 +194,14 @@
     gated = y_local * jax.nn.silu(gate_z.astype(jnp.float32))
     square_sum = jnp.sum(gated * gated, axis=1)
     scaled = (gated * norm_weight[None, :]).astype(jnp.bfloat16)
-    out_shard = w_out.astype(jnp.bfloat16)
-    out_block = lax.all_gather(out_shard, "seq", axis=1, tiled=True)
     partial = jnp.dot(scaled, out_block, preferred_element_type=jnp.float32)
     side = jnp.zeros((tok_dev, 128), jnp.float32).at[:, 0].set(square_sum)
     summed = lax.psum_scatter(
-        jnp.concatenate([partial, side], axis=1), "tp", scatter_dimension=0, tiled=True
-    )
+        jnp.concatenate([partial, side], axis=1).astype(jnp.bfloat16),
+        "tp",
+        scatter_dimension=0,
+        tiled=True,
+    ).astype(jnp.float32)
     d_model = out_block.shape[1]
     mean_square = summed[:, d_model] / INNER
     mixed = (summed[:, :d_model] * lax.rsqrt(mean_square + epsilon)[:, None]).astype(jnp.bfloat16)

time: 280 us -> 254 us (0.907)
  waiting for transfers between devices: 166 us -> 141 us
  blocking collectives: 17.1 us -> 0 us
  local copies, waits for them, and re-layouts: 24.3 us -> 36 us
  starting transfers between devices: 3.01 us -> 11.5 us
    all_to_all x1 -> x0, blocking collectives: 17.1 us -> none  [on_device(): lax.all_to_all(packed, 'tp', split_axis=1, concat_axis=0, tiled=True)]
    all_gather x2 -> x1, waiting for transfers between devices: 58.6 us -> 45.1 us  [on_device(): lax.all_gather(jnp.concatenate([block, out_piece], axis=1), 'seq', axis=0...]
    all_gather x1, waiting for transfers between devices: 31 us -> 20 us  [on_device(): every = lax.all_gather(sendable, 'seq', axis=0, tiled=False)]
    reduce_scatter x1, waiting for transfers between devices: 76.7 us -> 66.3 us  [on_device(): lax.psum_scatter(jnp.concatenate([partial, side], axis=1).astype(jnp.bflo...]
    all_to_all x0 -> x1, waiting for transfers between devices: none -> 9.54 us  [on_device(): lax.all_to_all(packed, 'tp', split_axis=1, concat_axis=0, tiled=True)]
    reshape x0 -> x3, local copies, waits for them, and re-layouts: none -> 8.41 us  [the longest x2 8.32 us: on_device(): out_block = gathered[:, width:].reshape(seq_count, out_rows, out_cols)]
    all_to_all x0 -> x1, starting transfers between devices: none -> 8.16 us  [on_device(): lax.all_to_all(packed, 'tp', split_axis=1, concat_axis=0, tiled=True)]
    slice x0 -> x1, local copies, waits for them, and re-layouts: none -> 3.09 us  [on_device(): out_block = gathered[:, width:].reshape(seq_count, out_rows, out_cols)]
  transfers between devices with their start and end apart: 5 -> 5, of which waited for: 4 -> 4; matrix products, arithmetic and copies ran while one was open for 15% -> 14% of each run, Pallas kernels for 0% -> 0%
where the time goes in v2:
time: 254 us; the launch traced here: 252 us
  waiting for transfers between devices  141 us (56%)
  local copies, waits for them, and re-layouts  36 us (14%)
  matrix products  26.6 us (10%)
  other arithmetic  23.1 us (9%)
  between operations  14.3 us (6%)
  starting transfers between devices  11.5 us (5%)
    reduce_scatter x1, waiting for transfers between devices, on_device(): lax.psum_scatter(jnp.concatenate([partial, side], axis=1).astype(jnp.bflo...  66.3 us
    all_gather x1, waiting for transfers between devices, on_device(): lax.all_gather(jnp.concatenate([block, out_piece], axis=1), 'seq', axis=0...  45.1 us
    all_gather x1, waiting for transfers between devices, on_device(): every = lax.all_gather(sendable, 'seq', axis=0, tiled=False)  20 us
    all_to_all x1, waiting for transfers between devices, on_device(): lax.all_to_all(packed, 'tp', split_axis=1, concat_axis=0, tiled=True)  9.54 us
    reshape x2, local copies, waits for them, and re-layouts, on_device(): out_block = gathered[:, width:].reshape(seq_count, out_rows, out_cols)  8.32 us
    all_to_all x1, starting transfers between devices, on_device(): lax.all_to_all(packed, 'tp', split_axis=1, concat_axis=0, tiled=True)  8.16 us
    dot_general x1, matrix products, on_device(): proj = jnp.dot(tokens, weights, preferred_element_type=jnp.float32)  7.02 us
    dot_general x1, matrix products, on_device(): jnp.einsum('jch,jchpn->hpn', own_coef, every_end, precision=lax.Precision...  6.27 us
  transfers between devices with their start and end apart: 5, of which 4 were waited for; matrix products, arithmetic and copies ran while one was open for 14% of the time, Pallas kernels for 0%

profile of v2, /device:TPU:1, one launch (start us, length us, event | category | flops | bytes accessed | tf_op | source)
XLA Modules:
  0.0 252.4 jit_solution(9752416855945971542)
XLA Ops:
  7.2 0.9 convert_element_type.126
  8.1 0.8 copy.117
  9.0 1.1 convert_element_type.125
  10.6 0.8 concatenate.38
  11.4 8.2 %all-to-all-start = ((bf16[16,8,1408]{2,0,1:T(8,128)(2,1)}), bf16[16,8,1408]{2,0,1:T(8,128)(2,1)S(1)}, u32[]{:S(2)}, u32[]{:S(2)}) async-start(bf16[16,8,1408]{2,0,1:T(8,128)(2,1)} %concatenate.38), calls=%async_computation | async-start | bytes 720896 | tf_op jit(solution)/shard_map/all_to_all | solution.py:69
  19.8 9.5 %all-to-all-done = bf16[16,8,1408]{2,0,1:T(8,128)(2,1)S(1)} async-done(((bf16[16,8,1408]{2,0,1:T(8,128)(2,1)}), bf16[16,8,1408]{2,0,1:T(8,128)(2,1)S(1)}, u32[]{:S(2)}, u32[]{:S(2)}) %all-to-all-start) | async-done | bytes 360480 | tf_op jit(solution)/shard_map/all_to_all | solution.py:69
  29.3 0.8 pad_maximum_fusion.1
  31.9 0.6 slice_reduce_fusion.5
  33.2 45.1 %all-gather.4.cloned.1.call-done = bf16[2048,1920]{1,0:T(8,128)(2,1)} async-done(((bf16[128,1920]{1,0:T(8,128)(2,1)}), bf16[2048,1920]{1,0:T(8,128)(2,1)}) %all-gather.4.cloned.1.call-update) | async-done | bytes 7864336 | tf_op jit(solution)/shard_map/all_gather | solution.py:73
  78.3 7.0 %fusion.65 = (bf16[512,1408]{0,1:T(8,128)(2,1)}, f32[512,1408]{0,1:T(8,128)S(1)}) fusion(bf16[512,2048]{1,0:T(8,128)(2,1)S(1)} %copy-done, bf16[2048,1920]{1,0:T(8,128)(2,1)} %all-gather.4.cloned.1.call-done), kind=kOutput, calls=%fused_computation.143 | convolution fusion | flops 2953510912 | bytes 12189696 | tf_op jit(solution)/shard_map/dot_general | solution.py:79
  85.5 1.1 reduce-window.19
  86.9 0.7 select_bitcast_fusion
  87.7 1.0 slice.203
  88.8 3.3 %collective-permute-start = (bf16[3,768]{0,1:T(8,128)(2,1)S(1)}, bf16[3,768]{0,1:T(8,128)(2,1)S(1)}, u32[]{:S(2)}, u32[]{:S(2)}) collective-permute-start(bf16[3,768]{0,1:T(8,128)(2,1)S(1)} %slice.203), channel_id=1, source_target_pairs={{0,8},{8,16},{16,24},{24,32},{32,40},{40,48},{48,56},{56,64},{64,7... | collective-permute-start | bytes 13832 | tf_op jit(solution)/shard_map/ppermute | solution.py:16
  92.1 0.7 select_multiply_fusion.1
  92.8 1.2 slice.204
  94.7 0.7 broadcast.361
  95.4 1.4 scatter.11
  96.8 2.9 %multiply_convert_fusion.3 = bf16[512,768]{0,1:T(8,128)(2,1)S(1)} fusion(bf16[512,768]{0,1:T(8,128)(2,1)S(1)} %slice.204, bf16[3,768]{0,1:T(8,128)(2,1)S(1)} %collective-permute-done, f32[768]{0:T(1024)} %get-tuple-element.107, f32[768]{0:T(1024)} %get-tuple-element.108, f32[768]{0:T(1024)} %get-tuple-element.109, f32[768]{0:T(1024)} %get-tuple-element.106, ...), kind=kLoop, calls=%fused_computation.26 | loop fusion | flops 11403264 | bytes 1594368 | tf_op jit(solution)/shard_map/convert_element_type | solution.py:103
  99.7 0.7 fusion.64
  100.5 0.9 reshape.472
  101.5 0.8 copy.124
  102.3 2.0 fusion.29
  104.3 2.9 %while.18 = (s32[]{:T(128)}, f32[8,64,128]{2,1,0:T(8,128)S(1)}, f32[2,8,64,128]{3,2,1,0:T(8,128)}, bf16[2,8,64,128]{3,2,1,0:T(8,128)(2,1)}, f32[2,8]{1,0:T(2,128...) while((s32[]{:T(128)}, f32[8,64,128]{2,1,0:T(8,128)S(1)}, ...), condition=%wide.region_7.8_spmd.clone, body=%wide.region_6.7_spmd.clone.sunk | while | flops 196611 | bytes 1310927 | solution.py:151
  104.3 0.7 fusion.70
  105.0 0.8 bitcast_dynamic-update-slice_fusion.3
  105.7 0.7 fusion.70
  106.4 0.8 bitcast_dynamic-update-slice_fusion.3
  107.2 1.7 pad_maximum_fusion.2
  109.0 0.7 compare_reduce_fusion
  110.9 1.6 compare_and_fusion
  112.4 3.1 %slice.226 = bf16[2048,512]{1,0:T(8,128)(2,1)} slice(bf16[2048,1920]{1,0:T(8,128)(2,1)} %all-gather.4.cloned.1.call-done), slice={[0:2048], [1408:1920]} | slice | bytes 4194304 | tf_op jit(solution)/shard_map/slice | solution.py:77
  115.5 4.3 %reshape.474 = bf16[16,512,128]{2,1,0:T(8,128)(2,1)} reshape(bf16[2048,512]{1,0:T(8,128)(2,1)} %slice.226) | data formatting | bytes 4194304 | tf_op jit(solution)/shard_map/reshape | solution.py:77
  119.9 4.0 %copy.132 = bf16[16,512,128]{1,2,0:T(8,128)(2,1)} copy(bf16[16,512,128]{2,1,0:T(8,128)(2,1)} %reshape.474) | data formatting | bytes 4194304 | tf_op jit(solution)/shard_map/reshape | solution.py:77
  124.8 3.3 %fusion.19 = f32[2,256,8,64]{1,3,2,0:T(8,128)} fusion(f32[2,8,256]{2,1,0:T(8,128)S(1)} %bitcast.108, f32[2,256,256]{2,1,0:T(8,128)S(1)} %fusion.40, f32[2,8,256]{2,1,0:T(8,128)} %copy-done.7, pred[2,256,256]{2,1,0:T(8,128)(4,1)} %compare_and_fusion, bf16[2,256,8,64]{1,0,3,2:T(2,128)(2,1)S(1)} %reshape.467), kind=kOutput, calls=%fused_computation.27 | convolution fusion | flops 140509184 | bytes 2260992 | tf_op jit(solution)/shard_map/chij,cjhp->cihp/dot_general | solution.py:125
  128.1 20.0 %all-gather.6.cloned.1.call-done = bf16[32,8,72,128]{3,2,1,0:T(8,128)(2,1)} async-done(((bf16[2,8,72,128]{3,2,1,0:T(8,128)(2,1)}), bf16[32,8,72,128]{3,2,1,0:T(8,128)(2,1)}) %all-gather.6.cloned.1.call-update) | async-done | bytes 4718608 | tf_op jit(solution)/shard_map/all_gather | solution.py:163
  148.1 1.5 fusion.63
  149.6 5.7 %slice.224 = bf16[16,2,8,64,128]{4,3,2,1,0:T(8,128)(2,1)} slice(bf16[16,2,8,72,128]{4,3,2,1,0:T(8,128)(2,1)} %bitcast.93), slice={[0:16], [0:2], [0:8], [0:64], [0:128]} | slice | bytes 8388608 | tf_op jit(solution)/shard_map/slice | solution.py:164
  156.3 6.3 %fusion.6 = f32[8,1,64,128,1]{3,1,4,2,0:T(1,128)S(1)} fusion(f32[16,2,8,1,1]{0,3,1,4,2:T(1,128)S(1)} %copy.138, bf16[16,2,8,64,128]{4,3,2,1,0:T(8,128)(2,1)} %slice.224), kind=kOutput, calls=%fused_computation.13 | convolution fusion | flops 25165824 | bytes 4457472 | tf_op jit(solution)/shard_map/jch,jchpn->hpn/dot_general | solution.py:181
  163.0 0.8 copy.131
  164.8 0.6 select_convert_fusion
  165.6 1.6 convolution_convert_fusion
  167.1 1.6 fusion.11
  171.1 5.8 %fusion.22 = f32[2,8,64,128]{3,0,2,1:T(2,128)S(1)} fusion(bf16[16,2,8,64,128]{4,3,2,1,0:T(8,128)(2,1)} %slice.224, f32[2,16,2]{1,0,2:T(2,128)S(1)} %and_convert_fusion, f32[2,16,8]{1,0,2:T(2,128)S(1)} %copy.135, f32[2]{0:T(128)S(1)} %copy-done.23), kind=kOutput, calls=%fused_computation.35 | convolution fusion | flops 50332672 | bytes 4719880 | tf_op jit(solution)/shard_map/rjch,jchpn->rhpn/dot_general | solution.py:220
  176.8 0.9 copy.136
  177.7 66.3 %reduce-scatter.2.cloned.1.call-done = bf16[64,2176]{1,0:T(8,128)(2,1)} async-done(((bf16[512,2176]{1,0:T(8,128)(2,1)}), bf16[64,2176]{1,0:T(8,128)(2,1)}) %reduce-scatter.2.cloned.1.call-update) | async-done | bytes 278544 | tf_op jit(solution)/shard_map/reduce_scatter | solution.py:199
  244.0 1.0 convert_element_type.149
  245.1 0.8 fusion.34
  (134 shorter events, 11.7 us)
Async XLA Ops:
  7.2 71.2 %copy-start = (bf16[512,2048]{1,0:T(8,128)(2,1)S(1)}, bf16[512,2048]{1,0:T(8,128)(2,1)}, u32[]{:S(2)}) copy-start(bf16[512,2048]{1,0:T(8,128)(2,1)} %param.23) | copy-start | bytes 6291460
  7.2 12.5 %copy-start.6 = (f32[512,128]{1,0:T(8,128)S(1)}, f32[512,128]{1,0:T(8,128)}, u32[]{:S(2)}) copy-start(f32[512,128]{1,0:T(8,128)} %param.35) | copy-start | bytes 786436
  10.3 19.9 %copy-start.25 = (s32[8]{0:T(128)S(1)}, s32[8]{0:T(128)}, u32[]{:S(2)}) copy-start(s32[8]{0:T(128)} %param.36) | copy-start | bytes 100
  10.3 20.8 %copy-start.16 = (f32[512]{0:T(512)S(1)}, f32[512]{0:T(512)}, u32[]{:S(2)}) copy-start(f32[512]{0:T(512)} %param.28) | copy-start | bytes 6148
  10.4 20.8 %copy-start.19 = (f32[256]{0:T(256)S(1)}, f32[256]{0:T(256)}, u32[]{:S(2)}) copy-start(f32[256]{0:T(256)} %param.30) | copy-start | bytes 3076
  10.4 21.4 %copy-start.11 = (f32[4,512]{1,0:T(4,128)S(1)}, f32[4,512]{1,0:T(4,128)}, u32[]{:S(2)}) copy-start(f32[4,512]{1,0:T(4,128)} %param.27) | copy-start | bytes 24580
  10.4 21.3 %copy-start.13 = (f32[4,256]{1,0:T(4,128)S(1)}, f32[4,256]{1,0:T(4,128)}, u32[]{:S(2)}) copy-start(f32[4,256]{1,0:T(4,128)} %param.29) | copy-start | bytes 12292
  10.4 22.2 %copy-start.26 = (f32[8]{0:T(128)S(1)}, f32[8]{0:T(128)}, u32[]{:S(2)}) copy-start(f32[8]{0:T(128)} %param.32) | copy-start | bytes 100
  11.4 17.9 %all-to-all-start = ((bf16[16,8,1408]{2,0,1:T(8,128)(2,1)}), bf16[16,8,1408]{2,0,1:T(8,128)(2,1)S(1)}, u32[]{:S(2)}, u32[]{:S(2)}) async-start(bf16[16,8,1408]{2,0,1:T(8,128)(2,1)} %concatenate.38), calls=%async_computation | async-start | bytes 720896 | tf_op jit(solution)/shard_map/all_to_all | solution.py:69
  19.6 58.7 %all-gather.4.cloned.1.call-start = ((), (), s32[]{:S(2)}) async-start(), calls=%async_computation.2 | async-start | bytes 8355840 | tf_op jit(solution)/shard_map/all_gather | solution.py:73
  30.2 117.9 %all-gather.6.cloned.1.call-start = ((), (), s32[]{:S(2)}) async-start(), calls=%async_computation.4 | async-start | bytes 5013504 | tf_op jit(solution)/shard_map/all_gather | solution.py:163
  30.9 54.4 %copy-start.9 = (s32[2,256]{1,0:T(2,128)}, s32[2,256]{1,0:T(2,128)S(1)}, u32[]{:S(2)}) copy-start(s32[2,256]{1,0:T(2,128)S(1)} %eq.111) | copy-start | bytes 6148
  33.2 52.1 %copy-start.20 = (f32[8]{0:T(128)S(1)}, f32[8]{0:T(128)}, u32[]{:S(2)}) copy-start(f32[8]{0:T(128)} %param.31) | copy-start | bytes 100
  87.6 5.3 %copy-start.7 = (f32[2,8,256]{2,1,0:T(8,128)}, f32[2,8,256]{2,1,0:T(8,128)S(1)}, u32[]{:S(2)}) copy-start(f32[2,8,256]{2,1,0:T(8,128)S(1)} %get-tuple-element.130) | copy-start | bytes 49156
  88.8 8.0 %collective-permute-start = (bf16[3,768]{0,1:T(8,128)(2,1)S(1)}, bf16[3,768]{0,1:T(8,128)(2,1)S(1)}, u32[]{:S(2)}, u32[]{:S(2)}) collective-permute-start(bf16[3,768]{0,1:T(8,128)(2,1)S(1)} %slice.203), channel_id=1, source_target_pairs={{0,8},{8,16},{16,24},{24,32},{32,40},{40,48},{48,56},{56,64},{64,7... | collective-permute-start | bytes 13832 | tf_op jit(solution)/shard_map/ppermute | solution.py:16
  92.1 0.7 copy-start.15
  92.1 0.7 copy-start.14
  108.9 135.1 %reduce-scatter.2.cloned.1.call-start = ((), (), s32[]{:S(2)}) async-start(), calls=%async_computation.3 | async-start | bytes 2506752 | tf_op jit(solution)/shard_map/reduce_scatter | solution.py:199
  109.7 2.8 %copy-start.17 = (pred[16]{0:T(512)(128)(4,1)}, pred[16]{0:T(512)(128)(4,1)S(1)}, u32[]{:S(2)}) copy-start(pred[16]{0:T(512)(128)(4,1)S(1)} %iota_compare_fusion.6) | copy-start | bytes 52
  119.9 4.0 %slice-start = ((f32[2,8]{1,0:T(2,128)}), f32[1,8]{1,0:T(1,128)S(1)}, s32[]{:S(2)}) async-start(f32[2,8]{1,0:T(2,128)} %copy-done.14), calls=%async_computation.5 | async-start | bytes 1024 | tf_op jit(solution)/shard_map/slice | solution.py:154
  119.9 4.6 %copy-start.3 = (bf16[512,128]{0,1:T(8,128)(2,1)S(1)}, bf16[512,128]{0,1:T(8,128)(2,1)}, u32[]{:S(2)}) copy-start(bf16[512,128]{0,1:T(8,128)(2,1)} %get-tuple-element.135) | copy-start | bytes 393220
  149.6 6.1 %copy-start.10 = (pred[16,16]{1,0:T(8,128)(4,1)S(1)}, pred[16,16]{1,0:T(8,128)(4,1)}, u32[]{:S(2)}) copy-start(pred[16,16]{1,0:T(8,128)(4,1)} %broadcast_and_fusion.1) | copy-start | bytes 772
  149.6 6.5 %copy-start.18 = (pred[16]{0:T(512)(128)(4,1)S(1)}, pred[16]{0:T(512)(128)(4,1)}, u32[]{:S(2)}) copy-start(pred[16]{0:T(512)(128)(4,1)} %copy-done.17) | copy-start | bytes 52
  149.6 6.5 %copy-start.23 = (f32[2]{0:T(128)S(1)}, f32[2]{0:T(128)}, u32[]{:S(2)}) copy-start(f32[2]{0:T(128)} %compare_convert_fusion) | copy-start | bytes 28
  156.3 6.3 %copy-start.4 = (f32[2,256,8,64]{1,3,2,0:T(8,128)S(1)}, f32[2,256,8,64]{1,3,2,0:T(8,128)}, u32[]{:S(2)}) copy-start(f32[2,256,8,64]{1,3,2,0:T(8,128)} %fusion.19) | copy-start | bytes 3145732
  156.3 6.3 %copy-start.5 = (f32[2,8,64,128]{3,2,1,0:T(8,128)S(1)}, f32[2,8,64,128]{3,2,1,0:T(8,128)}, u32[]{:S(2)}) copy-start(f32[2,8,64,128]{3,2,1,0:T(8,128)} %get-tuple-element.72) | copy-start | bytes 1572868
  156.3 6.3 %copy-start.8 = (f32[2,256,8]{1,2,0:T(8,128)S(1)}, f32[2,256,8]{1,2,0:T(8,128)}, u32[]{:S(2)}) copy-start(f32[2,256,8]{1,2,0:T(8,128)} %get-tuple-element.129) | copy-start | bytes 49156
  156.3 6.3 %copy-start.12 = (f32[2,8]{1,0:T(2,128)S(1)}, f32[2,8]{1,0:T(2,128)}, u32[]{:S(2)}) copy-start(f32[2,8]{1,0:T(2,128)} %concatenate.43) | copy-start | bytes 196
  156.3 6.3 %copy-start.21 = (f32[8]{0:T(128)S(1)}, f32[8]{0:T(128)}, u32[]{:S(2)}) copy-start(f32[8]{0:T(128)} %param.33) | copy-start | bytes 100
  163.0 1.4 copy-start.2
  163.9 1.7 copy-start.1
  163.9 1.7 copy-start.24
  168.7 0.7 copy-start.22
Sparse Core Ops, SparseCore 0:
  30.3 47.9 all-gather.3
  109.0 39.0 all-gather.5
  168.8 75.0 reduce-scatter.1

commit v3 on v2

--- a/solution.py
+++ b/solution.py
@@ -2,6 +2,9 @@
 import jax.numpy as jnp
 from jax import lax
 from jax.sharding import PartitionSpec as P
+from jax.experimental import pallas as pl
+from jax.experimental.pallas import tpu as pltpu
+import functools
 
 INNER = 4096
 GROUP = 256
@@ -19,6 +22,61 @@
 def segment_of(position, lengths):
     prompt_ends = jnp.cumsum(lengths)
     return jnp.sum((position[:, None] >= prompt_ends[None, :]).astype(jnp.int32), axis=1)
+
+
+def scatter_sum_kernel(count, rows, x_ref, o_ref, recv, send_sem, recv_sem):
+    me = lax.axis_index("tp")
+    barrier = pltpu.get_barrier_semaphore()
+    for d in range(1, count):
+        peer = lax.rem(me + d, count)
+        pl.semaphore_signal(barrier, inc=1, device_id={"tp": peer}, device_id_type=pl.DeviceIdType.MESH)
+    pl.semaphore_wait(barrier, count - 1)
+    copies = []
+    for d in range(1, count):
+        peer = lax.rem(me + d, count)
+        copy = pltpu.make_async_remote_copy(
+            src_ref=x_ref.at[pl.ds(pl.multiple_of(peer * rows, rows), rows)],
+            dst_ref=recv.at[me],
+            send_sem=send_sem.at[d],
+            recv_sem=recv_sem.at[me],
+            device_id={"tp": peer},
+            device_id_type=pl.DeviceIdType.MESH,
+        )
+        copy.start()
+        copies.append(copy)
+    total = x_ref[pl.ds(pl.multiple_of(me * rows, rows), rows), :].astype(jnp.float32)
+    for d in range(1, count):
+        sender = lax.rem(me + count - d, count)
+        arrival = pltpu.make_async_remote_copy(
+            src_ref=x_ref.at[pl.ds(0, rows)],
+            dst_ref=recv.at[sender],
+            send_sem=send_sem.at[d],
+            recv_sem=recv_sem.at[sender],
+            device_id={"tp": sender},
+            device_id_type=pl.DeviceIdType.MESH,
+        )
+        arrival.wait_recv()
+        total = total + recv[sender].astype(jnp.float32)
+    for copy in copies:
+        copy.wait_send()
+    o_ref[...] = total
+
+
+def scatter_sum(x, count):
+    rows = x.shape[0] // count
+    cols = x.shape[1]
+    return pl.pallas_call(
+        functools.partial(scatter_sum_kernel, count, rows),
+        out_shape=jax.ShapeDtypeStruct((rows, cols), jnp.float32),
+        in_specs=[pl.BlockSpec(memory_space=pltpu.VMEM)],
+        out_specs=pl.BlockSpec(memory_space=pltpu.VMEM),
+        scratch_shapes=[
+            pltpu.VMEM((count, rows, cols), x.dtype),
+            pltpu.SemaphoreType.DMA((count,)),
+            pltpu.SemaphoreType.DMA((count,)),
+        ],
+        compiler_params=pltpu.CompilerParams(collective_id=0, has_side_effects=True),
+    )(x)
 
 
 def round_up(n, m):
@@ -196,12 +254,7 @@
     scaled = (gated * norm_weight[None, :]).astype(jnp.bfloat16)
     partial = jnp.dot(scaled, out_block, preferred_element_type=jnp.float32)
     side = jnp.zeros((tok_dev, 128), jnp.float32).at[:, 0].set(square_sum)
-    summed = lax.psum_scatter(
-        jnp.concatenate([partial, side], axis=1).astype(jnp.bfloat16),
-        "tp",
-        scatter_dimension=0,
-        tiled=True,
-    ).astype(jnp.float32)
+    summed = scatter_sum(jnp.concatenate([partial, side], axis=1).astype(jnp.bfloat16), tp_count)
     d_model = out_block.shape[1]
     mean_square = summed[:, d_model] / INNER
     mixed = (summed[:, :d_model] * lax.rsqrt(mean_square + epsilon)[:, None]).astype(jnp.bfloat16)

time: 254 us -> 227 us (0.89)
  waiting for transfers between devices: 141 us -> 72 us
  Pallas kernels: 0 us -> 41.1 us
  other arithmetic: 23.1 us -> 26.5 us
    reduce_scatter x1 -> x0, waiting for transfers between devices: 66.3 us -> none  [on_device(): lax.psum_scatter(jnp.concatenate([partial, side], axis=1).astype(jnp.bflo...]
    pallas_call x0 -> x1, Pallas kernels: none -> 41.1 us  [scatter_sum(): pl.pallas_call(functools.partial(scatter_sum_kernel, count, rows), out_sh...]
    all_gather x1, waiting for transfers between devices: 20 us -> 17.4 us  [on_device(): every = lax.all_gather(sendable, 'seq', axis=0, tiled=False)]
  transfers between devices with their start and end apart: 5 -> 4, of which waited for: 4 -> 3; matrix products, arithmetic and copies ran while one was open for 14% -> 13% of each run, Pallas kernels for 0% -> 0%
where the time goes in v3:
time: 227 us; the launch traced here: 226 us
  waiting for transfers between devices  72 us (32%)
  Pallas kernels  41.1 us (18%)
  local copies, waits for them, and re-layouts  35.5 us (16%)
  other arithmetic  26.5 us (12%)
  matrix products  24.4 us (11%)
  between operations  14.6 us (6%)
  starting transfers between devices  11.5 us (5%)
    all_gather x1, waiting for transfers between devices, on_device(): lax.all_gather(jnp.concatenate([block, out_piece], axis=1), 'seq', axis=0...  45 us
    pallas_call x1, Pallas kernels, scatter_sum(): pl.pallas_call(functools.partial(scatter_sum_kernel, count, rows), out_sh...  41.1 us
    all_gather x1, waiting for transfers between devices, on_device(): every = lax.all_gather(sendable, 'seq', axis=0, tiled=False)  17.4 us
    all_to_all x1, waiting for transfers between devices, on_device(): lax.all_to_all(packed, 'tp', split_axis=1, concat_axis=0, tiled=True)  9.54 us
    reshape x2, local copies, waits for them, and re-layouts, on_device(): out_block = gathered[:, width:].reshape(seq_count, out_rows, out_cols)  8.5 us
    all_to_all x1, starting transfers between devices, on_device(): lax.all_to_all(packed, 'tp', split_axis=1, concat_axis=0, tiled=True)  8.16 us
    dot_general x1, matrix products, on_device(): proj = jnp.dot(tokens, weights, preferred_element_type=jnp.float32)  7.02 us
    dot_general x1, matrix products, on_device(): jnp.einsum('jch,jchpn->hpn', own_coef, every_end, precision=lax.Precision...  6.3 us
  transfers between devices with their start and end apart: 4, of which 3 were waited for; matrix products, arithmetic and copies ran while one was open for 13% of the time, Pallas kernels for 0%

profile of v3, /device:TPU:1, one launch (start us, length us, event | category | flops | bytes accessed | tf_op | source)
XLA Modules:
  0.0 225.7 jit_solution(5167139996053880330)
XLA Ops:
  7.2 0.9 convert_element_type.123
  8.1 0.8 copy.117
  9.0 1.1 convert_element_type.122
  10.6 0.8 concatenate.38
  11.4 8.2 %all-to-all-start = ((bf16[16,8,1408]{2,0,1:T(8,128)(2,1)}), bf16[16,8,1408]{2,0,1:T(8,128)(2,1)S(1)}, u32[]{:S(2)}, u32[]{:S(2)}) async-start(bf16[16,8,1408]{2,0,1:T(8,128)(2,1)} %concatenate.38), calls=%async_computation | async-start | bytes 720896 | tf_op jit(solution)/shard_map/all_to_all | solution.py:127
  19.8 9.5 %all-to-all-done = bf16[16,8,1408]{2,0,1:T(8,128)(2,1)S(1)} async-done(((bf16[16,8,1408]{2,0,1:T(8,128)(2,1)}), bf16[16,8,1408]{2,0,1:T(8,128)(2,1)S(1)}, u32[]{:S(2)}, u32[]{:S(2)}) %all-to-all-start) | async-done | bytes 360480 | tf_op jit(solution)/shard_map/all_to_all | solution.py:127
  29.3 0.8 pad_maximum_fusion.1
  32.6 0.7 slice_compare_fusion.2
  33.3 45.0 %all-gather.4.cloned.1.call-done = bf16[2048,1920]{1,0:T(8,128)(2,1)} async-done(((bf16[128,1920]{1,0:T(8,128)(2,1)}), bf16[2048,1920]{1,0:T(8,128)(2,1)}) %all-gather.4.cloned.1.call-update) | async-done | bytes 7864336 | tf_op jit(solution)/shard_map/all_gather | solution.py:131
  78.3 7.0 %fusion.61 = (bf16[512,1408]{0,1:T(8,128)(2,1)}, f32[512,1408]{0,1:T(8,128)S(1)}) fusion(bf16[512,2048]{1,0:T(8,128)(2,1)S(1)} %copy-done, bf16[2048,1920]{1,0:T(8,128)(2,1)} %all-gather.4.cloned.1.call-done), kind=kOutput, calls=%fused_computation.139 | convolution fusion | flops 2953510912 | bytes 12189696 | tf_op jit(solution)/shard_map/dot_general | solution.py:137
  85.5 1.1 reduce-window.19
  86.9 0.7 select_bitcast_fusion
  87.7 1.0 slice.203
  88.7 3.3 %collective-permute-start = (bf16[3,768]{0,1:T(8,128)(2,1)S(1)}, bf16[3,768]{0,1:T(8,128)(2,1)S(1)}, u32[]{:S(2)}, u32[]{:S(2)}) collective-permute-start(bf16[3,768]{0,1:T(8,128)(2,1)S(1)} %slice.203), channel_id=1, source_target_pairs={{0,8},{8,16},{16,24},{24,32},{32,40},{40,48},{48,56},{56,64},{64,7... | collective-permute-start | bytes 13832 | tf_op jit(solution)/shard_map/ppermute | solution.py:19
  92.1 0.7 select_multiply_fusion.1
  92.8 1.2 slice.204
  94.7 0.7 broadcast.361
  95.4 1.4 scatter.11
  96.8 2.9 %multiply_convert_fusion.3 = bf16[512,768]{0,1:T(8,128)(2,1)S(1)} fusion(bf16[512,768]{0,1:T(8,128)(2,1)S(1)} %slice.204, bf16[3,768]{0,1:T(8,128)(2,1)S(1)} %collective-permute-done, f32[768]{0:T(1024)} %get-tuple-element.107, f32[768]{0:T(1024)} %get-tuple-element.108, f32[768]{0:T(1024)} %get-tuple-element.109, f32[768]{0:T(1024)} %get-tuple-element.106, ...), kind=kLoop, calls=%fused_computation.26 | loop fusion | flops 11403264 | bytes 1594368 | tf_op jit(solution)/shard_map/convert_element_type | solution.py:161
  99.7 0.7 fusion.60
  100.5 0.9 reshape.472
  101.5 0.8 copy.124
  102.3 2.0 fusion.29
  104.3 2.8 %while.18 = (s32[]{:T(128)}, f32[8,64,128]{2,1,0:T(8,128)S(1)}, f32[2,8,64,128]{3,2,1,0:T(8,128)}, bf16[2,8,64,128]{3,2,1,0:T(8,128)(2,1)}, f32[2,8]{1,0:T(2,128...) while((s32[]{:T(128)}, f32[8,64,128]{2,1,0:T(8,128)S(1)}, ...), condition=%wide.region_7.8_spmd.clone, body=%wide.region_6.7_spmd.clone.sunk | while | flops 196611 | bytes 1310927 | solution.py:209
  104.3 0.6 fusion.66
  104.9 0.8 bitcast_dynamic-update-slice_fusion.3
  106.4 0.8 bitcast_dynamic-update-slice_fusion.3
  107.1 1.7 pad_maximum_fusion.2
  108.9 0.7 compare_reduce_fusion
  110.1 1.2 fusion.54
  113.3 1.6 compare_and_fusion
  114.9 3.1 %slice.226 = bf16[2048,512]{1,0:T(8,128)(2,1)} slice(bf16[2048,1920]{1,0:T(8,128)(2,1)} %all-gather.4.cloned.1.call-done), slice={[0:2048], [1408:1920]} | slice | bytes 4194304 | tf_op jit(solution)/shard_map/slice | solution.py:135
  117.9 4.5 %reshape.474 = bf16[16,512,128]{2,1,0:T(8,128)(2,1)} reshape(bf16[2048,512]{1,0:T(8,128)(2,1)} %slice.226) | data formatting | bytes 4194304 | tf_op jit(solution)/shard_map/reshape | solution.py:135
  122.5 4.0 %copy.132 = bf16[16,512,128]{1,2,0:T(8,128)(2,1)} copy(bf16[16,512,128]{2,1,0:T(8,128)(2,1)} %reshape.474) | data formatting | bytes 4194304 | tf_op jit(solution)/shard_map/reshape | solution.py:135
  127.4 3.3 %fusion.19 = f32[2,256,8,64]{1,3,2,0:T(8,128)} fusion(f32[2,8,256]{2,1,0:T(8,128)S(1)} %bitcast.108, f32[2,256,256]{2,1,0:T(8,128)S(1)} %fusion.39, f32[2,8,256]{2,1,0:T(8,128)} %copy-done.8, pred[2,256,256]{2,1,0:T(8,128)(4,1)} %compare_and_fusion, bf16[2,256,8,64]{1,0,3,2:T(2,128)(2,1)S(1)} %reshape.467), kind=kOutput, calls=%fused_computation.27 | convolution fusion | flops 140509184 | bytes 2260992 | tf_op jit(solution)/shard_map/chij,cjhp->cihp/dot_general | solution.py:183
  130.7 17.4 %all-gather.6.cloned.1.call-done = bf16[32,8,72,128]{3,2,1,0:T(8,128)(2,1)} async-done(((bf16[2,8,72,128]{3,2,1,0:T(8,128)(2,1)}), bf16[32,8,72,128]{3,2,1,0:T(8,128)(2,1)}) %all-gather.6.cloned.1.call-update) | async-done | bytes 4718608 | tf_op jit(solution)/shard_map/all_gather | solution.py:221
  148.1 1.5 fusion.59
  149.7 5.7 %slice.224 = bf16[16,2,8,64,128]{4,3,2,1,0:T(8,128)(2,1)} slice(bf16[16,2,8,72,128]{4,3,2,1,0:T(8,128)(2,1)} %bitcast.93), slice={[0:16], [0:2], [0:8], [0:64], [0:128]} | slice | bytes 8388608 | tf_op jit(solution)/shard_map/slice | solution.py:222
  157.8 6.3 %fusion.6 = f32[8,1,64,128,1]{3,1,4,2,0:T(1,128)S(1)} fusion(f32[16,2,8,1,1]{0,3,1,4,2:T(1,128)S(1)} %copy.138, bf16[16,2,8,64,128]{4,3,2,1,0:T(8,128)(2,1)} %slice.224), kind=kOutput, calls=%fused_computation.13 | convolution fusion | flops 25165824 | bytes 4457472 | tf_op jit(solution)/shard_map/jch,jchpn->hpn/dot_general | solution.py:239
  164.2 3.6 %fusion.22 = f32[2,8,64,128]{3,0,2,1:T(2,128)S(1)} fusion(bf16[16,2,8,64,128]{4,3,2,1,0:T(8,128)(2,1)S(1)} %copy-done.1, f32[2,16,2]{1,0,2:T(2,128)S(1)} %copy-done.24, f32[2,16,8]{1,0,2:T(2,128)S(1)} %copy.135, f32[2]{0:T(128)S(1)} %copy-done.28), kind=kOutput, calls=%fused_computation.35 | convolution fusion | flops 50332672 | bytes 4719880 | tf_op jit(solution)/shard_map/rjch,jchpn->rhpn/dot_general | solution.py:273
  167.8 0.9 copy.136
  169.0 0.8 copy.131
  171.0 0.7 select_convert_fusion
  171.8 1.6 convolution_convert_fusion
  173.4 1.6 fusion.11.x_ref
  175.0 41.1 %shard_map.158 = f32[64,2176]{1,0:T(8,128)} custom-call(bf16[512,2176]{1,0:T(8,128)(2,1)} %fusion.11.x_ref), custom_call_target="tpu_custom_call" | custom-call | tf_op jit(solution)/shard_map/pallas_call | solution.py:68
  216.1 0.9 rsqrt_reduce_fusion
  217.0 1.9 multiply_convert_fusion.9
  (141 shorter events, 12.7 us)
Async XLA Ops:
  7.2 71.2 %copy-start = (bf16[512,2048]{1,0:T(8,128)(2,1)S(1)}, bf16[512,2048]{1,0:T(8,128)(2,1)}, u32[]{:S(2)}) copy-start(bf16[512,2048]{1,0:T(8,128)(2,1)} %param.23) | copy-start | bytes 6291460
  7.2 12.5 %copy-start.7 = (f32[512,128]{1,0:T(8,128)S(1)}, f32[512,128]{1,0:T(8,128)}, u32[]{:S(2)}) copy-start(f32[512,128]{1,0:T(8,128)} %param.35) | copy-start | bytes 786436
  10.3 19.9 %copy-start.30 = (s32[8]{0:T(128)S(1)}, s32[8]{0:T(128)}, u32[]{:S(2)}) copy-start(s32[8]{0:T(128)} %param.36) | copy-start | bytes 100
  10.3 20.8 %copy-start.21 = (f32[512]{0:T(512)S(1)}, f32[512]{0:T(512)}, u32[]{:S(2)}) copy-start(f32[512]{0:T(512)} %param.28) | copy-start | bytes 6148
  10.4 20.7 %copy-start.25 = (f32[256]{0:T(256)S(1)}, f32[256]{0:T(256)}, u32[]{:S(2)}) copy-start(f32[256]{0:T(256)} %param.30) | copy-start | bytes 3076
  10.4 21.3 %copy-start.13 = (f32[4,512]{1,0:T(4,128)S(1)}, f32[4,512]{1,0:T(4,128)}, u32[]{:S(2)}) copy-start(f32[4,512]{1,0:T(4,128)} %param.27) | copy-start | bytes 24580
  10.4 21.3 %copy-start.16 = (f32[4,256]{1,0:T(4,128)S(1)}, f32[4,256]{1,0:T(4,128)}, u32[]{:S(2)}) copy-start(f32[4,256]{1,0:T(4,128)} %param.29) | copy-start | bytes 12292
  10.4 22.2 %copy-start.31 = (f32[8]{0:T(128)S(1)}, f32[8]{0:T(128)}, u32[]{:S(2)}) copy-start(f32[8]{0:T(128)} %param.32) | copy-start | bytes 100
  11.4 17.9 %all-to-all-start = ((bf16[16,8,1408]{2,0,1:T(8,128)(2,1)}), bf16[16,8,1408]{2,0,1:T(8,128)(2,1)S(1)}, u32[]{:S(2)}, u32[]{:S(2)}) async-start(bf16[16,8,1408]{2,0,1:T(8,128)(2,1)} %concatenate.38), calls=%async_computation | async-start | bytes 720896 | tf_op jit(solution)/shard_map/all_to_all | solution.py:127
  19.6 58.7 %all-gather.4.cloned.1.call-start = ((), (), s32[]{:S(2)}) async-start(), calls=%async_computation.1 | async-start | bytes 8355840 | tf_op jit(solution)/shard_map/all_gather | solution.py:131
  30.2 117.9 %all-gather.6.cloned.1.call-start = ((), (), s32[]{:S(2)}) async-start(), calls=%async_computation.2 | async-start | bytes 5013504 | tf_op jit(solution)/shard_map/all_gather | solution.py:221
  30.9 54.4 %copy-start.10 = (s32[2,256]{1,0:T(2,128)}, s32[2,256]{1,0:T(2,128)S(1)}, u32[]{:S(2)}) copy-start(s32[2,256]{1,0:T(2,128)S(1)} %eq.111) | copy-start | bytes 6148
  33.3 52.1 %copy-start.26 = (f32[8]{0:T(128)S(1)}, f32[8]{0:T(128)}, u32[]{:S(2)}) copy-start(f32[8]{0:T(128)} %param.31) | copy-start | bytes 100
  87.5 5.3 %copy-start.8 = (f32[2,8,256]{2,1,0:T(8,128)}, f32[2,8,256]{2,1,0:T(8,128)S(1)}, u32[]{:S(2)}) copy-start(f32[2,8,256]{2,1,0:T(8,128)S(1)} %get-tuple-element.130) | copy-start | bytes 49156
  88.7 8.0 %collective-permute-start = (bf16[3,768]{0,1:T(8,128)(2,1)S(1)}, bf16[3,768]{0,1:T(8,128)(2,1)S(1)}, u32[]{:S(2)}, u32[]{:S(2)}) collective-permute-start(bf16[3,768]{0,1:T(8,128)(2,1)S(1)} %slice.203), channel_id=1, source_target_pairs={{0,8},{8,16},{16,24},{24,32},{32,40},{40,48},{48,56},{56,64},{64,7... | collective-permute-start | bytes 13832 | tf_op jit(solution)/shard_map/ppermute | solution.py:19
  92.1 0.7 copy-start.18
  92.1 0.7 copy-start.17
  109.6 5.3 %copy-start.22 = (pred[16]{0:T(512)(128)(4,1)}, pred[16]{0:T(512)(128)(4,1)S(1)}, u32[]{:S(2)}) copy-start(pred[16]{0:T(512)(128)(4,1)S(1)} %iota_compare_fusion.6) | copy-start | bytes 52
  111.5 3.4 %copy-start.19 = (pred[2,16]{1,0:T(4,128)(4,1)}, pred[2,16]{1,0:T(4,128)(4,1)S(1)}, u32[]{:S(2)}) copy-start(pred[2,16]{1,0:T(4,128)(4,1)S(1)} %get-tuple-element.141) | copy-start | bytes 100
  122.4 4.0 %slice-start = ((f32[2,8]{1,0:T(2,128)}), f32[1,8]{1,0:T(1,128)S(1)}, s32[]{:S(2)}) async-start(f32[2,8]{1,0:T(2,128)} %copy-done.17), calls=%async_computation.3 | async-start | bytes 1024 | tf_op jit(solution)/shard_map/slice | solution.py:212
  122.5 4.6 %copy-start.4 = (bf16[512,128]{0,1:T(8,128)(2,1)S(1)}, bf16[512,128]{0,1:T(8,128)(2,1)}, u32[]{:S(2)}) copy-start(bf16[512,128]{0,1:T(8,128)(2,1)} %get-tuple-element.135) | copy-start | bytes 393220
  149.6 6.2 %copy-start.12 = (pred[16,16]{1,0:T(8,128)(4,1)S(1)}, pred[16,16]{1,0:T(8,128)(4,1)}, u32[]{:S(2)}) copy-start(pred[16,16]{1,0:T(8,128)(4,1)} %broadcast_and_fusion.1) | copy-start | bytes 772
  149.6 6.6 %copy-start.23 = (pred[16]{0:T(512)(128)(4,1)S(1)}, pred[16]{0:T(512)(128)(4,1)}, u32[]{:S(2)}) copy-start(pred[16]{0:T(512)(128)(4,1)} %copy-done.22) | copy-start | bytes 52
  149.6 6.6 %copy-start.28 = (f32[2]{0:T(128)S(1)}, f32[2]{0:T(128)}, u32[]{:S(2)}) copy-start(f32[2]{0:T(128)} %compare_convert_fusion) | copy-start | bytes 28
  149.6 6.8 %copy-start.11 = (pred[2,16,16]{2,1,0:T(8,128)(4,1)S(1)}, pred[2,16,16]{2,1,0:T(8,128)(4,1)}, u32[]{:S(2)}) copy-start(pred[2,16,16]{2,1,0:T(8,128)(4,1)} %broadcast_and_fusion) | copy-start | bytes 1540
  149.6 7.4 %copy-start.14 = (s32[2]{0:T(128)S(1)}, s32[2]{0:T(128)}, u32[]{:S(2)}) copy-start(s32[2]{0:T(128)} %get-tuple-element.124) | copy-start | bytes 28
  149.6 8.0 %copy-start.20 = (pred[2,16]{1,0:T(4,128)(4,1)S(1)}, pred[2,16]{1,0:T(4,128)(4,1)}, u32[]{:S(2)}) copy-start(pred[2,16]{1,0:T(4,128)(4,1)} %copy-done.19) | copy-start | bytes 100
  157.8 6.3 %copy-start.1 = (bf16[16,2,8,64,128]{4,3,2,1,0:T(8,128)(2,1)S(1)}, bf16[16,2,8,64,128]{4,3,2,1,0:T(8,128)(2,1)}, u32[]{:S(2)}) copy-start(bf16[16,2,8,64,128]{4,3,2,1,0:T(8,128)(2,1)} %slice.224) | copy-start | bytes 12582916
  157.8 6.3 %copy-start.24 = (f32[2,16,2]{1,0,2:T(2,128)S(1)}, f32[2,16,2]{1,0,2:T(2,128)}, u32[]{:S(2)}) copy-start(f32[2,16,2]{1,0,2:T(2,128)} %and_convert_fusion) | copy-start | bytes 772
  164.1 4.5 %copy-start.5 = (f32[2,256,8,64]{1,3,2,0:T(8,128)S(1)}, f32[2,256,8,64]{1,3,2,0:T(8,128)}, u32[]{:S(2)}) copy-start(f32[2,256,8,64]{1,3,2,0:T(8,128)} %fusion.19) | copy-start | bytes 3145732
  164.1 4.5 %copy-start.6 = (f32[2,8,64,128]{3,2,1,0:T(8,128)S(1)}, f32[2,8,64,128]{3,2,1,0:T(8,128)}, u32[]{:S(2)}) copy-start(f32[2,8,64,128]{3,2,1,0:T(8,128)} %get-tuple-element.72) | copy-start | bytes 1572868
  164.2 4.5 %copy-start.9 = (f32[2,256,8]{1,2,0:T(8,128)S(1)}, f32[2,256,8]{1,2,0:T(8,128)}, u32[]{:S(2)}) copy-start(f32[2,256,8]{1,2,0:T(8,128)} %get-tuple-element.129) | copy-start | bytes 49156
  164.2 4.5 %copy-start.15 = (f32[2,8]{1,0:T(2,128)S(1)}, f32[2,8]{1,0:T(2,128)}, u32[]{:S(2)}) copy-start(f32[2,8]{1,0:T(2,128)} %concatenate.43) | copy-start | bytes 196
  164.2 4.5 %copy-start.27 = (f32[8]{0:T(128)S(1)}, f32[8]{0:T(128)}, u32[]{:S(2)}) copy-start(f32[8]{0:T(128)} %param.33) | copy-start | bytes 100
  169.0 1.4 copy-start.3
  169.9 2.0 copy-start.2
  169.9 2.0 copy-start.29
Sparse Core Ops, SparseCore 0:
  30.3 47.9 all-gather.3
  109.0 39.0 all-gather.5

commit v4 on v3

--- a/solution.py
+++ b/solution.py
@@ -1,22 +1,30 @@
+import functools
+
 import jax
 import jax.numpy as jnp
 from jax import lax
-from jax.sharding import PartitionSpec as P
 from jax.experimental import pallas as pl
 from jax.experimental.pallas import tpu as pltpu
-import functools
+from jax.sharding import Mesh
+from jax.sharding import PartitionSpec as P
 
 INNER = 4096
 GROUP = 256
+SEQ = ("cs", "core")
 
 
 epsilon = 1e-05
 
 
-def from_behind(x, axis, by):
-    count = lax.axis_size(axis)
+def from_behind(x, by):
+    count = lax.axis_size(SEQ)
     pairs = [(i, i + by) for i in range(count) if 0 <= i + by < count]
-    return lax.ppermute(x, axis, pairs)
+    return lax.ppermute(x, SEQ, pairs)
+
+
+def gather_seq(x):
+    chips = lax.all_gather(x, "cs", axis=0, tiled=False)
+    return lax.all_gather(chips, "core", axis=0, tiled=False)
 
 
 def segment_of(position, lengths):
@@ -101,9 +109,12 @@
     request_group,
 ):
     tp_count = lax.axis_size("tp")
-    seq_count = lax.axis_size("seq")
-    seq_index = lax.axis_index("seq")
+    chip_count = lax.axis_size("cs")
+    core_count = lax.axis_size("core")
+    seq_count = chip_count * core_count
+    seq_index = lax.axis_index("cs") * core_count + lax.axis_index("core")
     tok_dev = tokens.shape[0]
+    d_model = tokens.shape[1]
     local_rows = w_zx.shape[0]
     inner_local = conv_x_weight.shape[1]
     heads_local = dt_bias.shape[0]
@@ -125,16 +136,14 @@
     packed = jnp.concatenate([zx_part, bc_part, dt_part, pad_part], axis=2)
     packed = packed.reshape(local_rows, tp_count * width)
     block = lax.all_to_all(packed, "tp", split_axis=1, concat_axis=0, tiled=True)
+    block_rows = block.shape[0]
     out_rows, out_cols = w_out.shape
-    block_rows = block.shape[0]
-    out_piece = w_out.astype(jnp.bfloat16).reshape(block_rows, out_rows * out_cols // block_rows)
-    gathered = lax.all_gather(
-        jnp.concatenate([block, out_piece], axis=1), "seq", axis=0, tiled=True
-    )
-    weights = gathered[:, :width]
-    out_block = gathered[:, width:].reshape(seq_count, out_rows, out_cols)
-    out_block = out_block.transpose(1, 0, 2).reshape(out_rows, seq_count * out_cols)
-    proj = jnp.dot(tokens, weights, preferred_element_type=jnp.float32)
+    out_piece = w_out.astype(jnp.bfloat16).T
+    gathered = gather_seq(jnp.concatenate([block, out_piece], axis=1))
+    gathered = gathered.reshape(seq_count * block_rows, width + out_rows)
+    tokens_perm = tokens.reshape(tok_dev, chip_count, core_count, block_rows)
+    tokens_perm = tokens_perm.transpose(0, 2, 1, 3).reshape(tok_dev, d_model)
+    proj = jnp.dot(tokens_perm, gathered[:, :width], preferred_element_type=jnp.float32)
     zx_low = proj[:, : 2 * inner_local].astype(jnp.bfloat16)
     gate_z = zx_low[:, :inner_local]
     x_raw = zx_low[:, inner_local:]
@@ -144,7 +153,7 @@
     raw_mix = jnp.concatenate([x_raw, bc_raw], axis=1)
     conv_weight = jnp.concatenate([conv_x_weight, conv_bc_weight], axis=1)
     conv_bias = jnp.concatenate([conv_x_bias, conv_bc_bias], axis=0)
-    rim_rows = from_behind(raw_mix[tok_dev - (taps - 1) :], "seq", 1)
+    rim_rows = from_behind(raw_mix[tok_dev - (taps - 1) :], 1)
     padded = jnp.concatenate([rim_rows, raw_mix], axis=0)
     offset = seq_index * tok_dev
     seg_pad = segment_of(
@@ -200,13 +209,11 @@
         (last_segment == seg_before)[:, None], jnp.exp(cumul_heads[:, :, -1]), 0.0
     )
 
-    def local_step(carry_state, group_item):
-        factor, source = group_item
-        next_state = factor[:, None, None] * carry_state + source
-        return (next_state, (carry_state, next_state))
-
-    zero_state = jnp.zeros((heads_local, head_width, state_width), jnp.float32)
-    _, (local_in, local_end) = lax.scan(local_step, zero_state, (pass_gate, contrib))
+    ends = [contrib[0]]
+    for c in range(1, groups_dev):
+        ends.append(pass_gate[c][:, None, None] * ends[-1] + contrib[c])
+    local_end = jnp.stack(ends)
+    local_in = jnp.concatenate([jnp.zeros_like(local_end[:1]), local_end[:-1]], axis=0)
     through_group = jnp.cumprod(pass_gate, axis=0)
     before_group = jnp.concatenate(
         [jnp.ones((1, heads_local), jnp.float32), through_group[:-1]], axis=0
@@ -218,28 +225,50 @@
     extra = extra.at[:, :, 0, :].set(jnp.broadcast_to(gate_hi[:, :, None], gate_hi.shape + (state_width,)))
     extra = extra.at[:, :, 1, :].set(jnp.broadcast_to(gate_lo[:, :, None], gate_lo.shape + (state_width,)))
     sendable = jnp.concatenate([local_end.astype(jnp.bfloat16), extra], axis=2)
-    every = lax.all_gather(sendable, "seq", axis=0, tiled=False)
-    every_end = every[:, :, :, :head_width].astype(jnp.float32)
-    every_gate = (
-        every[:, :, :, head_width, 0].astype(jnp.float32)
-        + every[:, :, :, head_width + 1, 0].astype(jnp.float32)
+    every = gather_seq(sendable).reshape(
+        (seq_count * groups_dev, heads_local, head_width + 8, state_width)
+    )
+    gate_rows = every[:, :, head_width : head_width + 2, :].astype(jnp.float32)
+    every_gate = (gate_rows[:, :, 0, 0] + gate_rows[:, :, 1, 0]).reshape(
+        seq_count, groups_dev, heads_local
     )
     dev_gate = every_gate[:, -1]
-    dev_ids = jnp.arange(seq_count, dtype=jnp.int32)
+    rows_at = jnp.arange(seq_count, dtype=jnp.int32)
+    dev_of = (rows_at % chip_count) * core_count + rows_at // chip_count
 
     def carry_weights(k):
-        between = (dev_ids[:, None] < dev_ids[None, :]) & (dev_ids[None, :] < k)
+        between = (dev_of[:, None] < dev_of[None, :]) & (dev_of[None, :] < k)
         factors = jnp.where(between[:, :, None], dev_gate[None, :, :], 1.0)
-        return jnp.where((dev_ids < k)[:, None], jnp.prod(factors, axis=1), 0.0)
-
-    own_weights = carry_weights(seq_index)
+        return jnp.where((dev_of < k)[:, None], jnp.prod(factors, axis=1), 0.0)
+
+    req_dev = request_group.shape[0] // seq_count
+    mine = lax.dynamic_slice_in_dim(request_group, seq_index * req_dev, req_dev)
+    req_k = mine // groups_dev
+    req_c = mine % groups_dev
+    req_row = (req_k % core_count) * chip_count + req_k // core_count
+    req_gate = every_gate[req_row, req_c]
+    wanted = jnp.concatenate([seq_index[None], req_k])
+    weights_all = jax.vmap(carry_weights)(wanted)
+    scales = jnp.concatenate([jnp.ones((1, heads_local), jnp.float32), req_gate], axis=0)
+    weights_all = weights_all * scales[:, None, :]
     slot_ids = jnp.arange(groups_dev, dtype=jnp.int32)
     last_slot = (slot_ids == groups_dev - 1).astype(jnp.float32)
-    own_coef = own_weights[:, None, :] * last_slot[None, :, None]
-    carried = jnp.einsum(
-        "jch,jchpn->hpn", own_coef, every_end, precision=lax.Precision.HIGHEST,
-        preferred_element_type=jnp.float32,
-    )
+    coef = weights_all[:, :, None, :] * last_slot[None, None, :, None]
+    own_row = jnp.concatenate([jnp.full((1,), -1, jnp.int32), req_row])
+    own_slot = jnp.concatenate([jnp.full((1,), -1, jnp.int32), req_c])
+    hit = (rows_at[None, :, None] == own_row[:, None, None]) & (
+        slot_ids[None, None, :] == own_slot[:, None, None]
+    )
+    coef = coef + hit[:, :, :, None].astype(jnp.float32)
+    coef = coef.reshape(wanted.shape[0], seq_count * groups_dev, heads_local)
+    coef_hi = coef.astype(jnp.bfloat16)
+    coef_lo = (coef - coef_hi.astype(jnp.float32)).astype(jnp.bfloat16)
+    summed_states = jnp.einsum(
+        "rjh,jhpn->rhpn", coef_hi, every, preferred_element_type=jnp.float32
+    ) + jnp.einsum("rjh,jhpn->rhpn", coef_lo, every, preferred_element_type=jnp.float32)
+    carried = summed_states[0, :, :head_width]
+    request_states = summed_states[1:, :, :head_width]
+
     group_in = before_group[:, :, None, None] * carried[None] + local_in
     state_low = group_in.astype(jnp.bfloat16)
     carry_keep = jnp.where((segments == seg_before[:, None])[:, None, :], jnp.exp(cumul_heads), 0.0)
@@ -252,40 +281,29 @@
     gated = y_local * jax.nn.silu(gate_z.astype(jnp.float32))
     square_sum = jnp.sum(gated * gated, axis=1)
     scaled = (gated * norm_weight[None, :]).astype(jnp.bfloat16)
-    partial = jnp.dot(scaled, out_block, preferred_element_type=jnp.float32)
+    partial = lax.dot_general(
+        scaled, gathered[:, width:], (((1,), (1,)), ((), ())), preferred_element_type=jnp.float32
+    )
+    partial = partial.reshape(tok_dev, core_count, chip_count, out_cols)
+    partial = partial.transpose(0, 2, 1, 3).reshape(tok_dev, d_model)
     side = jnp.zeros((tok_dev, 128), jnp.float32).at[:, 0].set(square_sum)
     summed = scatter_sum(jnp.concatenate([partial, side], axis=1).astype(jnp.bfloat16), tp_count)
-    d_model = out_block.shape[1]
     mean_square = summed[:, d_model] / INNER
     mixed = (summed[:, :d_model] * lax.rsqrt(mean_square + epsilon)[:, None]).astype(jnp.bfloat16)
-
-    req_dev = request_group.shape[0] // seq_count
-    mine = lax.dynamic_slice_in_dim(request_group, seq_index * req_dev, req_dev)
-    req_k = mine // groups_dev
-    req_c = mine % groups_dev
-    req_w = jax.vmap(carry_weights)(req_k)
-    req_gate = every_gate[req_k, req_c]
-    coef = req_gate[:, None, None, :] * req_w[:, :, None, :] * last_slot[None, None, :, None]
-    hit = (dev_ids[None, :, None] == req_k[:, None, None]) & (
-        slot_ids[None, None, :] == req_c[:, None, None]
-    )
-    coef = coef + hit[:, :, :, None].astype(jnp.float32)
-    request_states = jnp.einsum(
-        "rjch,jchpn->rhpn", coef, every_end, precision=lax.Precision.HIGHEST,
-        preferred_element_type=jnp.float32,
-    )
-    return (mixed.astype(jnp.bfloat16), request_states)
+    return (mixed, request_states)
 
 
 def solution(mesh):
+    seq_n, tp_n = mesh.devices.shape
+    view = Mesh(mesh.devices.reshape(seq_n // 2, 2, tp_n), ("cs", "core", "tp"))
     return jax.shard_map(
         on_device,
-        mesh=mesh,
+        mesh=view,
         in_specs=(
-            P("seq", None),
-            P(("seq", "tp"), None),
-            P(("seq", "tp"), None),
-            P(("seq", "tp"), None),
+            P(SEQ, None),
+            P((*SEQ, "tp"), None),
+            P((*SEQ, "tp"), None),
+            P((*SEQ, "tp"), None),
             P(None, "tp"),
             P("tp"),
             P(),
@@ -294,10 +312,10 @@
             P("tp"),
             P("tp"),
             P("tp"),
-            P("tp", "seq"),
+            P("tp", SEQ),
             P(),
             P(),
         ),
-        out_specs=(P(("seq", "tp"), None), P("seq", "tp", None, None)),
+        out_specs=(P((*SEQ, "tp"), None), P(SEQ, "tp", None, None)),
         check_vma=False,
     )

time: 227 us -> 320 us (1.41)
  waiting for transfers between devices: 72 us -> 189 us
  other arithmetic: 26.5 us -> 16 us
  matrix products: 24.4 us -> 17 us
  local copies, waits for them, and re-layouts: 35.5 us -> 29.2 us
    all_gather x2 -> x4, waiting for transfers between devices: 62.4 us -> 177 us  [the longest x2 140 us: gather_seq(): chips = lax.all_gather(x, 'cs', axis=0, tiled=False)]
    slice x4 -> x6, local copies, waits for them, and re-layouts: 11.3 us -> 0.68 us  [the longest x1 0.27 us: on_device(): request_states = summed_states[1:, :, :head_width]]
    all_gather x0 -> x1, local copies, waits for them, and re-layouts: none -> 9.29 us  [gather_seq(): return lax.all_gather(chips, 'core', axis=0, tiled=False)]
    dot_general x4, matrix products: 18.5 us -> 13.6 us  [the longest x1 6.47 us: on_device(): jnp.dot(tokens_perm, gathered[:, :width], preferred_element_type=jnp.floa...]
    reshape x3 -> x2, local copies, waits for them, and re-layouts: 8.59 us -> 7.02 us  [the longest x1 3.73 us: on_device(): partial = partial.reshape(tok_dev, core_count, chip_count, out_cols)]
  transfers between devices with their start and end apart: 4 -> 6, of which waited for: 3 -> 6; matrix products, arithmetic and copies ran while one was open for 13% -> 3% of each run, Pallas kernels for 0% -> 0%
where the time goes in v4:
time: 320 us; the launch traced here: 319 us
  waiting for transfers between devices  189 us (59%)
  Pallas kernels  41.9 us (13%)
  local copies, waits for them, and re-layouts  29.2 us (9%)
  matrix products  17 us (5%)
  other arithmetic  16 us (5%)
  between operations  14.4 us (4%)
  starting transfers between devices  11.7 us (4%)
    all_gather x2, waiting for transfers between devices, gather_seq(): chips = lax.all_gather(x, 'cs', axis=0, tiled=False)  140 us
    pallas_call x1, Pallas kernels, scatter_sum(): pl.pallas_call(functools.partial(scatter_sum_kernel, count, rows), out_sh...  41.9 us
    all_gather x2, waiting for transfers between devices, gather_seq(): return lax.all_gather(chips, 'core', axis=0, tiled=False)  36.8 us
    all_to_all x1, waiting for transfers between devices, on_device(): lax.all_to_all(packed, 'tp', split_axis=1, concat_axis=0, tiled=True)  9.55 us
    all_gather x1, local copies, waits for them, and re-layouts, gather_seq(): return lax.all_gather(chips, 'core', axis=0, tiled=False)  9.29 us
    all_to_all x1, starting transfers between devices, on_device(): lax.all_to_all(packed, 'tp', split_axis=1, concat_axis=0, tiled=True)  8.16 us
    dot_general x1, matrix products, on_device(): jnp.dot(tokens_perm, gathered[:, :width], preferred_element_type=jnp.floa...  6.47 us
  transfers between devices with their start and end apart: 6, of which 6 were waited for; matrix products, arithmetic and copies ran while one was open for 3% of the time, Pallas kernels for 0%

profile of v4, /device:TPU:1, one launch (start us, length us, event | category | flops | bytes accessed | tf_op | source)
XLA Modules:
  0.0 319.0 jit_solution(14814879751704983874)
XLA Ops:
  7.2 1.1 convert_element_type.120
  8.4 0.2 copy.192
  9.0 0.8 concatenate.53
  9.9 8.2 %all-to-all-start = ((bf16[16,8,1408]{2,0,1:T(8,128)(2,1)}), bf16[16,8,1408]{2,0,1:T(8,128)(2,1)S(1)}, u32[]{:S(2)}, u32[]{:S(2)}) async-start(bf16[16,8,1408]{2,0,1:T(8,128)(2,1)} %concatenate.53), calls=%async_computation | async-start | bytes 720896 | tf_op jit(solution)/shard_map/all_to_all | solution.py:138
  18.2 9.6 %all-to-all-done = bf16[16,8,1408]{2,0,1:T(8,128)(2,1)S(1)} async-done(((bf16[16,8,1408]{2,0,1:T(8,128)(2,1)}), bf16[16,8,1408]{2,0,1:T(8,128)(2,1)S(1)}, u32[]{:S(2)}, u32[]{:S(2)}) %all-to-all-start) | async-done | bytes 360480 | tf_op jit(solution)/shard_map/all_to_all | solution.py:138
  27.8 0.8 pad_maximum_fusion.1
  28.7 82.5 %all-gather.9.cloned.1.call-done = bf16[1024,1920]{1,0:T(8,128)(2,1)} async-done(((bf16[128,1920]{1,0:T(8,128)(2,1)}), bf16[1024,1920]{1,0:T(8,128)(2,1)}) %all-gather.9.cloned.1.call-update) | async-done | bytes 3932176 | tf_op jit(solution)/shard_map/all_gather | solution.py:26
  111.6 2.9 copy.134
  114.5 1.7 copy.135
  116.2 0.2 fusion.49
  116.5 0.2 slice_reduce_fusion.6
  116.7 0.2 compare_reduce_fusion.1
  117.1 19.2 %all-gather.11.cloned.1.call-done = bf16[16,128,1920]{2,1,0:T(8,128)(2,1)} async-done(((bf16[8,128,1920]{2,1,0:T(8,128)(2,1)}), bf16[16,128,1920]{2,1,0:T(8,128)(2,1)}) %all-gather.11.cloned.1.call-update) | async-done | bytes 7864336 | tf_op jit(solution)/shard_map/all_gather | solution.py:27
  136.4 6.5 %fusion.64 = (bf16[512,1408]{0,1:T(8,128)(2,1)S(1)}, f32[512,1408]{0,1:T(8,128)S(1)}) fusion(bf16[512,2048]{0,1:T(8,128)(2,1)} %bitcast.98, bf16[2048,1920]{1,0:T(8,128)(2,1)} %bitcast.119), kind=kOutput, calls=%fused_computation.153 | convolution fusion | flops 2953510912 | bytes 12189696 | tf_op jit(solution)/shard_map/dot_general | solution.py:146
  143.0 1.1 reduce-window.19
  144.7 3.4 %collective-permute-start = (bf16[3,768]{0,1:T(8,128)(2,1)S(1)}, bf16[3,768]{0,1:T(8,128)(2,1)S(1)}, u32[]{:S(2)}, u32[]{:S(2)}) collective-permute-start(bf16[3,768]{0,1:T(8,128)(2,1)S(1)} %slice.223), channel_id=1, source_target_pairs={{0,8},{8,16},{16,24},{24,32},{32,40},{40,48},{48,56},{56,64},{64,7... | collective-permute-start | bytes 13832 | tf_op jit(solution)/shard_map/ppermute | solution.py:22
  148.6 2.1 collective-permute-done
  150.7 2.1 multiply_convert_fusion.3
  153.2 1.0 fusion.26
  154.4 0.7 pad_maximum_fusion.2
  155.2 57.8 %all-gather.13.cloned.1.call-done = bf16[16,8,72,128]{3,2,1,0:T(8,128)(2,1)} async-done(((bf16[2,8,72,128]{3,2,1,0:T(8,128)(2,1)}), bf16[16,8,72,128]{3,2,1,0:T(8,128)(2,1)}) %all-gather.13.cloned.1.call-update) | async-done | bytes 2359312 | tf_op jit(solution)/shard_map/all_gather | solution.py:26
  213.6 0.6 compare_reduce_fusion
  214.8 0.3 fusion.37
  215.0 1.8 fusion.19
  216.9 17.5 %all-gather.15.cloned.1.call-done = bf16[16,2,8,72,128]{4,3,2,1,0:T(8,128)(2,1)} async-done(((bf16[8,2,8,72,128]{4,3,2,1,0:T(8,128)(2,1)}), bf16[16,2,8,72,128]{4,3,2,1,0:T(8,128)(2,1)}) %all-gather.15.cloned.1.call-update) | async-done | bytes 4718608 | tf_op jit(solution)/shard_map/all_gather | solution.py:27
  234.4 9.3 %copy.143 = bf16[16,2,8,72,128]{4,1,0,3,2:T(2,128)(2,1)} copy(bf16[16,2,8,72,128]{4,3,2,1,0:T(8,128)(2,1)} %all-gather.15.cloned.1.call-done) | data formatting | bytes 9437184 | tf_op jit(solution)/shard_map/all_gather | solution.py:27
  243.7 0.9 slice_convert_fusion
  244.7 0.3 copy.144
  245.0 0.6 gather_fusion
  245.6 0.9 select_reduce_fusion
  246.7 3.2 %fusion.45 = f32[8,72,128,3]{2,3,1,0:T(4,128)S(1)} fusion(bf16[32,8,72,128]{3,0,2,1:T(8,128)(2,1)} %bitcast.88, bf16[3,32,8,1]{1,2,0,3:T(8,128)(2,1)S(1)} %get-tuple-element.67), kind=kOutput, calls=%fused_computation.87 | convolution fusion | flops 14155776 | bytes 5604864 | tf_op jit(solution)/shard_map/rjh,jhpn->rhpn/dot_general | solution.py:266
  249.9 0.5 copy-done
  250.5 0.7 fusion.18
  251.4 0.3 slice.250
  251.7 0.3 fusion.21
  252.0 0.8 copy.151
  253.0 0.4 copy-done.2
  253.4 0.4 multiply_reduce_fusion
  253.8 3.2 fusion.15
  256.9 0.6 copy.169
  257.6 3.7 %copy.191 = bf16[512,2,8,128]{3,1,2,0:T(2,128)(2,1)} copy(bf16[512,2,8,128]{3,2,1,0:T(8,128)(2,1)S(1)} %bitcast.90) | data formatting | bytes 4194304 | tf_op jit(solution)/shard_map/reshape | solution.py:287
  261.3 3.3 %reshape.538 = bf16[512,2048]{1,0:T(8,128)(2,1)S(1)} reshape(bf16[512,8,2,128]{3,2,1,0:T(2,128)(2,1)} %bitcast.91) | data formatting | bytes 4194304 | tf_op jit(solution)/shard_map/reshape | solution.py:288
  264.6 0.7 select_convert_fusion
  265.4 1.6 fusion.6.x_ref
  267.0 41.9 %shard_map.158 = f32[64,2176]{1,0:T(8,128)} custom-call(bf16[512,2176]{1,0:T(8,128)(2,1)} %fusion.6.x_ref), custom_call_target="tpu_custom_call" | custom-call | tf_op jit(solution)/shard_map/pallas_call | solution.py:76
  308.9 0.9 rsqrt_reduce_fusion
  309.8 1.9 multiply_convert_fusion.9
  311.6 0.9 copy.154
  (115 shorter events, 4.9 us)
Async XLA Ops:
  7.2 1.6 copy-start.4
  7.2 1.6 copy-start.5
  7.2 10.9 %copy-start.3 = (f32[512,128]{1,0:T(8,128)S(1)}, f32[512,128]{1,0:T(8,128)}, u32[]{:S(2)}) copy-start(f32[512,128]{1,0:T(8,128)} %param.33) | copy-start | bytes 786436
  9.9 17.9 %all-to-all-start = ((bf16[16,8,1408]{2,0,1:T(8,128)(2,1)}), bf16[16,8,1408]{2,0,1:T(8,128)(2,1)S(1)}, u32[]{:S(2)}, u32[]{:S(2)}) async-start(bf16[16,8,1408]{2,0,1:T(8,128)(2,1)} %concatenate.53), calls=%async_computation | async-start | bytes 720896 | tf_op jit(solution)/shard_map/all_to_all | solution.py:138
  18.0 93.1 %all-gather.9.cloned.1.call-start = ((), (), s32[]{:S(2)}) async-start(), calls=%async_computation.1 | async-start | bytes 4423680 | tf_op jit(solution)/shard_map/all_gather | solution.py:26
  28.6 82.6 %copy-start.14 = (s32[8]{0:T(128)S(1)}, s32[8]{0:T(128)}, u32[]{:S(2)}) copy-start(s32[8]{0:T(128)} %param.34) | copy-start | bytes 100
  28.6 107.8 %all-gather.11.cloned.1.call-start = ((), (), s32[]{:S(2)}) async-start(), calls=%async_computation.2 | async-start | bytes 11796480 | tf_op jit(solution)/shard_map/all_gather | solution.py:27
  111.2 101.8 %all-gather.13.cloned.1.call-start = ((), (), s32[]{:S(2)}) async-start(), calls=%async_computation.3 | async-start | bytes 2654208 | tf_op jit(solution)/shard_map/all_gather | solution.py:26
  114.5 2.2 copy-start.6
  114.5 2.2 copy-start.7
  114.5 2.2 copy-start.8
  114.5 2.2 copy-start.9
  114.5 2.4 copy-start.15
  136.4 6.5 %copy-start.10 = (f32[8]{0:T(128)S(1)}, f32[8]{0:T(128)}, u32[]{:S(2)}) copy-start(f32[8]{0:T(128)} %param.29) | copy-start | bytes 100
  142.9 7.9 %copy-start.1 = (bf16[512,1408]{0,1:T(8,128)(2,1)}, bf16[512,1408]{0,1:T(8,128)(2,1)S(1)}, u32[]{:S(2)}) copy-start(bf16[512,1408]{0,1:T(8,128)(2,1)S(1)} %get-tuple-element.73) | copy-start | bytes 4325380
  144.7 6.0 %collective-permute-start = (bf16[3,768]{0,1:T(8,128)(2,1)S(1)}, bf16[3,768]{0,1:T(8,128)(2,1)S(1)}, u32[]{:S(2)}, u32[]{:S(2)}) collective-permute-start(bf16[3,768]{0,1:T(8,128)(2,1)S(1)} %slice.223), channel_id=1, source_target_pairs={{0,8},{8,16},{16,24},{24,32},{32,40},{40,48},{48,56},{56,64},{64,7... | collective-permute-start | bytes 13832 | tf_op jit(solution)/shard_map/ppermute | solution.py:22
  154.3 58.7 %copy-start.12 = (s32[32]{0:T(128)S(1)}, s32[32]{0:T(128)}, u32[]{:S(2)}) copy-start(s32[32]{0:T(128)} %param.35) | copy-start | bytes 388
  155.2 79.2 %all-gather.15.cloned.1.call-start = ((), (), s32[]{:S(2)}) async-start(), calls=%async_computation.4 | async-start | bytes 7077888 | tf_op jit(solution)/shard_map/all_gather | solution.py:27
  246.7 3.8 %copy-start = (bf16[16,2,8,72,128]{4,1,0,3,2:T(2,128)(2,1)S(1)}, bf16[16,2,8,72,128]{4,1,0,3,2:T(2,128)(2,1)}, u32[]{:S(2)}) copy-start(bf16[16,2,8,72,128]{4,1,0,3,2:T(2,128)(2,1)} %copy.143) | copy-start | bytes 14155780
  250.5 1.2 copy-start.11
  252.0 1.4 copy-start.2
  252.9 0.9 copy-start.13
Sparse Core Ops, SparseCore 0:
  28.7 82.3 all-gather.8
  112.8 23.5 all-gather.10
  155.3 57.6 all-gather.12
  214.5 19.8 all-gather.14

commit v5 on v4

--- a/solution.py
+++ b/solution.py
@@ -5,12 +5,11 @@
 from jax import lax
 from jax.experimental import pallas as pl
 from jax.experimental.pallas import tpu as pltpu
-from jax.sharding import Mesh
 from jax.sharding import PartitionSpec as P
 
 INNER = 4096
 GROUP = 256
-SEQ = ("cs", "core")
+SEQ = "seq"
 
 
 epsilon = 1e-05
@@ -23,8 +22,7 @@
 
 
 def gather_seq(x):
-    chips = lax.all_gather(x, "cs", axis=0, tiled=False)
-    return lax.all_gather(chips, "core", axis=0, tiled=False)
+    return lax.all_gather(x, SEQ, axis=0, tiled=False)
 
 
 def segment_of(position, lengths):
@@ -109,10 +107,8 @@
     request_group,
 ):
     tp_count = lax.axis_size("tp")
-    chip_count = lax.axis_size("cs")
-    core_count = lax.axis_size("core")
-    seq_count = chip_count * core_count
-    seq_index = lax.axis_index("cs") * core_count + lax.axis_index("core")
+    seq_count = lax.axis_size(SEQ)
+    seq_index = lax.axis_index(SEQ)
     tok_dev = tokens.shape[0]
     d_model = tokens.shape[1]
     local_rows = w_zx.shape[0]
@@ -141,9 +137,7 @@
     out_piece = w_out.astype(jnp.bfloat16).T
     gathered = gather_seq(jnp.concatenate([block, out_piece], axis=1))
     gathered = gathered.reshape(seq_count * block_rows, width + out_rows)
-    tokens_perm = tokens.reshape(tok_dev, chip_count, core_count, block_rows)
-    tokens_perm = tokens_perm.transpose(0, 2, 1, 3).reshape(tok_dev, d_model)
-    proj = jnp.dot(tokens_perm, gathered[:, :width], preferred_element_type=jnp.float32)
+    proj = jnp.dot(tokens, gathered[:, :width], preferred_element_type=jnp.float32)
     zx_low = proj[:, : 2 * inner_local].astype(jnp.bfloat16)
     gate_z = zx_low[:, :inner_local]
     x_raw = zx_low[:, inner_local:]
@@ -234,7 +228,7 @@
     )
     dev_gate = every_gate[:, -1]
     rows_at = jnp.arange(seq_count, dtype=jnp.int32)
-    dev_of = (rows_at % chip_count) * core_count + rows_at // chip_count
+    dev_of = rows_at
 
     def carry_weights(k):
         between = (dev_of[:, None] < dev_of[None, :]) & (dev_of[None, :] < k)
@@ -245,7 +239,7 @@
     mine = lax.dynamic_slice_in_dim(request_group, seq_index * req_dev, req_dev)
     req_k = mine // groups_dev
     req_c = mine % groups_dev
-    req_row = (req_k % core_count) * chip_count + req_k // core_count
+    req_row = req_k
     req_gate = every_gate[req_row, req_c]
     wanted = jnp.concatenate([seq_index[None], req_k])
     weights_all = jax.vmap(carry_weights)(wanted)
@@ -284,8 +278,6 @@
     partial = lax.dot_general(
         scaled, gathered[:, width:], (((1,), (1,)), ((), ())), preferred_element_type=jnp.float32
     )
-    partial = partial.reshape(tok_dev, core_count, chip_count, out_cols)
-    partial = partial.transpose(0, 2, 1, 3).reshape(tok_dev, d_model)
     side = jnp.zeros((tok_dev, 128), jnp.float32).at[:, 0].set(square_sum)
     summed = scatter_sum(jnp.concatenate([partial, side], axis=1).astype(jnp.bfloat16), tp_count)
     mean_square = summed[:, d_model] / INNER
@@ -294,16 +286,14 @@
 
 
 def solution(mesh):
-    seq_n, tp_n = mesh.devices.shape
-    view = Mesh(mesh.devices.reshape(seq_n // 2, 2, tp_n), ("cs", "core", "tp"))
     return jax.shard_map(
         on_device,
-        mesh=view,
+        mesh=mesh,
         in_specs=(
             P(SEQ, None),
-            P((*SEQ, "tp"), None),
-            P((*SEQ, "tp"), None),
-            P((*SEQ, "tp"), None),
+            P((SEQ, "tp"), None),
+            P((SEQ, "tp"), None),
+            P((SEQ, "tp"), None),
             P(None, "tp"),
             P("tp"),
             P(),
@@ -316,6 +306,6 @@
             P(),
             P(),
         ),
-        out_specs=(P((*SEQ, "tp"), None), P(SEQ, "tp", None, None)),
+        out_specs=(P((SEQ, "tp"), None), P(SEQ, "tp", None, None)),
         check_vma=False,
     )

time: 320 us -> 223 us (0.70)
  waiting for transfers between devices: 189 us -> 87.2 us
  other arithmetic: 16 us -> 31.2 us
  local copies, waits for them, and re-layouts: 29.2 us -> 14.4 us
  matrix products: 17 us -> 21.2 us
    all_gather x4 -> x2, waiting for transfers between devices: 177 us -> 77.6 us  [gather_seq(): return lax.all_gather(x, SEQ, axis=0, tiled=False)]
    all_gather x1 -> x0, local copies, waits for them, and re-layouts: 9.29 us -> none  [gather_seq(): return lax.all_gather(chips, 'core', axis=0, tiled=False)]
    reshape x2 -> x0, local copies, waits for them, and re-layouts: 7.02 us -> none  [the longest x1 3.73 us: on_device(): partial = partial.reshape(tok_dev, core_count, chip_count, out_cols)]
    another operation x7, other arithmetic: 2.82 us -> 7.47 us
    dot_general x1, matrix products: 0.73 us -> 5.19 us  [on_device(): jnp.einsum('rjh,jhpn->rhpn', coef_lo, every, preferred_element_type=jnp.f...]
  transfers between devices with their start and end apart: 6 -> 4, of which waited for: 6 -> 3; matrix products, arithmetic and copies ran while one was open for 3% -> 8% of each run, Pallas kernels for 0% -> 0%
where the time goes in v5:
time: 223 us; the launch traced here: 221 us
  waiting for transfers between devices  87.2 us (39%)
  Pallas kernels  41.1 us (18%)
  other arithmetic  31.2 us (14%)
  matrix products  21.2 us (10%)
  between operations  14.8 us (7%)
  local copies, waits for them, and re-layouts  14.4 us (6%)
  starting transfers between devices  11.5 us (5%)
    all_gather x2, waiting for transfers between devices, gather_seq(): return lax.all_gather(x, SEQ, axis=0, tiled=False)  77.6 us
    pallas_call x1, Pallas kernels, scatter_sum(): pl.pallas_call(functools.partial(scatter_sum_kernel, count, rows), out_sh...  41.1 us
    all_to_all x1, waiting for transfers between devices, on_device(): lax.all_to_all(packed, 'tp', split_axis=1, concat_axis=0, tiled=True)  9.56 us
    all_to_all x1, starting transfers between devices, on_device(): lax.all_to_all(packed, 'tp', split_axis=1, concat_axis=0, tiled=True)  8.16 us
    another operation x7, other arithmetic  7.47 us
    dot_general x1, matrix products, on_device(): jnp.dot(tokens, gathered[:, :width], preferred_element_type=jnp.float32)  5.92 us
    dot_general x1, matrix products, on_device(): jnp.einsum('rjh,jhpn->rhpn', coef_lo, every, preferred_element_type=jnp.f...  5.19 us
  transfers between devices with their start and end apart: 4, of which 3 were waited for; matrix products, arithmetic and copies ran while one was open for 8% of the time, Pallas kernels for 0%

profile of v5, /device:TPU:1, one launch (start us, length us, event | category | flops | bytes accessed | tf_op | source)
XLA Modules:
  0.0 221.5 jit_solution(543129929340934355)
XLA Ops:
  7.2 1.2 convert_element_type.120
  9.2 0.8 concatenate.53
  10.1 8.2 %all-to-all-start = ((bf16[16,8,1408]{2,0,1:T(8,128)(2,1)}), bf16[16,8,1408]{2,0,1:T(8,128)(2,1)S(1)}, u32[]{:S(2)}, u32[]{:S(2)}) async-start(bf16[16,8,1408]{2,0,1:T(8,128)(2,1)} %concatenate.53), calls=%async_computation | async-start | bytes 720896 | tf_op jit(solution)/shard_map/all_to_all | solution.py:134
  18.4 9.6 %all-to-all-done = bf16[16,8,1408]{2,0,1:T(8,128)(2,1)S(1)} async-done(((bf16[16,8,1408]{2,0,1:T(8,128)(2,1)}), bf16[16,8,1408]{2,0,1:T(8,128)(2,1)S(1)}, u32[]{:S(2)}, u32[]{:S(2)}) %all-to-all-start) | async-done | bytes 360480 | tf_op jit(solution)/shard_map/all_to_all | solution.py:134
  27.9 0.8 pad_maximum_fusion.1
  29.7 0.6 pad_maximum_fusion.3
  30.3 0.8 compare_reduce_fusion.1
  31.1 0.6 slice_reduce_fusion.5
  32.3 0.7 broadcast_compare_fusion.1
  32.9 0.6 slice_compare_fusion.2
  33.6 43.4 %all-gather.5.cloned.1.call-done = bf16[2048,1920]{1,0:T(8,128)(2,1)} async-done(((bf16[128,1920]{1,0:T(8,128)(2,1)}), bf16[2048,1920]{1,0:T(8,128)(2,1)}) %all-gather.5.cloned.1.call-update) | async-done | bytes 7864336 | tf_op jit(solution)/shard_map/all_gather | solution.py:25
  77.0 5.9 %fusion.65 = (bf16[512,1408]{0,1:T(8,128)(2,1)S(1)}, f32[512,1408]{0,1:T(8,128)S(1)}) fusion(bf16[512,2048]{1,0:T(8,128)(2,1)S(1)} %copy-done, bf16[2048,1920]{1,0:T(8,128)(2,1)} %all-gather.5.cloned.1.call-done), kind=kOutput, calls=%fused_computation.141 | convolution fusion | flops 2953510912 | bytes 12189696 | tf_op jit(solution)/shard_map/dot_general | solution.py:140
  83.0 0.9 multiply_bitcast_fusion
  84.0 3.1 %reduce-window.19 = f32[2,8,2,128]{3,1,2,0:T(8,128)} reduce-window(f32[2,8,2,128]{3,1,2,0:T(8,128)} %multiply_bitcast_fusion, f32[]{:T(128)} %constant.149.clone.1), window={size=1x1x1x128 pad=0_0x0_0x0_0x127_0}, to_apply=%region_2.3 | reduce-window | flops 520192 | bytes 32772 | tf_op jit(solution)/shard_map/reduce-window.1
  87.1 1.5 slice_reduce_fusion
  88.5 1.3 reduce-window.20
  89.8 0.7 slice.236
  90.5 1.4 select_bitcast_fusion
  91.9 0.6 copy-done.7
  92.7 0.8 slice.223
  93.5 3.2 %collective-permute-start = (bf16[3,768]{0,1:T(8,128)(2,1)}, bf16[3,768]{0,1:T(8,128)(2,1)}, u32[]{:S(2)}, u32[]{:S(2)}) collective-permute-start(bf16[3,768]{0,1:T(8,128)(2,1)} %slice.223), channel_id=1, source_target_pairs={{0,8},{8,16},{16,24},{24,32},{32,40},{40,48},{48,56},{56,64},{64,7... | collective-permute-start | bytes 13832 | tf_op jit(solution)/shard_map/ppermute | solution.py:21
  96.7 1.3 exponential_select_fusion
  98.1 1.2 reduce_window.9
  99.2 0.7 subtract_convert_fusion.1
  99.9 1.4 select_multiply_fusion.1
  101.3 1.2 slice_bitcast_fusion
  102.5 1.2 slice.224
  104.0 3.4 %multiply_convert_fusion.3 = bf16[512,768]{0,1:T(8,128)(2,1)S(1)} fusion(bf16[512,768]{0,1:T(8,128)(2,1)S(1)} %slice.224, bf16[3,768]{0,1:T(8,128)(2,1)} %collective-permute-done, f32[768]{0:T(1024)} %get-tuple-element.51, f32[768]{0:T(1024)} %get-tuple-element.52, f32[768]{0:T(1024)} %get-tuple-element.53, f32[768]{0:T(1024)} %get-tuple-element.50, ...), kind=kLoop, calls=%fused_computation.22 | loop fusion | flops 11403264 | bytes 1594368 | tf_op jit(solution)/shard_map/convert_element_type | solution.py:164
  107.8 1.0 fusion.32
  108.9 0.7 fusion.40
  109.6 0.7 pad_maximum_fusion.2
  111.0 0.6 compare_reduce_fusion
  112.8 2.5 %fusion.19 = f32[2,256,8,64]{1,3,2,0:T(8,128)} fusion(f32[2,8,256]{2,1,0:T(8,128)S(1)} %bitcast.85, f32[2,256,256]{2,1,0:T(8,128)S(1)} %fusion.43, f32[2,8,256]{2,1,0:T(8,128)S(1)} %copy-done.8, pred[2,256,256]{2,1,0:T(8,128)(4,1)S(1)} %compare_and_fusion, bf16[2,256,8,64]{1,0,3,2:T(2,128)(2,1)S(1)} %reshape.417), kind=kOutput, calls=%fused_computation.23 | convolution fusion | flops 140509184 | bytes 2260992 | tf_op jit(solution)/shard_map/chij,cjhp->cihp/dot_general | solution.py:186
  115.3 34.2 %all-gather.7.cloned.1.call-done = bf16[32,8,72,128]{3,2,1,0:T(8,128)(2,1)} async-done(((bf16[2,8,72,128]{3,2,1,0:T(8,128)(2,1)}), bf16[32,8,72,128]{3,2,1,0:T(8,128)(2,1)}) %all-gather.7.cloned.1.call-update) | async-done | bytes 4718608 | tf_op jit(solution)/shard_map/all_gather | solution.py:25
  149.5 1.1 slice_convert_fusion
  150.7 0.6 fusion.49
  151.4 0.6 gather_fusion
  152.0 0.9 select_reduce_fusion
  153.1 5.2 %fusion.3 = f32[8,72,128,3]{2,3,1,0:T(4,128)S(1)} fusion(bf16[32,8,72,128]{3,2,1,0:T(8,128)(2,1)} %all-gather.7.cloned.1.call-done, bf16[3,32,8,1]{1,2,0,3:T(8,128)(2,1)S(1)} %get-tuple-element.66), kind=kOutput, calls=%fused_computation.6 | convolution fusion | flops 14155776 | bytes 5604864 | tf_op jit(solution)/shard_map/rjh,jhpn->rhpn/dot_general | solution.py:262
  158.3 2.8 %fusion.25 = f32[3,8,72,128]{3,0,2,1:T(4,128)S(1)} fusion(f32[8,72,128,3]{2,3,1,0:T(4,128)S(1)} %fusion.3, bf16[32,8,72,128]{3,2,1,0:T(8,128)(2,1)S(1)} %copy-done.1, bf16[3,32,8,1]{1,2,0,3:T(8,128)(2,1)S(1)} %get-tuple-element.65), kind=kOutput, calls=%fused_computation.28 | convolution fusion | flops 14376960 | bytes 6489600 | tf_op jit(solution)/shard_map/rjh,jhpn->rhpn/dot_general | solution.py:260
  161.6 0.7 copy-done.5
  162.7 0.8 copy.138
  165.1 3.2 %convolution_convert_fusion = bf16[512,2048]{1,0:T(8,128)(2,1)S(1)} fusion(bf16[2048,1920]{1,0:T(8,128)(2,1)} %all-gather.5.cloned.1.call-done, f32[512]{0:T(512)S(1)} %copy-done.26, f32[512,512]{0,1:T(8,128)S(1)} %bitcast.71, bf16[512,1408]{0,1:T(8,128)(2,1)S(1)} %copy-done.3), kind=kOutput, calls=%fused_computation.11 | convolution fusion | flops 1076887552 | bytes 5769216 | tf_op jit(solution)/shard_map/dot_general | solution.py:278
  168.3 1.6 fusion.10.x_ref
  169.9 41.1 %shard_map.158 = f32[64,2176]{1,0:T(8,128)} custom-call(bf16[512,2176]{1,0:T(8,128)(2,1)} %fusion.10.x_ref), custom_call_target="tpu_custom_call" | custom-call | tf_op jit(solution)/shard_map/pallas_call | solution.py:74
  211.0 0.9 rsqrt_reduce_fusion
  211.9 1.9 multiply_convert_fusion.9
  213.8 0.9 copy.140
  (127 shorter events, 7.6 us)
Async XLA Ops:
  7.2 69.8 %copy-start = (bf16[512,2048]{1,0:T(8,128)(2,1)S(1)}, bf16[512,2048]{1,0:T(8,128)(2,1)}, u32[]{:S(2)}) copy-start(bf16[512,2048]{1,0:T(8,128)(2,1)} %param.21) | copy-start | bytes 6291460
  7.2 1.8 copy-start.13
  7.2 1.8 copy-start.15
  7.2 11.1 %copy-start.6 = (f32[512,128]{1,0:T(8,128)S(1)}, f32[512,128]{1,0:T(8,128)}, u32[]{:S(2)}) copy-start(f32[512,128]{1,0:T(8,128)} %param.33) | copy-start | bytes 786436
  8.7 20.1 %copy-start.27 = (s32[8]{0:T(128)S(1)}, s32[8]{0:T(128)}, u32[]{:S(2)}) copy-start(s32[8]{0:T(128)} %param.34) | copy-start | bytes 100
  8.7 20.9 %copy-start.16 = (f32[4,512]{1,0:T(4,128)S(1)}, f32[4,512]{1,0:T(4,128)}, u32[]{:S(2)}) copy-start(f32[4,512]{1,0:T(4,128)} %param.25) | copy-start | bytes 24580
  8.8 20.9 %copy-start.18 = (f32[4,256]{1,0:T(4,128)S(1)}, f32[4,256]{1,0:T(4,128)}, u32[]{:S(2)}) copy-start(f32[4,256]{1,0:T(4,128)} %param.27) | copy-start | bytes 12292
  8.8 21.0 %copy-start.19 = (f32[512]{0:T(512)S(1)}, f32[512]{0:T(512)}, u32[]{:S(2)}) copy-start(f32[512]{0:T(512)} %param.26) | copy-start | bytes 6148
  8.8 21.0 %copy-start.20 = (f32[256]{0:T(256)S(1)}, f32[256]{0:T(256)}, u32[]{:S(2)}) copy-start(f32[256]{0:T(256)} %param.28) | copy-start | bytes 3076
  8.8 22.9 %copy-start.28 = (f32[8]{0:T(128)S(1)}, f32[8]{0:T(128)}, u32[]{:S(2)}) copy-start(f32[8]{0:T(128)} %param.30) | copy-start | bytes 100
  10.1 17.9 %all-to-all-start = ((bf16[16,8,1408]{2,0,1:T(8,128)(2,1)}), bf16[16,8,1408]{2,0,1:T(8,128)(2,1)S(1)}, u32[]{:S(2)}, u32[]{:S(2)}) async-start(bf16[16,8,1408]{2,0,1:T(8,128)(2,1)} %concatenate.53), calls=%async_computation | async-start | bytes 720896 | tf_op jit(solution)/shard_map/all_to_all | solution.py:134
  18.2 58.7 %all-gather.5.cloned.1.call-start = ((), (), s32[]{:S(2)}) async-start(), calls=%async_computation.1 | async-start | bytes 8355840 | tf_op jit(solution)/shard_map/all_gather | solution.py:25
  28.8 120.8 %all-gather.7.cloned.1.call-start = ((), (), s32[]{:S(2)}) async-start(), calls=%async_computation.2 | async-start | bytes 5013504 | tf_op jit(solution)/shard_map/all_gather | solution.py:25
  29.2 4.3 %copy-start.10 = (s32[2,256]{1,0:T(2,128)}, s32[2,256]{1,0:T(2,128)S(1)}, u32[]{:S(2)}) copy-start(s32[2,256]{1,0:T(2,128)S(1)} %eq.107) | copy-start | bytes 6148
  77.0 5.9 %copy-start.21 = (f32[8]{0:T(128)S(1)}, f32[8]{0:T(128)}, u32[]{:S(2)}) copy-start(f32[8]{0:T(128)} %param.29) | copy-start | bytes 100
  77.0 6.0 %copy-start.24 = (f32[8]{0:T(128)S(1)}, f32[8]{0:T(128)}, u32[]{:S(2)}) copy-start(f32[8]{0:T(128)} %exponential_negate_fusion) | copy-start | bytes 100
  82.9 18.5 %copy-start.2 = (bf16[512,1408]{0,1:T(8,128)(2,1)}, bf16[512,1408]{0,1:T(8,128)(2,1)S(1)}, u32[]{:S(2)}) copy-start(bf16[512,1408]{0,1:T(8,128)(2,1)S(1)} %get-tuple-element.74) | copy-start | bytes 4325380
  91.9 0.6 copy-start.7
  92.7 4.1 %copy-start.14 = (f32[2,8]{1,0:T(2,128)}, f32[2,8]{1,0:T(2,128)S(1)}, u32[]{:S(2)}) copy-start(f32[2,8]{1,0:T(2,128)S(1)} %slice_reduce_fusion.1) | copy-start | bytes 196
  93.5 10.5 %collective-permute-start = (bf16[3,768]{0,1:T(8,128)(2,1)}, bf16[3,768]{0,1:T(8,128)(2,1)}, u32[]{:S(2)}, u32[]{:S(2)}) collective-permute-start(bf16[3,768]{0,1:T(8,128)(2,1)} %slice.223), channel_id=1, source_target_pairs={{0,8},{8,16},{16,24},{24,32},{32,40},{40,48},{48,56},{56,64},{64,7... | collective-permute-start | bytes 13832 | tf_op jit(solution)/shard_map/ppermute | solution.py:21
  104.0 3.8 %copy-start.12 = (f32[2,8,256]{2,1,0:T(8,128)S(1)}, f32[2,8,256]{2,1,0:T(8,128)}, u32[]{:S(2)}) copy-start(f32[2,8,256]{2,1,0:T(8,128)} %select_multiply_fusion.1) | copy-start | bytes 49156
  107.4 1.5 copy-start.23
  107.6 2.8 %copy-start.25 = (s32[32]{0:T(128)S(1)}, s32[32]{0:T(128)}, u32[]{:S(2)}) copy-start(s32[32]{0:T(128)} %param.35) | copy-start | bytes 388
  107.6 4.1 %copy-start.11 = (s32[2,256]{1,0:T(2,128)S(1)}, s32[2,256]{1,0:T(2,128)}, u32[]{:S(2)}) copy-start(s32[2,256]{1,0:T(2,128)} %copy-done.10) | copy-start | bytes 6148
  107.6 4.3 %slice-start = ((f32[2,8]{1,0:T(2,128)}), f32[1,8]{1,0:T(1,128)S(1)}, s32[]{:S(2)}) async-start(f32[2,8]{1,0:T(2,128)} %reduce_window.9), calls=%async_computation.3 | async-start | bytes 1024 | tf_op jit(solution)/shard_map/slice | solution.py:213
  108.8 4.0 %copy-start.8 = (f32[2,8,256]{2,1,0:T(8,128)S(1)}, f32[2,8,256]{2,1,0:T(8,128)}, u32[]{:S(2)}) copy-start(f32[2,8,256]{2,1,0:T(8,128)} %copy-done.7) | copy-start | bytes 49156
  153.1 5.2 %copy-start.1 = (bf16[32,8,72,128]{3,2,1,0:T(8,128)(2,1)S(1)}, bf16[32,8,72,128]{3,2,1,0:T(8,128)(2,1)}, u32[]{:S(2)}) copy-start(bf16[32,8,72,128]{3,2,1,0:T(8,128)(2,1)} %all-gather.7.cloned.1.call-done) | copy-start | bytes 14155780
  158.3 3.3 %copy-start.4 = (f32[1,8,64,128]{3,2,1,0:T(8,128)S(1)}, f32[1,8,64,128]{3,2,1,0:T(8,128)}, u32[]{:S(2)}) copy-start(f32[1,8,64,128]{3,2,1,0:T(8,128)} %get-tuple-element.64) | copy-start | bytes 786436
  158.3 3.3 %copy-start.9 = (f32[2,256,8]{1,2,0:T(8,128)S(1)}, f32[2,256,8]{1,2,0:T(8,128)}, u32[]{:S(2)}) copy-start(f32[2,256,8]{1,2,0:T(8,128)} %get-tuple-element.59) | copy-start | bytes 49156
  158.3 3.3 %copy-start.17 = (f32[2,8]{1,0:T(2,128)S(1)}, f32[2,8]{1,0:T(2,128)}, u32[]{:S(2)}) copy-start(f32[2,8]{1,0:T(2,128)} %concatenate.58) | copy-start | bytes 196
  158.3 3.3 %copy-start.22 = (f32[8]{0:T(128)S(1)}, f32[8]{0:T(128)}, u32[]{:S(2)}) copy-start(f32[8]{0:T(128)} %param.31) | copy-start | bytes 100
  161.1 1.2 copy-start.5
  162.7 1.4 copy-start.3
  163.5 1.6 copy-start.26
Sparse Core Ops, SparseCore 0:
  28.9 47.9 all-gather.4
  110.5 39.0 all-gather.6

commit v6 on v5

--- a/solution.py
+++ b/solution.py
@@ -83,6 +83,70 @@
         ],
         compiler_params=pltpu.CompilerParams(collective_id=0, has_side_effects=True),
     )(x)
+
+
+def carry_kernel(count, width, mine_ref, out_ref, recv, acc, send_sem, recv_sem):
+    me = lax.axis_index(SEQ)
+    barrier = pltpu.get_barrier_semaphore()
+    for d in range(1, count):
+        peer = lax.rem(me + d, count)
+        pl.semaphore_signal(barrier, inc=1, device_id={SEQ: peer}, device_id_type=pl.DeviceIdType.MESH)
+    pl.semaphore_wait(barrier, count - 1)
+
+    def send_to(d):
+        return pltpu.make_async_remote_copy(
+            src_ref=mine_ref,
+            dst_ref=recv.at[me],
+            send_sem=send_sem.at[d],
+            recv_sem=recv_sem.at[me],
+            device_id={SEQ: me + d},
+            device_id_type=pl.DeviceIdType.MESH,
+        )
+
+    for d in range(1, count):
+        @pl.when(me + d < count)
+        def _():
+            send_to(d).start()
+
+    acc[...] = jnp.zeros_like(acc)
+    for j in range(count - 1):
+        @pl.when(j < me)
+        def _():
+            pltpu.make_async_remote_copy(
+                src_ref=mine_ref,
+                dst_ref=recv.at[j],
+                send_sem=send_sem.at[0],
+                recv_sem=recv_sem.at[j],
+                device_id={SEQ: j},
+                device_id_type=pl.DeviceIdType.MESH,
+            ).wait_recv()
+            tail = recv[j, :, width : width + 16, :].astype(jnp.float32)
+            gate = tail[:, 0:1, :] + tail[:, 1:2, :]
+            acc[...] = gate * acc[...] + recv[j, :, :width, :].astype(jnp.float32)
+
+    for d in range(1, count):
+        @pl.when(me + d < count)
+        def _():
+            send_to(d).wait_send()
+    out_ref[...] = acc[...]
+
+
+def carry_in(mine, width):
+    count = lax.axis_size(SEQ)
+    heads, _, lanes = mine.shape
+    return pl.pallas_call(
+        functools.partial(carry_kernel, count, width),
+        out_shape=jax.ShapeDtypeStruct((heads, width, lanes), jnp.float32),
+        in_specs=[pl.BlockSpec(memory_space=pltpu.VMEM)],
+        out_specs=pl.BlockSpec(memory_space=pltpu.VMEM),
+        scratch_shapes=[
+            pltpu.VMEM((count,) + mine.shape, mine.dtype),
+            pltpu.VMEM((heads, width, lanes), jnp.float32),
+            pltpu.SemaphoreType.DMA((count,)),
+            pltpu.SemaphoreType.DMA((count,)),
+        ],
+        compiler_params=pltpu.CompilerParams(collective_id=1, has_side_effects=True),
+    )(mine)
 
 
 def round_up(n, m):
@@ -215,12 +279,13 @@
 
     gate_hi = through_group.astype(jnp.bfloat16)
     gate_lo = (through_group - gate_hi.astype(jnp.float32)).astype(jnp.bfloat16)
-    extra = jnp.zeros((groups_dev, heads_local, 8, state_width), jnp.bfloat16)
+    extra = jnp.zeros((groups_dev, heads_local, 16, state_width), jnp.bfloat16)
     extra = extra.at[:, :, 0, :].set(jnp.broadcast_to(gate_hi[:, :, None], gate_hi.shape + (state_width,)))
     extra = extra.at[:, :, 1, :].set(jnp.broadcast_to(gate_lo[:, :, None], gate_lo.shape + (state_width,)))
     sendable = jnp.concatenate([local_end.astype(jnp.bfloat16), extra], axis=2)
+    carried = carry_in(sendable[-1], head_width)
     every = gather_seq(sendable).reshape(
-        (seq_count * groups_dev, heads_local, head_width + 8, state_width)
+        (seq_count * groups_dev, heads_local, head_width + 16, state_width)
     )
     gate_rows = every[:, :, head_width : head_width + 2, :].astype(jnp.float32)
     every_gate = (gate_rows[:, :, 0, 0] + gate_rows[:, :, 1, 0]).reshape(
@@ -241,15 +306,14 @@
     req_c = mine % groups_dev
     req_row = req_k
     req_gate = every_gate[req_row, req_c]
-    wanted = jnp.concatenate([seq_index[None], req_k])
+    wanted = req_k
     weights_all = jax.vmap(carry_weights)(wanted)
-    scales = jnp.concatenate([jnp.ones((1, heads_local), jnp.float32), req_gate], axis=0)
-    weights_all = weights_all * scales[:, None, :]
+    weights_all = weights_all * req_gate[:, None, :]
     slot_ids = jnp.arange(groups_dev, dtype=jnp.int32)
     last_slot = (slot_ids == groups_dev - 1).astype(jnp.float32)
     coef = weights_all[:, :, None, :] * last_slot[None, None, :, None]
-    own_row = jnp.concatenate([jnp.full((1,), -1, jnp.int32), req_row])
-    own_slot = jnp.concatenate([jnp.full((1,), -1, jnp.int32), req_c])
+    own_row = req_row
+    own_slot = req_c
     hit = (rows_at[None, :, None] == own_row[:, None, None]) & (
         slot_ids[None, None, :] == own_slot[:, None, None]
     )
@@ -260,8 +324,7 @@
     summed_states = jnp.einsum(
         "rjh,jhpn->rhpn", coef_hi, every, preferred_element_type=jnp.float32
     ) + jnp.einsum("rjh,jhpn->rhpn", coef_lo, every, preferred_element_type=jnp.float32)
-    carried = summed_states[0, :, :head_width]
-    request_states = summed_states[1:, :, :head_width]
+    request_states = summed_states[:, :, :head_width]
 
     group_in = before_group[:, :, None, None] * carried[None] + local_in
     state_low = group_in.astype(jnp.bfloat16)

time: 223 us -> 225 us (level)
  Pallas kernels: 41.1 us -> 92 us
  waiting for transfers between devices: 87.2 us -> 56.4 us
  other arithmetic: 31.2 us -> 16.3 us
  local copies, waits for them, and re-layouts: 14.4 us -> 10.3 us
    pallas_call x0 -> x1, Pallas kernels: none -> 57.2 us  [carry_in(): pl.pallas_call(functools.partial(carry_kernel, count, width), out_shape=j...]
    all_gather x2, waiting for transfers between devices: 77.6 us -> 46.8 us  [gather_seq(): return lax.all_gather(x, SEQ, axis=0, tiled=False)]
    pallas_call x1, Pallas kernels: 41.1 us -> 34.8 us  [scatter_sum(): pl.pallas_call(functools.partial(scatter_sum_kernel, count, rows), out_sh...]
    another operation x7, other arithmetic: 7.47 us -> 2.8 us
  transfers between devices with their start and end apart: 4 -> 4, of which waited for: 3 -> 2; matrix products, arithmetic and copies ran while one was open for 8% -> 9% of each run, Pallas kernels for 0% -> 41%
where the time goes in v6:
time: 225 us; the launch traced here: 223 us
  Pallas kernels  92 us (41%)
  waiting for transfers between devices  56.4 us (25%)
  matrix products  21.3 us (9%)
  other arithmetic  16.3 us (7%)
  between operations  14.7 us (7%)
  starting transfers between devices  11.5 us (5%)
  local copies, waits for them, and re-layouts  10.3 us (5%)
    pallas_call x1, Pallas kernels, carry_in(): pl.pallas_call(functools.partial(carry_kernel, count, width), out_shape=j...  57.2 us
    all_gather x2, waiting for transfers between devices, gather_seq(): return lax.all_gather(x, SEQ, axis=0, tiled=False)  46.8 us
    pallas_call x1, Pallas kernels, scatter_sum(): pl.pallas_call(functools.partial(scatter_sum_kernel, count, rows), out_sh...  34.8 us
    all_to_all x1, waiting for transfers between devices, on_device(): lax.all_to_all(packed, 'tp', split_axis=1, concat_axis=0, tiled=True)  9.56 us
    all_to_all x1, starting transfers between devices, on_device(): lax.all_to_all(packed, 'tp', split_axis=1, concat_axis=0, tiled=True)  8.16 us
    dot_general x1, matrix products, on_device(): jnp.dot(tokens, gathered[:, :width], preferred_element_type=jnp.float32)  5.9 us
    dot_general x1, matrix products, on_device(): jnp.einsum('rjh,jhpn->rhpn', coef_lo, every, preferred_element_type=jnp.f...  5.63 us
  transfers between devices with their start and end apart: 4, of which 2 were waited for; matrix products, arithmetic and copies ran while one was open for 9% of the time, Pallas kernels for 41%

profile of v6, /device:TPU:1, one launch (start us, length us, event | category | flops | bytes accessed | tf_op | source)
XLA Modules:
  0.0 222.6 jit_solution(5103307507119345640)
XLA Ops:
  7.2 1.2 convert_element_type.120
  8.5 0.2 copy.183
  8.8 0.2 reshape.414
  9.2 0.8 concatenate.41
  10.1 8.2 %all-to-all-start = ((bf16[16,8,1408]{2,0,1:T(8,128)(2,1)}), bf16[16,8,1408]{2,0,1:T(8,128)(2,1)S(1)}, u32[]{:S(2)}, u32[]{:S(2)}) async-start(bf16[16,8,1408]{2,0,1:T(8,128)(2,1)} %concatenate.41), calls=%async_computation | async-start | bytes 720896 | tf_op jit(solution)/shard_map/all_to_all | solution.py:198
  18.4 9.6 %all-to-all-done = bf16[16,8,1408]{2,0,1:T(8,128)(2,1)S(1)} async-done(((bf16[16,8,1408]{2,0,1:T(8,128)(2,1)}), bf16[16,8,1408]{2,0,1:T(8,128)(2,1)S(1)}, u32[]{:S(2)}, u32[]{:S(2)}) %all-to-all-start) | async-done | bytes 360480 | tf_op jit(solution)/shard_map/all_to_all | solution.py:198
  27.9 0.8 pad_maximum_fusion.1
  28.9 0.2 reduce-window.18
  29.2 0.2 fusion.55
  29.5 0.2 slice_reduce_fusion.6
  29.8 0.2 compare_reduce_fusion.1
  30.2 46.8 %all-gather.5.cloned.1.call-done = bf16[2048,1920]{1,0:T(8,128)(2,1)} async-done(((bf16[128,1920]{1,0:T(8,128)(2,1)}), bf16[2048,1920]{1,0:T(8,128)(2,1)}) %all-gather.5.cloned.1.call-update) | async-done | bytes 7864336 | tf_op jit(solution)/shard_map/all_gather | solution.py:25
  77.0 5.9 %fusion.65 = (bf16[512,1408]{0,1:T(8,128)(2,1)S(1)}, f32[512,1408]{0,1:T(8,128)S(1)}) fusion(bf16[512,2048]{1,0:T(8,128)(2,1)S(1)} %copy-done, bf16[2048,1920]{1,0:T(8,128)(2,1)} %all-gather.5.cloned.1.call-done), kind=kOutput, calls=%fused_computation.139 | convolution fusion | flops 2953510912 | bytes 12189696 | tf_op jit(solution)/shard_map/dot_general | solution.py:204
  82.9 1.1 copy-done.1
  84.1 3.3 %collective-permute-start = (bf16[3,768]{0,1:T(8,128)(2,1)S(1)}, bf16[3,768]{0,1:T(8,128)(2,1)S(1)}, u32[]{:S(2)}, u32[]{:S(2)}) collective-permute-start(bf16[3,768]{0,1:T(8,128)(2,1)S(1)} %slice.223), channel_id=1, source_target_pairs={{0,8},{8,16},{16,24},{24,32},{32,40},{40,48},{48,56},{56,64},{64,7... | collective-permute-start | bytes 13832 | tf_op jit(solution)/shard_map/ppermute | solution.py:21
  87.5 1.1 reduce-window.19
  88.7 0.2 slice_reduce_fusion
  89.0 0.2 slice_reduce_fusion.1
  89.3 1.2 slice.224
  90.8 2.1 multiply_convert_fusion.3
  93.0 0.1 reshape.417
  93.2 0.1 copy.128
  93.3 1.0 fusion.32
  94.5 0.7 pad_maximum_fusion.2
  95.8 0.7 compare_reduce_fusion
  96.5 0.2 compare_and_fusion
  96.7 1.6 slice_bitcast_fusion.mine_ref
  98.3 57.2 %shard_map.158 = f32[8,64,128]{2,1,0:T(8,128)} custom-call(bf16[8,80,128]{2,1,0:T(8,128)(2,1)} %slice_bitcast_fusion.mine_ref), custom_call_target="tpu_custom_call" | custom-call | tf_op jit(solution)/shard_map/pallas_call | solution.py:137
  155.6 0.3 fusion.43
  155.9 1.8 fusion.19
  157.7 0.4 fusion.21
  158.1 0.8 copy.132
  159.0 0.4 copy-done.2
  159.5 0.4 multiply_reduce_fusion
  159.9 0.6 select_convert_fusion
  160.5 0.1 reshape.452
  160.6 3.2 %convolution_convert_fusion = bf16[512,2048]{1,0:T(8,128)(2,1)S(1)} fusion(bf16[2048,1920]{1,0:T(8,128)(2,1)} %all-gather.5.cloned.1.call-done, f32[512]{0:T(512)S(1)} %copy-done.15, f32[512,512]{0,1:T(8,128)S(1)} %bitcast.71, bf16[512,1408]{0,1:T(8,128)(2,1)S(1)} %copy-done.2), kind=kOutput, calls=%fused_computation.11 | convolution fusion | flops 1076887552 | bytes 5769216 | tf_op jit(solution)/shard_map/dot_general | solution.py:341
  163.8 1.6 fusion.10.x_ref
  165.4 34.8 %shard_map.159 = f32[64,2176]{1,0:T(8,128)} custom-call(bf16[512,2176]{1,0:T(8,128)(2,1)} %fusion.10.x_ref), custom_call_target="tpu_custom_call" | custom-call | tf_op jit(solution)/shard_map/pallas_call | solution.py:74
  200.2 0.9 rsqrt_reduce_fusion
  201.0 1.9 multiply_convert_fusion.9
  202.9 1.1 slice_convert_fusion
  204.0 0.6 fusion.49
  204.7 0.6 gather_fusion
  205.3 0.6 select_reduce_fusion
  206.1 5.6 %fusion.2 = f32[8,80,128,2]{2,3,1,0:T(2,128)S(1)} fusion(bf16[32,8,80,128]{3,2,1,0:T(8,128)(2,1)} %all-gather.7.cloned.1.call-done, bf16[2,32,8,1]{1,2,0,3:T(8,128)(2,1)S(1)} %get-tuple-element.66), kind=kOutput, calls=%fused_computation.3 | convolution fusion | flops 10485760 | bytes 5899264 | tf_op jit(solution)/shard_map/rjh,jhpn->rhpn/dot_general | solution.py:326
  211.7 3.1 %fusion.25 = f32[2,8,80,128]{3,0,2,1:T(2,128)S(1)} fusion(f32[8,80,128,2]{2,3,1,0:T(2,128)S(1)} %fusion.2, bf16[32,8,80,128]{3,2,1,0:T(8,128)(2,1)S(1)} %copy-done.9, bf16[2,32,8,1]{1,2,0,3:T(8,128)(2,1)S(1)} %get-tuple-element.65), kind=kOutput, calls=%fused_computation.32 | convolution fusion | flops 10649600 | bytes 6554624 | tf_op jit(solution)/shard_map/rjh,jhpn->rhpn/dot_general | solution.py:324
  214.9 0.9 copy.140
  (102 shorter events, 3.1 us)
Async XLA Ops:
  7.2 69.8 %copy-start = (bf16[512,2048]{1,0:T(8,128)(2,1)S(1)}, bf16[512,2048]{1,0:T(8,128)(2,1)}, u32[]{:S(2)}) copy-start(bf16[512,2048]{1,0:T(8,128)(2,1)} %param.21) | copy-start | bytes 6291460
  7.2 1.8 copy-start.5
  7.2 1.8 copy-start.6
  7.2 11.1 %copy-start.4 = (f32[512,128]{1,0:T(8,128)S(1)}, f32[512,128]{1,0:T(8,128)}, u32[]{:S(2)}) copy-start(f32[512,128]{1,0:T(8,128)} %param.33) | copy-start | bytes 786436
  8.7 20.1 %copy-start.16 = (s32[8]{0:T(128)S(1)}, s32[8]{0:T(128)}, u32[]{:S(2)}) copy-start(s32[8]{0:T(128)} %param.34) | copy-start | bytes 100
  8.7 20.9 %copy-start.7 = (f32[4,512]{1,0:T(4,128)S(1)}, f32[4,512]{1,0:T(4,128)}, u32[]{:S(2)}) copy-start(f32[4,512]{1,0:T(4,128)} %param.25) | copy-start | bytes 24580
  8.8 20.9 %copy-start.8 = (f32[4,256]{1,0:T(4,128)S(1)}, f32[4,256]{1,0:T(4,128)}, u32[]{:S(2)}) copy-start(f32[4,256]{1,0:T(4,128)} %param.27) | copy-start | bytes 12292
  8.8 21.0 %copy-start.10 = (f32[512]{0:T(512)S(1)}, f32[512]{0:T(512)}, u32[]{:S(2)}) copy-start(f32[512]{0:T(512)} %param.26) | copy-start | bytes 6148
  8.8 21.0 %copy-start.11 = (f32[256]{0:T(256)S(1)}, f32[256]{0:T(256)}, u32[]{:S(2)}) copy-start(f32[256]{0:T(256)} %param.28) | copy-start | bytes 3076
  8.8 21.2 %copy-start.17 = (f32[8]{0:T(128)S(1)}, f32[8]{0:T(128)}, u32[]{:S(2)}) copy-start(f32[8]{0:T(128)} %param.30) | copy-start | bytes 100
  10.1 17.9 %all-to-all-start = ((bf16[16,8,1408]{2,0,1:T(8,128)(2,1)}), bf16[16,8,1408]{2,0,1:T(8,128)(2,1)S(1)}, u32[]{:S(2)}, u32[]{:S(2)}) async-start(bf16[16,8,1408]{2,0,1:T(8,128)(2,1)} %concatenate.41), calls=%async_computation | async-start | bytes 720896 | tf_op jit(solution)/shard_map/all_to_all | solution.py:198
  18.2 58.7 %all-gather.5.cloned.1.call-start = ((), (), s32[]{:S(2)}) async-start(), calls=%async_computation.1 | async-start | bytes 8355840 | tf_op jit(solution)/shard_map/all_gather | solution.py:25
  28.8 174.1 %all-gather.7.cloned.1.call-start = ((), (), s32[]{:S(2)}) async-start(), calls=%async_computation.2 | async-start | bytes 5570560 | tf_op jit(solution)/shard_map/all_gather | solution.py:25
  30.2 57.2 %copy-start.12 = (f32[8]{0:T(128)S(1)}, f32[8]{0:T(128)}, u32[]{:S(2)}) copy-start(f32[8]{0:T(128)} %param.29) | copy-start | bytes 100
  82.9 1.1 copy-start.1
  84.1 6.7 %collective-permute-start = (bf16[3,768]{0,1:T(8,128)(2,1)S(1)}, bf16[3,768]{0,1:T(8,128)(2,1)S(1)}, u32[]{:S(2)}, u32[]{:S(2)}) collective-permute-start(bf16[3,768]{0,1:T(8,128)(2,1)S(1)} %slice.223), channel_id=1, source_target_pairs={{0,8},{8,16},{16,24},{24,32},{32,40},{40,48},{48,56},{56,64},{64,7... | collective-permute-start | bytes 13832 | tf_op jit(solution)/shard_map/ppermute | solution.py:21
  93.2 2.1 copy-start.14
  155.8 1.9 copy-start.3
  155.9 1.9 copy-start.13
  158.1 1.4 copy-start.2
  159.0 1.7 copy-start.15
  206.1 5.6 %copy-start.9 = (bf16[32,8,80,128]{3,2,1,0:T(8,128)(2,1)S(1)}, bf16[32,8,80,128]{3,2,1,0:T(8,128)(2,1)}, u32[]{:S(2)}) copy-start(bf16[32,8,80,128]{3,2,1,0:T(8,128)(2,1)} %all-gather.7.cloned.1.call-done) | copy-start | bytes 15728644
Sparse Core Ops, SparseCore 0:
  28.9 47.9 all-gather.4
  95.4 63.5 all-gather.6

commit v7 on v6

--- a/solution.py
+++ b/solution.py
@@ -284,7 +284,8 @@
     extra = extra.at[:, :, 1, :].set(jnp.broadcast_to(gate_lo[:, :, None], gate_lo.shape + (state_width,)))
     sendable = jnp.concatenate([local_end.astype(jnp.bfloat16), extra], axis=2)
     carried = carry_in(sendable[-1], head_width)
-    every = gather_seq(sendable).reshape(
+    carried, later = lax.optimization_barrier((carried, sendable))
+    every = gather_seq(later).reshape(
         (seq_count * groups_dev, heads_local, head_width + 16, state_width)
     )
     gate_rows = every[:, :, head_width : head_width + 2, :].astype(jnp.float32)

time: 225 us -> 220 us (0.978)
  Pallas kernels: 92 us -> 73.9 us
  waiting for transfers between devices: 56.4 us -> 72.1 us
    pallas_call x1, Pallas kernels: 57.2 us -> 34 us  [carry_in(): pl.pallas_call(functools.partial(carry_kernel, count, width), out_shape=j...]
    all_gather x2, waiting for transfers between devices: 46.8 us -> 62.5 us  [gather_seq(): return lax.all_gather(x, SEQ, axis=0, tiled=False)]
    pallas_call x1, Pallas kernels: 34.8 us -> 39.9 us  [scatter_sum(): pl.pallas_call(functools.partial(scatter_sum_kernel, count, rows), out_sh...]
  transfers between devices with their start and end apart: 4 -> 4, of which waited for: 2 -> 3; matrix products, arithmetic and copies ran while one was open for 9% -> 8% of each run, Pallas kernels for 41% -> 18%
where the time goes in v7:
time: 220 us; the launch traced here: 219 us
  Pallas kernels  73.9 us (34%)
  waiting for transfers between devices  72.1 us (33%)
  matrix products  21.3 us (10%)
  other arithmetic  16.2 us (7%)
  between operations  14.7 us (7%)
  starting transfers between devices  11.5 us (5%)
  local copies, waits for them, and re-layouts  9.48 us (4%)
    all_gather x2, waiting for transfers between devices, gather_seq(): return lax.all_gather(x, SEQ, axis=0, tiled=False)  62.5 us
    pallas_call x1, Pallas kernels, scatter_sum(): pl.pallas_call(functools.partial(scatter_sum_kernel, count, rows), out_sh...  39.9 us
    pallas_call x1, Pallas kernels, carry_in(): pl.pallas_call(functools.partial(carry_kernel, count, width), out_shape=j...  34 us
    all_to_all x1, waiting for transfers between devices, on_device(): lax.all_to_all(packed, 'tp', split_axis=1, concat_axis=0, tiled=True)  9.56 us
    all_to_all x1, starting transfers between devices, on_device(): lax.all_to_all(packed, 'tp', split_axis=1, concat_axis=0, tiled=True)  8.16 us
    dot_general x1, matrix products, on_device(): jnp.dot(tokens, gathered[:, :width], preferred_element_type=jnp.float32)  5.9 us
    dot_general x1, matrix products, on_device(): jnp.einsum('rjh,jhpn->rhpn', coef_lo, every, preferred_element_type=jnp.f...  5.63 us
  transfers between devices with their start and end apart: 4, of which 3 were waited for; matrix products, arithmetic and copies ran while one was open for 8% of the time, Pallas kernels for 18%

profile of v7, /device:TPU:1, one launch (start us, length us, event | category | flops | bytes accessed | tf_op | source)
XLA Modules:
  0.0 219.3 jit_solution(5579884811084830040)
XLA Ops:
  7.2 1.2 convert_element_type.120
  8.5 0.2 copy.183
  8.8 0.2 reshape.414
  9.2 0.8 concatenate.41
  10.1 8.2 %all-to-all-start = ((bf16[16,8,1408]{2,0,1:T(8,128)(2,1)}), bf16[16,8,1408]{2,0,1:T(8,128)(2,1)S(1)}, u32[]{:S(2)}, u32[]{:S(2)}) async-start(bf16[16,8,1408]{2,0,1:T(8,128)(2,1)} %concatenate.41), calls=%async_computation | async-start | bytes 720896 | tf_op jit(solution)/shard_map/all_to_all | solution.py:198
  18.4 9.6 %all-to-all-done = bf16[16,8,1408]{2,0,1:T(8,128)(2,1)S(1)} async-done(((bf16[16,8,1408]{2,0,1:T(8,128)(2,1)}), bf16[16,8,1408]{2,0,1:T(8,128)(2,1)S(1)}, u32[]{:S(2)}, u32[]{:S(2)}) %all-to-all-start) | async-done | bytes 360480 | tf_op jit(solution)/shard_map/all_to_all | solution.py:198
  27.9 0.8 pad_maximum_fusion.1
  28.9 0.2 reduce-window.18
  29.2 0.2 fusion.55
  29.5 0.2 slice_reduce_fusion.6
  29.8 0.2 compare_reduce_fusion.1
  30.2 46.8 %all-gather.5.cloned.1.call-done = bf16[2048,1920]{1,0:T(8,128)(2,1)} async-done(((bf16[128,1920]{1,0:T(8,128)(2,1)}), bf16[2048,1920]{1,0:T(8,128)(2,1)}) %all-gather.5.cloned.1.call-update) | async-done | bytes 7864336 | tf_op jit(solution)/shard_map/all_gather | solution.py:25
  77.0 5.9 %fusion.65 = (bf16[512,1408]{0,1:T(8,128)(2,1)S(1)}, f32[512,1408]{0,1:T(8,128)S(1)}) fusion(bf16[512,2048]{1,0:T(8,128)(2,1)S(1)} %copy-done, bf16[2048,1920]{1,0:T(8,128)(2,1)} %all-gather.5.cloned.1.call-done), kind=kOutput, calls=%fused_computation.139 | convolution fusion | flops 2953510912 | bytes 12189696 | tf_op jit(solution)/shard_map/dot_general | solution.py:204
  82.9 1.1 copy-done.2
  84.1 3.3 %collective-permute-start = (bf16[3,768]{0,1:T(8,128)(2,1)S(1)}, bf16[3,768]{0,1:T(8,128)(2,1)S(1)}, u32[]{:S(2)}, u32[]{:S(2)}) collective-permute-start(bf16[3,768]{0,1:T(8,128)(2,1)S(1)} %slice.223), channel_id=1, source_target_pairs={{0,8},{8,16},{16,24},{24,32},{32,40},{40,48},{48,56},{56,64},{64,7... | collective-permute-start | bytes 13832 | tf_op jit(solution)/shard_map/ppermute | solution.py:21
  87.5 1.1 reduce-window.19
  88.7 0.2 slice_reduce_fusion
  89.0 0.2 slice_reduce_fusion.1
  89.3 1.2 slice.224
  90.8 2.1 multiply_convert_fusion.3
  93.0 0.1 reshape.417
  93.3 1.0 fusion.32
  94.4 0.7 fusion.40
  95.1 0.7 slice_bitcast_fusion.mine_ref
  95.9 34.0 %shard_map.158 = f32[8,64,128]{2,1,0:T(8,128)} custom-call(bf16[8,80,128]{2,1,0:T(8,128)(2,1)} %slice_bitcast_fusion.mine_ref), custom_call_target="tpu_custom_call" | custom-call | tf_op jit(solution)/shard_map/pallas_call | solution.py:137
  130.4 0.7 compare_reduce_fusion
  131.2 0.2 compare_and_fusion
  131.4 0.3 fusion.43
  131.7 1.8 fusion.19
  133.6 0.4 fusion.21
  134.0 0.8 copy.132
  134.9 0.4 copy-done.3
  135.4 0.4 multiply_reduce_fusion
  135.7 0.6 select_convert_fusion
  136.3 0.1 reshape.452
  136.5 3.2 %convolution_convert_fusion = bf16[512,2048]{1,0:T(8,128)(2,1)S(1)} fusion(bf16[2048,1920]{1,0:T(8,128)(2,1)} %all-gather.5.cloned.1.call-done, f32[512]{0:T(512)S(1)} %copy-done.17, f32[512,512]{0,1:T(8,128)S(1)} %bitcast.71, bf16[512,1408]{0,1:T(8,128)(2,1)S(1)} %copy-done.3), kind=kOutput, calls=%fused_computation.11 | convolution fusion | flops 1076887552 | bytes 5769216 | tf_op jit(solution)/shard_map/dot_general | solution.py:342
  139.6 1.6 fusion.10.x_ref
  141.2 39.9 %shard_map.159 = f32[64,2176]{1,0:T(8,128)} custom-call(bf16[512,2176]{1,0:T(8,128)(2,1)} %fusion.10.x_ref), custom_call_target="tpu_custom_call" | custom-call | tf_op jit(solution)/shard_map/pallas_call | solution.py:74
  181.1 0.9 rsqrt_reduce_fusion
  182.0 1.8 multiply_convert_fusion.9
  183.9 15.8 %all-gather.7.cloned.1.call-done = bf16[32,8,80,128]{3,2,1,0:T(8,128)(2,1)} async-done(((bf16[2,8,80,128]{3,2,1,0:T(8,128)(2,1)}), bf16[32,8,80,128]{3,2,1,0:T(8,128)(2,1)}) %all-gather.7.cloned.1.call-update) | async-done | bytes 5242896 | tf_op jit(solution)/shard_map/all_gather | solution.py:25
  199.6 1.1 slice_convert_fusion
  200.7 0.6 fusion.49
  201.5 0.6 gather_fusion
  202.1 0.6 select_reduce_fusion
  202.9 5.6 %fusion.2 = f32[8,80,128,2]{2,3,1,0:T(2,128)S(1)} fusion(bf16[32,8,80,128]{3,2,1,0:T(8,128)(2,1)} %all-gather.7.cloned.1.call-done, bf16[2,32,8,1]{1,2,0,3:T(8,128)(2,1)S(1)} %get-tuple-element.70), kind=kOutput, calls=%fused_computation.3 | convolution fusion | flops 10485760 | bytes 5899264 | tf_op jit(solution)/shard_map/rjh,jhpn->rhpn/dot_general | solution.py:327
  208.5 3.1 %fusion.25 = f32[2,8,80,128]{3,0,2,1:T(2,128)S(1)} fusion(f32[8,80,128,2]{2,3,1,0:T(2,128)S(1)} %fusion.2, bf16[32,8,80,128]{3,2,1,0:T(8,128)(2,1)S(1)} %copy-done.11, bf16[2,32,8,1]{1,2,0,3:T(8,128)(2,1)S(1)} %get-tuple-element.69), kind=kOutput, calls=%fused_computation.32 | convolution fusion | flops 10649600 | bytes 6554624 | tf_op jit(solution)/shard_map/rjh,jhpn->rhpn/dot_general | solution.py:325
  211.6 0.9 copy.140
  (106 shorter events, 3.1 us)
Async XLA Ops:
  7.2 69.8 %copy-start = (bf16[512,2048]{1,0:T(8,128)(2,1)S(1)}, bf16[512,2048]{1,0:T(8,128)(2,1)}, u32[]{:S(2)}) copy-start(bf16[512,2048]{1,0:T(8,128)(2,1)} %param.21) | copy-start | bytes 6291460
  7.2 1.8 copy-start.7
  7.2 1.8 copy-start.8
  7.2 11.1 %copy-start.6 = (f32[512,128]{1,0:T(8,128)S(1)}, f32[512,128]{1,0:T(8,128)}, u32[]{:S(2)}) copy-start(f32[512,128]{1,0:T(8,128)} %param.33) | copy-start | bytes 786436
  8.7 20.1 %copy-start.18 = (s32[8]{0:T(128)S(1)}, s32[8]{0:T(128)}, u32[]{:S(2)}) copy-start(s32[8]{0:T(128)} %param.34) | copy-start | bytes 100
  8.7 20.9 %copy-start.9 = (f32[4,512]{1,0:T(4,128)S(1)}, f32[4,512]{1,0:T(4,128)}, u32[]{:S(2)}) copy-start(f32[4,512]{1,0:T(4,128)} %param.25) | copy-start | bytes 24580
  8.8 20.9 %copy-start.10 = (f32[4,256]{1,0:T(4,128)S(1)}, f32[4,256]{1,0:T(4,128)}, u32[]{:S(2)}) copy-start(f32[4,256]{1,0:T(4,128)} %param.27) | copy-start | bytes 12292
  8.8 21.0 %copy-start.12 = (f32[512]{0:T(512)S(1)}, f32[512]{0:T(512)}, u32[]{:S(2)}) copy-start(f32[512]{0:T(512)} %param.26) | copy-start | bytes 6148
  8.8 21.0 %copy-start.13 = (f32[256]{0:T(256)S(1)}, f32[256]{0:T(256)}, u32[]{:S(2)}) copy-start(f32[256]{0:T(256)} %param.28) | copy-start | bytes 3076
  8.8 21.2 %copy-start.19 = (f32[8]{0:T(128)S(1)}, f32[8]{0:T(128)}, u32[]{:S(2)}) copy-start(f32[8]{0:T(128)} %param.30) | copy-start | bytes 100
  10.1 17.9 %all-to-all-start = ((bf16[16,8,1408]{2,0,1:T(8,128)(2,1)}), bf16[16,8,1408]{2,0,1:T(8,128)(2,1)S(1)}, u32[]{:S(2)}, u32[]{:S(2)}) async-start(bf16[16,8,1408]{2,0,1:T(8,128)(2,1)} %concatenate.41), calls=%async_computation | async-start | bytes 720896 | tf_op jit(solution)/shard_map/all_to_all | solution.py:198
  18.2 58.7 %all-gather.5.cloned.1.call-start = ((), (), s32[]{:S(2)}) async-start(), calls=%async_computation.1 | async-start | bytes 8355840 | tf_op jit(solution)/shard_map/all_gather | solution.py:25
  28.8 170.8 %all-gather.7.cloned.1.call-start = ((), (), s32[]{:S(2)}) async-start(), calls=%async_computation.2 | async-start | bytes 5570560 | tf_op jit(solution)/shard_map/all_gather | solution.py:25
  30.2 57.2 %copy-start.14 = (f32[8]{0:T(128)S(1)}, f32[8]{0:T(128)}, u32[]{:S(2)}) copy-start(f32[8]{0:T(128)} %param.29) | copy-start | bytes 100
  82.9 1.1 copy-start.2
  84.1 6.7 %collective-permute-start = (bf16[3,768]{0,1:T(8,128)(2,1)S(1)}, bf16[3,768]{0,1:T(8,128)(2,1)S(1)}, u32[]{:S(2)}, u32[]{:S(2)}) collective-permute-start(bf16[3,768]{0,1:T(8,128)(2,1)S(1)} %slice.223), channel_id=1, source_target_pairs={{0,8},{8,16},{16,24},{24,32},{32,40},{40,48},{48,56},{56,64},{64,7... | collective-permute-start | bytes 13832 | tf_op jit(solution)/shard_map/ppermute | solution.py:21
  93.3 36.6 %copy-start.16 = (s32[32]{0:T(128)S(1)}, s32[32]{0:T(128)}, u32[]{:S(2)}) copy-start(s32[32]{0:T(128)} %param.35) | copy-start | bytes 388
  95.1 34.7 %copy-start.1 = (bf16[2,8,80,128]{3,2,1,0:T(8,128)(2,1)}, bf16[2,8,80,128]{3,2,1,0:T(8,128)(2,1)S(1)}, u32[]{:S(2)}) copy-start(bf16[2,8,80,128]{3,2,1,0:T(8,128)(2,1)S(1)} %pad_maximum_fusion.2) | copy-start | bytes 983044
  131.7 1.9 copy-start.4
  131.7 1.9 copy-start.5
  131.7 1.9 copy-start.15
  134.0 1.4 copy-start.3
  134.8 1.7 copy-start.17
  202.9 5.6 %copy-start.11 = (bf16[32,8,80,128]{3,2,1,0:T(8,128)(2,1)S(1)}, bf16[32,8,80,128]{3,2,1,0:T(8,128)(2,1)}, u32[]{:S(2)}) copy-start(bf16[32,8,80,128]{3,2,1,0:T(8,128)(2,1)} %all-gather.7.cloned.1.call-done) | copy-start | bytes 15728644
Sparse Core Ops, SparseCore 0:
  28.9 47.9 all-gather.4
  130.0 69.5 all-gather.6

commit v8 on v7

--- a/solution.py
+++ b/solution.py
@@ -147,6 +147,61 @@
         ],
         compiler_params=pltpu.CompilerParams(collective_id=1, has_side_effects=True),
     )(mine)
+
+
+def exchange_kernel(count, rows, width, x_ref, o_ref, recv, send_sem, recv_sem):
+    me = lax.axis_index("tp")
+    barrier = pltpu.get_barrier_semaphore()
+    for d in range(1, count):
+        peer = lax.rem(me + d, count)
+        pl.semaphore_signal(barrier, inc=1, device_id={"tp": peer}, device_id_type=pl.DeviceIdType.MESH)
+    pl.semaphore_wait(barrier, count - 1)
+    copies = []
+    for d in range(1, count):
+        peer = lax.rem(me + d, count)
+        copy = pltpu.make_async_remote_copy(
+            src_ref=x_ref.at[:, pl.ds(pl.multiple_of(peer * width, 128), width)],
+            dst_ref=recv.at[me],
+            send_sem=send_sem.at[d],
+            recv_sem=recv_sem.at[me],
+            device_id={"tp": peer},
+            device_id_type=pl.DeviceIdType.MESH,
+        )
+        copy.start()
+        copies.append(copy)
+    o_ref[pl.ds(pl.multiple_of(me * rows, rows), rows), :] = x_ref[
+        :, pl.ds(pl.multiple_of(me * width, 128), width)
+    ]
+    for d in range(1, count):
+        sender = lax.rem(me + count - d, count)
+        pltpu.make_async_remote_copy(
+            src_ref=x_ref.at[:, pl.ds(0, width)],
+            dst_ref=recv.at[sender],
+            send_sem=send_sem.at[0],
+            recv_sem=recv_sem.at[sender],
+            device_id={"tp": sender},
+            device_id_type=pl.DeviceIdType.MESH,
+        ).wait_recv()
+        o_ref[pl.ds(pl.multiple_of(sender * rows, rows), rows), :] = recv[sender]
+    for copy in copies:
+        copy.wait_send()
+
+
+def exchange(x, count):
+    rows = x.shape[0]
+    width = x.shape[1] // count
+    return pl.pallas_call(
+        functools.partial(exchange_kernel, count, rows, width),
+        out_shape=jax.ShapeDtypeStruct((count * rows, width), x.dtype),
+        in_specs=[pl.BlockSpec(memory_space=pltpu.VMEM)],
+        out_specs=pl.BlockSpec(memory_space=pltpu.VMEM),
+        scratch_shapes=[
+            pltpu.VMEM((count, rows, width), x.dtype),
+            pltpu.SemaphoreType.DMA((count,)),
+            pltpu.SemaphoreType.DMA((count,)),
+        ],
+        compiler_params=pltpu.CompilerParams(collective_id=2, has_side_effects=True),
+    )(x)
 
 
 def round_up(n, m):
@@ -195,7 +250,7 @@
     pad_part = jnp.zeros((local_rows, tp_count, width - used), jnp.bfloat16)
     packed = jnp.concatenate([zx_part, bc_part, dt_part, pad_part], axis=2)
     packed = packed.reshape(local_rows, tp_count * width)
-    block = lax.all_to_all(packed, "tp", split_axis=1, concat_axis=0, tiled=True)
+    block = exchange(packed, tp_count)
     block_rows = block.shape[0]
     out_rows, out_cols = w_out.shape
     out_piece = w_out.astype(jnp.bfloat16).T

time: 220 us -> 223 us (1.014)
  Pallas kernels: 73.9 us -> 87.7 us
  starting transfers between devices: 11.5 us -> 3.34 us
  waiting for transfers between devices: 72.1 us -> 66.2 us
    pallas_call x0 -> x1, Pallas kernels: none -> 13.6 us  [exchange(): pl.pallas_call(functools.partial(exchange_kernel, count, rows, width), ou...]
    all_to_all x1 -> x0, waiting for transfers between devices: 9.56 us -> none  [on_device(): lax.all_to_all(packed, 'tp', split_axis=1, concat_axis=0, tiled=True)]
    all_to_all x1 -> x0, starting transfers between devices: 8.16 us -> none  [on_device(): lax.all_to_all(packed, 'tp', split_axis=1, concat_axis=0, tiled=True)]
    all_gather x2, waiting for transfers between devices: 62.5 us -> 66.2 us  [gather_seq(): return lax.all_gather(x, SEQ, axis=0, tiled=False)]
    unnamed x46 -> x41, local copies, waits for them, and re-layouts: 2.86 us -> 5.41 us
  transfers between devices with their start and end apart: 4 -> 3, of which waited for: 3 -> 2; matrix products, arithmetic and copies ran while one was open for 8% -> 8% of each run, Pallas kernels for 18% -> 18%
where the time goes in v8:
time: 223 us; the launch traced here: 222 us
  Pallas kernels  87.7 us (39%)
  waiting for transfers between devices  66.2 us (30%)
  matrix products  21.3 us (10%)
  other arithmetic  17.8 us (8%)
  between operations  14.7 us (7%)
  local copies, waits for them, and re-layouts  10.9 us (5%)
  starting transfers between devices  3.34 us (1%)
    all_gather x2, waiting for transfers between devices, gather_seq(): return lax.all_gather(x, SEQ, axis=0, tiled=False)  66.2 us
    pallas_call x1, Pallas kernels, scatter_sum(): pl.pallas_call(functools.partial(scatter_sum_kernel, count, rows), out_sh...  40.1 us
    pallas_call x1, Pallas kernels, carry_in(): pl.pallas_call(functools.partial(carry_kernel, count, width), out_shape=j...  34 us
    pallas_call x1, Pallas kernels, exchange(): pl.pallas_call(functools.partial(exchange_kernel, count, rows, width), ou...  13.6 us
    dot_general x1, matrix products, on_device(): jnp.dot(tokens, gathered[:, :width], preferred_element_type=jnp.float32)  5.9 us
    dot_general x1, matrix products, on_device(): jnp.einsum('rjh,jhpn->rhpn', coef_lo, every, preferred_element_type=jnp.f...  5.63 us
    unnamed x41, local copies, waits for them, and re-layouts  5.41 us
  transfers between devices with their start and end apart: 3, of which 2 were waited for; matrix products, arithmetic and copies ran while one was open for 8% of the time, Pallas kernels for 18%

profile of v8, /device:TPU:1, one launch (start us, length us, event | category | flops | bytes accessed | tf_op | source)
XLA Modules:
  0.0 222.0 jit_solution(12650707199217345143)
XLA Ops:
  7.2 1.2 copy.117
  8.4 1.1 convert_element_type.120
  9.7 0.7 convert_element_type.121
  10.4 0.8 copy.115
  11.4 0.8 copy.149
  12.2 13.6 %shard_map.158 = bf16[128,1408]{1,0:T(8,128)(2,1)} custom-call(bf16[16,11264]{1,0:T(8,128)(2,1)} %bitcast.72), custom_call_target="tpu_custom_call" | custom-call | tf_op jit(solution)/shard_map/pallas_call | solution.py:193
  25.9 1.8 pad_maximum_fusion.1
  27.7 0.2 reduce-window.18
  28.1 0.2 fusion.55
  28.4 0.2 slice_reduce_fusion.6
  28.6 0.2 compare_reduce_fusion.1
  29.1 50.5 %all-gather.5.cloned.1.call-done = bf16[2048,1920]{1,0:T(8,128)(2,1)} async-done(((bf16[128,1920]{1,0:T(8,128)(2,1)}), bf16[2048,1920]{1,0:T(8,128)(2,1)}) %all-gather.5.cloned.1.call-update) | async-done | bytes 7864336 | tf_op jit(solution)/shard_map/all_gather | solution.py:25
  79.6 5.9 %fusion.65 = (bf16[512,1408]{0,1:T(8,128)(2,1)S(1)}, f32[512,1408]{0,1:T(8,128)S(1)}) fusion(bf16[512,2048]{1,0:T(8,128)(2,1)S(1)} %copy-done, bf16[2048,1920]{1,0:T(8,128)(2,1)} %all-gather.5.cloned.1.call-done), kind=kOutput, calls=%fused_computation.138 | convolution fusion | flops 2953510912 | bytes 12189696 | tf_op jit(solution)/shard_map/dot_general | solution.py:259
  85.5 1.1 copy-done.2
  86.7 3.3 %collective-permute-start = (bf16[3,768]{0,1:T(8,128)(2,1)S(1)}, bf16[3,768]{0,1:T(8,128)(2,1)S(1)}, u32[]{:S(2)}, u32[]{:S(2)}) collective-permute-start(bf16[3,768]{0,1:T(8,128)(2,1)S(1)} %slice.223), channel_id=1, source_target_pairs={{0,8},{8,16},{16,24},{24,32},{32,40},{40,48},{48,56},{56,64},{64,7... | collective-permute-start | bytes 13832 | tf_op jit(solution)/shard_map/ppermute | solution.py:21
  90.2 1.1 reduce-window.19
  91.3 0.2 slice_reduce_fusion
  91.6 0.2 slice_reduce_fusion.1
  92.0 1.2 slice.224
  93.4 2.1 multiply_convert_fusion.3
  95.7 0.1 reshape.416
  96.0 1.0 fusion.32
  97.0 0.7 fusion.40
  97.8 0.7 slice_bitcast_fusion.mine_ref
  98.5 34.0 %shard_map.159 = f32[8,64,128]{2,1,0:T(8,128)} custom-call(bf16[8,80,128]{2,1,0:T(8,128)(2,1)} %slice_bitcast_fusion.mine_ref), custom_call_target="tpu_custom_call" | custom-call | tf_op jit(solution)/shard_map/pallas_call | solution.py:137
  133.1 0.7 compare_reduce_fusion
  133.8 0.2 compare_and_fusion
  134.0 0.3 fusion.43
  134.3 1.8 fusion.19
  136.2 0.4 fusion.21
  136.6 0.8 copy.127
  137.6 0.4 copy-done.3
  138.0 0.4 multiply_reduce_fusion
  138.4 0.6 select_convert_fusion
  139.0 0.1 reshape.451
  139.1 3.2 %convolution_convert_fusion = bf16[512,2048]{1,0:T(8,128)(2,1)S(1)} fusion(bf16[2048,1920]{1,0:T(8,128)(2,1)} %all-gather.5.cloned.1.call-done, f32[512]{0:T(512)S(1)} %copy-done.14, f32[512,512]{0,1:T(8,128)S(1)} %bitcast.69, bf16[512,1408]{0,1:T(8,128)(2,1)S(1)} %copy-done.3), kind=kOutput, calls=%fused_computation.11 | convolution fusion | flops 1076887552 | bytes 5769216 | tf_op jit(solution)/shard_map/dot_general | solution.py:397
  142.3 1.6 fusion.10.x_ref
  143.9 40.1 %shard_map.160 = f32[64,2176]{1,0:T(8,128)} custom-call(bf16[512,2176]{1,0:T(8,128)(2,1)} %fusion.10.x_ref), custom_call_target="tpu_custom_call" | custom-call | tf_op jit(solution)/shard_map/pallas_call | solution.py:74
  183.9 0.9 rsqrt_reduce_fusion
  184.8 1.8 multiply_convert_fusion.9
  186.7 15.6 %all-gather.7.cloned.1.call-done = bf16[32,8,80,128]{3,2,1,0:T(8,128)(2,1)} async-done(((bf16[2,8,80,128]{3,2,1,0:T(8,128)(2,1)}), bf16[32,8,80,128]{3,2,1,0:T(8,128)(2,1)}) %all-gather.7.cloned.1.call-update) | async-done | bytes 5242896 | tf_op jit(solution)/shard_map/all_gather | solution.py:25
  202.3 1.1 slice_convert_fusion
  203.4 0.6 fusion.49
  204.1 0.6 gather_fusion
  204.7 0.6 select_reduce_fusion
  205.5 5.6 %fusion.2 = f32[8,80,128,2]{2,3,1,0:T(2,128)S(1)} fusion(bf16[32,8,80,128]{3,2,1,0:T(8,128)(2,1)} %all-gather.7.cloned.1.call-done, bf16[2,32,8,1]{1,2,0,3:T(8,128)(2,1)S(1)} %get-tuple-element.70), kind=kOutput, calls=%fused_computation.3 | convolution fusion | flops 10485760 | bytes 5899264 | tf_op jit(solution)/shard_map/rjh,jhpn->rhpn/dot_general | solution.py:382
  211.1 3.1 %fusion.25 = f32[2,8,80,128]{3,0,2,1:T(2,128)S(1)} fusion(f32[8,80,128,2]{2,3,1,0:T(2,128)S(1)} %fusion.2, bf16[32,8,80,128]{3,2,1,0:T(8,128)(2,1)S(1)} %copy-done.8, bf16[2,32,8,1]{1,2,0,3:T(8,128)(2,1)S(1)} %get-tuple-element.69), kind=kOutput, calls=%fused_computation.32 | convolution fusion | flops 10649600 | bytes 6554624 | tf_op jit(solution)/shard_map/rjh,jhpn->rhpn/dot_general | solution.py:380
  214.3 0.9 copy.135
  (98 shorter events, 3.0 us)
Async XLA Ops:
  7.2 72.4 %copy-start = (bf16[512,2048]{1,0:T(8,128)(2,1)S(1)}, bf16[512,2048]{1,0:T(8,128)(2,1)}, u32[]{:S(2)}) copy-start(bf16[512,2048]{1,0:T(8,128)(2,1)} %param.21) | copy-start | bytes 6291460
  7.2 72.4 %all-gather.5.cloned.1.call-start = ((), (), s32[]{:S(2)}) async-start(), calls=%async_computation | async-start | bytes 8355840 | tf_op jit(solution)/shard_map/all_gather | solution.py:25
  9.5 18.2 %copy-start.15 = (s32[8]{0:T(128)S(1)}, s32[8]{0:T(128)}, u32[]{:S(2)}) copy-start(s32[8]{0:T(128)} %param.34) | copy-start | bytes 100
  9.6 19.0 %copy-start.6 = (f32[4,512]{1,0:T(4,128)S(1)}, f32[4,512]{1,0:T(4,128)}, u32[]{:S(2)}) copy-start(f32[4,512]{1,0:T(4,128)} %param.25) | copy-start | bytes 24580
  9.6 19.0 %copy-start.7 = (f32[4,256]{1,0:T(4,128)S(1)}, f32[4,256]{1,0:T(4,128)}, u32[]{:S(2)}) copy-start(f32[4,256]{1,0:T(4,128)} %param.27) | copy-start | bytes 12292
  9.6 19.0 %copy-start.9 = (f32[512]{0:T(512)S(1)}, f32[512]{0:T(512)}, u32[]{:S(2)}) copy-start(f32[512]{0:T(512)} %param.26) | copy-start | bytes 6148
  9.6 19.0 %copy-start.10 = (f32[256]{0:T(256)S(1)}, f32[256]{0:T(256)}, u32[]{:S(2)}) copy-start(f32[256]{0:T(256)} %param.28) | copy-start | bytes 3076
  9.6 19.2 %copy-start.16 = (f32[8]{0:T(128)S(1)}, f32[8]{0:T(128)}, u32[]{:S(2)}) copy-start(f32[8]{0:T(128)} %param.30) | copy-start | bytes 100
  27.7 174.6 %all-gather.7.cloned.1.call-start = ((), (), s32[]{:S(2)}) async-start(), calls=%async_computation.1 | async-start | bytes 5570560 | tf_op jit(solution)/shard_map/all_gather | solution.py:25
  29.1 61.0 %copy-start.11 = (f32[8]{0:T(128)S(1)}, f32[8]{0:T(128)}, u32[]{:S(2)}) copy-start(f32[8]{0:T(128)} %param.29) | copy-start | bytes 100
  85.5 1.1 copy-start.2
  86.7 6.7 %collective-permute-start = (bf16[3,768]{0,1:T(8,128)(2,1)S(1)}, bf16[3,768]{0,1:T(8,128)(2,1)S(1)}, u32[]{:S(2)}, u32[]{:S(2)}) collective-permute-start(bf16[3,768]{0,1:T(8,128)(2,1)S(1)} %slice.223), channel_id=1, source_target_pairs={{0,8},{8,16},{16,24},{24,32},{32,40},{40,48},{48,56},{56,64},{64,7... | collective-permute-start | bytes 13832 | tf_op jit(solution)/shard_map/ppermute | solution.py:21
  95.9 36.6 %copy-start.13 = (s32[32]{0:T(128)S(1)}, s32[32]{0:T(128)}, u32[]{:S(2)}) copy-start(s32[32]{0:T(128)} %param.35) | copy-start | bytes 388
  97.8 34.7 %copy-start.1 = (bf16[2,8,80,128]{3,2,1,0:T(8,128)(2,1)}, bf16[2,8,80,128]{3,2,1,0:T(8,128)(2,1)S(1)}, u32[]{:S(2)}) copy-start(bf16[2,8,80,128]{3,2,1,0:T(8,128)(2,1)S(1)} %pad_maximum_fusion.2) | copy-start | bytes 983044
  134.3 1.9 copy-start.4
  134.3 1.9 copy-start.5
  134.3 1.9 copy-start.12
  136.6 1.4 copy-start.3
  137.5 1.7 copy-start.14
  205.5 5.6 %copy-start.8 = (bf16[32,8,80,128]{3,2,1,0:T(8,128)(2,1)S(1)}, bf16[32,8,80,128]{3,2,1,0:T(8,128)(2,1)}, u32[]{:S(2)}) copy-start(bf16[32,8,80,128]{3,2,1,0:T(8,128)(2,1)} %all-gather.7.cloned.1.call-done) | copy-start | bytes 15728644
Sparse Core Ops, SparseCore 0:
  27.8 51.7 all-gather.4
  132.7 69.5 all-gather.6

commit v9 on v7

--- a/solution.py
+++ b/solution.py
@@ -85,65 +85,75 @@
     )(x)
 
 
-def carry_kernel(count, width, mine_ref, out_ref, recv, acc, send_sem, recv_sem):
+def scan_kernel(count, width, mine_ref, out_ref, acc, send_buf, recv, send_sem, recv_sem):
     me = lax.axis_index(SEQ)
     barrier = pltpu.get_barrier_semaphore()
     for d in range(1, count):
         peer = lax.rem(me + d, count)
         pl.semaphore_signal(barrier, inc=1, device_id={SEQ: peer}, device_id_type=pl.DeviceIdType.MESH)
     pl.semaphore_wait(barrier, count - 1)
-
-    def send_to(d):
+    distances = [1]
+    while distances[-1] * 2 < count:
+        distances.append(distances[-1] * 2)
+    rounds = [1] + distances
+
+    def link(r, dist, target):
         return pltpu.make_async_remote_copy(
-            src_ref=mine_ref,
-            dst_ref=recv.at[me],
-            send_sem=send_sem.at[d],
-            recv_sem=recv_sem.at[me],
-            device_id={SEQ: me + d},
+            src_ref=mine_ref if r == 0 else send_buf.at[r],
+            dst_ref=recv.at[r],
+            send_sem=send_sem.at[r],
+            recv_sem=recv_sem.at[r],
+            device_id={SEQ: target},
             device_id_type=pl.DeviceIdType.MESH,
         )
 
-    for d in range(1, count):
-        @pl.when(me + d < count)
+    rows = acc.shape[1]
+    is_gate_row = lax.broadcasted_iota(jnp.int32, acc.shape, 1) == width
+    acc[...] = jnp.where(is_gate_row, 1.0, 0.0).astype(acc.dtype)
+    for r, dist in enumerate(rounds):
+        if r > 0:
+            send_buf[r] = acc[...]
+
+        @pl.when(me + dist < count)
         def _():
-            send_to(d).start()
-
-    acc[...] = jnp.zeros_like(acc)
-    for j in range(count - 1):
-        @pl.when(j < me)
+            link(r, dist, me + dist).start()
+
+        @pl.when(me >= dist)
         def _():
-            pltpu.make_async_remote_copy(
-                src_ref=mine_ref,
-                dst_ref=recv.at[j],
-                send_sem=send_sem.at[0],
-                recv_sem=recv_sem.at[j],
-                device_id={SEQ: j},
-                device_id_type=pl.DeviceIdType.MESH,
-            ).wait_recv()
-            tail = recv[j, :, width : width + 16, :].astype(jnp.float32)
-            gate = tail[:, 0:1, :] + tail[:, 1:2, :]
-            acc[...] = gate * acc[...] + recv[j, :, :width, :].astype(jnp.float32)
-
-    for d in range(1, count):
-        @pl.when(me + d < count)
+            link(r, dist, me - dist).wait_recv()
+            if r == 0:
+                acc[...] = recv[0]
+            else:
+                came = recv[r]
+                mine_gate = acc[:, width : width + 8, :][:, 0:1, :]
+                came_gate = came[:, width : width + 8, :][:, 0:1, :]
+                state = mine_gate * came + acc[...]
+                acc[...] = jnp.where(is_gate_row, mine_gate * came_gate, state)
+
+    for r, dist in enumerate(rounds):
+        @pl.when(me + dist < count)
         def _():
-            send_to(d).wait_send()
-    out_ref[...] = acc[...]
+            link(r, dist, me + dist).wait_send()
+    out_ref[...] = acc[:, :width, :]
 
 
 def carry_in(mine, width):
     count = lax.axis_size(SEQ)
-    heads, _, lanes = mine.shape
+    heads, rows, lanes = mine.shape
+    steps = 1
+    while (1 << (steps - 1)) < count:
+        steps += 1
     return pl.pallas_call(
-        functools.partial(carry_kernel, count, width),
+        functools.partial(scan_kernel, count, width),
         out_shape=jax.ShapeDtypeStruct((heads, width, lanes), jnp.float32),
         in_specs=[pl.BlockSpec(memory_space=pltpu.VMEM)],
         out_specs=pl.BlockSpec(memory_space=pltpu.VMEM),
         scratch_shapes=[
-            pltpu.VMEM((count,) + mine.shape, mine.dtype),
-            pltpu.VMEM((heads, width, lanes), jnp.float32),
-            pltpu.SemaphoreType.DMA((count,)),
-            pltpu.SemaphoreType.DMA((count,)),
+            pltpu.VMEM(mine.shape, jnp.float32),
+            pltpu.VMEM((steps,) + mine.shape, jnp.float32),
+            pltpu.VMEM((steps,) + mine.shape, jnp.float32),
+            pltpu.SemaphoreType.DMA((steps,)),
+            pltpu.SemaphoreType.DMA((steps,)),
         ],
         compiler_params=pltpu.CompilerParams(collective_id=1, has_side_effects=True),
     )(mine)
@@ -283,7 +293,11 @@
     extra = extra.at[:, :, 0, :].set(jnp.broadcast_to(gate_hi[:, :, None], gate_hi.shape + (state_width,)))
     extra = extra.at[:, :, 1, :].set(jnp.broadcast_to(gate_lo[:, :, None], gate_lo.shape + (state_width,)))
     sendable = jnp.concatenate([local_end.astype(jnp.bfloat16), extra], axis=2)
-    carried = carry_in(sendable[-1], head_width)
+    dev_row = jnp.zeros((heads_local, 8, state_width), jnp.float32)
+    dev_row = dev_row.at[:, 0, :].set(
+        jnp.broadcast_to(through_group[-1][:, None], (heads_local, state_width))
+    )
+    carried = carry_in(jnp.concatenate([local_end[-1], dev_row], axis=1), head_width)
     carried, later = lax.optimization_barrier((carried, sendable))
     every = gather_seq(later).reshape(
         (seq_count * groups_dev, heads_local, head_width + 16, state_width)

time: 220 us -> 217 us (0.986)
  Pallas kernels: 73.9 us -> 61.5 us
  waiting for transfers between devices: 72.1 us -> 81.4 us
    pallas_call x1, Pallas kernels: 34 us -> 19.3 us  [carry_in(): pl.pallas_call(functools.partial(scan_kernel, count, width), out_shape=ja...]
    all_gather x2, waiting for transfers between devices: 62.5 us -> 71.8 us  [gather_seq(): return lax.all_gather(x, SEQ, axis=0, tiled=False)]
    pallas_call x1, Pallas kernels: 39.9 us -> 42.2 us  [scatter_sum(): pl.pallas_call(functools.partial(scatter_sum_kernel, count, rows), out_sh...]
  transfers between devices with their start and end apart: 4 -> 4, of which waited for: 3 -> 3; matrix products, arithmetic and copies ran while one was open for 8% -> 8% of each run, Pallas kernels for 18% -> 19%
where the time goes in v9:
time: 217 us; the launch traced here: 216 us
  waiting for transfers between devices  81.4 us (38%)
  Pallas kernels  61.5 us (28%)
  matrix products  21.3 us (10%)
  other arithmetic  17.2 us (8%)
  between operations  14.7 us (7%)
  starting transfers between devices  11.5 us (5%)
  local copies, waits for them, and re-layouts  8.81 us (4%)
    all_gather x2, waiting for transfers between devices, gather_seq(): return lax.all_gather(x, SEQ, axis=0, tiled=False)  71.8 us
    pallas_call x1, Pallas kernels, scatter_sum(): pl.pallas_call(functools.partial(scatter_sum_kernel, count, rows), out_sh...  42.2 us
    pallas_call x1, Pallas kernels, carry_in(): pl.pallas_call(functools.partial(scan_kernel, count, width), out_shape=ja...  19.3 us
    all_to_all x1, waiting for transfers between devices, on_device(): lax.all_to_all(packed, 'tp', split_axis=1, concat_axis=0, tiled=True)  9.56 us
    all_to_all x1, starting transfers between devices, on_device(): lax.all_to_all(packed, 'tp', split_axis=1, concat_axis=0, tiled=True)  8.16 us
    dot_general x1, matrix products, on_device(): jnp.dot(tokens, gathered[:, :width], preferred_element_type=jnp.float32)  5.9 us
    dot_general x1, matrix products, on_device(): jnp.einsum('rjh,jhpn->rhpn', coef_lo, every, preferred_element_type=jnp.f...  5.63 us
  transfers between devices with their start and end apart: 4, of which 3 were waited for; matrix products, arithmetic and copies ran while one was open for 8% of the time, Pallas kernels for 19%

profile of v9, /device:TPU:1, one launch (start us, length us, event | category | flops | bytes accessed | tf_op | source)
XLA Modules:
  0.0 216.5 jit_solution(1120055233586767394)
XLA Ops:
  7.2 1.2 convert_element_type.120
  8.5 0.2 copy.183
  8.8 0.2 reshape.453
  9.2 0.8 concatenate.46
  10.1 8.2 %all-to-all-start = ((bf16[16,8,1408]{2,0,1:T(8,128)(2,1)}), bf16[16,8,1408]{2,0,1:T(8,128)(2,1)S(1)}, u32[]{:S(2)}, u32[]{:S(2)}) async-start(bf16[16,8,1408]{2,0,1:T(8,128)(2,1)} %concatenate.46), calls=%async_computation | async-start | bytes 720896 | tf_op jit(solution)/shard_map/all_to_all | solution.py:208
  18.4 9.6 %all-to-all-done = bf16[16,8,1408]{2,0,1:T(8,128)(2,1)S(1)} async-done(((bf16[16,8,1408]{2,0,1:T(8,128)(2,1)}), bf16[16,8,1408]{2,0,1:T(8,128)(2,1)S(1)}, u32[]{:S(2)}, u32[]{:S(2)}) %all-to-all-start) | async-done | bytes 360480 | tf_op jit(solution)/shard_map/all_to_all | solution.py:208
  27.9 0.8 pad_maximum_fusion.1
  28.9 0.2 reduce-window.18
  29.2 0.2 fusion.54
  29.5 0.2 slice_reduce_fusion.6
  29.8 0.2 compare_reduce_fusion.1
  30.2 46.8 %all-gather.5.cloned.1.call-done = bf16[2048,1920]{1,0:T(8,128)(2,1)} async-done(((bf16[128,1920]{1,0:T(8,128)(2,1)}), bf16[2048,1920]{1,0:T(8,128)(2,1)}) %all-gather.5.cloned.1.call-update) | async-done | bytes 7864336 | tf_op jit(solution)/shard_map/all_gather | solution.py:25
  77.0 5.9 %fusion.65 = (bf16[512,1408]{0,1:T(8,128)(2,1)S(1)}, f32[512,1408]{0,1:T(8,128)S(1)}) fusion(bf16[512,2048]{1,0:T(8,128)(2,1)S(1)} %copy-done, bf16[2048,1920]{1,0:T(8,128)(2,1)} %all-gather.5.cloned.1.call-done), kind=kOutput, calls=%fused_computation.143 | convolution fusion | flops 2953510912 | bytes 12189696 | tf_op jit(solution)/shard_map/dot_general | solution.py:214
  82.9 1.1 copy-done.1
  84.1 3.3 %collective-permute-start = (bf16[3,768]{0,1:T(8,128)(2,1)S(1)}, bf16[3,768]{0,1:T(8,128)(2,1)S(1)}, u32[]{:S(2)}, u32[]{:S(2)}) collective-permute-start(bf16[3,768]{0,1:T(8,128)(2,1)S(1)} %slice.242), channel_id=1, source_target_pairs={{0,8},{8,16},{16,24},{24,32},{32,40},{40,48},{48,56},{56,64},{64,7... | collective-permute-start | bytes 13832 | tf_op jit(solution)/shard_map/ppermute | solution.py:21
  87.5 1.1 reduce-window.19
  88.7 0.2 slice_reduce_fusion
  89.0 0.2 slice_reduce_fusion.1
  89.3 1.2 slice.243
  90.8 2.1 multiply_convert_fusion.3
  93.0 0.1 reshape.456
  93.3 1.0 fusion.32
  94.7 0.7 select_maximum_fusion.mine_ref
  95.4 19.3 %shard_map.158 = f32[8,64,128]{2,1,0:T(8,128)} custom-call(f32[8,72,128]{2,1,0:T(8,128)} %select_maximum_fusion.mine_ref), custom_call_target="tpu_custom_call" | custom-call | tf_op jit(solution)/shard_map/pallas_call | solution.py:146
  114.7 0.7 pad_maximum_fusion.2
  116.0 0.6 compare_reduce_fusion
  116.7 0.2 compare_and_fusion
  117.0 0.3 fusion.42
  117.2 1.9 fusion.19
  119.1 0.4 fusion.21
  119.5 0.8 copy.132
  120.4 0.4 copy-done.2
  120.9 0.4 multiply_reduce_fusion
  121.3 0.6 select_convert_fusion
  121.9 0.1 reshape.492
  122.1 3.2 %convolution_convert_fusion = bf16[512,2048]{1,0:T(8,128)(2,1)S(1)} fusion(bf16[2048,1920]{1,0:T(8,128)(2,1)} %all-gather.5.cloned.1.call-done, f32[512]{0:T(512)S(1)} %copy-done.15, f32[512,512]{0,1:T(8,128)S(1)} %bitcast.77, bf16[512,1408]{0,1:T(8,128)(2,1)S(1)} %copy-done.2), kind=kOutput, calls=%fused_computation.11 | convolution fusion | flops 1076887552 | bytes 5769216 | tf_op jit(solution)/shard_map/dot_general | solution.py:356
  125.2 1.6 fusion.10.x_ref
  126.8 42.2 %shard_map.159 = f32[64,2176]{1,0:T(8,128)} custom-call(bf16[512,2176]{1,0:T(8,128)(2,1)} %fusion.10.x_ref), custom_call_target="tpu_custom_call" | custom-call | tf_op jit(solution)/shard_map/pallas_call | solution.py:74
  169.0 0.9 rsqrt_reduce_fusion
  169.9 1.9 multiply_convert_fusion.9
  171.7 25.0 %all-gather.7.cloned.1.call-done = bf16[32,8,80,128]{3,2,1,0:T(8,128)(2,1)} async-done(((bf16[2,8,80,128]{3,2,1,0:T(8,128)(2,1)}), bf16[32,8,80,128]{3,2,1,0:T(8,128)(2,1)}) %all-gather.7.cloned.1.call-update) | async-done | bytes 5242896 | tf_op jit(solution)/shard_map/all_gather | solution.py:25
  196.8 1.1 slice_convert_fusion
  197.9 0.6 fusion.48
  198.6 0.6 gather_fusion
  199.2 0.6 select_reduce_fusion
  200.0 5.6 %fusion.2 = f32[8,80,128,2]{2,3,1,0:T(2,128)S(1)} fusion(bf16[32,8,80,128]{3,2,1,0:T(8,128)(2,1)} %all-gather.7.cloned.1.call-done, bf16[2,32,8,1]{1,2,0,3:T(8,128)(2,1)S(1)} %get-tuple-element.82), kind=kOutput, calls=%fused_computation.3 | convolution fusion | flops 10485760 | bytes 5899264 | tf_op jit(solution)/shard_map/rjh,jhpn->rhpn/dot_general | solution.py:341
  205.6 3.1 %fusion.25 = f32[2,8,80,128]{3,0,2,1:T(2,128)S(1)} fusion(f32[8,80,128,2]{2,3,1,0:T(2,128)S(1)} %fusion.2, bf16[32,8,80,128]{3,2,1,0:T(8,128)(2,1)S(1)} %copy-done.9, bf16[2,32,8,1]{1,2,0,3:T(8,128)(2,1)S(1)} %get-tuple-element.81), kind=kOutput, calls=%fused_computation.32 | convolution fusion | flops 10649600 | bytes 6554624 | tf_op jit(solution)/shard_map/rjh,jhpn->rhpn/dot_general | solution.py:339
  208.8 0.9 copy.140
  (104 shorter events, 3.3 us)
Async XLA Ops:
  7.2 69.8 %copy-start = (bf16[512,2048]{1,0:T(8,128)(2,1)S(1)}, bf16[512,2048]{1,0:T(8,128)(2,1)}, u32[]{:S(2)}) copy-start(bf16[512,2048]{1,0:T(8,128)(2,1)} %param.23) | copy-start | bytes 6291460
  7.2 1.8 copy-start.5
  7.2 1.8 copy-start.6
  7.2 11.1 %copy-start.4 = (f32[512,128]{1,0:T(8,128)S(1)}, f32[512,128]{1,0:T(8,128)}, u32[]{:S(2)}) copy-start(f32[512,128]{1,0:T(8,128)} %param.35) | copy-start | bytes 786436
  8.7 20.1 %copy-start.16 = (s32[8]{0:T(128)S(1)}, s32[8]{0:T(128)}, u32[]{:S(2)}) copy-start(s32[8]{0:T(128)} %param.36) | copy-start | bytes 100
  8.7 20.9 %copy-start.7 = (f32[4,512]{1,0:T(4,128)S(1)}, f32[4,512]{1,0:T(4,128)}, u32[]{:S(2)}) copy-start(f32[4,512]{1,0:T(4,128)} %param.27) | copy-start | bytes 24580
  8.8 20.9 %copy-start.8 = (f32[4,256]{1,0:T(4,128)S(1)}, f32[4,256]{1,0:T(4,128)}, u32[]{:S(2)}) copy-start(f32[4,256]{1,0:T(4,128)} %param.29) | copy-start | bytes 12292
  8.8 21.0 %copy-start.10 = (f32[512]{0:T(512)S(1)}, f32[512]{0:T(512)}, u32[]{:S(2)}) copy-start(f32[512]{0:T(512)} %param.28) | copy-start | bytes 6148
  8.8 21.0 %copy-start.11 = (f32[256]{0:T(256)S(1)}, f32[256]{0:T(256)}, u32[]{:S(2)}) copy-start(f32[256]{0:T(256)} %param.30) | copy-start | bytes 3076
  8.8 21.2 %copy-start.17 = (f32[8]{0:T(128)S(1)}, f32[8]{0:T(128)}, u32[]{:S(2)}) copy-start(f32[8]{0:T(128)} %param.32) | copy-start | bytes 100
  10.1 17.9 %all-to-all-start = ((bf16[16,8,1408]{2,0,1:T(8,128)(2,1)}), bf16[16,8,1408]{2,0,1:T(8,128)(2,1)S(1)}, u32[]{:S(2)}, u32[]{:S(2)}) async-start(bf16[16,8,1408]{2,0,1:T(8,128)(2,1)} %concatenate.46), calls=%async_computation | async-start | bytes 720896 | tf_op jit(solution)/shard_map/all_to_all | solution.py:208
  18.2 58.7 %all-gather.5.cloned.1.call-start = ((), (), s32[]{:S(2)}) async-start(), calls=%async_computation.1 | async-start | bytes 8355840 | tf_op jit(solution)/shard_map/all_gather | solution.py:25
  28.8 168.0 %all-gather.7.cloned.1.call-start = ((), (), s32[]{:S(2)}) async-start(), calls=%async_computation.2 | async-start | bytes 5570560 | tf_op jit(solution)/shard_map/all_gather | solution.py:25
  30.2 57.2 %copy-start.12 = (f32[8]{0:T(128)S(1)}, f32[8]{0:T(128)}, u32[]{:S(2)}) copy-start(f32[8]{0:T(128)} %param.31) | copy-start | bytes 100
  82.9 1.1 copy-start.1
  84.1 6.7 %collective-permute-start = (bf16[3,768]{0,1:T(8,128)(2,1)S(1)}, bf16[3,768]{0,1:T(8,128)(2,1)S(1)}, u32[]{:S(2)}, u32[]{:S(2)}) collective-permute-start(bf16[3,768]{0,1:T(8,128)(2,1)S(1)} %slice.242), channel_id=1, source_target_pairs={{0,8},{8,16},{16,24},{24,32},{32,40},{40,48},{48,56},{56,64},{64,7... | collective-permute-start | bytes 13832 | tf_op jit(solution)/shard_map/ppermute | solution.py:21
  94.3 21.2 %copy-start.14 = (s32[32]{0:T(128)S(1)}, s32[32]{0:T(128)}, u32[]{:S(2)}) copy-start(s32[32]{0:T(128)} %param.37) | copy-start | bytes 388
  117.2 1.9 copy-start.3
  117.2 1.9 copy-start.13
  119.5 1.4 copy-start.2
  120.3 1.7 copy-start.15
  200.0 5.6 %copy-start.9 = (bf16[32,8,80,128]{3,2,1,0:T(8,128)(2,1)S(1)}, bf16[32,8,80,128]{3,2,1,0:T(8,128)(2,1)}, u32[]{:S(2)}) copy-start(bf16[32,8,80,128]{3,2,1,0:T(8,128)(2,1)} %all-gather.7.cloned.1.call-done) | copy-start | bytes 15728644
Sparse Core Ops, SparseCore 0:
  28.9 47.9 all-gather.4
  115.6 81.0 all-gather.6

commit v10 on v9

--- a/solution.py
+++ b/solution.py
@@ -298,8 +298,7 @@
         jnp.broadcast_to(through_group[-1][:, None], (heads_local, state_width))
     )
     carried = carry_in(jnp.concatenate([local_end[-1], dev_row], axis=1), head_width)
-    carried, later = lax.optimization_barrier((carried, sendable))
-    every = gather_seq(later).reshape(
+    every = gather_seq(sendable).reshape(
         (seq_count * groups_dev, heads_local, head_width + 16, state_width)
     )
     gate_rows = every[:, :, head_width : head_width + 2, :].astype(jnp.float32)

time: 217 us -> 228 us (1.051)
  the two profiles are of different devices: /device:TPU:1 before, /device:TPU:48 now
where the time goes in v10:
time: 228 us; the launch traced here: 227 us
  Pallas kernels  96.6 us (42%)
  waiting for transfers between devices  57.1 us (25%)
  matrix products  22.2 us (10%)
  other arithmetic  18.4 us (8%)
  between operations  14.7 us (6%)
  local copies, waits for them, and re-layouts  9.52 us (4%)
  starting transfers between devices  8.95 us (4%)
    pallas_call x1, Pallas kernels, carry_in(): pl.pallas_call(functools.partial(scan_kernel, count, width), out_shape=ja...  57 us
    all_gather x2, waiting for transfers between devices, gather_seq(): return lax.all_gather(x, SEQ, axis=0, tiled=False)  46 us
    pallas_call x1, Pallas kernels, scatter_sum(): pl.pallas_call(functools.partial(scatter_sum_kernel, count, rows), out_sh...  39.5 us
    all_to_all x1, waiting for transfers between devices, on_device(): lax.all_to_all(packed, 'tp', split_axis=1, concat_axis=0, tiled=True)  9.67 us
    all_to_all x1, starting transfers between devices, on_device(): lax.all_to_all(packed, 'tp', split_axis=1, concat_axis=0, tiled=True)  6.71 us
    dot_general x1, matrix products, on_device(): jnp.dot(tokens, gathered[:, :width], preferred_element_type=jnp.float32)  5.9 us
    dot_general x1, matrix products, on_device(): jnp.einsum('rjh,jhpn->rhpn', coef_lo, every, preferred_element_type=jnp.f...  5.63 us
  transfers between devices with their start and end apart: 4, of which 3 were waited for; matrix products, arithmetic and copies ran while one was open for 9% of the time, Pallas kernels for 42%

profile of v10, /device:TPU:48, one launch (start us, length us, event | category | flops | bytes accessed | tf_op | source)
XLA Modules:
  0.0 227.5 jit_solution(11893505607745264520)
XLA Ops:
  7.2 1.2 convert_element_type.120
  8.5 0.2 copy.183
  8.8 0.2 reshape.453
  9.2 0.8 concatenate.46
  10.1 6.7 %all-to-all-start = ((bf16[16,8,1408]{2,0,1:T(8,128)(2,1)}), bf16[16,8,1408]{2,0,1:T(8,128)(2,1)S(1)}, u32[]{:S(2)}, u32[]{:S(2)}) async-start(bf16[16,8,1408]{2,0,1:T(8,128)(2,1)} %concatenate.46), calls=%async_computation | async-start | bytes 720896 | tf_op jit(solution)/shard_map/all_to_all | solution.py:208
  16.9 9.7 %all-to-all-done = bf16[16,8,1408]{2,0,1:T(8,128)(2,1)S(1)} async-done(((bf16[16,8,1408]{2,0,1:T(8,128)(2,1)}), bf16[16,8,1408]{2,0,1:T(8,128)(2,1)S(1)}, u32[]{:S(2)}, u32[]{:S(2)}) %all-to-all-start) | async-done | bytes 360480 | tf_op jit(solution)/shard_map/all_to_all | solution.py:208
  26.6 0.8 pad_maximum_fusion.1
  27.5 0.2 reduce-window.18
  27.9 0.2 fusion.54
  28.2 0.2 slice_reduce_fusion.6
  28.4 0.2 compare_reduce_fusion.1
  28.8 46.0 %all-gather.5.cloned.1.call-done = bf16[2048,1920]{1,0:T(8,128)(2,1)} async-done(((bf16[128,1920]{1,0:T(8,128)(2,1)}), bf16[2048,1920]{1,0:T(8,128)(2,1)}) %all-gather.5.cloned.1.call-update) | async-done | bytes 7864336 | tf_op jit(solution)/shard_map/all_gather | solution.py:25
  74.8 5.9 %fusion.65 = (bf16[512,1408]{0,1:T(8,128)(2,1)S(1)}, f32[512,1408]{0,1:T(8,128)S(1)}) fusion(bf16[512,2048]{1,0:T(8,128)(2,1)S(1)} %copy-done, bf16[2048,1920]{1,0:T(8,128)(2,1)} %all-gather.5.cloned.1.call-done), kind=kOutput, calls=%fused_computation.143 | convolution fusion | flops 2953510912 | bytes 12189696 | tf_op jit(solution)/shard_map/dot_general | solution.py:214
  80.7 1.1 copy-done.1
  82.0 2.2 collective-permute-start
  84.3 1.1 reduce-window.19
  85.4 0.2 slice_reduce_fusion
  85.7 0.2 slice_reduce_fusion.1
  86.1 1.2 slice.243
  87.5 1.4 collective-permute-done
  88.9 2.1 multiply_convert_fusion.3
  91.3 0.8 copy.128
  92.1 1.9 fusion.32
  94.1 0.7 add_convert_fusion.2
  94.8 0.7 pad_maximum_fusion.2
  96.1 0.7 compare_reduce_fusion
  96.9 0.8 compare_and_fusion
  97.9 0.7 select_maximum_fusion.mine_ref
  98.6 57.0 %shard_map.158 = f32[8,64,128]{2,1,0:T(8,128)} custom-call(f32[8,72,128]{2,1,0:T(8,128)} %select_maximum_fusion.mine_ref), custom_call_target="tpu_custom_call" | custom-call | tf_op jit(solution)/shard_map/pallas_call | solution.py:146
  155.7 0.3 fusion.42
  156.0 1.9 fusion.19
  157.9 0.4 fusion.21
  158.3 0.8 copy.132
  159.2 0.4 copy-done.2
  159.6 0.4 multiply_reduce_fusion
  160.0 0.6 select_convert_fusion
  160.8 3.2 %convolution_convert_fusion = bf16[512,2048]{1,0:T(8,128)(2,1)S(1)} fusion(bf16[2048,1920]{1,0:T(8,128)(2,1)} %all-gather.5.cloned.1.call-done, f32[512]{0:T(512)S(1)} %copy-done.17, f32[512,512]{0,1:T(8,128)S(1)} %bitcast.77, bf16[512,1408]{0,1:T(8,128)(2,1)S(1)} %copy-done.2), kind=kOutput, calls=%fused_computation.11 | convolution fusion | flops 1076887552 | bytes 5769216 | tf_op jit(solution)/shard_map/dot_general | solution.py:355
  164.0 1.6 fusion.10.x_ref
  165.5 39.5 %shard_map.159 = f32[64,2176]{1,0:T(8,128)} custom-call(bf16[512,2176]{1,0:T(8,128)(2,1)} %fusion.10.x_ref), custom_call_target="tpu_custom_call" | custom-call | tf_op jit(solution)/shard_map/pallas_call | solution.py:74
  205.1 0.9 rsqrt_reduce_fusion
  205.9 1.9 multiply_convert_fusion.9
  207.8 1.1 slice_convert_fusion
  208.9 0.6 fusion.48
  209.6 0.6 gather_fusion
  210.2 0.6 select_reduce_fusion
  211.0 5.6 %fusion.2 = f32[8,80,128,2]{2,3,1,0:T(2,128)S(1)} fusion(bf16[32,8,80,128]{3,2,1,0:T(8,128)(2,1)} %all-gather.7.cloned.1.call-done, bf16[2,32,8,1]{1,2,0,3:T(8,128)(2,1)S(1)} %get-tuple-element.78), kind=kOutput, calls=%fused_computation.3 | convolution fusion | flops 10485760 | bytes 5899264 | tf_op jit(solution)/shard_map/rjh,jhpn->rhpn/dot_general | solution.py:340
  216.7 3.1 %fusion.25 = f32[2,8,80,128]{3,0,2,1:T(2,128)S(1)} fusion(f32[8,80,128,2]{2,3,1,0:T(2,128)S(1)} %fusion.2, bf16[32,8,80,128]{3,2,1,0:T(8,128)(2,1)S(1)} %copy-done.11, bf16[2,32,8,1]{1,2,0,3:T(8,128)(2,1)S(1)} %get-tuple-element.77), kind=kOutput, calls=%fused_computation.32 | convolution fusion | flops 10649600 | bytes 6554624 | tf_op jit(solution)/shard_map/rjh,jhpn->rhpn/dot_general | solution.py:338
  219.8 0.9 copy.140
  (108 shorter events, 3.4 us)
Async XLA Ops:
  7.2 67.6 %copy-start = (bf16[512,2048]{1,0:T(8,128)(2,1)S(1)}, bf16[512,2048]{1,0:T(8,128)(2,1)}, u32[]{:S(2)}) copy-start(bf16[512,2048]{1,0:T(8,128)(2,1)} %param.23) | copy-start | bytes 6291460
  7.2 1.8 copy-start.7
  7.2 1.8 copy-start.8
  7.2 9.6 %copy-start.5 = (f32[512,128]{1,0:T(8,128)S(1)}, f32[512,128]{1,0:T(8,128)}, u32[]{:S(2)}) copy-start(f32[512,128]{1,0:T(8,128)} %param.35) | copy-start | bytes 786436
  8.7 18.8 %copy-start.18 = (s32[8]{0:T(128)S(1)}, s32[8]{0:T(128)}, u32[]{:S(2)}) copy-start(s32[8]{0:T(128)} %param.36) | copy-start | bytes 100
  8.7 19.6 %copy-start.9 = (f32[4,512]{1,0:T(4,128)S(1)}, f32[4,512]{1,0:T(4,128)}, u32[]{:S(2)}) copy-start(f32[4,512]{1,0:T(4,128)} %param.27) | copy-start | bytes 24580
  8.8 19.6 %copy-start.10 = (f32[4,256]{1,0:T(4,128)S(1)}, f32[4,256]{1,0:T(4,128)}, u32[]{:S(2)}) copy-start(f32[4,256]{1,0:T(4,128)} %param.29) | copy-start | bytes 12292
  8.8 19.6 %copy-start.12 = (f32[512]{0:T(512)S(1)}, f32[512]{0:T(512)}, u32[]{:S(2)}) copy-start(f32[512]{0:T(512)} %param.28) | copy-start | bytes 6148
  8.8 19.6 %copy-start.13 = (f32[256]{0:T(256)S(1)}, f32[256]{0:T(256)}, u32[]{:S(2)}) copy-start(f32[256]{0:T(256)} %param.30) | copy-start | bytes 3076
  8.8 19.9 %copy-start.19 = (f32[8]{0:T(128)S(1)}, f32[8]{0:T(128)}, u32[]{:S(2)}) copy-start(f32[8]{0:T(128)} %param.32) | copy-start | bytes 100
  10.1 16.5 %all-to-all-start = ((bf16[16,8,1408]{2,0,1:T(8,128)(2,1)}), bf16[16,8,1408]{2,0,1:T(8,128)(2,1)S(1)}, u32[]{:S(2)}, u32[]{:S(2)}) async-start(bf16[16,8,1408]{2,0,1:T(8,128)(2,1)} %concatenate.46), calls=%async_computation | async-start | bytes 720896 | tf_op jit(solution)/shard_map/all_to_all | solution.py:208
  16.8 58.0 %all-gather.5.cloned.1.call-start = ((), (), s32[]{:S(2)}) async-start(), calls=%async_computation.1 | async-start | bytes 8355840 | tf_op jit(solution)/shard_map/all_gather | solution.py:25
  27.5 180.3 %all-gather.7.cloned.1.call-start = ((), (), s32[]{:S(2)}) async-start(), calls=%async_computation.2 | async-start | bytes 5570560 | tf_op jit(solution)/shard_map/all_gather | solution.py:25
  28.8 55.3 %copy-start.14 = (f32[8]{0:T(128)S(1)}, f32[8]{0:T(128)}, u32[]{:S(2)}) copy-start(f32[8]{0:T(128)} %param.31) | copy-start | bytes 100
  80.7 1.1 copy-start.1
  82.0 7.0 %collective-permute-start = (bf16[3,768]{0,1:T(8,128)(2,1)S(1)}, bf16[3,768]{0,1:T(8,128)(2,1)S(1)}, u32[]{:S(2)}, u32[]{:S(2)}) collective-permute-start(bf16[3,768]{0,1:T(8,128)(2,1)S(1)} %slice.242), channel_id=1, source_target_pairs={{0,8},{8,16},{16,24},{24,32},{32,40},{40,48},{48,56},{56,64},{64,7... | collective-permute-start | bytes 13832 | tf_op jit(solution)/shard_map/ppermute | solution.py:21
  91.3 4.3 %copy-start.16 = (s32[32]{0:T(128)S(1)}, s32[32]{0:T(128)}, u32[]{:S(2)}) copy-start(s32[32]{0:T(128)} %param.37) | copy-start | bytes 388
  97.8 58.2 %copy-start.6 = (pred[2,256,256]{2,1,0:T(8,128)(4,1)S(1)}, pred[2,256,256]{2,1,0:T(8,128)(4,1)}, u32[]{:S(2)}) copy-start(pred[2,256,256]{2,1,0:T(8,128)(4,1)} %compare_and_fusion) | copy-start | bytes 393220
  156.0 1.9 copy-start.3
  156.0 1.9 copy-start.4
  156.0 1.9 copy-start.15
  158.3 1.4 copy-start.2
  159.1 1.7 copy-start.17
  211.0 5.6 %copy-start.11 = (bf16[32,8,80,128]{3,2,1,0:T(8,128)(2,1)S(1)}, bf16[32,8,80,128]{3,2,1,0:T(8,128)(2,1)}, u32[]{:S(2)}) copy-start(bf16[32,8,80,128]{3,2,1,0:T(8,128)(2,1)} %all-gather.7.cloned.1.call-done) | copy-start | bytes 15728644
Sparse Core Ops, SparseCore 0:
  27.6 47.1 all-gather.4
  95.7 53.7 all-gather.6

commit v11 on v9

--- a/solution.py
+++ b/solution.py
@@ -38,8 +38,10 @@
         pl.semaphore_signal(barrier, inc=1, device_id={"tp": peer}, device_id_type=pl.DeviceIdType.MESH)
     pl.semaphore_wait(barrier, count - 1)
     copies = []
-    for d in range(1, count):
-        peer = lax.rem(me + d, count)
+    half = count // 2
+    order = [(1, k) for k in range(half)] + [(0, k) for k in range(1, half)]
+    for d, (other, k) in enumerate(order, start=1):
+        peer = lax.rem(me // half + other, 2) * half + lax.rem(me + k, half)
         copy = pltpu.make_async_remote_copy(
             src_ref=x_ref.at[pl.ds(pl.multiple_of(peer * rows, rows), rows)],
             dst_ref=recv.at[me],

time: 217 us -> 217 us (level)
  no operation moved by 1% of the time
where the time goes in v11:
time: 217 us; the launch traced here: 216 us
  waiting for transfers between devices  81.5 us (38%)
  Pallas kernels  61.4 us (28%)
  matrix products  21.3 us (10%)
  other arithmetic  17.2 us (8%)
  between operations  14.7 us (7%)
  starting transfers between devices  11.5 us (5%)
  local copies, waits for them, and re-layouts  8.81 us (4%)
    all_gather x2, waiting for transfers between devices, gather_seq(): return lax.all_gather(x, SEQ, axis=0, tiled=False)  71.9 us
    pallas_call x1, Pallas kernels, scatter_sum(): pl.pallas_call(functools.partial(scatter_sum_kernel, count, rows), out_sh...  42.1 us
    pallas_call x1, Pallas kernels, carry_in(): pl.pallas_call(functools.partial(scan_kernel, count, width), out_shape=ja...  19.3 us
    all_to_all x1, waiting for transfers between devices, on_device(): lax.all_to_all(packed, 'tp', split_axis=1, concat_axis=0, tiled=True)  9.56 us
    all_to_all x1, starting transfers between devices, on_device(): lax.all_to_all(packed, 'tp', split_axis=1, concat_axis=0, tiled=True)  8.16 us
    dot_general x1, matrix products, on_device(): jnp.dot(tokens, gathered[:, :width], preferred_element_type=jnp.float32)  5.9 us
    dot_general x1, matrix products, on_device(): jnp.einsum('rjh,jhpn->rhpn', coef_lo, every, preferred_element_type=jnp.f...  5.63 us
  transfers between devices with their start and end apart: 4, of which 3 were waited for; matrix products, arithmetic and copies ran while one was open for 8% of the time, Pallas kernels for 19%

profile of v11, /device:TPU:1, one launch (start us, length us, event | category | flops | bytes accessed | tf_op | source)
XLA Modules:
  0.0 216.5 jit_solution(5236225177679922398)
XLA Ops:
  7.2 1.2 convert_element_type.120
  8.5 0.2 copy.183
  8.8 0.2 reshape.453
  9.2 0.8 concatenate.46
  10.1 8.2 %all-to-all-start = ((bf16[16,8,1408]{2,0,1:T(8,128)(2,1)}), bf16[16,8,1408]{2,0,1:T(8,128)(2,1)S(1)}, u32[]{:S(2)}, u32[]{:S(2)}) async-start(bf16[16,8,1408]{2,0,1:T(8,128)(2,1)} %concatenate.46), calls=%async_computation | async-start | bytes 720896 | tf_op jit(solution)/shard_map/all_to_all | solution.py:210
  18.4 9.6 %all-to-all-done = bf16[16,8,1408]{2,0,1:T(8,128)(2,1)S(1)} async-done(((bf16[16,8,1408]{2,0,1:T(8,128)(2,1)}), bf16[16,8,1408]{2,0,1:T(8,128)(2,1)S(1)}, u32[]{:S(2)}, u32[]{:S(2)}) %all-to-all-start) | async-done | bytes 360480 | tf_op jit(solution)/shard_map/all_to_all | solution.py:210
  27.9 0.8 pad_maximum_fusion.1
  28.9 0.2 reduce-window.18
  29.2 0.2 fusion.54
  29.5 0.2 slice_reduce_fusion.6
  29.8 0.2 compare_reduce_fusion.1
  30.2 46.8 %all-gather.5.cloned.1.call-done = bf16[2048,1920]{1,0:T(8,128)(2,1)} async-done(((bf16[128,1920]{1,0:T(8,128)(2,1)}), bf16[2048,1920]{1,0:T(8,128)(2,1)}) %all-gather.5.cloned.1.call-update) | async-done | bytes 7864336 | tf_op jit(solution)/shard_map/all_gather | solution.py:25
  77.0 5.9 %fusion.65 = (bf16[512,1408]{0,1:T(8,128)(2,1)S(1)}, f32[512,1408]{0,1:T(8,128)S(1)}) fusion(bf16[512,2048]{1,0:T(8,128)(2,1)S(1)} %copy-done, bf16[2048,1920]{1,0:T(8,128)(2,1)} %all-gather.5.cloned.1.call-done), kind=kOutput, calls=%fused_computation.143 | convolution fusion | flops 2953510912 | bytes 12189696 | tf_op jit(solution)/shard_map/dot_general | solution.py:216
  82.9 1.1 copy-done.1
  84.1 3.3 %collective-permute-start = (bf16[3,768]{0,1:T(8,128)(2,1)S(1)}, bf16[3,768]{0,1:T(8,128)(2,1)S(1)}, u32[]{:S(2)}, u32[]{:S(2)}) collective-permute-start(bf16[3,768]{0,1:T(8,128)(2,1)S(1)} %slice.242), channel_id=1, source_target_pairs={{0,8},{8,16},{16,24},{24,32},{32,40},{40,48},{48,56},{56,64},{64,7... | collective-permute-start | bytes 13832 | tf_op jit(solution)/shard_map/ppermute | solution.py:21
  87.5 1.1 reduce-window.19
  88.7 0.2 slice_reduce_fusion
  89.0 0.2 slice_reduce_fusion.1
  89.3 1.2 slice.243
  90.8 2.1 multiply_convert_fusion.3
  93.0 0.1 reshape.456
  93.3 1.0 fusion.32
  94.7 0.7 select_maximum_fusion.mine_ref
  95.4 19.3 %shard_map.158 = f32[8,64,128]{2,1,0:T(8,128)} custom-call(f32[8,72,128]{2,1,0:T(8,128)} %select_maximum_fusion.mine_ref), custom_call_target="tpu_custom_call" | custom-call | tf_op jit(solution)/shard_map/pallas_call | solution.py:148
  114.7 0.7 pad_maximum_fusion.2
  116.0 0.6 compare_reduce_fusion
  116.7 0.2 compare_and_fusion
  117.0 0.3 fusion.42
  117.2 1.9 fusion.19
  119.1 0.4 fusion.21
  119.5 0.8 copy.132
  120.4 0.4 copy-done.2
  120.9 0.4 multiply_reduce_fusion
  121.3 0.6 select_convert_fusion
  121.9 0.1 reshape.492
  122.1 3.2 %convolution_convert_fusion = bf16[512,2048]{1,0:T(8,128)(2,1)S(1)} fusion(bf16[2048,1920]{1,0:T(8,128)(2,1)} %all-gather.5.cloned.1.call-done, f32[512]{0:T(512)S(1)} %copy-done.15, f32[512,512]{0,1:T(8,128)S(1)} %bitcast.77, bf16[512,1408]{0,1:T(8,128)(2,1)S(1)} %copy-done.2), kind=kOutput, calls=%fused_computation.11 | convolution fusion | flops 1076887552 | bytes 5769216 | tf_op jit(solution)/shard_map/dot_general | solution.py:358
  125.2 1.6 fusion.10.x_ref
  126.8 42.1 %shard_map.159 = f32[64,2176]{1,0:T(8,128)} custom-call(bf16[512,2176]{1,0:T(8,128)(2,1)} %fusion.10.x_ref), custom_call_target="tpu_custom_call" | custom-call | tf_op jit(solution)/shard_map/pallas_call | solution.py:76
  168.9 0.9 rsqrt_reduce_fusion
  169.8 1.9 multiply_convert_fusion.9
  171.6 25.1 %all-gather.7.cloned.1.call-done = bf16[32,8,80,128]{3,2,1,0:T(8,128)(2,1)} async-done(((bf16[2,8,80,128]{3,2,1,0:T(8,128)(2,1)}), bf16[32,8,80,128]{3,2,1,0:T(8,128)(2,1)}) %all-gather.7.cloned.1.call-update) | async-done | bytes 5242896 | tf_op jit(solution)/shard_map/all_gather | solution.py:25
  196.8 1.1 slice_convert_fusion
  197.9 0.6 fusion.48
  198.6 0.6 gather_fusion
  199.2 0.6 select_reduce_fusion
  200.0 5.6 %fusion.2 = f32[8,80,128,2]{2,3,1,0:T(2,128)S(1)} fusion(bf16[32,8,80,128]{3,2,1,0:T(8,128)(2,1)} %all-gather.7.cloned.1.call-done, bf16[2,32,8,1]{1,2,0,3:T(8,128)(2,1)S(1)} %get-tuple-element.82), kind=kOutput, calls=%fused_computation.3 | convolution fusion | flops 10485760 | bytes 5899264 | tf_op jit(solution)/shard_map/rjh,jhpn->rhpn/dot_general | solution.py:343
  205.6 3.1 %fusion.25 = f32[2,8,80,128]{3,0,2,1:T(2,128)S(1)} fusion(f32[8,80,128,2]{2,3,1,0:T(2,128)S(1)} %fusion.2, bf16[32,8,80,128]{3,2,1,0:T(8,128)(2,1)S(1)} %copy-done.9, bf16[2,32,8,1]{1,2,0,3:T(8,128)(2,1)S(1)} %get-tuple-element.81), kind=kOutput, calls=%fused_computation.32 | convolution fusion | flops 10649600 | bytes 6554624 | tf_op jit(solution)/shard_map/rjh,jhpn->rhpn/dot_general | solution.py:341
  208.8 0.9 copy.140
  (104 shorter events, 3.3 us)
Async XLA Ops:
  7.2 69.8 %copy-start = (bf16[512,2048]{1,0:T(8,128)(2,1)S(1)}, bf16[512,2048]{1,0:T(8,128)(2,1)}, u32[]{:S(2)}) copy-start(bf16[512,2048]{1,0:T(8,128)(2,1)} %param.23) | copy-start | bytes 6291460
  7.2 1.8 copy-start.5
  7.2 1.8 copy-start.6
  7.2 11.1 %copy-start.4 = (f32[512,128]{1,0:T(8,128)S(1)}, f32[512,128]{1,0:T(8,128)}, u32[]{:S(2)}) copy-start(f32[512,128]{1,0:T(8,128)} %param.35) | copy-start | bytes 786436
  8.7 20.1 %copy-start.16 = (s32[8]{0:T(128)S(1)}, s32[8]{0:T(128)}, u32[]{:S(2)}) copy-start(s32[8]{0:T(128)} %param.36) | copy-start | bytes 100
  8.7 20.9 %copy-start.7 = (f32[4,512]{1,0:T(4,128)S(1)}, f32[4,512]{1,0:T(4,128)}, u32[]{:S(2)}) copy-start(f32[4,512]{1,0:T(4,128)} %param.27) | copy-start | bytes 24580
  8.8 20.9 %copy-start.8 = (f32[4,256]{1,0:T(4,128)S(1)}, f32[4,256]{1,0:T(4,128)}, u32[]{:S(2)}) copy-start(f32[4,256]{1,0:T(4,128)} %param.29) | copy-start | bytes 12292
  8.8 21.0 %copy-start.10 = (f32[512]{0:T(512)S(1)}, f32[512]{0:T(512)}, u32[]{:S(2)}) copy-start(f32[512]{0:T(512)} %param.28) | copy-start | bytes 6148
  8.8 21.0 %copy-start.11 = (f32[256]{0:T(256)S(1)}, f32[256]{0:T(256)}, u32[]{:S(2)}) copy-start(f32[256]{0:T(256)} %param.30) | copy-start | bytes 3076
  8.8 21.2 %copy-start.17 = (f32[8]{0:T(128)S(1)}, f32[8]{0:T(128)}, u32[]{:S(2)}) copy-start(f32[8]{0:T(128)} %param.32) | copy-start | bytes 100
  10.1 17.9 %all-to-all-start = ((bf16[16,8,1408]{2,0,1:T(8,128)(2,1)}), bf16[16,8,1408]{2,0,1:T(8,128)(2,1)S(1)}, u32[]{:S(2)}, u32[]{:S(2)}) async-start(bf16[16,8,1408]{2,0,1:T(8,128)(2,1)} %concatenate.46), calls=%async_computation | async-start | bytes 720896 | tf_op jit(solution)/shard_map/all_to_all | solution.py:210
  18.2 58.7 %all-gather.5.cloned.1.call-start = ((), (), s32[]{:S(2)}) async-start(), calls=%async_computation.1 | async-start | bytes 8355840 | tf_op jit(solution)/shard_map/all_gather | solution.py:25
  28.8 168.0 %all-gather.7.cloned.1.call-start = ((), (), s32[]{:S(2)}) async-start(), calls=%async_computation.2 | async-start | bytes 5570560 | tf_op jit(solution)/shard_map/all_gather | solution.py:25
  30.2 57.2 %copy-start.12 = (f32[8]{0:T(128)S(1)}, f32[8]{0:T(128)}, u32[]{:S(2)}) copy-start(f32[8]{0:T(128)} %param.31) | copy-start | bytes 100
  82.9 1.1 copy-start.1
  84.1 6.7 %collective-permute-start = (bf16[3,768]{0,1:T(8,128)(2,1)S(1)}, bf16[3,768]{0,1:T(8,128)(2,1)S(1)}, u32[]{:S(2)}, u32[]{:S(2)}) collective-permute-start(bf16[3,768]{0,1:T(8,128)(2,1)S(1)} %slice.242), channel_id=1, source_target_pairs={{0,8},{8,16},{16,24},{24,32},{32,40},{40,48},{48,56},{56,64},{64,7... | collective-permute-start | bytes 13832 | tf_op jit(solution)/shard_map/ppermute | solution.py:21
  94.3 21.2 %copy-start.14 = (s32[32]{0:T(128)S(1)}, s32[32]{0:T(128)}, u32[]{:S(2)}) copy-start(s32[32]{0:T(128)} %param.37) | copy-start | bytes 388
  117.2 1.9 copy-start.3
  117.2 1.9 copy-start.13
  119.5 1.4 copy-start.2
  120.3 1.7 copy-start.15
  200.0 5.6 %copy-start.9 = (bf16[32,8,80,128]{3,2,1,0:T(8,128)(2,1)S(1)}, bf16[32,8,80,128]{3,2,1,0:T(8,128)(2,1)}, u32[]{:S(2)}) copy-start(bf16[32,8,80,128]{3,2,1,0:T(8,128)(2,1)} %all-gather.7.cloned.1.call-done) | copy-start | bytes 15728644
Sparse Core Ops, SparseCore 0:
  28.9 47.9 all-gather.4
  115.6 81.0 all-gather.6

commit v12 on v10

--- a/solution.py
+++ b/solution.py
@@ -287,58 +287,20 @@
         [jnp.ones((1, heads_local), jnp.float32), through_group[:-1]], axis=0
     )
 
-    gate_hi = through_group.astype(jnp.bfloat16)
-    gate_lo = (through_group - gate_hi.astype(jnp.float32)).astype(jnp.bfloat16)
-    extra = jnp.zeros((groups_dev, heads_local, 16, state_width), jnp.bfloat16)
-    extra = extra.at[:, :, 0, :].set(jnp.broadcast_to(gate_hi[:, :, None], gate_hi.shape + (state_width,)))
-    extra = extra.at[:, :, 1, :].set(jnp.broadcast_to(gate_lo[:, :, None], gate_lo.shape + (state_width,)))
-    sendable = jnp.concatenate([local_end.astype(jnp.bfloat16), extra], axis=2)
     dev_row = jnp.zeros((heads_local, 8, state_width), jnp.float32)
     dev_row = dev_row.at[:, 0, :].set(
         jnp.broadcast_to(through_group[-1][:, None], (heads_local, state_width))
     )
     carried = carry_in(jnp.concatenate([local_end[-1], dev_row], axis=1), head_width)
-    every = gather_seq(sendable).reshape(
-        (seq_count * groups_dev, heads_local, head_width + 16, state_width)
-    )
-    gate_rows = every[:, :, head_width : head_width + 2, :].astype(jnp.float32)
-    every_gate = (gate_rows[:, :, 0, 0] + gate_rows[:, :, 1, 0]).reshape(
-        seq_count, groups_dev, heads_local
-    )
-    dev_gate = every_gate[:, -1]
-    rows_at = jnp.arange(seq_count, dtype=jnp.int32)
-    dev_of = rows_at
-
-    def carry_weights(k):
-        between = (dev_of[:, None] < dev_of[None, :]) & (dev_of[None, :] < k)
-        factors = jnp.where(between[:, :, None], dev_gate[None, :, :], 1.0)
-        return jnp.where((dev_of < k)[:, None], jnp.prod(factors, axis=1), 0.0)
-
+    group_end = through_group[:, :, None, None] * carried[None] + local_end
+    every = gather_seq(group_end.astype(jnp.bfloat16)).reshape(
+        (seq_count * groups_dev,) + group_end.shape[1:]
+    )
     req_dev = request_group.shape[0] // seq_count
     mine = lax.dynamic_slice_in_dim(request_group, seq_index * req_dev, req_dev)
-    req_k = mine // groups_dev
-    req_c = mine % groups_dev
-    req_row = req_k
-    req_gate = every_gate[req_row, req_c]
-    wanted = req_k
-    weights_all = jax.vmap(carry_weights)(wanted)
-    weights_all = weights_all * req_gate[:, None, :]
-    slot_ids = jnp.arange(groups_dev, dtype=jnp.int32)
-    last_slot = (slot_ids == groups_dev - 1).astype(jnp.float32)
-    coef = weights_all[:, :, None, :] * last_slot[None, None, :, None]
-    own_row = req_row
-    own_slot = req_c
-    hit = (rows_at[None, :, None] == own_row[:, None, None]) & (
-        slot_ids[None, None, :] == own_slot[:, None, None]
-    )
-    coef = coef + hit[:, :, :, None].astype(jnp.float32)
-    coef = coef.reshape(wanted.shape[0], seq_count * groups_dev, heads_local)
-    coef_hi = coef.astype(jnp.bfloat16)
-    coef_lo = (coef - coef_hi.astype(jnp.float32)).astype(jnp.bfloat16)
-    summed_states = jnp.einsum(
-        "rjh,jhpn->rhpn", coef_hi, every, preferred_element_type=jnp.float32
-    ) + jnp.einsum("rjh,jhpn->rhpn", coef_lo, every, preferred_element_type=jnp.float32)
-    request_states = summed_states[:, :, :head_width]
+    request_states = jnp.stack(
+        [lax.dynamic_index_in_dim(every, mine[i], 0, keepdims=False) for i in range(req_dev)]
+    ).astype(jnp.float32)
 
     group_in = before_group[:, :, None, None] * carried[None] + local_in
     state_low = group_in.astype(jnp.bfloat16)

time: 228 us -> 223 us (0.978)
  the two profiles are of different devices: /device:TPU:48 before, /device:TPU:1 now
where the time goes in v12:
time: 223 us; the launch traced here: 222 us
  waiting for transfers between devices  74.2 us (33%)
  Pallas kernels  60.9 us (27%)
  other arithmetic  29.3 us (13%)
  between operations  18.5 us (8%)
  local copies, waits for them, and re-layouts  14.6 us (7%)
  matrix products  13.1 us (6%)
  starting transfers between devices  11.5 us (5%)
    all_gather x2, waiting for transfers between devices, gather_seq(): return lax.all_gather(x, SEQ, axis=0, tiled=False)  64.6 us
    pallas_call x1, Pallas kernels, scatter_sum(): pl.pallas_call(functools.partial(scatter_sum_kernel, count, rows), out_sh...  42 us
    pallas_call x1, Pallas kernels, carry_in(): pl.pallas_call(functools.partial(scan_kernel, count, width), out_shape=ja...  18.8 us
    all_to_all x1, waiting for transfers between devices, on_device(): lax.all_to_all(packed, 'tp', split_axis=1, concat_axis=0, tiled=True)  9.56 us
    all_to_all x1, starting transfers between devices, on_device(): lax.all_to_all(packed, 'tp', split_axis=1, concat_axis=0, tiled=True)  8.16 us
    another operation x6, other arithmetic  6.53 us
    dot_general x1, matrix products, on_device(): jnp.dot(tokens, gathered[:, :width], preferred_element_type=jnp.float32)  5.91 us
  transfers between devices with their start and end apart: 4, of which 3 were waited for; matrix products, arithmetic and copies ran while one was open for 14% of the time, Pallas kernels for 19%

profile of v12, /device:TPU:1, one launch (start us, length us, event | category | flops | bytes accessed | tf_op | source)
XLA Modules:
  0.0 222.1 jit_solution(13449807375947827443)
XLA Ops:
  7.2 1.2 convert_element_type.78
  9.2 0.8 concatenate.43
  10.1 8.2 %all-to-all-start = ((bf16[16,8,1408]{2,0,1:T(8,128)(2,1)}), bf16[16,8,1408]{2,0,1:T(8,128)(2,1)S(1)}, u32[]{:S(2)}, u32[]{:S(2)}) async-start(bf16[16,8,1408]{2,0,1:T(8,128)(2,1)} %concatenate.43), calls=%async_computation | async-start | bytes 720896 | tf_op jit(solution)/shard_map/all_to_all | solution.py:208
  18.4 9.6 %all-to-all-done = bf16[16,8,1408]{2,0,1:T(8,128)(2,1)S(1)} async-done(((bf16[16,8,1408]{2,0,1:T(8,128)(2,1)}), bf16[16,8,1408]{2,0,1:T(8,128)(2,1)S(1)}, u32[]{:S(2)}, u32[]{:S(2)}) %all-to-all-start) | async-done | bytes 360480 | tf_op jit(solution)/shard_map/all_to_all | solution.py:208
  27.9 0.8 pad_maximum_fusion.1
  29.7 0.6 pad_maximum_fusion.2
  30.3 0.7 compare_reduce_fusion.1
  31.0 0.6 slice_reduce_fusion.5
  31.7 0.6 exponential_negate_fusion
  32.3 0.6 broadcast_compare_fusion.1
  32.9 0.6 slice_compare_fusion.2
  33.5 43.5 %all-gather.6.cloned.1.call-done = bf16[2048,1920]{1,0:T(8,128)(2,1)} async-done(((bf16[128,1920]{1,0:T(8,128)(2,1)}), bf16[2048,1920]{1,0:T(8,128)(2,1)}) %all-gather.6.cloned.1.call-update) | async-done | bytes 7864336 | tf_op jit(solution)/shard_map/all_gather | solution.py:25
  77.0 5.9 %fusion.46 = (bf16[512,1408]{0,1:T(8,128)(2,1)S(1)}, f32[512,1408]{0,1:T(8,128)S(1)}) fusion(bf16[512,2048]{1,0:T(8,128)(2,1)S(1)} %copy-done, bf16[2048,1920]{1,0:T(8,128)(2,1)} %all-gather.6.cloned.1.call-done), kind=kOutput, calls=%fused_computation.109 | convolution fusion | flops 2953510912 | bytes 12189696 | tf_op jit(solution)/shard_map/dot_general | solution.py:214
  82.9 1.0 slice.179
  83.9 3.2 %collective-permute-start = (bf16[3,768]{0,1:T(8,128)(2,1)}, bf16[3,768]{0,1:T(8,128)(2,1)}, u32[]{:S(2)}, u32[]{:S(2)}) collective-permute-start(bf16[3,768]{0,1:T(8,128)(2,1)} %slice.179), channel_id=1, source_target_pairs={{0,8},{8,16},{16,24},{24,32},{32,40},{40,48},{48,56},{56,64},{64,7... | collective-permute-start | bytes 13832 | tf_op jit(solution)/shard_map/ppermute | solution.py:21
  87.2 0.7 multiply_bitcast_fusion
  87.9 3.1 %reduce-window.19 = f32[2,8,2,128]{3,1,2,0:T(8,128)} reduce-window(f32[2,8,2,128]{3,1,2,0:T(8,128)} %multiply_bitcast_fusion, f32[]{:T(128)} %constant.102.clone.1), window={size=1x1x1x128 pad=0_0x0_0x0_0x127_0}, to_apply=%region_2.3 | reduce-window | flops 520192 | bytes 32772 | tf_op jit(solution)/shard_map/reduce-window.1
  91.0 1.4 slice_reduce_fusion
  92.5 1.3 reduce-window.20
  93.7 0.7 slice.192
  94.4 1.4 select_bitcast_fusion
  95.8 0.6 copy-done.7
  96.6 0.6 copy-done.14
  97.2 0.7 exponential_select_fusion
  98.9 1.3 reduce_window.9
  100.2 1.4 select_multiply_fusion
  101.6 1.3 fusion.44
  103.0 3.4 %multiply_convert_fusion.3 = bf16[512,768]{0,1:T(8,128)(2,1)S(1)} fusion(bf16[512,768]{0,1:T(8,128)(2,1)S(1)} %slice.180, bf16[3,768]{0,1:T(8,128)(2,1)} %collective-permute-done, f32[768]{0:T(1024)} %get-tuple-element.27, f32[768]{0:T(1024)} %get-tuple-element.28, f32[768]{0:T(1024)} %get-tuple-element.29, f32[768]{0:T(1024)} %get-tuple-element.26, ...), kind=kLoop, calls=%fused_computation.17 | loop fusion | flops 11403264 | bytes 1594368 | tf_op jit(solution)/shard_map/convert_element_type | solution.py:238
  106.4 0.7 fusion.43
  107.3 0.7 copy-done.5
  108.2 1.7 fusion.22
  110.0 0.8 slice_bitcast_fusion.2
  111.0 0.7 select_maximum_fusion.mine_ref
  111.7 18.8 %shard_map.158 = f32[8,64,128]{2,1,0:T(8,128)} custom-call(f32[8,72,128]{2,1,0:T(8,128)} %select_maximum_fusion.mine_ref), custom_call_target="tpu_custom_call" | custom-call | tf_op jit(solution)/shard_map/pallas_call | solution.py:146
  130.6 1.9 fusion.27
  132.5 0.6 fusion.45
  137.0 0.6 compare_reduce_fusion
  138.2 1.7 fusion.15
  140.3 0.8 copy.99
  142.1 0.6 select_convert_fusion
  142.9 3.2 %convolution_convert_fusion = bf16[512,2048]{1,0:T(8,128)(2,1)S(1)} fusion(bf16[2048,1920]{1,0:T(8,128)(2,1)} %all-gather.6.cloned.1.call-done, f32[512]{0:T(512)S(1)} %copy-done.27, f32[512,512]{0,1:T(8,128)S(1)} %bitcast.75, bf16[512,1408]{0,1:T(8,128)(2,1)S(1)} %copy-done.3), kind=kOutput, calls=%fused_computation.6 | convolution fusion | flops 1076887552 | bytes 5769216 | tf_op jit(solution)/shard_map/dot_general | solution.py:317
  146.0 1.6 fusion.6.x_ref
  147.6 42.0 %shard_map.159 = f32[64,2176]{1,0:T(8,128)} custom-call(bf16[512,2176]{1,0:T(8,128)(2,1)} %fusion.6.x_ref), custom_call_target="tpu_custom_call" | custom-call | tf_op jit(solution)/shard_map/pallas_call | solution.py:74
  189.6 0.9 rsqrt_reduce_fusion
  190.5 1.9 multiply_convert_fusion.9
  192.3 21.1 %all-gather.4.cloned.1.call-done = bf16[16,2,8,64,128]{4,3,2,1,0:T(8,128)(2,1)} async-done(((bf16[1,2,8,64,128]{4,3,2,1,0:T(8,128)(2,1)}), bf16[16,2,8,64,128]{4,3,2,1,0:T(8,128)(2,1)}) %all-gather.4.cloned.1.call-update) | async-done | bytes 4194320 | tf_op jit(solution)/shard_map/all_gather | solution.py:25
  213.5 1.0 constant_dynamic-slice_fusion.1
  214.5 0.8 maximum_convert_fusion
  (104 shorter events, 5.7 us)
Async XLA Ops:
  7.2 69.8 %copy-start = (bf16[512,2048]{1,0:T(8,128)(2,1)S(1)}, bf16[512,2048]{1,0:T(8,128)(2,1)}, u32[]{:S(2)}) copy-start(bf16[512,2048]{1,0:T(8,128)(2,1)} %param.19) | copy-start | bytes 6291460
  7.2 1.8 copy-start.12
  7.2 1.8 copy-start.15
  7.2 11.1 %copy-start.6 = (f32[512,128]{1,0:T(8,128)S(1)}, f32[512,128]{1,0:T(8,128)}, u32[]{:S(2)}) copy-start(f32[512,128]{1,0:T(8,128)} %param.31) | copy-start | bytes 786436
  8.7 20.1 %copy-start.28 = (s32[8]{0:T(128)S(1)}, s32[8]{0:T(128)}, u32[]{:S(2)}) copy-start(s32[8]{0:T(128)} %param.32) | copy-start | bytes 100
  8.7 20.9 %copy-start.16 = (f32[4,512]{1,0:T(4,128)S(1)}, f32[4,512]{1,0:T(4,128)}, u32[]{:S(2)}) copy-start(f32[4,512]{1,0:T(4,128)} %param.23) | copy-start | bytes 24580
  8.8 20.9 %copy-start.17 = (f32[4,256]{1,0:T(4,128)S(1)}, f32[4,256]{1,0:T(4,128)}, u32[]{:S(2)}) copy-start(f32[4,256]{1,0:T(4,128)} %param.25) | copy-start | bytes 12292
  8.8 21.0 %copy-start.19 = (f32[512]{0:T(512)S(1)}, f32[512]{0:T(512)}, u32[]{:S(2)}) copy-start(f32[512]{0:T(512)} %param.24) | copy-start | bytes 6148
  8.8 21.0 %copy-start.23 = (f32[256]{0:T(256)S(1)}, f32[256]{0:T(256)}, u32[]{:S(2)}) copy-start(f32[256]{0:T(256)} %param.26) | copy-start | bytes 3076
  8.8 22.9 %copy-start.29 = (f32[8]{0:T(128)S(1)}, f32[8]{0:T(128)}, u32[]{:S(2)}) copy-start(f32[8]{0:T(128)} %param.28) | copy-start | bytes 100
  10.1 17.9 %all-to-all-start = ((bf16[16,8,1408]{2,0,1:T(8,128)(2,1)}), bf16[16,8,1408]{2,0,1:T(8,128)(2,1)S(1)}, u32[]{:S(2)}, u32[]{:S(2)}) async-start(bf16[16,8,1408]{2,0,1:T(8,128)(2,1)} %concatenate.43), calls=%async_computation | async-start | bytes 720896 | tf_op jit(solution)/shard_map/all_to_all | solution.py:208
  18.2 58.7 %all-gather.6.cloned.1.call-start = ((), (), s32[]{:S(2)}) async-start(), calls=%async_computation.2 | async-start | bytes 8355840 | tf_op jit(solution)/shard_map/all_gather | solution.py:25
  28.8 184.7 %all-gather.4.cloned.1.call-start = ((), (), s32[]{:S(2)}) async-start(), calls=%async_computation.1 | async-start | bytes 4456448 | tf_op jit(solution)/shard_map/all_gather | solution.py:25
  29.2 53.7 %copy-start.10 = (s32[2,256]{1,0:T(2,128)}, s32[2,256]{1,0:T(2,128)S(1)}, u32[]{:S(2)}) copy-start(s32[2,256]{1,0:T(2,128)S(1)} %eq.62) | copy-start | bytes 6148
  77.0 10.2 %copy-start.24 = (f32[8]{0:T(128)S(1)}, f32[8]{0:T(128)}, u32[]{:S(2)}) copy-start(f32[8]{0:T(128)} %param.27) | copy-start | bytes 100
  77.0 10.3 %copy-start.26 = (f32[8]{0:T(128)S(1)}, f32[8]{0:T(128)}, u32[]{:S(2)}) copy-start(f32[8]{0:T(128)} %exponential_negate_fusion) | copy-start | bytes 100
  82.9 23.5 %copy-start.2 = (bf16[512,1408]{0,1:T(8,128)(2,1)}, bf16[512,1408]{0,1:T(8,128)(2,1)S(1)}, u32[]{:S(2)}) copy-start(bf16[512,1408]{0,1:T(8,128)(2,1)S(1)} %get-tuple-element.48) | copy-start | bytes 4325380
  83.9 19.1 %collective-permute-start = (bf16[3,768]{0,1:T(8,128)(2,1)}, bf16[3,768]{0,1:T(8,128)(2,1)}, u32[]{:S(2)}, u32[]{:S(2)}) collective-permute-start(bf16[3,768]{0,1:T(8,128)(2,1)} %slice.179), channel_id=1, source_target_pairs={{0,8},{8,16},{16,24},{24,32},{32,40},{40,48},{48,56},{56,64},{64,7... | collective-permute-start | bytes 13832 | tf_op jit(solution)/shard_map/ppermute | solution.py:21
  95.8 0.6 copy-start.7
  96.6 0.6 copy-start.14
  97.8 0.6 copy-start.18
  107.1 0.9 copy-start.5
  107.1 2.8 %copy-start.22 = (f32[8]{0:T(128)S(1)}, f32[8]{0:T(128)}, u32[]{:S(2)}) copy-start(f32[8]{0:T(128)} %slice_bitcast_fusion.1) | copy-start | bytes 100
  108.0 2.9 %copy-start.20 = (f32[8]{0:T(128)S(1)}, f32[8]{0:T(128)}, u32[]{:S(2)}) copy-start(f32[8]{0:T(128)} %get-tuple-element.45) | copy-start | bytes 100
  108.2 22.4 %copy-start.13 = (f32[2,8]{1,0:T(2,128)S(1)}, f32[2,8]{1,0:T(2,128)}, u32[]{:S(2)}) copy-start(f32[2,8]{1,0:T(2,128)} %reduce_window.9) | copy-start | bytes 196
  109.9 22.5 %copy-start.30 = (s32[32]{0:T(128)S(1)}, s32[32]{0:T(128)}, u32[]{:S(2)}) copy-start(s32[32]{0:T(128)} %param.33) | copy-start | bytes 388
  109.9 27.7 %copy-start.11 = (s32[2,256]{1,0:T(2,128)S(1)}, s32[2,256]{1,0:T(2,128)}, u32[]{:S(2)}) copy-start(s32[2,256]{1,0:T(2,128)} %copy-done.10) | copy-start | bytes 6148
  110.0 27.9 %copy-start.21 = (f32[1,8]{1,0:T(1,128)S(1)}, f32[1,8]{1,0:T(1,128)}, u32[]{:S(2)}) copy-start(f32[1,8]{1,0:T(1,128)} %get-tuple-element.44) | copy-start | bytes 100
  110.0 27.9 %copy-start.4 = (bf16[512,128]{0,1:T(8,128)(2,1)S(1)}, bf16[512,128]{0,1:T(8,128)(2,1)}, u32[]{:S(2)}) copy-start(bf16[512,128]{0,1:T(8,128)(2,1)} %get-tuple-element.34) | copy-start | bytes 393220
  110.9 27.3 %copy-start.8 = (f32[2,8,256]{2,1,0:T(8,128)S(1)}, f32[2,8,256]{2,1,0:T(8,128)}, u32[]{:S(2)}) copy-start(f32[2,8,256]{2,1,0:T(8,128)} %copy-done.7) | copy-start | bytes 49156
  138.2 1.7 copy-start.1
  138.2 1.7 copy-start.9
  138.2 1.7 copy-start.25
  140.3 1.4 copy-start.3
  141.2 1.7 copy-start.27
Sparse Core Ops, SparseCore 0:
  28.9 47.9 all-gather.5
  132.6 80.8 all-gather.3

commit v13 on v12

--- a/solution.py
+++ b/solution.py
@@ -244,7 +244,15 @@
     step_size = jax.nn.softplus(dt_pre + dt_bias[None, :]).reshape(groups_dev, GROUP, heads_local)
     step_heads = step_size.transpose(0, 2, 1)
     decay_rate = -jnp.exp(a_log)
-    cumul_heads = jnp.cumsum(step_size * decay_rate[None, None, :], axis=1).transpose(0, 2, 1)
+    within_group = jnp.arange(GROUP, dtype=jnp.int32)
+    lower = (within_group[:, None] >= within_group[None, :]).astype(jnp.float32)
+    cumul_heads = jnp.einsum(
+        "ij,cjh->chi",
+        lower,
+        step_size * decay_rate[None, None, :],
+        precision=lax.Precision.HIGHEST,
+        preferred_element_type=jnp.float32,
+    )
     segments = seg_tok.reshape(groups_dev, GROUP)
     seg_before = segment_of(offset + jnp.arange(groups_dev, dtype=jnp.int32) * GROUP - 1, lengths)
     within = jnp.arange(GROUP, dtype=jnp.int32)

time: 223 us -> 214 us (0.960)
  other arithmetic: 29.3 us -> 22.3 us
    another operation x6 -> x3, other arithmetic: 6.53 us -> 1.47 us
  transfers between devices with their start and end apart: 4 -> 4, of which waited for: 3 -> 3; matrix products, arithmetic and copies ran while one was open for 14% -> 11% of each run, Pallas kernels for 19% -> 20%
where the time goes in v13:
time: 214 us
  waiting for transfers between devices  74.7 us (35%)
  Pallas kernels  60.9 us (28%)
  other arithmetic  22.3 us (10%)
  between operations  18.3 us (9%)
  matrix products  13.3 us (6%)
  local copies, waits for them, and re-layouts  12.5 us (6%)
  starting transfers between devices  11.5 us (5%)
    all_gather x2, waiting for transfers between devices, gather_seq(): return lax.all_gather(x, SEQ, axis=0, tiled=False)  65.2 us
    pallas_call x1, Pallas kernels, scatter_sum(): pl.pallas_call(functools.partial(scatter_sum_kernel, count, rows), out_sh...  42.1 us
    pallas_call x1, Pallas kernels, carry_in(): pl.pallas_call(functools.partial(scan_kernel, count, width), out_shape=ja...  18.8 us
    all_to_all x1, waiting for transfers between devices, on_device(): lax.all_to_all(packed, 'tp', split_axis=1, concat_axis=0, tiled=True)  9.56 us
    all_to_all x1, starting transfers between devices, on_device(): lax.all_to_all(packed, 'tp', split_axis=1, concat_axis=0, tiled=True)  8.16 us
    dot_general x1, matrix products, on_device(): jnp.dot(tokens, gathered[:, :width], preferred_element_type=jnp.float32)  5.91 us
  transfers between devices with their start and end apart: 4, of which 3 were waited for; matrix products, arithmetic and copies ran while one was open for 11% of the time, Pallas kernels for 20%

profile of v13, /device:TPU:1, one launch (start us, length us, event | category | flops | bytes accessed | tf_op | source)
XLA Modules:
  0.0 213.5 jit_solution(3946349521116191523)
XLA Ops:
  7.2 1.2 convert_element_type.79
  8.5 0.2 copy.123
  9.2 0.8 concatenate.43
  10.1 8.2 %all-to-all-start = ((bf16[16,8,1408]{2,0,1:T(8,128)(2,1)}), bf16[16,8,1408]{2,0,1:T(8,128)(2,1)S(1)}, u32[]{:S(2)}, u32[]{:S(2)}) async-start(bf16[16,8,1408]{2,0,1:T(8,128)(2,1)} %concatenate.43), calls=%async_computation | async-start | bytes 720896 | tf_op jit(solution)/shard_map/all_to_all | solution.py:208
  18.4 9.6 %all-to-all-done = bf16[16,8,1408]{2,0,1:T(8,128)(2,1)S(1)} async-done(((bf16[16,8,1408]{2,0,1:T(8,128)(2,1)}), bf16[16,8,1408]{2,0,1:T(8,128)(2,1)S(1)}, u32[]{:S(2)}, u32[]{:S(2)}) %all-to-all-start) | async-done | bytes 360480 | tf_op jit(solution)/shard_map/all_to_all | solution.py:208
  27.9 0.8 pad_maximum_fusion.1
  29.7 0.6 pad_maximum_fusion.2
  30.3 0.7 compare_reduce_fusion.1
  31.0 0.6 slice_reduce_fusion.4
  31.7 0.6 exponential_negate_fusion
  32.3 0.6 broadcast_compare_fusion.1
  32.9 0.7 slice_compare_fusion.2
  33.6 43.4 %all-gather.6.cloned.1.call-done = bf16[2048,1920]{1,0:T(8,128)(2,1)} async-done(((bf16[128,1920]{1,0:T(8,128)(2,1)}), bf16[2048,1920]{1,0:T(8,128)(2,1)}) %all-gather.6.cloned.1.call-update) | async-done | bytes 7864336 | tf_op jit(solution)/shard_map/all_gather | solution.py:25
  77.0 5.9 %fusion.50 = (bf16[512,1408]{0,1:T(8,128)(2,1)S(1)}, f32[512,1408]{0,1:T(8,128)S(1)}) fusion(bf16[512,2048]{1,0:T(8,128)(2,1)S(1)} %copy-done, bf16[2048,1920]{1,0:T(8,128)(2,1)} %all-gather.6.cloned.1.call-done), kind=kOutput, calls=%fused_computation.110 | convolution fusion | flops 2953510912 | bytes 12189696 | tf_op jit(solution)/shard_map/dot_general | solution.py:214
  82.9 1.0 slice.171
  83.9 3.2 %collective-permute-start = (bf16[3,768]{0,1:T(8,128)(2,1)}, bf16[3,768]{0,1:T(8,128)(2,1)}, u32[]{:S(2)}, u32[]{:S(2)}) collective-permute-start(bf16[3,768]{0,1:T(8,128)(2,1)} %slice.171), channel_id=1, source_target_pairs={{0,8},{8,16},{16,24},{24,32},{32,40},{40,48},{48,56},{56,64},{64,7... | collective-permute-start | bytes 13832 | tf_op jit(solution)/shard_map/ppermute | solution.py:21
  87.5 0.7 copy-done.11
  88.3 0.6 copy-done.14
  88.9 0.6 copy-done.19
  89.5 0.5 slice_bitcast_fusion.1
  90.0 1.2 reduce_window.9
  91.2 1.4 select_multiply_fusion
  92.7 1.3 fusion.48
  94.0 3.4 %multiply_convert_fusion.3 = bf16[512,768]{0,1:T(8,128)(2,1)S(1)} fusion(bf16[512,768]{0,1:T(8,128)(2,1)S(1)} %slice.172, bf16[3,768]{0,1:T(8,128)(2,1)} %collective-permute-done, f32[768]{0:T(1024)} %get-tuple-element.27, f32[768]{0:T(1024)} %get-tuple-element.28, f32[768]{0:T(1024)} %get-tuple-element.29, f32[768]{0:T(1024)} %get-tuple-element.26, ...), kind=kLoop, calls=%fused_computation.17 | loop fusion | flops 11403264 | bytes 1594368 | tf_op jit(solution)/shard_map/convert_element_type | solution.py:238
  97.4 0.7 fusion.47
  98.3 0.7 copy-done.5
  99.2 1.7 fusion.22
  101.0 0.8 slice_bitcast_fusion.2
  101.9 0.7 select_maximum_fusion.mine_ref
  102.7 18.8 %shard_map.158 = f32[8,64,128]{2,1,0:T(8,128)} custom-call(f32[8,72,128]{2,1,0:T(8,128)} %select_maximum_fusion.mine_ref), custom_call_target="tpu_custom_call" | custom-call | tf_op jit(solution)/shard_map/pallas_call | solution.py:146
  121.5 1.9 fusion.27
  123.5 0.6 fusion.49
  127.7 0.6 compare_reduce_fusion
  128.6 0.3 fusion.35
  128.9 1.7 fusion.15
  130.6 0.4 fusion.17
  131.0 0.8 copy.97
  131.9 0.4 copy-done.3
  132.4 0.4 multiply_reduce_fusion
  132.7 0.6 select_convert_fusion
  133.5 3.2 %convolution_convert_fusion = bf16[512,2048]{1,0:T(8,128)(2,1)S(1)} fusion(bf16[2048,1920]{1,0:T(8,128)(2,1)} %all-gather.6.cloned.1.call-done, f32[512]{0:T(512)S(1)} %copy-done.28, f32[512,512]{0,1:T(8,128)S(1)} %bitcast.71, bf16[512,1408]{0,1:T(8,128)(2,1)S(1)} %copy-done.3), kind=kOutput, calls=%fused_computation.6 | convolution fusion | flops 1076887552 | bytes 5769216 | tf_op jit(solution)/shard_map/dot_general | solution.py:325
  136.7 1.6 fusion.6.x_ref
  138.3 42.1 %shard_map.159 = f32[64,2176]{1,0:T(8,128)} custom-call(bf16[512,2176]{1,0:T(8,128)(2,1)} %fusion.6.x_ref), custom_call_target="tpu_custom_call" | custom-call | tf_op jit(solution)/shard_map/pallas_call | solution.py:74
  180.3 0.9 rsqrt_reduce_fusion
  181.2 1.9 multiply_convert_fusion.9
  183.1 21.8 %all-gather.4.cloned.1.call-done = bf16[16,2,8,64,128]{4,3,2,1,0:T(8,128)(2,1)} async-done(((bf16[1,2,8,64,128]{4,3,2,1,0:T(8,128)(2,1)}), bf16[16,2,8,64,128]{4,3,2,1,0:T(8,128)(2,1)}) %all-gather.4.cloned.1.call-update) | async-done | bytes 4194320 | tf_op jit(solution)/shard_map/all_gather | solution.py:25
  204.8 1.0 constant_dynamic-slice_fusion.1
  205.8 0.8 maximum_convert_fusion
  (103 shorter events, 3.2 us)
Async XLA Ops:
  7.2 69.8 %copy-start = (bf16[512,2048]{1,0:T(8,128)(2,1)S(1)}, bf16[512,2048]{1,0:T(8,128)(2,1)}, u32[]{:S(2)}) copy-start(bf16[512,2048]{1,0:T(8,128)(2,1)} %param.19) | copy-start | bytes 6291460
  7.2 1.8 copy-start.13
  7.2 1.8 copy-start.16
  7.2 11.1 %copy-start.6 = (f32[512,128]{1,0:T(8,128)S(1)}, f32[512,128]{1,0:T(8,128)}, u32[]{:S(2)}) copy-start(f32[512,128]{1,0:T(8,128)} %param.31) | copy-start | bytes 786436
  8.7 20.1 %copy-start.29 = (s32[8]{0:T(128)S(1)}, s32[8]{0:T(128)}, u32[]{:S(2)}) copy-start(s32[8]{0:T(128)} %param.32) | copy-start | bytes 100
  8.7 20.9 %copy-start.17 = (f32[4,512]{1,0:T(4,128)S(1)}, f32[4,512]{1,0:T(4,128)}, u32[]{:S(2)}) copy-start(f32[4,512]{1,0:T(4,128)} %param.23) | copy-start | bytes 24580
  8.8 20.9 %copy-start.18 = (f32[4,256]{1,0:T(4,128)S(1)}, f32[4,256]{1,0:T(4,128)}, u32[]{:S(2)}) copy-start(f32[4,256]{1,0:T(4,128)} %param.25) | copy-start | bytes 12292
  8.8 21.0 %copy-start.20 = (f32[512]{0:T(512)S(1)}, f32[512]{0:T(512)}, u32[]{:S(2)}) copy-start(f32[512]{0:T(512)} %param.24) | copy-start | bytes 6148
  8.8 21.0 %copy-start.25 = (f32[256]{0:T(256)S(1)}, f32[256]{0:T(256)}, u32[]{:S(2)}) copy-start(f32[256]{0:T(256)} %param.26) | copy-start | bytes 3076
  8.8 22.9 %copy-start.30 = (f32[8]{0:T(128)S(1)}, f32[8]{0:T(128)}, u32[]{:S(2)}) copy-start(f32[8]{0:T(128)} %param.28) | copy-start | bytes 100
  10.1 17.9 %all-to-all-start = ((bf16[16,8,1408]{2,0,1:T(8,128)(2,1)}), bf16[16,8,1408]{2,0,1:T(8,128)(2,1)S(1)}, u32[]{:S(2)}, u32[]{:S(2)}) async-start(bf16[16,8,1408]{2,0,1:T(8,128)(2,1)} %concatenate.43), calls=%async_computation | async-start | bytes 720896 | tf_op jit(solution)/shard_map/all_to_all | solution.py:208
  18.2 58.7 %all-gather.6.cloned.1.call-start = ((), (), s32[]{:S(2)}) async-start(), calls=%async_computation.2 | async-start | bytes 8355840 | tf_op jit(solution)/shard_map/all_gather | solution.py:25
  28.8 176.1 %all-gather.4.cloned.1.call-start = ((), (), s32[]{:S(2)}) async-start(), calls=%async_computation.1 | async-start | bytes 4456448 | tf_op jit(solution)/shard_map/all_gather | solution.py:25
  29.2 53.7 %copy-start.9 = (s32[2,256]{1,0:T(2,128)}, s32[2,256]{1,0:T(2,128)S(1)}, u32[]{:S(2)}) copy-start(s32[2,256]{1,0:T(2,128)S(1)} %eq.62) | copy-start | bytes 6148
  77.0 10.2 %copy-start.26 = (f32[8]{0:T(128)S(1)}, f32[8]{0:T(128)}, u32[]{:S(2)}) copy-start(f32[8]{0:T(128)} %param.27) | copy-start | bytes 100
  77.0 10.3 %copy-start.32 = (f32[8]{0:T(128)S(1)}, f32[8]{0:T(128)}, u32[]{:S(2)}) copy-start(f32[8]{0:T(128)} %exponential_negate_fusion) | copy-start | bytes 100
  77.0 11.9 %copy-start.21 = (pred[2]{0:T(512)(128)(4,1)S(1)}, pred[2]{0:T(512)(128)(4,1)}, u32[]{:S(2)}) copy-start(pred[2]{0:T(512)(128)(4,1)} %compare_reduce_fusion.1) | copy-start | bytes 10
  82.9 14.5 %copy-start.2 = (bf16[512,1408]{0,1:T(8,128)(2,1)}, bf16[512,1408]{0,1:T(8,128)(2,1)S(1)}, u32[]{:S(2)}) copy-start(bf16[512,1408]{0,1:T(8,128)(2,1)S(1)} %get-tuple-element.48) | copy-start | bytes 4325380
  83.9 10.1 %collective-permute-start = (bf16[3,768]{0,1:T(8,128)(2,1)}, bf16[3,768]{0,1:T(8,128)(2,1)}, u32[]{:S(2)}, u32[]{:S(2)}) collective-permute-start(bf16[3,768]{0,1:T(8,128)(2,1)} %slice.171), channel_id=1, source_target_pairs={{0,8},{8,16},{16,24},{24,32},{32,40},{40,48},{48,56},{56,64},{64,7... | collective-permute-start | bytes 13832 | tf_op jit(solution)/shard_map/ppermute | solution.py:21
  87.2 4.0 %copy-start.7 = (f32[512,8]{0,1:T(8,128)}, f32[512,8]{0,1:T(8,128)S(1)}, u32[]{:S(2)}) copy-start(f32[512,8]{0,1:T(8,128)S(1)} %compare_select_fusion) | copy-start | bytes 49156
  87.4 0.7 copy-start.11
  88.3 0.6 copy-start.14
  88.9 0.6 copy-start.19
  98.1 0.9 copy-start.5
  98.1 2.8 %copy-start.24 = (f32[8]{0:T(128)S(1)}, f32[8]{0:T(128)}, u32[]{:S(2)}) copy-start(f32[8]{0:T(128)} %slice_bitcast_fusion.1) | copy-start | bytes 100
  99.0 2.9 %copy-start.22 = (f32[8]{0:T(128)S(1)}, f32[8]{0:T(128)}, u32[]{:S(2)}) copy-start(f32[8]{0:T(128)} %get-tuple-element.45) | copy-start | bytes 100
  99.2 22.4 %copy-start.15 = (f32[2,8]{1,0:T(2,128)S(1)}, f32[2,8]{1,0:T(2,128)}, u32[]{:S(2)}) copy-start(f32[2,8]{1,0:T(2,128)} %reduce_window.9) | copy-start | bytes 196
  100.9 22.5 %copy-start.31 = (s32[32]{0:T(128)S(1)}, s32[32]{0:T(128)}, u32[]{:S(2)}) copy-start(s32[32]{0:T(128)} %param.33) | copy-start | bytes 388
  100.9 27.4 %copy-start.10 = (s32[2,256]{1,0:T(2,128)S(1)}, s32[2,256]{1,0:T(2,128)}, u32[]{:S(2)}) copy-start(s32[2,256]{1,0:T(2,128)} %copy-done.9) | copy-start | bytes 6148
  100.9 27.6 %copy-start.23 = (f32[1,8]{1,0:T(1,128)S(1)}, f32[1,8]{1,0:T(1,128)}, u32[]{:S(2)}) copy-start(f32[1,8]{1,0:T(1,128)} %get-tuple-element.44) | copy-start | bytes 100
  100.9 27.6 %copy-start.4 = (bf16[512,128]{0,1:T(8,128)(2,1)S(1)}, bf16[512,128]{0,1:T(8,128)(2,1)}, u32[]{:S(2)}) copy-start(bf16[512,128]{0,1:T(8,128)(2,1)} %get-tuple-element.32) | copy-start | bytes 393220
  101.8 27.0 %copy-start.8 = (f32[512,8]{0,1:T(8,128)S(1)}, f32[512,8]{0,1:T(8,128)}, u32[]{:S(2)}) copy-start(f32[512,8]{0,1:T(8,128)} %copy-done.7) | copy-start | bytes 49156
  101.9 27.0 %copy-start.12 = (f32[2,8,256]{2,1,0:T(8,128)S(1)}, f32[2,8,256]{2,1,0:T(8,128)}, u32[]{:S(2)}) copy-start(f32[2,8,256]{2,1,0:T(8,128)} %copy-done.11) | copy-start | bytes 49156
  128.9 1.7 copy-start.1
  128.9 1.7 copy-start.27
  131.0 1.4 copy-start.3
  131.8 1.7 copy-start.28
Sparse Core Ops, SparseCore 0:
  28.9 47.9 all-gather.5
  123.6 81.2 all-gather.3

commit v14 on v13

--- a/solution.py
+++ b/solution.py
@@ -30,59 +30,75 @@
     return jnp.sum((position[:, None] >= prompt_ends[None, :]).astype(jnp.int32), axis=1)
 
 
-def scatter_sum_kernel(count, rows, x_ref, o_ref, recv, send_sem, recv_sem):
+def scatter_sum_kernel(count, rows, x_ref, q_ref, o_ref, qo_ref, recv, recv_q, send_sem, recv_sem):
     me = lax.axis_index("tp")
     barrier = pltpu.get_barrier_semaphore()
     for d in range(1, count):
         peer = lax.rem(me + d, count)
         pl.semaphore_signal(barrier, inc=1, device_id={"tp": peer}, device_id_type=pl.DeviceIdType.MESH)
     pl.semaphore_wait(barrier, count - 1)
+
+    def pair(d, peer, slot):
+        big = pltpu.make_async_remote_copy(
+            src_ref=x_ref.at[pl.ds(pl.multiple_of(peer * rows, rows), rows)],
+            dst_ref=recv.at[slot],
+            send_sem=send_sem.at[0, d],
+            recv_sem=recv_sem.at[0, slot],
+            device_id={"tp": peer},
+            device_id_type=pl.DeviceIdType.MESH,
+        )
+        small = pltpu.make_async_remote_copy(
+            src_ref=q_ref.at[pl.ds(pl.multiple_of(peer * 8, 8), 8)],
+            dst_ref=recv_q.at[slot],
+            send_sem=send_sem.at[1, d],
+            recv_sem=recv_sem.at[1, slot],
+            device_id={"tp": peer},
+            device_id_type=pl.DeviceIdType.MESH,
+        )
+        return big, small
+
     copies = []
     for d in range(1, count):
         peer = lax.rem(me + d, count)
-        copy = pltpu.make_async_remote_copy(
-            src_ref=x_ref.at[pl.ds(pl.multiple_of(peer * rows, rows), rows)],
-            dst_ref=recv.at[me],
-            send_sem=send_sem.at[d],
-            recv_sem=recv_sem.at[me],
-            device_id={"tp": peer},
-            device_id_type=pl.DeviceIdType.MESH,
-        )
-        copy.start()
-        copies.append(copy)
+        big, small = pair(d, peer, me)
+        big.start()
+        small.start()
+        copies.append((big, small))
     total = x_ref[pl.ds(pl.multiple_of(me * rows, rows), rows), :].astype(jnp.float32)
+    side = q_ref[pl.ds(pl.multiple_of(me * 8, 8), 8), :]
     for d in range(1, count):
         sender = lax.rem(me + count - d, count)
-        arrival = pltpu.make_async_remote_copy(
-            src_ref=x_ref.at[pl.ds(0, rows)],
-            dst_ref=recv.at[sender],
-            send_sem=send_sem.at[d],
-            recv_sem=recv_sem.at[sender],
-            device_id={"tp": sender},
-            device_id_type=pl.DeviceIdType.MESH,
-        )
-        arrival.wait_recv()
+        big, small = pair(0, sender, sender)
+        big.wait_recv()
+        small.wait_recv()
         total = total + recv[sender].astype(jnp.float32)
-    for copy in copies:
-        copy.wait_send()
+        side = side + recv_q[sender]
+    for big, small in copies:
+        big.wait_send()
+        small.wait_send()
     o_ref[...] = total
-
-
-def scatter_sum(x, count):
+    qo_ref[...] = side
+
+
+def scatter_sum(x, q, count):
     rows = x.shape[0] // count
     cols = x.shape[1]
     return pl.pallas_call(
         functools.partial(scatter_sum_kernel, count, rows),
-        out_shape=jax.ShapeDtypeStruct((rows, cols), jnp.float32),
-        in_specs=[pl.BlockSpec(memory_space=pltpu.VMEM)],
-        out_specs=pl.BlockSpec(memory_space=pltpu.VMEM),
+        out_shape=(
+            jax.ShapeDtypeStruct((rows, cols), jnp.float32),
+            jax.ShapeDtypeStruct((8, q.shape[1]), jnp.float32),
+        ),
+        in_specs=[pl.BlockSpec(memory_space=pltpu.VMEM)] * 2,
+        out_specs=(pl.BlockSpec(memory_space=pltpu.VMEM), pl.BlockSpec(memory_space=pltpu.VMEM)),
         scratch_shapes=[
             pltpu.VMEM((count, rows, cols), x.dtype),
-            pltpu.SemaphoreType.DMA((count,)),
-            pltpu.SemaphoreType.DMA((count,)),
+            pltpu.VMEM((count, 8, q.shape[1]), jnp.float32),
+            pltpu.SemaphoreType.DMA((2, count)),
+            pltpu.SemaphoreType.DMA((2, count)),
         ],
         compiler_params=pltpu.CompilerParams(collective_id=0, has_side_effects=True),
-    )(x)
+    )(x, q)
 
 
 def scan_kernel(count, width, mine_ref, out_ref, acc, send_buf, recv, send_sem, recv_sem):
@@ -325,10 +341,17 @@
     partial = lax.dot_general(
         scaled, gathered[:, width:], (((1,), (1,)), ((), ())), preferred_element_type=jnp.float32
     )
-    side = jnp.zeros((tok_dev, 128), jnp.float32).at[:, 0].set(square_sum)
-    summed = scatter_sum(jnp.concatenate([partial, side], axis=1).astype(jnp.bfloat16), tp_count)
-    mean_square = summed[:, d_model] / INNER
-    mixed = (summed[:, :d_model] * lax.rsqrt(mean_square + epsilon)[:, None]).astype(jnp.bfloat16)
+    rows_out = tok_dev // tp_count
+    side = square_sum.reshape(tp_count, 1, rows_out)
+    side = jnp.concatenate(
+        [side, jnp.zeros((tp_count, 1, 128 - rows_out), jnp.float32)], axis=2
+    )
+    side = jnp.concatenate([side, jnp.zeros((tp_count, 7, 128), jnp.float32)], axis=1)
+    summed, side_sum = scatter_sum(
+        partial.astype(jnp.bfloat16), side.reshape(tp_count * 8, 128), tp_count
+    )
+    mean_square = side_sum[0, :rows_out] / INNER
+    mixed = (summed * lax.rsqrt(mean_square + epsilon)[:, None]).astype(jnp.bfloat16)
     return (mixed, request_states)
 
 

time: 214 us -> 213 us (level)
  transfers between devices with their start and end apart: 4 -> 4, of which waited for: 3 -> 3; matrix products, arithmetic and copies ran while one was open for 11% -> 11% of each run, Pallas kernels for 20% -> 19%
where the time goes in v14:
time: 213 us; the launch traced here: 212 us
  waiting for transfers between devices  75.6 us (35%)
  Pallas kernels  59.3 us (28%)
  other arithmetic  20.3 us (10%)
  between operations  18.4 us (9%)
  matrix products  14.1 us (7%)
  local copies, waits for them, and re-layouts  12.6 us (6%)
  starting transfers between devices  11.5 us (5%)
    all_gather x2, waiting for transfers between devices, gather_seq(): return lax.all_gather(x, SEQ, axis=0, tiled=False)  66 us
    pallas_call x1, Pallas kernels, scatter_sum(): pl.pallas_call(functools.partial(scatter_sum_kernel, count, rows), out_sh...  40.4 us
    pallas_call x1, Pallas kernels, carry_in(): pl.pallas_call(functools.partial(scan_kernel, count, width), out_shape=ja...  18.9 us
    all_to_all x1, waiting for transfers between devices, on_device(): lax.all_to_all(packed, 'tp', split_axis=1, concat_axis=0, tiled=True)  9.56 us
    all_to_all x1, starting transfers between devices, on_device(): lax.all_to_all(packed, 'tp', split_axis=1, concat_axis=0, tiled=True)  8.16 us
    dot_general x1, matrix products, on_device(): jnp.dot(tokens, gathered[:, :width], preferred_element_type=jnp.float32)  5.91 us
    dot_general x1, matrix products, on_device(): lax.dot_general(scaled, gathered[:, width:], (((1,), (1,)), ((), ())), pr...  4.66 us
  transfers between devices with their start and end apart: 4, of which 3 were waited for; matrix products, arithmetic and copies ran while one was open for 11% of the time, Pallas kernels for 19%

profile of v14, /device:TPU:1, one launch (start us, length us, event | category | flops | bytes accessed | tf_op | source)
XLA Modules:
  0.0 211.8 jit_solution(741977187954907484)
XLA Ops:
  7.2 1.2 convert_element_type.81
  8.5 0.2 copy.118
  9.2 0.8 concatenate.43
  10.1 8.2 %all-to-all-start = ((bf16[16,8,1408]{2,0,1:T(8,128)(2,1)}), bf16[16,8,1408]{2,0,1:T(8,128)(2,1)S(1)}, u32[]{:S(2)}, u32[]{:S(2)}) async-start(bf16[16,8,1408]{2,0,1:T(8,128)(2,1)} %concatenate.43), calls=%async_computation | async-start | bytes 720896 | tf_op jit(solution)/shard_map/all_to_all | solution.py:224
  18.4 9.6 %all-to-all-done = bf16[16,8,1408]{2,0,1:T(8,128)(2,1)S(1)} async-done(((bf16[16,8,1408]{2,0,1:T(8,128)(2,1)}), bf16[16,8,1408]{2,0,1:T(8,128)(2,1)S(1)}, u32[]{:S(2)}, u32[]{:S(2)}) %all-to-all-start) | async-done | bytes 360480 | tf_op jit(solution)/shard_map/all_to_all | solution.py:224
  27.9 0.8 pad_maximum_fusion.1
  29.2 0.2 fusion.41
  29.5 0.2 slice_reduce_fusion.5
  29.7 0.6 pad_maximum_fusion.2
  30.3 0.7 compare_reduce_fusion
  31.0 0.6 slice_reduce_fusion.4
  31.7 0.6 exponential_negate_fusion
  32.2 0.7 broadcast_compare_fusion.1
  32.9 0.6 slice_compare_fusion.2
  33.5 43.4 %all-gather.6.cloned.1.call-done = bf16[2048,1920]{1,0:T(8,128)(2,1)} async-done(((bf16[128,1920]{1,0:T(8,128)(2,1)}), bf16[2048,1920]{1,0:T(8,128)(2,1)}) %all-gather.6.cloned.1.call-update) | async-done | bytes 7864336 | tf_op jit(solution)/shard_map/all_gather | solution.py:25
  77.0 5.9 %fusion.48 = (bf16[512,1408]{0,1:T(8,128)(2,1)S(1)}, f32[512,1408]{0,1:T(8,128)S(1)}) fusion(bf16[512,2048]{1,0:T(8,128)(2,1)S(1)} %copy-done, bf16[2048,1920]{1,0:T(8,128)(2,1)} %all-gather.6.cloned.1.call-done), kind=kOutput, calls=%fused_computation.106 | convolution fusion | flops 2953510912 | bytes 12189696 | tf_op jit(solution)/shard_map/dot_general | solution.py:230
  82.9 1.0 slice.153
  83.9 3.2 %collective-permute-start = (bf16[3,768]{0,1:T(8,128)(2,1)}, bf16[3,768]{0,1:T(8,128)(2,1)}, u32[]{:S(2)}, u32[]{:S(2)}) collective-permute-start(bf16[3,768]{0,1:T(8,128)(2,1)} %slice.153), channel_id=1, source_target_pairs={{0,8},{8,16},{16,24},{24,32},{32,40},{40,48},{48,56},{56,64},{64,7... | collective-permute-start | bytes 13832 | tf_op jit(solution)/shard_map/ppermute | solution.py:21
  87.2 0.2 fusion.31
  87.4 0.7 copy-done.10
  88.3 0.6 copy-done.19
  88.9 0.6 copy-done.24
  89.5 0.5 slice_bitcast_fusion.1
  90.0 1.2 reduce_window.9
  91.3 1.4 select_multiply_fusion
  92.7 1.2 fusion.46
  94.1 3.4 %multiply_convert_fusion.3 = bf16[512,768]{0,1:T(8,128)(2,1)S(1)} fusion(bf16[512,768]{0,1:T(8,128)(2,1)S(1)} %slice.154, bf16[3,768]{0,1:T(8,128)(2,1)} %collective-permute-done, f32[768]{0:T(1024)S(1)} %copy-done.13, f32[768]{0:T(1024)S(1)} %copy-done.14, f32[768]{0:T(1024)S(1)} %copy-done.15, f32[768]{0:T(1024)S(1)} %copy-done.12, f32[768]{0:T(1024)S(1)} %copy-done.16, ...), kind=kLoop, calls=%fused_computation.14 | loop fusion | flops 11403264 | bytes 1594368 | tf_op jit(solution)/shard_map/convert_element_type | solution.py:254
  97.5 0.7 fusion.45
  98.4 0.7 copy-done.4
  99.3 1.0 fusion.20
  100.4 0.8 slice_bitcast_fusion.2
  101.4 0.7 select_maximum_fusion.mine_ref
  102.1 18.9 %shard_map.158 = f32[8,64,128]{2,1,0:T(8,128)} custom-call(f32[8,72,128]{2,1,0:T(8,128)} %select_maximum_fusion.mine_ref), custom_call_target="tpu_custom_call" | custom-call | tf_op jit(solution)/shard_map/pallas_call | solution.py:162
  121.0 1.9 fusion.25
  123.0 0.6 fusion.47
  127.5 0.3 fusion.33
  127.8 1.7 fusion.13
  129.5 0.4 fusion.15
  129.9 0.8 copy.93
  130.8 1.4 multiply_reduce_fusion
  132.3 0.6 pad_bitcast_fusion.q_ref
  132.9 4.7 %convolution_convert_fusion.x_ref = bf16[512,2048]{1,0:T(8,128)(2,1)} fusion(bf16[2048,1920]{1,0:T(8,128)(2,1)} %all-gather.6.cloned.1.call-done, f32[512]{0:T(512)S(1)} %copy-done.36, f32[512,512]{0,1:T(8,128)S(1)} %bitcast.75, bf16[512,1408]{0,1:T(8,128)(2,1)} %copy-done.2), kind=kOutput, calls=%fused_computation.4 | convolution fusion | flops 1076887552 | bytes 5769216 | tf_op jit(solution)/shard_map/dot_general | solution.py:341
  137.6 40.4 %shard_map.159 = (f32[64,2048]{1,0:T(8,128)}, f32[8,128]{1,0:T(8,128)}) custom-call(bf16[512,2048]{1,0:T(8,128)(2,1)} %convolution_convert_fusion.x_ref, f32[64,128]{1,0:T(8,128)} %pad_bitcast_fusion.q_ref), custom_call_target="tpu_custom_call" | custom-call | tf_op jit(solution)/shard_map/pallas_call | solution.py:86
  178.0 0.7 rsqrt_bitcast_fusion
  178.7 1.8 multiply_convert_fusion.9
  180.5 22.6 %all-gather.4.cloned.1.call-done = bf16[16,2,8,64,128]{4,3,2,1,0:T(8,128)(2,1)} async-done(((bf16[1,2,8,64,128]{4,3,2,1,0:T(8,128)(2,1)}), bf16[16,2,8,64,128]{4,3,2,1,0:T(8,128)(2,1)}) %all-gather.4.cloned.1.call-update) | async-done | bytes 4194320 | tf_op jit(solution)/shard_map/all_gather | solution.py:25
  203.1 1.0 constant_dynamic-slice_fusion.1
  204.1 0.8 maximum_convert_fusion
  (117 shorter events, 2.6 us)
Async XLA Ops:
  7.2 69.8 %copy-start = (bf16[512,2048]{1,0:T(8,128)(2,1)S(1)}, bf16[512,2048]{1,0:T(8,128)(2,1)}, u32[]{:S(2)}) copy-start(bf16[512,2048]{1,0:T(8,128)(2,1)} %param.17) | copy-start | bytes 6291460
  7.2 1.7 copy-start.17
  7.2 1.7 copy-start.21
  8.4 9.9 %copy-start.5 = (f32[512,128]{1,0:T(8,128)S(1)}, f32[512,128]{1,0:T(8,128)}, u32[]{:S(2)}) copy-start(f32[512,128]{1,0:T(8,128)} %param.29) | copy-start | bytes 786436
  9.2 19.7 %copy-start.37 = (s32[8]{0:T(128)S(1)}, s32[8]{0:T(128)}, u32[]{:S(2)}) copy-start(s32[8]{0:T(128)} %param.30) | copy-start | bytes 100
  9.2 20.5 %copy-start.22 = (f32[4,512]{1,0:T(4,128)S(1)}, f32[4,512]{1,0:T(4,128)}, u32[]{:S(2)}) copy-start(f32[4,512]{1,0:T(4,128)} %param.21) | copy-start | bytes 24580
  9.2 20.5 %copy-start.23 = (f32[4,256]{1,0:T(4,128)S(1)}, f32[4,256]{1,0:T(4,128)}, u32[]{:S(2)}) copy-start(f32[4,256]{1,0:T(4,128)} %param.23) | copy-start | bytes 12292
  9.2 20.5 %copy-start.28 = (f32[512]{0:T(512)S(1)}, f32[512]{0:T(512)}, u32[]{:S(2)}) copy-start(f32[512]{0:T(512)} %param.22) | copy-start | bytes 6148
  9.2 20.5 %copy-start.33 = (f32[256]{0:T(256)S(1)}, f32[256]{0:T(256)}, u32[]{:S(2)}) copy-start(f32[256]{0:T(256)} %param.24) | copy-start | bytes 3076
  9.2 22.4 %copy-start.38 = (f32[8]{0:T(128)S(1)}, f32[8]{0:T(128)}, u32[]{:S(2)}) copy-start(f32[8]{0:T(128)} %param.26) | copy-start | bytes 100
  10.1 17.9 %all-to-all-start = ((bf16[16,8,1408]{2,0,1:T(8,128)(2,1)}), bf16[16,8,1408]{2,0,1:T(8,128)(2,1)S(1)}, u32[]{:S(2)}, u32[]{:S(2)}) async-start(bf16[16,8,1408]{2,0,1:T(8,128)(2,1)} %concatenate.43), calls=%async_computation | async-start | bytes 720896 | tf_op jit(solution)/shard_map/all_to_all | solution.py:224
  18.2 58.7 %all-gather.6.cloned.1.call-start = ((), (), s32[]{:S(2)}) async-start(), calls=%async_computation.2 | async-start | bytes 8355840 | tf_op jit(solution)/shard_map/all_gather | solution.py:25
  28.8 174.3 %all-gather.4.cloned.1.call-start = ((), (), s32[]{:S(2)}) async-start(), calls=%async_computation.1 | async-start | bytes 4456448 | tf_op jit(solution)/shard_map/all_gather | solution.py:25
  29.2 53.7 %copy-start.8 = (s32[2,256]{1,0:T(2,128)}, s32[2,256]{1,0:T(2,128)S(1)}, u32[]{:S(2)}) copy-start(s32[2,256]{1,0:T(2,128)S(1)} %eq.62) | copy-start | bytes 6148
  76.9 10.2 %copy-start.34 = (f32[8]{0:T(128)S(1)}, f32[8]{0:T(128)}, u32[]{:S(2)}) copy-start(f32[8]{0:T(128)} %param.25) | copy-start | bytes 100
  77.0 10.3 %copy-start.40 = (f32[8]{0:T(128)S(1)}, f32[8]{0:T(128)}, u32[]{:S(2)}) copy-start(f32[8]{0:T(128)} %exponential_negate_fusion) | copy-start | bytes 100
  77.0 11.9 %copy-start.29 = (pred[2]{0:T(512)(128)(4,1)S(1)}, pred[2]{0:T(512)(128)(4,1)}, u32[]{:S(2)}) copy-start(pred[2]{0:T(512)(128)(4,1)} %compare_reduce_fusion) | copy-start | bytes 10
  82.9 14.6 %copy-start.2 = (bf16[512,1408]{0,1:T(8,128)(2,1)}, bf16[512,1408]{0,1:T(8,128)(2,1)S(1)}, u32[]{:S(2)}) copy-start(bf16[512,1408]{0,1:T(8,128)(2,1)S(1)} %get-tuple-element.40) | copy-start | bytes 4325380
  83.9 10.2 %collective-permute-start = (bf16[3,768]{0,1:T(8,128)(2,1)}, bf16[3,768]{0,1:T(8,128)(2,1)}, u32[]{:S(2)}, u32[]{:S(2)}) collective-permute-start(bf16[3,768]{0,1:T(8,128)(2,1)} %slice.153), channel_id=1, source_target_pairs={{0,8},{8,16},{16,24},{24,32},{32,40},{40,48},{48,56},{56,64},{64,7... | collective-permute-start | bytes 13832 | tf_op jit(solution)/shard_map/ppermute | solution.py:21
  87.2 4.1 %copy-start.6 = (f32[512,8]{0,1:T(8,128)}, f32[512,8]{0,1:T(8,128)S(1)}, u32[]{:S(2)}) copy-start(f32[512,8]{0,1:T(8,128)S(1)} %compare_select_fusion) | copy-start | bytes 49156
  87.4 0.7 copy-start.10
  88.3 0.6 copy-start.19
  88.9 0.6 copy-start.24
  91.2 2.8 %copy-start.12 = (f32[768]{0:T(1024)S(1)}, f32[768]{0:T(1024)}, u32[]{:S(2)}) copy-start(f32[768]{0:T(1024)} %get-tuple-element.18) | copy-start | bytes 9220
  91.2 2.8 %copy-start.13 = (f32[768]{0:T(1024)S(1)}, f32[768]{0:T(1024)}, u32[]{:S(2)}) copy-start(f32[768]{0:T(1024)} %get-tuple-element.19) | copy-start | bytes 9220
  91.2 2.8 %copy-start.14 = (f32[768]{0:T(1024)S(1)}, f32[768]{0:T(1024)}, u32[]{:S(2)}) copy-start(f32[768]{0:T(1024)} %get-tuple-element.20) | copy-start | bytes 9220
  91.2 2.8 %copy-start.15 = (f32[768]{0:T(1024)S(1)}, f32[768]{0:T(1024)}, u32[]{:S(2)}) copy-start(f32[768]{0:T(1024)} %get-tuple-element.21) | copy-start | bytes 9220
  91.2 2.8 %copy-start.16 = (f32[768]{0:T(1024)S(1)}, f32[768]{0:T(1024)}, u32[]{:S(2)}) copy-start(f32[768]{0:T(1024)} %pad_maximum_fusion.2) | copy-start | bytes 9220
  91.2 2.8 %copy-start.25 = (pred[512]{0:T(512)(128)(4,1)S(1)}, pred[512]{0:T(512)(128)(4,1)}, u32[]{:S(2)}) copy-start(pred[512]{0:T(512)(128)(4,1)} %get-tuple-element.31) | copy-start | bytes 1540
  91.3 2.8 %copy-start.26 = (pred[512]{0:T(512)(128)(4,1)S(1)}, pred[512]{0:T(512)(128)(4,1)}, u32[]{:S(2)}) copy-start(pred[512]{0:T(512)(128)(4,1)} %get-tuple-element.32) | copy-start | bytes 1540
  91.3 2.8 %copy-start.27 = (pred[512]{0:T(512)(128)(4,1)S(1)}, pred[512]{0:T(512)(128)(4,1)}, u32[]{:S(2)}) copy-start(pred[512]{0:T(512)(128)(4,1)} %get-tuple-element.33) | copy-start | bytes 1540
  98.2 0.9 copy-start.4
  98.2 1.1 copy-start.18
  98.3 2.1 copy-start.32
  99.3 2.0 copy-start.30
  100.4 20.6 %copy-start.20 = (f32[2,8]{1,0:T(2,128)S(1)}, f32[2,8]{1,0:T(2,128)}, u32[]{:S(2)}) copy-start(f32[2,8]{1,0:T(2,128)} %reduce_window.9) | copy-start | bytes 196
  101.2 21.7 %copy-start.39 = (s32[32]{0:T(128)S(1)}, s32[32]{0:T(128)}, u32[]{:S(2)}) copy-start(s32[32]{0:T(128)} %param.31) | copy-start | bytes 388
  101.2 26.0 %copy-start.9 = (s32[2,256]{1,0:T(2,128)S(1)}, s32[2,256]{1,0:T(2,128)}, u32[]{:S(2)}) copy-start(s32[2,256]{1,0:T(2,128)} %copy-done.8) | copy-start | bytes 6148
  101.2 26.2 %copy-start.31 = (f32[1,8]{1,0:T(1,128)S(1)}, f32[1,8]{1,0:T(1,128)}, u32[]{:S(2)}) copy-start(f32[1,8]{1,0:T(1,128)} %get-tuple-element.36) | copy-start | bytes 100
  101.2 26.2 %copy-start.3 = (bf16[512,128]{0,1:T(8,128)(2,1)S(1)}, bf16[512,128]{0,1:T(8,128)(2,1)}, u32[]{:S(2)}) copy-start(bf16[512,128]{0,1:T(8,128)(2,1)} %get-tuple-element.24) | copy-start | bytes 393220
  102.1 25.6 %copy-start.7 = (f32[512,8]{0,1:T(8,128)S(1)}, f32[512,8]{0,1:T(8,128)}, u32[]{:S(2)}) copy-start(f32[512,8]{0,1:T(8,128)} %copy-done.6) | copy-start | bytes 49156
  102.1 25.6 %copy-start.11 = (f32[2,8,256]{2,1,0:T(8,128)S(1)}, f32[2,8,256]{2,1,0:T(8,128)}, u32[]{:S(2)}) copy-start(f32[2,8,256]{2,1,0:T(8,128)} %copy-done.10) | copy-start | bytes 49156
  127.8 1.7 copy-start.1
  127.8 1.7 copy-start.35
  130.7 2.2 %copy-start.36 = (f32[512]{0:T(512)S(1)}, f32[512]{0:T(512)}, u32[]{:S(2)}) copy-start(f32[512]{0:T(512)} %param.28) | copy-start | bytes 6148
Sparse Core Ops, SparseCore 0:
  28.9 47.9 all-gather.5
  123.0 80.0 all-gather.3

commit v15 on v14

--- a/solution.py
+++ b/solution.py
@@ -30,7 +30,7 @@
     return jnp.sum((position[:, None] >= prompt_ends[None, :]).astype(jnp.int32), axis=1)
 
 
-def scatter_sum_kernel(count, rows, x_ref, q_ref, o_ref, qo_ref, recv, recv_q, send_sem, recv_sem):
+def scatter_sum_kernel(count, rows, x_ref, q_ref, o_ref, recv, recv_q, send_sem, recv_sem):
     me = lax.axis_index("tp")
     barrier = pltpu.get_barrier_semaphore()
     for d in range(1, count):
@@ -76,8 +76,8 @@
     for big, small in copies:
         big.wait_send()
         small.wait_send()
-    o_ref[...] = total
-    qo_ref[...] = side
+    mean_square = jnp.transpose(side)[:rows, 0:1] / INNER
+    o_ref[...] = (total * lax.rsqrt(mean_square + epsilon)).astype(o_ref.dtype)
 
 
 def scatter_sum(x, q, count):
@@ -85,12 +85,9 @@
     cols = x.shape[1]
     return pl.pallas_call(
         functools.partial(scatter_sum_kernel, count, rows),
-        out_shape=(
-            jax.ShapeDtypeStruct((rows, cols), jnp.float32),
-            jax.ShapeDtypeStruct((8, q.shape[1]), jnp.float32),
-        ),
+        out_shape=jax.ShapeDtypeStruct((rows, cols), jnp.bfloat16),
         in_specs=[pl.BlockSpec(memory_space=pltpu.VMEM)] * 2,
-        out_specs=(pl.BlockSpec(memory_space=pltpu.VMEM), pl.BlockSpec(memory_space=pltpu.VMEM)),
+        out_specs=pl.BlockSpec(memory_space=pltpu.VMEM),
         scratch_shapes=[
             pltpu.VMEM((count, rows, cols), x.dtype),
             pltpu.VMEM((count, 8, q.shape[1]), jnp.float32),
@@ -347,11 +344,7 @@
         [side, jnp.zeros((tp_count, 1, 128 - rows_out), jnp.float32)], axis=2
     )
     side = jnp.concatenate([side, jnp.zeros((tp_count, 7, 128), jnp.float32)], axis=1)
-    summed, side_sum = scatter_sum(
-        partial.astype(jnp.bfloat16), side.reshape(tp_count * 8, 128), tp_count
-    )
-    mean_square = side_sum[0, :rows_out] / INNER
-    mixed = (summed * lax.rsqrt(mean_square + epsilon)[:, None]).astype(jnp.bfloat16)
+    mixed = scatter_sum(partial.astype(jnp.bfloat16), side.reshape(tp_count * 8, 128), tp_count)
     return (mixed, request_states)
 
 

time: 213 us -> 214 us (level)
  waiting for transfers between devices: 75.6 us -> 78 us
  other arithmetic: 20.3 us -> 17.9 us
    all_gather x2, waiting for transfers between devices: 66 us -> 68.4 us  [gather_seq(): return lax.all_gather(x, SEQ, axis=0, tiled=False)]
    unnamed x87 -> x88, local copies, waits for them, and re-layouts: 3.06 us -> 4.73 us
  transfers between devices with their start and end apart: 4 -> 4, of which waited for: 3 -> 3; matrix products, arithmetic and copies ran while one was open for 11% -> 10% of each run, Pallas kernels for 19% -> 19%
where the time goes in v15:
time: 214 us
  waiting for transfers between devices  78 us (36%)
  Pallas kernels  59.3 us (28%)
  between operations  18.5 us (9%)
  other arithmetic  17.9 us (8%)
  local copies, waits for them, and re-layouts  14.4 us (7%)
  matrix products  14.1 us (7%)
  starting transfers between devices  11.5 us (5%)
    all_gather x2, waiting for transfers between devices, gather_seq(): return lax.all_gather(x, SEQ, axis=0, tiled=False)  68.4 us
    pallas_call x1, Pallas kernels, scatter_sum(): pl.pallas_call(functools.partial(scatter_sum_kernel, count, rows), out_sh...  40.5 us
    pallas_call x1, Pallas kernels, carry_in(): pl.pallas_call(functools.partial(scan_kernel, count, width), out_shape=ja...  18.9 us
    all_to_all x1, waiting for transfers between devices, on_device(): lax.all_to_all(packed, 'tp', split_axis=1, concat_axis=0, tiled=True)  9.56 us
    all_to_all x1, starting transfers between devices, on_device(): lax.all_to_all(packed, 'tp', split_axis=1, concat_axis=0, tiled=True)  8.16 us
    dot_general x1, matrix products, on_device(): jnp.dot(tokens, gathered[:, :width], preferred_element_type=jnp.float32)  5.91 us
    unnamed x88, local copies, waits for them, and re-layouts  4.73 us
    dot_general x1, matrix products, on_device(): lax.dot_general(scaled, gathered[:, width:], (((1,), (1,)), ((), ())), pr...  4.66 us
  transfers between devices with their start and end apart: 4, of which 3 were waited for; matrix products, arithmetic and copies ran while one was open for 10% of the time, Pallas kernels for 19%

profile of v15, /device:TPU:1, one launch (start us, length us, event | category | flops | bytes accessed | tf_op | source)
XLA Modules:
  0.0 213.8 jit_solution(204529384586610233)
XLA Ops:
  7.2 1.2 convert_element_type.78
  8.5 0.2 copy.118
  9.2 0.8 concatenate.43
  10.1 8.2 %all-to-all-start = ((bf16[16,8,1408]{2,0,1:T(8,128)(2,1)}), bf16[16,8,1408]{2,0,1:T(8,128)(2,1)S(1)}, u32[]{:S(2)}, u32[]{:S(2)}) async-start(bf16[16,8,1408]{2,0,1:T(8,128)(2,1)} %concatenate.43), calls=%async_computation | async-start | bytes 720896 | tf_op jit(solution)/shard_map/all_to_all | solution.py:221
  18.4 9.6 %all-to-all-done = bf16[16,8,1408]{2,0,1:T(8,128)(2,1)S(1)} async-done(((bf16[16,8,1408]{2,0,1:T(8,128)(2,1)}), bf16[16,8,1408]{2,0,1:T(8,128)(2,1)S(1)}, u32[]{:S(2)}, u32[]{:S(2)}) %all-to-all-start) | async-done | bytes 360480 | tf_op jit(solution)/shard_map/all_to_all | solution.py:221
  27.9 0.8 pad_maximum_fusion.1
  28.9 0.2 reduce-window.8
  29.2 0.2 fusion.41
  29.5 0.2 slice_reduce_fusion.5
  29.7 0.6 pad_maximum_fusion.2
  30.3 0.7 compare_reduce_fusion
  31.1 0.6 slice_reduce_fusion.4
  31.7 0.6 exponential_negate_fusion
  32.3 0.6 broadcast_compare_fusion.1
  32.9 0.7 slice_compare_fusion.2
  33.6 43.4 %all-gather.6.cloned.1.call-done = bf16[2048,1920]{1,0:T(8,128)(2,1)} async-done(((bf16[128,1920]{1,0:T(8,128)(2,1)}), bf16[2048,1920]{1,0:T(8,128)(2,1)}) %all-gather.6.cloned.1.call-update) | async-done | bytes 7864336 | tf_op jit(solution)/shard_map/all_gather | solution.py:25
  77.0 5.9 %fusion.48 = (bf16[512,1408]{0,1:T(8,128)(2,1)S(1)}, f32[512,1408]{0,1:T(8,128)S(1)}) fusion(bf16[512,2048]{1,0:T(8,128)(2,1)S(1)} %copy-done, bf16[2048,1920]{1,0:T(8,128)(2,1)} %all-gather.6.cloned.1.call-done), kind=kOutput, calls=%fused_computation.104 | convolution fusion | flops 2953510912 | bytes 12189696 | tf_op jit(solution)/shard_map/dot_general | solution.py:227
  82.9 1.0 slice.149
  83.9 3.2 %collective-permute-start = (bf16[3,768]{0,1:T(8,128)(2,1)}, bf16[3,768]{0,1:T(8,128)(2,1)}, u32[]{:S(2)}, u32[]{:S(2)}) collective-permute-start(bf16[3,768]{0,1:T(8,128)(2,1)} %slice.149), channel_id=1, source_target_pairs={{0,8},{8,16},{16,24},{24,32},{32,40},{40,48},{48,56},{56,64},{64,7... | collective-permute-start | bytes 13832 | tf_op jit(solution)/shard_map/ppermute | solution.py:21
  87.2 0.2 fusion.31
  87.4 0.7 copy-done.10
  88.3 0.6 copy-done.19
  88.9 0.6 copy-done.24
  89.5 0.5 slice_bitcast_fusion.1
  90.0 1.3 reduce_window.9
  91.4 1.4 select_multiply_fusion
  92.8 1.3 fusion.46
  94.2 3.4 %multiply_convert_fusion.3 = bf16[512,768]{0,1:T(8,128)(2,1)S(1)} fusion(bf16[512,768]{0,1:T(8,128)(2,1)S(1)} %slice.150, bf16[3,768]{0,1:T(8,128)(2,1)} %collective-permute-done, f32[768]{0:T(1024)S(1)} %copy-done.13, f32[768]{0:T(1024)S(1)} %copy-done.14, f32[768]{0:T(1024)S(1)} %copy-done.15, f32[768]{0:T(1024)S(1)} %copy-done.12, f32[768]{0:T(1024)S(1)} %copy-done.16, ...), kind=kLoop, calls=%fused_computation.14 | loop fusion | flops 11403264 | bytes 1594368 | tf_op jit(solution)/shard_map/convert_element_type | solution.py:251
  97.7 0.7 fusion.45
  98.6 0.7 copy-done.4
  99.5 1.0 fusion.20
  100.6 0.8 slice_bitcast_fusion.2
  101.5 0.7 select_maximum_fusion.mine_ref
  102.3 18.9 %shard_map.158 = f32[8,64,128]{2,1,0:T(8,128)} custom-call(f32[8,72,128]{2,1,0:T(8,128)} %select_maximum_fusion.mine_ref), custom_call_target="tpu_custom_call" | custom-call | tf_op jit(solution)/shard_map/pallas_call | solution.py:159
  121.2 1.9 fusion.25
  123.2 0.6 fusion.47
  127.8 0.3 fusion.33
  128.1 1.7 fusion.13
  129.8 0.4 fusion.15
  130.2 0.8 copy.93
  131.1 1.4 multiply_reduce_fusion
  132.6 0.6 pad_bitcast_fusion.q_ref
  133.3 4.7 %convolution_convert_fusion.x_ref = bf16[512,2048]{1,0:T(8,128)(2,1)} fusion(bf16[2048,1920]{1,0:T(8,128)(2,1)} %all-gather.6.cloned.1.call-done, f32[512]{0:T(512)S(1)} %copy-done.36, f32[512,512]{0,1:T(8,128)S(1)} %bitcast.73, bf16[512,1408]{0,1:T(8,128)(2,1)} %copy-done.2), kind=kOutput, calls=%fused_computation.4 | convolution fusion | flops 1076887552 | bytes 5769216 | tf_op jit(solution)/shard_map/dot_general | solution.py:338
  137.9 40.5 %shard_map.159 = bf16[64,2048]{1,0:T(8,128)(2,1)} custom-call(bf16[512,2048]{1,0:T(8,128)(2,1)} %convolution_convert_fusion.x_ref, f32[64,128]{1,0:T(8,128)} %pad_bitcast_fusion.q_ref), custom_call_target="tpu_custom_call" | custom-call | tf_op jit(solution)/shard_map/pallas_call | solution.py:86
  178.4 25.0 %all-gather.4.cloned.1.call-done = bf16[16,2,8,64,128]{4,3,2,1,0:T(8,128)(2,1)} async-done(((bf16[1,2,8,64,128]{4,3,2,1,0:T(8,128)(2,1)}), bf16[16,2,8,64,128]{4,3,2,1,0:T(8,128)(2,1)}) %all-gather.4.cloned.1.call-update) | async-done | bytes 4194320 | tf_op jit(solution)/shard_map/all_gather | solution.py:25
  203.4 1.0 constant_dynamic-slice_fusion.1
  204.4 0.8 maximum_convert_fusion
  205.2 1.7 copy.121
  (116 shorter events, 2.4 us)
Async XLA Ops:
  7.2 69.8 %copy-start = (bf16[512,2048]{1,0:T(8,128)(2,1)S(1)}, bf16[512,2048]{1,0:T(8,128)(2,1)}, u32[]{:S(2)}) copy-start(bf16[512,2048]{1,0:T(8,128)(2,1)} %param.17) | copy-start | bytes 6291460
  7.2 1.7 copy-start.17
  7.2 1.7 copy-start.21
  8.4 9.9 %copy-start.5 = (f32[512,128]{1,0:T(8,128)S(1)}, f32[512,128]{1,0:T(8,128)}, u32[]{:S(2)}) copy-start(f32[512,128]{1,0:T(8,128)} %param.29) | copy-start | bytes 786436
  9.2 19.7 %copy-start.37 = (s32[8]{0:T(128)S(1)}, s32[8]{0:T(128)}, u32[]{:S(2)}) copy-start(s32[8]{0:T(128)} %param.30) | copy-start | bytes 100
  9.2 20.5 %copy-start.22 = (f32[4,512]{1,0:T(4,128)S(1)}, f32[4,512]{1,0:T(4,128)}, u32[]{:S(2)}) copy-start(f32[4,512]{1,0:T(4,128)} %param.21) | copy-start | bytes 24580
  9.2 20.5 %copy-start.23 = (f32[4,256]{1,0:T(4,128)S(1)}, f32[4,256]{1,0:T(4,128)}, u32[]{:S(2)}) copy-start(f32[4,256]{1,0:T(4,128)} %param.23) | copy-start | bytes 12292
  9.2 20.5 %copy-start.28 = (f32[512]{0:T(512)S(1)}, f32[512]{0:T(512)}, u32[]{:S(2)}) copy-start(f32[512]{0:T(512)} %param.22) | copy-start | bytes 6148
  9.2 20.5 %copy-start.33 = (f32[256]{0:T(256)S(1)}, f32[256]{0:T(256)}, u32[]{:S(2)}) copy-start(f32[256]{0:T(256)} %param.24) | copy-start | bytes 3076
  9.2 22.5 %copy-start.38 = (f32[8]{0:T(128)S(1)}, f32[8]{0:T(128)}, u32[]{:S(2)}) copy-start(f32[8]{0:T(128)} %param.26) | copy-start | bytes 100
  10.1 17.9 %all-to-all-start = ((bf16[16,8,1408]{2,0,1:T(8,128)(2,1)}), bf16[16,8,1408]{2,0,1:T(8,128)(2,1)S(1)}, u32[]{:S(2)}, u32[]{:S(2)}) async-start(bf16[16,8,1408]{2,0,1:T(8,128)(2,1)} %concatenate.43), calls=%async_computation | async-start | bytes 720896 | tf_op jit(solution)/shard_map/all_to_all | solution.py:221
  18.2 58.7 %all-gather.6.cloned.1.call-start = ((), (), s32[]{:S(2)}) async-start(), calls=%async_computation.2 | async-start | bytes 8355840 | tf_op jit(solution)/shard_map/all_gather | solution.py:25
  28.8 174.6 %all-gather.4.cloned.1.call-start = ((), (), s32[]{:S(2)}) async-start(), calls=%async_computation.1 | async-start | bytes 4456448 | tf_op jit(solution)/shard_map/all_gather | solution.py:25
  29.2 53.7 %copy-start.8 = (s32[2,256]{1,0:T(2,128)}, s32[2,256]{1,0:T(2,128)S(1)}, u32[]{:S(2)}) copy-start(s32[2,256]{1,0:T(2,128)S(1)} %eq.62) | copy-start | bytes 6148
  76.9 10.2 %copy-start.34 = (f32[8]{0:T(128)S(1)}, f32[8]{0:T(128)}, u32[]{:S(2)}) copy-start(f32[8]{0:T(128)} %param.25) | copy-start | bytes 100
  77.0 10.3 %copy-start.40 = (f32[8]{0:T(128)S(1)}, f32[8]{0:T(128)}, u32[]{:S(2)}) copy-start(f32[8]{0:T(128)} %exponential_negate_fusion) | copy-start | bytes 100
  77.0 11.9 %copy-start.29 = (pred[2]{0:T(512)(128)(4,1)S(1)}, pred[2]{0:T(512)(128)(4,1)}, u32[]{:S(2)}) copy-start(pred[2]{0:T(512)(128)(4,1)} %compare_reduce_fusion) | copy-start | bytes 10
  82.9 14.8 %copy-start.2 = (bf16[512,1408]{0,1:T(8,128)(2,1)}, bf16[512,1408]{0,1:T(8,128)(2,1)S(1)}, u32[]{:S(2)}) copy-start(bf16[512,1408]{0,1:T(8,128)(2,1)S(1)} %get-tuple-element.36) | copy-start | bytes 4325380
  83.9 10.3 %collective-permute-start = (bf16[3,768]{0,1:T(8,128)(2,1)}, bf16[3,768]{0,1:T(8,128)(2,1)}, u32[]{:S(2)}, u32[]{:S(2)}) collective-permute-start(bf16[3,768]{0,1:T(8,128)(2,1)} %slice.149), channel_id=1, source_target_pairs={{0,8},{8,16},{16,24},{24,32},{32,40},{40,48},{48,56},{56,64},{64,7... | collective-permute-start | bytes 13832 | tf_op jit(solution)/shard_map/ppermute | solution.py:21
  87.2 4.1 %copy-start.6 = (f32[512,8]{0,1:T(8,128)}, f32[512,8]{0,1:T(8,128)S(1)}, u32[]{:S(2)}) copy-start(f32[512,8]{0,1:T(8,128)S(1)} %compare_select_fusion) | copy-start | bytes 49156
  87.4 0.7 copy-start.10
  88.3 0.6 copy-start.19
  88.9 0.6 copy-start.24
  91.3 2.8 %copy-start.12 = (f32[768]{0:T(1024)S(1)}, f32[768]{0:T(1024)}, u32[]{:S(2)}) copy-start(f32[768]{0:T(1024)} %get-tuple-element.14) | copy-start | bytes 9220
  91.3 2.9 %copy-start.13 = (f32[768]{0:T(1024)S(1)}, f32[768]{0:T(1024)}, u32[]{:S(2)}) copy-start(f32[768]{0:T(1024)} %get-tuple-element.15) | copy-start | bytes 9220
  91.3 2.9 %copy-start.14 = (f32[768]{0:T(1024)S(1)}, f32[768]{0:T(1024)}, u32[]{:S(2)}) copy-start(f32[768]{0:T(1024)} %get-tuple-element.16) | copy-start | bytes 9220
  91.3 2.9 %copy-start.15 = (f32[768]{0:T(1024)S(1)}, f32[768]{0:T(1024)}, u32[]{:S(2)}) copy-start(f32[768]{0:T(1024)} %get-tuple-element.17) | copy-start | bytes 9220
  91.3 2.9 %copy-start.16 = (f32[768]{0:T(1024)S(1)}, f32[768]{0:T(1024)}, u32[]{:S(2)}) copy-start(f32[768]{0:T(1024)} %pad_maximum_fusion.2) | copy-start | bytes 9220
  91.3 2.9 %copy-start.25 = (pred[512]{0:T(512)(128)(4,1)S(1)}, pred[512]{0:T(512)(128)(4,1)}, u32[]{:S(2)}) copy-start(pred[512]{0:T(512)(128)(4,1)} %get-tuple-element.27) | copy-start | bytes 1540
  91.3 2.9 %copy-start.26 = (pred[512]{0:T(512)(128)(4,1)S(1)}, pred[512]{0:T(512)(128)(4,1)}, u32[]{:S(2)}) copy-start(pred[512]{0:T(512)(128)(4,1)} %get-tuple-element.28) | copy-start | bytes 1540
  91.4 2.9 %copy-start.27 = (pred[512]{0:T(512)(128)(4,1)S(1)}, pred[512]{0:T(512)(128)(4,1)}, u32[]{:S(2)}) copy-start(pred[512]{0:T(512)(128)(4,1)} %get-tuple-element.29) | copy-start | bytes 1540
  98.4 0.9 copy-start.4
  98.4 1.1 copy-start.18
  98.5 2.1 copy-start.32
  99.5 2.0 copy-start.30
  100.6 20.6 %copy-start.20 = (f32[2,8]{1,0:T(2,128)S(1)}, f32[2,8]{1,0:T(2,128)}, u32[]{:S(2)}) copy-start(f32[2,8]{1,0:T(2,128)} %reduce_window.9) | copy-start | bytes 196
  101.4 21.7 %copy-start.39 = (s32[32]{0:T(128)S(1)}, s32[32]{0:T(128)}, u32[]{:S(2)}) copy-start(s32[32]{0:T(128)} %param.31) | copy-start | bytes 388
  101.4 26.2 %copy-start.9 = (s32[2,256]{1,0:T(2,128)S(1)}, s32[2,256]{1,0:T(2,128)}, u32[]{:S(2)}) copy-start(s32[2,256]{1,0:T(2,128)} %copy-done.8) | copy-start | bytes 6148
  101.4 26.4 %copy-start.31 = (f32[1,8]{1,0:T(1,128)S(1)}, f32[1,8]{1,0:T(1,128)}, u32[]{:S(2)}) copy-start(f32[1,8]{1,0:T(1,128)} %get-tuple-element.32) | copy-start | bytes 100
  101.4 26.4 %copy-start.3 = (bf16[512,128]{0,1:T(8,128)(2,1)S(1)}, bf16[512,128]{0,1:T(8,128)(2,1)}, u32[]{:S(2)}) copy-start(bf16[512,128]{0,1:T(8,128)(2,1)} %get-tuple-element.20) | copy-start | bytes 393220
  102.3 25.8 %copy-start.7 = (f32[512,8]{0,1:T(8,128)S(1)}, f32[512,8]{0,1:T(8,128)}, u32[]{:S(2)}) copy-start(f32[512,8]{0,1:T(8,128)} %copy-done.6) | copy-start | bytes 49156
  102.3 25.8 %copy-start.11 = (f32[2,8,256]{2,1,0:T(8,128)S(1)}, f32[2,8,256]{2,1,0:T(8,128)}, u32[]{:S(2)}) copy-start(f32[2,8,256]{2,1,0:T(8,128)} %copy-done.10) | copy-start | bytes 49156
  128.1 1.7 copy-start.1
  128.1 1.7 copy-start.35
  131.1 2.2 %copy-start.36 = (f32[512]{0:T(512)S(1)}, f32[512]{0:T(512)}, u32[]{:S(2)}) copy-start(f32[512]{0:T(512)} %param.28) | copy-start | bytes 6148
Sparse Core Ops, SparseCore 0:
  28.9 47.9 all-gather.5
  123.2 80.1 all-gather.3

commit v16 on v14

--- a/solution.py
+++ b/solution.py
@@ -26,7 +26,9 @@
 
 
 def segment_of(position, lengths):
-    prompt_ends = jnp.cumsum(lengths)
+    count = lengths.shape[0]
+    upto = jnp.arange(count)[:, None] >= jnp.arange(count)[None, :]
+    prompt_ends = jnp.sum(jnp.where(upto, lengths[None, :], 0), axis=1)
     return jnp.sum((position[:, None] >= prompt_ends[None, :]).astype(jnp.int32), axis=1)
 
 

time: 213 us -> 213 us (level)
  no operation moved by 1% of the time
where the time goes in v16:
time: 213 us; the launch traced here: 212 us
  waiting for transfers between devices  75.6 us (35%)
  Pallas kernels  59.3 us (28%)
  other arithmetic  20.3 us (10%)
  between operations  18.4 us (9%)
  matrix products  14.1 us (7%)
  local copies, waits for them, and re-layouts  12.6 us (6%)
  starting transfers between devices  11.5 us (5%)
    all_gather x2, waiting for transfers between devices, gather_seq(): return lax.all_gather(x, SEQ, axis=0, tiled=False)  66 us
    pallas_call x1, Pallas kernels, scatter_sum(): pl.pallas_call(functools.partial(scatter_sum_kernel, count, rows), out_sh...  40.4 us
    pallas_call x1, Pallas kernels, carry_in(): pl.pallas_call(functools.partial(scan_kernel, count, width), out_shape=ja...  18.9 us
    all_to_all x1, waiting for transfers between devices, on_device(): lax.all_to_all(packed, 'tp', split_axis=1, concat_axis=0, tiled=True)  9.56 us
    all_to_all x1, starting transfers between devices, on_device(): lax.all_to_all(packed, 'tp', split_axis=1, concat_axis=0, tiled=True)  8.16 us
    dot_general x1, matrix products, on_device(): jnp.dot(tokens, gathered[:, :width], preferred_element_type=jnp.float32)  5.91 us
    dot_general x1, matrix products, on_device(): lax.dot_general(scaled, gathered[:, width:], (((1,), (1,)), ((), ())), pr...  4.66 us
  transfers between devices with their start and end apart: 4, of which 3 were waited for; matrix products, arithmetic and copies ran while one was open for 11% of the time, Pallas kernels for 19%

profile of v16, /device:TPU:1, one launch (start us, length us, event | category | flops | bytes accessed | tf_op | source)
XLA Modules:
  0.0 211.8 jit_solution(5028144329796724476)
XLA Ops:
  7.2 1.2 convert_element_type.81
  8.5 0.2 copy.118
  9.2 0.8 concatenate.43
  10.1 8.2 %all-to-all-start = ((bf16[16,8,1408]{2,0,1:T(8,128)(2,1)}), bf16[16,8,1408]{2,0,1:T(8,128)(2,1)S(1)}, u32[]{:S(2)}, u32[]{:S(2)}) async-start(bf16[16,8,1408]{2,0,1:T(8,128)(2,1)} %concatenate.43), calls=%async_computation | async-start | bytes 720896 | tf_op jit(solution)/shard_map/all_to_all | solution.py:226
  18.4 9.6 %all-to-all-done = bf16[16,8,1408]{2,0,1:T(8,128)(2,1)S(1)} async-done(((bf16[16,8,1408]{2,0,1:T(8,128)(2,1)}), bf16[16,8,1408]{2,0,1:T(8,128)(2,1)S(1)}, u32[]{:S(2)}, u32[]{:S(2)}) %all-to-all-start) | async-done | bytes 360480 | tf_op jit(solution)/shard_map/all_to_all | solution.py:226
  27.9 0.8 pad_maximum_fusion.1
  29.2 0.2 fusion.41
  29.4 0.2 slice_reduce_fusion.5
  29.7 0.6 pad_maximum_fusion.2
  30.3 0.7 compare_reduce_fusion
  31.0 0.6 slice_reduce_fusion.4
  31.6 0.6 exponential_negate_fusion
  32.2 0.7 broadcast_compare_fusion.1
  32.8 0.6 slice_compare_fusion.2
  33.5 43.5 %all-gather.6.cloned.1.call-done = bf16[2048,1920]{1,0:T(8,128)(2,1)} async-done(((bf16[128,1920]{1,0:T(8,128)(2,1)}), bf16[2048,1920]{1,0:T(8,128)(2,1)}) %all-gather.6.cloned.1.call-update) | async-done | bytes 7864336 | tf_op jit(solution)/shard_map/all_gather | solution.py:25
  77.0 5.9 %fusion.48 = (bf16[512,1408]{0,1:T(8,128)(2,1)S(1)}, f32[512,1408]{0,1:T(8,128)S(1)}) fusion(bf16[512,2048]{1,0:T(8,128)(2,1)S(1)} %copy-done, bf16[2048,1920]{1,0:T(8,128)(2,1)} %all-gather.6.cloned.1.call-done), kind=kOutput, calls=%fused_computation.108 | convolution fusion | flops 2953510912 | bytes 12189696 | tf_op jit(solution)/shard_map/dot_general | solution.py:232
  82.9 1.0 slice.153
  83.9 3.2 %collective-permute-start = (bf16[3,768]{0,1:T(8,128)(2,1)}, bf16[3,768]{0,1:T(8,128)(2,1)}, u32[]{:S(2)}, u32[]{:S(2)}) collective-permute-start(bf16[3,768]{0,1:T(8,128)(2,1)} %slice.153), channel_id=1, source_target_pairs={{0,8},{8,16},{16,24},{24,32},{32,40},{40,48},{48,56},{56,64},{64,7... | collective-permute-start | bytes 13832 | tf_op jit(solution)/shard_map/ppermute | solution.py:21
  87.2 0.2 fusion.31
  87.4 0.7 copy-done.10
  88.3 0.6 copy-done.19
  88.9 0.6 copy-done.24
  89.5 0.5 slice_bitcast_fusion.1
  90.0 1.2 reduce_window.9
  91.3 1.4 select_multiply_fusion
  92.7 1.2 fusion.46
  94.1 3.4 %multiply_convert_fusion.3 = bf16[512,768]{0,1:T(8,128)(2,1)S(1)} fusion(bf16[512,768]{0,1:T(8,128)(2,1)S(1)} %slice.154, bf16[3,768]{0,1:T(8,128)(2,1)} %collective-permute-done, f32[768]{0:T(1024)S(1)} %copy-done.13, f32[768]{0:T(1024)S(1)} %copy-done.14, f32[768]{0:T(1024)S(1)} %copy-done.15, f32[768]{0:T(1024)S(1)} %copy-done.12, f32[768]{0:T(1024)S(1)} %copy-done.16, ...), kind=kLoop, calls=%fused_computation.14 | loop fusion | flops 11403264 | bytes 1594368 | tf_op jit(solution)/shard_map/convert_element_type | solution.py:256
  97.5 0.7 fusion.45
  98.4 0.7 copy-done.4
  99.3 1.0 fusion.20
  100.4 0.8 slice_bitcast_fusion.2
  101.4 0.7 select_maximum_fusion.mine_ref
  102.1 18.9 %shard_map.158 = f32[8,64,128]{2,1,0:T(8,128)} custom-call(f32[8,72,128]{2,1,0:T(8,128)} %select_maximum_fusion.mine_ref), custom_call_target="tpu_custom_call" | custom-call | tf_op jit(solution)/shard_map/pallas_call | solution.py:164
  121.0 1.9 fusion.25
  123.0 0.6 fusion.47
  127.5 0.3 fusion.33
  127.8 1.7 fusion.13
  129.5 0.4 fusion.15
  129.9 0.8 copy.93
  130.8 1.4 multiply_reduce_fusion
  132.3 0.6 pad_bitcast_fusion.q_ref
  132.9 4.7 %convolution_convert_fusion.x_ref = bf16[512,2048]{1,0:T(8,128)(2,1)} fusion(bf16[2048,1920]{1,0:T(8,128)(2,1)} %all-gather.6.cloned.1.call-done, f32[512]{0:T(512)S(1)} %copy-done.36, f32[512,512]{0,1:T(8,128)S(1)} %bitcast.73, bf16[512,1408]{0,1:T(8,128)(2,1)} %copy-done.2), kind=kOutput, calls=%fused_computation.4 | convolution fusion | flops 1076887552 | bytes 5769216 | tf_op jit(solution)/shard_map/dot_general | solution.py:343
  137.6 40.4 %shard_map.159 = (f32[64,2048]{1,0:T(8,128)}, f32[8,128]{1,0:T(8,128)}) custom-call(bf16[512,2048]{1,0:T(8,128)(2,1)} %convolution_convert_fusion.x_ref, f32[64,128]{1,0:T(8,128)} %pad_bitcast_fusion.q_ref), custom_call_target="tpu_custom_call" | custom-call | tf_op jit(solution)/shard_map/pallas_call | solution.py:88
  178.0 0.7 rsqrt_bitcast_fusion
  178.7 1.8 multiply_convert_fusion.9
  180.5 22.6 %all-gather.4.cloned.1.call-done = bf16[16,2,8,64,128]{4,3,2,1,0:T(8,128)(2,1)} async-done(((bf16[1,2,8,64,128]{4,3,2,1,0:T(8,128)(2,1)}), bf16[16,2,8,64,128]{4,3,2,1,0:T(8,128)(2,1)}) %all-gather.4.cloned.1.call-update) | async-done | bytes 4194320 | tf_op jit(solution)/shard_map/all_gather | solution.py:25
  203.1 1.0 constant_dynamic-slice_fusion.1
  204.1 0.8 maximum_convert_fusion
  (117 shorter events, 2.6 us)
Async XLA Ops:
  7.2 69.8 %copy-start = (bf16[512,2048]{1,0:T(8,128)(2,1)S(1)}, bf16[512,2048]{1,0:T(8,128)(2,1)}, u32[]{:S(2)}) copy-start(bf16[512,2048]{1,0:T(8,128)(2,1)} %param.17) | copy-start | bytes 6291460
  7.2 1.7 copy-start.17
  7.2 1.7 copy-start.21
  8.4 9.9 %copy-start.5 = (f32[512,128]{1,0:T(8,128)S(1)}, f32[512,128]{1,0:T(8,128)}, u32[]{:S(2)}) copy-start(f32[512,128]{1,0:T(8,128)} %param.29) | copy-start | bytes 786436
  9.2 19.7 %copy-start.37 = (s32[8]{0:T(128)S(1)}, s32[8]{0:T(128)}, u32[]{:S(2)}) copy-start(s32[8]{0:T(128)} %param.30) | copy-start | bytes 100
  9.2 20.5 %copy-start.22 = (f32[4,512]{1,0:T(4,128)S(1)}, f32[4,512]{1,0:T(4,128)}, u32[]{:S(2)}) copy-start(f32[4,512]{1,0:T(4,128)} %param.21) | copy-start | bytes 24580
  9.2 20.5 %copy-start.23 = (f32[4,256]{1,0:T(4,128)S(1)}, f32[4,256]{1,0:T(4,128)}, u32[]{:S(2)}) copy-start(f32[4,256]{1,0:T(4,128)} %param.23) | copy-start | bytes 12292
  9.2 20.5 %copy-start.28 = (f32[512]{0:T(512)S(1)}, f32[512]{0:T(512)}, u32[]{:S(2)}) copy-start(f32[512]{0:T(512)} %param.22) | copy-start | bytes 6148
  9.2 20.5 %copy-start.33 = (f32[256]{0:T(256)S(1)}, f32[256]{0:T(256)}, u32[]{:S(2)}) copy-start(f32[256]{0:T(256)} %param.24) | copy-start | bytes 3076
  9.2 22.4 %copy-start.38 = (f32[8]{0:T(128)S(1)}, f32[8]{0:T(128)}, u32[]{:S(2)}) copy-start(f32[8]{0:T(128)} %param.26) | copy-start | bytes 100
  10.1 17.9 %all-to-all-start = ((bf16[16,8,1408]{2,0,1:T(8,128)(2,1)}), bf16[16,8,1408]{2,0,1:T(8,128)(2,1)S(1)}, u32[]{:S(2)}, u32[]{:S(2)}) async-start(bf16[16,8,1408]{2,0,1:T(8,128)(2,1)} %concatenate.43), calls=%async_computation | async-start | bytes 720896 | tf_op jit(solution)/shard_map/all_to_all | solution.py:226
  18.2 58.7 %all-gather.6.cloned.1.call-start = ((), (), s32[]{:S(2)}) async-start(), calls=%async_computation.2 | async-start | bytes 8355840 | tf_op jit(solution)/shard_map/all_gather | solution.py:25
  28.8 174.3 %all-gather.4.cloned.1.call-start = ((), (), s32[]{:S(2)}) async-start(), calls=%async_computation.1 | async-start | bytes 4456448 | tf_op jit(solution)/shard_map/all_gather | solution.py:25
  29.2 53.7 %copy-start.8 = (s32[2,256]{1,0:T(2,128)}, s32[2,256]{1,0:T(2,128)S(1)}, u32[]{:S(2)}) copy-start(s32[2,256]{1,0:T(2,128)S(1)} %eq.62) | copy-start | bytes 6148
  76.9 10.2 %copy-start.34 = (f32[8]{0:T(128)S(1)}, f32[8]{0:T(128)}, u32[]{:S(2)}) copy-start(f32[8]{0:T(128)} %param.25) | copy-start | bytes 100
  77.0 10.3 %copy-start.40 = (f32[8]{0:T(128)S(1)}, f32[8]{0:T(128)}, u32[]{:S(2)}) copy-start(f32[8]{0:T(128)} %exponential_negate_fusion) | copy-start | bytes 100
  77.0 11.9 %copy-start.29 = (pred[2]{0:T(512)(128)(4,1)S(1)}, pred[2]{0:T(512)(128)(4,1)}, u32[]{:S(2)}) copy-start(pred[2]{0:T(512)(128)(4,1)} %compare_reduce_fusion) | copy-start | bytes 10
  82.9 14.6 %copy-start.2 = (bf16[512,1408]{0,1:T(8,128)(2,1)}, bf16[512,1408]{0,1:T(8,128)(2,1)S(1)}, u32[]{:S(2)}) copy-start(bf16[512,1408]{0,1:T(8,128)(2,1)S(1)} %get-tuple-element.40) | copy-start | bytes 4325380
  83.9 10.2 %collective-permute-start = (bf16[3,768]{0,1:T(8,128)(2,1)}, bf16[3,768]{0,1:T(8,128)(2,1)}, u32[]{:S(2)}, u32[]{:S(2)}) collective-permute-start(bf16[3,768]{0,1:T(8,128)(2,1)} %slice.153), channel_id=1, source_target_pairs={{0,8},{8,16},{16,24},{24,32},{32,40},{40,48},{48,56},{56,64},{64,7... | collective-permute-start | bytes 13832 | tf_op jit(solution)/shard_map/ppermute | solution.py:21
  87.2 4.1 %copy-start.6 = (f32[512,8]{0,1:T(8,128)}, f32[512,8]{0,1:T(8,128)S(1)}, u32[]{:S(2)}) copy-start(f32[512,8]{0,1:T(8,128)S(1)} %compare_select_fusion) | copy-start | bytes 49156
  87.4 0.7 copy-start.10
  88.3 0.6 copy-start.19
  88.9 0.6 copy-start.24
  91.2 2.8 %copy-start.12 = (f32[768]{0:T(1024)S(1)}, f32[768]{0:T(1024)}, u32[]{:S(2)}) copy-start(f32[768]{0:T(1024)} %get-tuple-element.18) | copy-start | bytes 9220
  91.2 2.8 %copy-start.13 = (f32[768]{0:T(1024)S(1)}, f32[768]{0:T(1024)}, u32[]{:S(2)}) copy-start(f32[768]{0:T(1024)} %get-tuple-element.19) | copy-start | bytes 9220
  91.2 2.8 %copy-start.14 = (f32[768]{0:T(1024)S(1)}, f32[768]{0:T(1024)}, u32[]{:S(2)}) copy-start(f32[768]{0:T(1024)} %get-tuple-element.20) | copy-start | bytes 9220
  91.2 2.8 %copy-start.15 = (f32[768]{0:T(1024)S(1)}, f32[768]{0:T(1024)}, u32[]{:S(2)}) copy-start(f32[768]{0:T(1024)} %get-tuple-element.21) | copy-start | bytes 9220
  91.2 2.8 %copy-start.16 = (f32[768]{0:T(1024)S(1)}, f32[768]{0:T(1024)}, u32[]{:S(2)}) copy-start(f32[768]{0:T(1024)} %pad_maximum_fusion.2) | copy-start | bytes 9220
  91.2 2.8 %copy-start.25 = (pred[512]{0:T(512)(128)(4,1)S(1)}, pred[512]{0:T(512)(128)(4,1)}, u32[]{:S(2)}) copy-start(pred[512]{0:T(512)(128)(4,1)} %get-tuple-element.31) | copy-start | bytes 1540
  91.3 2.8 %copy-start.26 = (pred[512]{0:T(512)(128)(4,1)S(1)}, pred[512]{0:T(512)(128)(4,1)}, u32[]{:S(2)}) copy-start(pred[512]{0:T(512)(128)(4,1)} %get-tuple-element.32) | copy-start | bytes 1540
  91.3 2.8 %copy-start.27 = (pred[512]{0:T(512)(128)(4,1)S(1)}, pred[512]{0:T(512)(128)(4,1)}, u32[]{:S(2)}) copy-start(pred[512]{0:T(512)(128)(4,1)} %get-tuple-element.33) | copy-start | bytes 1540
  98.2 0.9 copy-start.4
  98.2 1.1 copy-start.18
  98.3 2.1 copy-start.32
  99.3 2.0 copy-start.30
  100.4 20.6 %copy-start.20 = (f32[2,8]{1,0:T(2,128)S(1)}, f32[2,8]{1,0:T(2,128)}, u32[]{:S(2)}) copy-start(f32[2,8]{1,0:T(2,128)} %reduce_window.9) | copy-start | bytes 196
  101.2 21.7 %copy-start.39 = (s32[32]{0:T(128)S(1)}, s32[32]{0:T(128)}, u32[]{:S(2)}) copy-start(s32[32]{0:T(128)} %param.31) | copy-start | bytes 388
  101.2 26.0 %copy-start.9 = (s32[2,256]{1,0:T(2,128)S(1)}, s32[2,256]{1,0:T(2,128)}, u32[]{:S(2)}) copy-start(s32[2,256]{1,0:T(2,128)} %copy-done.8) | copy-start | bytes 6148
  101.2 26.2 %copy-start.31 = (f32[1,8]{1,0:T(1,128)S(1)}, f32[1,8]{1,0:T(1,128)}, u32[]{:S(2)}) copy-start(f32[1,8]{1,0:T(1,128)} %get-tuple-element.36) | copy-start | bytes 100
  101.2 26.2 %copy-start.3 = (bf16[512,128]{0,1:T(8,128)(2,1)S(1)}, bf16[512,128]{0,1:T(8,128)(2,1)}, u32[]{:S(2)}) copy-start(bf16[512,128]{0,1:T(8,128)(2,1)} %get-tuple-element.24) | copy-start | bytes 393220
  102.1 25.6 %copy-start.7 = (f32[512,8]{0,1:T(8,128)S(1)}, f32[512,8]{0,1:T(8,128)}, u32[]{:S(2)}) copy-start(f32[512,8]{0,1:T(8,128)} %copy-done.6) | copy-start | bytes 49156
  102.1 25.6 %copy-start.11 = (f32[2,8,256]{2,1,0:T(8,128)S(1)}, f32[2,8,256]{2,1,0:T(8,128)}, u32[]{:S(2)}) copy-start(f32[2,8,256]{2,1,0:T(8,128)} %copy-done.10) | copy-start | bytes 49156
  127.8 1.7 copy-start.1
  127.8 1.7 copy-start.35
  130.7 2.2 %copy-start.36 = (f32[512]{0:T(512)S(1)}, f32[512]{0:T(512)}, u32[]{:S(2)}) copy-start(f32[512]{0:T(512)} %param.28) | copy-start | bytes 6148
Sparse Core Ops, SparseCore 0:
  28.9 47.9 all-gather.5
  123.0 80.0 all-gather.3

commit v17 on v16

--- a/solution.py
+++ b/solution.py
@@ -308,7 +308,10 @@
         ends.append(pass_gate[c][:, None, None] * ends[-1] + contrib[c])
     local_end = jnp.stack(ends)
     local_in = jnp.concatenate([jnp.zeros_like(local_end[:1]), local_end[:-1]], axis=0)
-    through_group = jnp.cumprod(pass_gate, axis=0)
+    products = [pass_gate[0]]
+    for c in range(1, groups_dev):
+        products.append(products[-1] * pass_gate[c])
+    through_group = jnp.stack(products)
     before_group = jnp.concatenate(
         [jnp.ones((1, heads_local), jnp.float32), through_group[:-1]], axis=0
     )

time: 213 us -> 206 us (0.967)
  other arithmetic: 20.3 us -> 13.6 us
  local copies, waits for them, and re-layouts: 12.6 us -> 6.14 us
  waiting for transfers between devices: 75.6 us -> 81.4 us
    all_gather x2, waiting for transfers between devices: 66 us -> 69.4 us  [gather_seq(): return lax.all_gather(x, SEQ, axis=0, tiled=False)]
    unnamed x87 -> x37, local copies, waits for them, and re-layouts: 3.06 us -> 0.44 us
    ppermute x1, waiting for transfers between devices: 0.01 us -> 2.43 us  [from_behind(): return lax.ppermute(x, SEQ, pairs)]
  transfers between devices with their start and end apart: 4 -> 4, of which waited for: 3 -> 4; matrix products, arithmetic and copies ran while one was open for 11% -> 7% of each run, Pallas kernels for 19% -> 20%
where the time goes in v17:
time: 206 us
  waiting for transfers between devices  81.4 us (40%)
  Pallas kernels  60.7 us (29%)
  between operations  18.2 us (9%)
  matrix products  14.1 us (7%)
  other arithmetic  13.6 us (7%)
  starting transfers between devices  11.5 us (6%)
  local copies, waits for them, and re-layouts  6.14 us (3%)
    all_gather x2, waiting for transfers between devices, gather_seq(): return lax.all_gather(x, SEQ, axis=0, tiled=False)  69.4 us
    pallas_call x1, Pallas kernels, scatter_sum(): pl.pallas_call(functools.partial(scatter_sum_kernel, count, rows), out_sh...  40.5 us
    pallas_call x1, Pallas kernels, carry_in(): pl.pallas_call(functools.partial(scan_kernel, count, width), out_shape=ja...  20.2 us
    all_to_all x1, waiting for transfers between devices, on_device(): lax.all_to_all(packed, 'tp', split_axis=1, concat_axis=0, tiled=True)  9.56 us
    all_to_all x1, starting transfers between devices, on_device(): lax.all_to_all(packed, 'tp', split_axis=1, concat_axis=0, tiled=True)  8.16 us
    dot_general x1, matrix products, on_device(): jnp.dot(tokens, gathered[:, :width], preferred_element_type=jnp.float32)  5.9 us
    dot_general x1, matrix products, on_device(): lax.dot_general(scaled, gathered[:, width:], (((1,), (1,)), ((), ())), pr...  4.7 us
  transfers between devices with their start and end apart: 4, of which 4 were waited for; matrix products, arithmetic and copies ran while one was open for 7% of the time, Pallas kernels for 20%

profile of v17, /device:TPU:1, one launch (start us, length us, event | category | flops | bytes accessed | tf_op | source)
XLA Modules:
  0.0 205.8 jit_solution(16965021278595673910)
XLA Ops:
  7.2 1.2 convert_element_type.81
  8.5 0.2 copy.118
  8.7 0.2 reshape.225
  8.9 0.1 copy.81
  9.0 0.1 copy.82
  9.2 0.8 concatenate.43
  10.1 8.2 %all-to-all-start = ((bf16[16,8,1408]{2,0,1:T(8,128)(2,1)}), bf16[16,8,1408]{2,0,1:T(8,128)(2,1)S(1)}, u32[]{:S(2)}, u32[]{:S(2)}) async-start(bf16[16,8,1408]{2,0,1:T(8,128)(2,1)} %concatenate.43), calls=%async_computation | async-start | bytes 720896 | tf_op jit(solution)/shard_map/all_to_all | solution.py:226
  18.3 0.1 copy.83
  18.4 9.6 %all-to-all-done = bf16[16,8,1408]{2,0,1:T(8,128)(2,1)S(1)} async-done(((bf16[16,8,1408]{2,0,1:T(8,128)(2,1)}), bf16[16,8,1408]{2,0,1:T(8,128)(2,1)S(1)}, u32[]{:S(2)}, u32[]{:S(2)}) %all-to-all-start) | async-done | bytes 360480 | tf_op jit(solution)/shard_map/all_to_all | solution.py:226
  27.9 0.8 pad_maximum_fusion.1
  28.9 0.1 select_reduce_fusion
  29.2 0.2 fusion.41
  29.3 0.1 copy.88
  29.4 0.2 slice_reduce_fusion.5
  29.7 0.2 compare_reduce_fusion
  30.1 46.8 %all-gather.6.cloned.1.call-done = bf16[2048,1920]{1,0:T(8,128)(2,1)} async-done(((bf16[128,1920]{1,0:T(8,128)(2,1)}), bf16[2048,1920]{1,0:T(8,128)(2,1)}) %all-gather.6.cloned.1.call-update) | async-done | bytes 7864336 | tf_op jit(solution)/shard_map/all_gather | solution.py:25
  77.0 5.9 %fusion.47 = (bf16[512,1408]{0,1:T(8,128)(2,1)S(1)}, f32[512,1408]{0,1:T(8,128)S(1)}) fusion(bf16[512,2048]{1,0:T(8,128)(2,1)S(1)} %copy-done, bf16[2048,1920]{1,0:T(8,128)(2,1)} %all-gather.6.cloned.1.call-done), kind=kOutput, calls=%fused_computation.109 | convolution fusion | flops 2953510912 | bytes 12189696 | tf_op jit(solution)/shard_map/dot_general | solution.py:232
  82.9 0.1 compare_select_fusion
  83.0 0.2 fusion.31
  83.2 0.2 slice_reduce_fusion
  83.5 0.1 slice.150
  83.6 3.3 %collective-permute-start = (bf16[3,768]{0,1:T(8,128)(2,1)S(1)}, bf16[3,768]{0,1:T(8,128)(2,1)S(1)}, u32[]{:S(2)}, u32[]{:S(2)}) collective-permute-start(bf16[3,768]{0,1:T(8,128)(2,1)S(1)} %slice.150), channel_id=1, source_target_pairs={{0,8},{8,16},{16,24},{24,32},{32,40},{40,48},{48,56},{56,64},{64,7... | collective-permute-start | bytes 13832 | tf_op jit(solution)/shard_map/ppermute | solution.py:21
  87.0 2.4 %collective-permute-done = bf16[3,768]{0,1:T(8,128)(2,1)S(1)} collective-permute-done((bf16[3,768]{0,1:T(8,128)(2,1)S(1)}, bf16[3,768]{0,1:T(8,128)(2,1)S(1)}, u32[]{:S(2)}, u32[]{:S(2)}) %collective-permute-start) | collective-permute-done | bytes 4640 | tf_op jit(solution)/shard_map/ppermute | solution.py:21
  89.5 2.1 %multiply_convert_fusion.3 = bf16[512,768]{0,1:T(8,128)(2,1)S(1)} fusion(bf16[512,768]{0,1:T(8,128)(2,1)S(1)} %slice.151, bf16[3,768]{0,1:T(8,128)(2,1)S(1)} %collective-permute-done, f32[768]{0:T(1024)S(1)} %get-tuple-element.19, f32[768]{0:T(1024)S(1)} %get-tuple-element.20, f32[768]{0:T(1024)S(1)} %get-tuple-element.21, f32[768]{0:T(1024)S(1)} %get-tuple-element.18, ...), kind=kLoop, calls=%fused_computation.14 | loop fusion | flops 11403264 | bytes 1594368 | tf_op jit(solution)/shard_map/convert_element_type | solution.py:256
  91.7 0.1 reshape.228
  91.8 0.1 copy.89
  92.0 1.0 fusion.20
  93.0 0.8 slice_bitcast_fusion.1
  93.8 0.1 bitcast_add_fusion
  94.0 0.7 select_maximum_fusion.mine_ref
  94.7 20.2 %shard_map.158 = f32[8,64,128]{2,1,0:T(8,128)} custom-call(f32[8,72,128]{2,1,0:T(8,128)} %select_maximum_fusion.mine_ref), custom_call_target="tpu_custom_call" | custom-call | tf_op jit(solution)/shard_map/pallas_call | solution.py:164
  114.9 1.9 fusion.25
  116.9 0.6 fusion.46
  121.1 0.2 compare_and_fusion
  121.3 0.3 fusion.33
  121.6 1.7 fusion.13
  123.3 0.4 fusion.15
  123.7 0.8 copy.93
  124.6 1.4 multiply_reduce_fusion
  126.0 0.1 reshape.233
  126.1 0.6 pad_bitcast_fusion.q_ref
  126.8 4.7 %convolution_convert_fusion.x_ref = bf16[512,2048]{1,0:T(8,128)(2,1)} fusion(bf16[2048,1920]{1,0:T(8,128)(2,1)} %all-gather.6.cloned.1.call-done, f32[512]{0:T(512)S(1)} %copy-done.12, f32[512,512]{0,1:T(8,128)S(1)} %bitcast.75, bf16[512,1408]{0,1:T(8,128)(2,1)} %copy-done.2), kind=kOutput, calls=%fused_computation.4 | convolution fusion | flops 1076887552 | bytes 5769216 | tf_op jit(solution)/shard_map/dot_general | solution.py:346
  131.5 40.5 %shard_map.159 = (f32[64,2048]{1,0:T(8,128)}, f32[8,128]{1,0:T(8,128)}) custom-call(bf16[512,2048]{1,0:T(8,128)(2,1)} %convolution_convert_fusion.x_ref, f32[64,128]{1,0:T(8,128)} %pad_bitcast_fusion.q_ref), custom_call_target="tpu_custom_call" | custom-call | tf_op jit(solution)/shard_map/pallas_call | solution.py:88
  172.0 0.7 rsqrt_bitcast_fusion
  172.7 1.8 multiply_convert_fusion.9
  174.5 22.6 %all-gather.4.cloned.1.call-done = bf16[16,2,8,64,128]{4,3,2,1,0:T(8,128)(2,1)} async-done(((bf16[1,2,8,64,128]{4,3,2,1,0:T(8,128)(2,1)}), bf16[16,2,8,64,128]{4,3,2,1,0:T(8,128)(2,1)}) %all-gather.4.cloned.1.call-update) | async-done | bytes 4194320 | tf_op jit(solution)/shard_map/all_gather | solution.py:25
  197.1 1.0 constant_dynamic-slice_fusion.1
  198.1 0.8 maximum_convert_fusion
  (66 shorter events, 1.3 us)
Async XLA Ops:
  7.2 69.8 %copy-start = (bf16[512,2048]{1,0:T(8,128)(2,1)S(1)}, bf16[512,2048]{1,0:T(8,128)(2,1)}, u32[]{:S(2)}) copy-start(bf16[512,2048]{1,0:T(8,128)(2,1)} %param.17) | copy-start | bytes 6291460
  7.2 1.7 copy-start.4
  7.2 1.7 copy-start.5
  8.4 9.9 %copy-start.3 = (f32[512,128]{1,0:T(8,128)S(1)}, f32[512,128]{1,0:T(8,128)}, u32[]{:S(2)}) copy-start(f32[512,128]{1,0:T(8,128)} %param.29) | copy-start | bytes 786436
  9.2 19.7 %copy-start.13 = (s32[8]{0:T(128)S(1)}, s32[8]{0:T(128)}, u32[]{:S(2)}) copy-start(s32[8]{0:T(128)} %param.30) | copy-start | bytes 100
  9.2 20.5 %copy-start.6 = (f32[4,512]{1,0:T(4,128)S(1)}, f32[4,512]{1,0:T(4,128)}, u32[]{:S(2)}) copy-start(f32[4,512]{1,0:T(4,128)} %param.21) | copy-start | bytes 24580
  9.2 20.5 %copy-start.7 = (f32[4,256]{1,0:T(4,128)S(1)}, f32[4,256]{1,0:T(4,128)}, u32[]{:S(2)}) copy-start(f32[4,256]{1,0:T(4,128)} %param.23) | copy-start | bytes 12292
  9.2 20.5 %copy-start.8 = (f32[512]{0:T(512)S(1)}, f32[512]{0:T(512)}, u32[]{:S(2)}) copy-start(f32[512]{0:T(512)} %param.22) | copy-start | bytes 6148
  9.2 20.5 %copy-start.9 = (f32[256]{0:T(256)S(1)}, f32[256]{0:T(256)}, u32[]{:S(2)}) copy-start(f32[256]{0:T(256)} %param.24) | copy-start | bytes 3076
  9.2 20.7 %copy-start.14 = (f32[8]{0:T(128)S(1)}, f32[8]{0:T(128)}, u32[]{:S(2)}) copy-start(f32[8]{0:T(128)} %param.26) | copy-start | bytes 100
  10.1 17.9 %all-to-all-start = ((bf16[16,8,1408]{2,0,1:T(8,128)(2,1)}), bf16[16,8,1408]{2,0,1:T(8,128)(2,1)S(1)}, u32[]{:S(2)}, u32[]{:S(2)}) async-start(bf16[16,8,1408]{2,0,1:T(8,128)(2,1)} %concatenate.43), calls=%async_computation | async-start | bytes 720896 | tf_op jit(solution)/shard_map/all_to_all | solution.py:226
  18.2 58.7 %all-gather.6.cloned.1.call-start = ((), (), s32[]{:S(2)}) async-start(), calls=%async_computation.2 | async-start | bytes 8355840 | tf_op jit(solution)/shard_map/all_gather | solution.py:25
  28.8 168.3 %all-gather.4.cloned.1.call-start = ((), (), s32[]{:S(2)}) async-start(), calls=%async_computation.1 | async-start | bytes 4456448 | tf_op jit(solution)/shard_map/all_gather | solution.py:25
  30.1 52.8 %copy-start.10 = (f32[8]{0:T(128)S(1)}, f32[8]{0:T(128)}, u32[]{:S(2)}) copy-start(f32[8]{0:T(128)} %param.25) | copy-start | bytes 100
  82.9 8.7 %copy-start.2 = (bf16[512,1408]{0,1:T(8,128)(2,1)}, bf16[512,1408]{0,1:T(8,128)(2,1)S(1)}, u32[]{:S(2)}) copy-start(bf16[512,1408]{0,1:T(8,128)(2,1)S(1)} %get-tuple-element.43) | copy-start | bytes 4325380
  83.6 5.9 %collective-permute-start = (bf16[3,768]{0,1:T(8,128)(2,1)S(1)}, bf16[3,768]{0,1:T(8,128)(2,1)S(1)}, u32[]{:S(2)}, u32[]{:S(2)}) collective-permute-start(bf16[3,768]{0,1:T(8,128)(2,1)S(1)} %slice.150), channel_id=1, source_target_pairs={{0,8},{8,16},{16,24},{24,32},{32,40},{40,48},{48,56},{56,64},{64,7... | collective-permute-start | bytes 13832 | tf_op jit(solution)/shard_map/ppermute | solution.py:21
  93.8 23.0 %copy-start.15 = (s32[32]{0:T(128)S(1)}, s32[32]{0:T(128)}, u32[]{:S(2)}) copy-start(s32[32]{0:T(128)} %param.31) | copy-start | bytes 388
  121.6 1.7 copy-start.1
  121.6 1.7 copy-start.11
  124.5 2.2 %copy-start.12 = (f32[512]{0:T(512)S(1)}, f32[512]{0:T(512)}, u32[]{:S(2)}) copy-start(f32[512]{0:T(512)} %param.28) | copy-start | bytes 6148
Sparse Core Ops, SparseCore 0:
  28.9 47.9 all-gather.5
  116.9 80.1 all-gather.3

commit v18 on v17

--- a/solution.py
+++ b/solution.py
@@ -103,7 +103,7 @@
     )(x, q)
 
 
-def scan_kernel(count, width, mine_ref, out_ref, acc, send_buf, recv, send_sem, recv_sem):
+def scan_kernel(count, width, mine_ref, out_ref, acc_s, acc_g, send_s, send_g, recv_s, recv_g, send_sem, recv_sem):
     me = lax.axis_index(SEQ)
     barrier = pltpu.get_barrier_semaphore()
     for d in range(1, count):
@@ -115,44 +115,61 @@
         distances.append(distances[-1] * 2)
     rounds = [1] + distances
 
-    def link(r, dist, target):
-        return pltpu.make_async_remote_copy(
-            src_ref=mine_ref if r == 0 else send_buf.at[r],
-            dst_ref=recv.at[r],
-            send_sem=send_sem.at[r],
-            recv_sem=recv_sem.at[r],
+    def links(r, target):
+        state = pltpu.make_async_remote_copy(
+            src_ref=send_s.at[r],
+            dst_ref=recv_s.at[r],
+            send_sem=send_sem.at[0, r],
+            recv_sem=recv_sem.at[0, r],
             device_id={SEQ: target},
             device_id_type=pl.DeviceIdType.MESH,
         )
-
-    rows = acc.shape[1]
-    is_gate_row = lax.broadcasted_iota(jnp.int32, acc.shape, 1) == width
-    acc[...] = jnp.where(is_gate_row, 1.0, 0.0).astype(acc.dtype)
+        gate = pltpu.make_async_remote_copy(
+            src_ref=send_g.at[r],
+            dst_ref=recv_g.at[r],
+            send_sem=send_sem.at[1, r],
+            recv_sem=recv_sem.at[1, r],
+            device_id={SEQ: target},
+            device_id_type=pl.DeviceIdType.MESH,
+        )
+        return state, gate
+
+    acc_s[...] = jnp.zeros_like(acc_s)
+    acc_g[...] = jnp.ones_like(acc_g)
     for r, dist in enumerate(rounds):
-        if r > 0:
-            send_buf[r] = acc[...]
+        if r == 0:
+            send_s[0] = mine_ref[:, :width, :].astype(send_s.dtype)
+            send_g[0] = mine_ref[:, width : width + 8, :]
+        else:
+            send_s[r] = acc_s[...].astype(send_s.dtype)
+            send_g[r] = acc_g[...]
 
         @pl.when(me + dist < count)
         def _():
-            link(r, dist, me + dist).start()
+            state, gate = links(r, me + dist)
+            state.start()
+            gate.start()
 
         @pl.when(me >= dist)
         def _():
-            link(r, dist, me - dist).wait_recv()
+            state, gate = links(r, me - dist)
+            state.wait_recv()
+            gate.wait_recv()
             if r == 0:
-                acc[...] = recv[0]
+                acc_s[...] = recv_s[0].astype(jnp.float32)
+                acc_g[...] = recv_g[0]
             else:
-                came = recv[r]
-                mine_gate = acc[:, width : width + 8, :][:, 0:1, :]
-                came_gate = came[:, width : width + 8, :][:, 0:1, :]
-                state = mine_gate * came + acc[...]
-                acc[...] = jnp.where(is_gate_row, mine_gate * came_gate, state)
+                mine_gate = acc_g[...][:, 0:1, :]
+                acc_s[...] = mine_gate * recv_s[r].astype(jnp.float32) + acc_s[...]
+                acc_g[...] = mine_gate * recv_g[r]
 
     for r, dist in enumerate(rounds):
         @pl.when(me + dist < count)
         def _():
-            link(r, dist, me + dist).wait_send()
-    out_ref[...] = acc[:, :width, :]
+            state, gate = links(r, me + dist)
+            state.wait_send()
+            gate.wait_send()
+    out_ref[...] = acc_s[...]
 
 
 def carry_in(mine, width):
@@ -167,11 +184,14 @@
         in_specs=[pl.BlockSpec(memory_space=pltpu.VMEM)],
         out_specs=pl.BlockSpec(memory_space=pltpu.VMEM),
         scratch_shapes=[
-            pltpu.VMEM(mine.shape, jnp.float32),
-            pltpu.VMEM((steps,) + mine.shape, jnp.float32),
-            pltpu.VMEM((steps,) + mine.shape, jnp.float32),
-            pltpu.SemaphoreType.DMA((steps,)),
-            pltpu.SemaphoreType.DMA((steps,)),
+            pltpu.VMEM((heads, width, lanes), jnp.float32),
+            pltpu.VMEM((heads, 8, lanes), jnp.float32),
+            pltpu.VMEM((steps, heads, width, lanes), jnp.bfloat16),
+            pltpu.VMEM((steps, heads, 8, lanes), jnp.float32),
+            pltpu.VMEM((steps, heads, width, lanes), jnp.bfloat16),
+            pltpu.VMEM((steps, heads, 8, lanes), jnp.float32),
+            pltpu.SemaphoreType.DMA((2, steps)),
+            pltpu.SemaphoreType.DMA((2, steps)),
         ],
         compiler_params=pltpu.CompilerParams(collective_id=1, has_side_effects=True),
     )(mine)

time: 206 us -> 194 us (0.942)
  waiting for transfers between devices: 81.4 us -> 72.9 us
  Pallas kernels: 60.7 us -> 56.8 us
    all_gather x2, waiting for transfers between devices: 69.4 us -> 60.9 us  [gather_seq(): return lax.all_gather(x, SEQ, axis=0, tiled=False)]
    pallas_call x1, Pallas kernels: 20.2 us -> 14.7 us  [carry_in(): pl.pallas_call(functools.partial(scan_kernel, count, width), out_shape=ja...]
  transfers between devices with their start and end apart: 4 -> 4, of which waited for: 4 -> 4; matrix products, arithmetic and copies ran while one was open for 7% -> 8% of each run, Pallas kernels for 20% -> 22%
where the time goes in v18:
time: 194 us; the launch traced here: 193 us
  waiting for transfers between devices  72.9 us (38%)
  Pallas kernels  56.8 us (29%)
  between operations  18.2 us (9%)
  matrix products  14.2 us (7%)
  other arithmetic  13.6 us (7%)
  starting transfers between devices  11.5 us (6%)
  local copies, waits for them, and re-layouts  6.14 us (3%)
    all_gather x2, waiting for transfers between devices, gather_seq(): return lax.all_gather(x, SEQ, axis=0, tiled=False)  60.9 us
    pallas_call x1, Pallas kernels, scatter_sum(): pl.pallas_call(functools.partial(scatter_sum_kernel, count, rows), out_sh...  42.2 us
    pallas_call x1, Pallas kernels, carry_in(): pl.pallas_call(functools.partial(scan_kernel, count, width), out_shape=ja...  14.7 us
    all_to_all x1, waiting for transfers between devices, on_device(): lax.all_to_all(packed, 'tp', split_axis=1, concat_axis=0, tiled=True)  9.56 us
    all_to_all x1, starting transfers between devices, on_device(): lax.all_to_all(packed, 'tp', split_axis=1, concat_axis=0, tiled=True)  8.16 us
    dot_general x1, matrix products, on_device(): jnp.dot(tokens, gathered[:, :width], preferred_element_type=jnp.float32)  5.9 us
    dot_general x1, matrix products, on_device(): lax.dot_general(scaled, gathered[:, width:], (((1,), (1,)), ((), ())), pr...  4.7 us
  transfers between devices with their start and end apart: 4, of which 4 were waited for; matrix products, arithmetic and copies ran while one was open for 8% of the time, Pallas kernels for 22%

profile of v18, /device:TPU:1, one launch (start us, length us, event | category | flops | bytes accessed | tf_op | source)
XLA Modules:
  0.0 193.3 jit_solution(10498429666533910557)
XLA Ops:
  7.2 1.2 convert_element_type.81
  8.5 0.2 copy.118
  8.7 0.2 reshape.225
  8.9 0.1 copy.81
  9.0 0.1 copy.82
  9.2 0.8 concatenate.43
  10.1 8.2 %all-to-all-start = ((bf16[16,8,1408]{2,0,1:T(8,128)(2,1)}), bf16[16,8,1408]{2,0,1:T(8,128)(2,1)S(1)}, u32[]{:S(2)}, u32[]{:S(2)}) async-start(bf16[16,8,1408]{2,0,1:T(8,128)(2,1)} %concatenate.43), calls=%async_computation | async-start | bytes 720896 | tf_op jit(solution)/shard_map/all_to_all | solution.py:246
  18.3 0.1 copy.83
  18.4 9.6 %all-to-all-done = bf16[16,8,1408]{2,0,1:T(8,128)(2,1)S(1)} async-done(((bf16[16,8,1408]{2,0,1:T(8,128)(2,1)}), bf16[16,8,1408]{2,0,1:T(8,128)(2,1)S(1)}, u32[]{:S(2)}, u32[]{:S(2)}) %all-to-all-start) | async-done | bytes 360480 | tf_op jit(solution)/shard_map/all_to_all | solution.py:246
  27.9 0.8 pad_maximum_fusion.1
  28.9 0.1 select_reduce_fusion
  29.2 0.2 fusion.41
  29.3 0.1 copy.88
  29.4 0.2 slice_reduce_fusion.5
  29.7 0.2 compare_reduce_fusion
  30.1 46.8 %all-gather.6.cloned.1.call-done = bf16[2048,1920]{1,0:T(8,128)(2,1)} async-done(((bf16[128,1920]{1,0:T(8,128)(2,1)}), bf16[2048,1920]{1,0:T(8,128)(2,1)}) %all-gather.6.cloned.1.call-update) | async-done | bytes 7864336 | tf_op jit(solution)/shard_map/all_gather | solution.py:25
  77.0 5.9 %fusion.47 = (bf16[512,1408]{0,1:T(8,128)(2,1)S(1)}, f32[512,1408]{0,1:T(8,128)S(1)}) fusion(bf16[512,2048]{1,0:T(8,128)(2,1)S(1)} %copy-done, bf16[2048,1920]{1,0:T(8,128)(2,1)} %all-gather.6.cloned.1.call-done), kind=kOutput, calls=%fused_computation.109 | convolution fusion | flops 2953510912 | bytes 12189696 | tf_op jit(solution)/shard_map/dot_general | solution.py:252
  82.9 0.1 compare_select_fusion
  83.0 0.2 fusion.31
  83.2 0.2 slice_reduce_fusion
  83.5 0.1 slice.150
  83.6 3.3 %collective-permute-start = (bf16[3,768]{0,1:T(8,128)(2,1)S(1)}, bf16[3,768]{0,1:T(8,128)(2,1)S(1)}, u32[]{:S(2)}, u32[]{:S(2)}) collective-permute-start(bf16[3,768]{0,1:T(8,128)(2,1)S(1)} %slice.150), channel_id=1, source_target_pairs={{0,8},{8,16},{16,24},{24,32},{32,40},{40,48},{48,56},{56,64},{64,7... | collective-permute-start | bytes 13832 | tf_op jit(solution)/shard_map/ppermute | solution.py:21
  87.0 2.4 %collective-permute-done = bf16[3,768]{0,1:T(8,128)(2,1)S(1)} collective-permute-done((bf16[3,768]{0,1:T(8,128)(2,1)S(1)}, bf16[3,768]{0,1:T(8,128)(2,1)S(1)}, u32[]{:S(2)}, u32[]{:S(2)}) %collective-permute-start) | collective-permute-done | bytes 4640 | tf_op jit(solution)/shard_map/ppermute | solution.py:21
  89.5 2.1 %multiply_convert_fusion.3 = bf16[512,768]{0,1:T(8,128)(2,1)S(1)} fusion(bf16[512,768]{0,1:T(8,128)(2,1)S(1)} %slice.151, bf16[3,768]{0,1:T(8,128)(2,1)S(1)} %collective-permute-done, f32[768]{0:T(1024)S(1)} %get-tuple-element.19, f32[768]{0:T(1024)S(1)} %get-tuple-element.20, f32[768]{0:T(1024)S(1)} %get-tuple-element.21, f32[768]{0:T(1024)S(1)} %get-tuple-element.18, ...), kind=kLoop, calls=%fused_computation.14 | loop fusion | flops 11403264 | bytes 1594368 | tf_op jit(solution)/shard_map/convert_element_type | solution.py:276
  91.7 0.1 reshape.228
  91.8 0.1 copy.89
  92.0 1.0 fusion.20
  93.0 0.8 slice_bitcast_fusion.1
  93.8 0.1 bitcast_add_fusion
  94.0 0.7 select_maximum_fusion.mine_ref
  94.7 14.7 %shard_map.158 = f32[8,64,128]{2,1,0:T(8,128)} custom-call(f32[8,72,128]{2,1,0:T(8,128)} %select_maximum_fusion.mine_ref), custom_call_target="tpu_custom_call" | custom-call | tf_op jit(solution)/shard_map/pallas_call | solution.py:181
  109.4 1.9 fusion.25
  111.4 0.6 fusion.46
  115.6 0.2 compare_and_fusion
  115.8 0.3 fusion.33
  116.1 1.7 fusion.13
  117.8 0.4 fusion.15
  118.2 0.8 copy.93
  119.1 1.4 multiply_reduce_fusion
  120.5 0.1 reshape.233
  120.6 0.6 pad_bitcast_fusion.q_ref
  121.3 4.7 %convolution_convert_fusion.x_ref = bf16[512,2048]{1,0:T(8,128)(2,1)} fusion(bf16[2048,1920]{1,0:T(8,128)(2,1)} %all-gather.6.cloned.1.call-done, f32[512]{0:T(512)S(1)} %copy-done.12, f32[512,512]{0,1:T(8,128)S(1)} %bitcast.75, bf16[512,1408]{0,1:T(8,128)(2,1)} %copy-done.2), kind=kOutput, calls=%fused_computation.4 | convolution fusion | flops 1076887552 | bytes 5769216 | tf_op jit(solution)/shard_map/dot_general | solution.py:366
  126.0 42.2 %shard_map.159 = (f32[64,2048]{1,0:T(8,128)}, f32[8,128]{1,0:T(8,128)}) custom-call(bf16[512,2048]{1,0:T(8,128)(2,1)} %convolution_convert_fusion.x_ref, f32[64,128]{1,0:T(8,128)} %pad_bitcast_fusion.q_ref), custom_call_target="tpu_custom_call" | custom-call | tf_op jit(solution)/shard_map/pallas_call | solution.py:88
  168.1 0.7 rsqrt_bitcast_fusion
  168.8 1.9 multiply_convert_fusion.9
  170.7 14.0 %all-gather.4.cloned.1.call-done = bf16[16,2,8,64,128]{4,3,2,1,0:T(8,128)(2,1)} async-done(((bf16[1,2,8,64,128]{4,3,2,1,0:T(8,128)(2,1)}), bf16[16,2,8,64,128]{4,3,2,1,0:T(8,128)(2,1)}) %all-gather.4.cloned.1.call-update) | async-done | bytes 4194320 | tf_op jit(solution)/shard_map/all_gather | solution.py:25
  184.7 1.0 constant_dynamic-slice_fusion.1
  185.7 0.8 maximum_convert_fusion
  (66 shorter events, 1.3 us)
Async XLA Ops:
  7.2 69.8 %copy-start = (bf16[512,2048]{1,0:T(8,128)(2,1)S(1)}, bf16[512,2048]{1,0:T(8,128)(2,1)}, u32[]{:S(2)}) copy-start(bf16[512,2048]{1,0:T(8,128)(2,1)} %param.17) | copy-start | bytes 6291460
  7.2 1.7 copy-start.4
  7.2 1.7 copy-start.5
  8.4 9.9 %copy-start.3 = (f32[512,128]{1,0:T(8,128)S(1)}, f32[512,128]{1,0:T(8,128)}, u32[]{:S(2)}) copy-start(f32[512,128]{1,0:T(8,128)} %param.29) | copy-start | bytes 786436
  9.2 19.7 %copy-start.13 = (s32[8]{0:T(128)S(1)}, s32[8]{0:T(128)}, u32[]{:S(2)}) copy-start(s32[8]{0:T(128)} %param.30) | copy-start | bytes 100
  9.2 20.5 %copy-start.6 = (f32[4,512]{1,0:T(4,128)S(1)}, f32[4,512]{1,0:T(4,128)}, u32[]{:S(2)}) copy-start(f32[4,512]{1,0:T(4,128)} %param.21) | copy-start | bytes 24580
  9.2 20.5 %copy-start.7 = (f32[4,256]{1,0:T(4,128)S(1)}, f32[4,256]{1,0:T(4,128)}, u32[]{:S(2)}) copy-start(f32[4,256]{1,0:T(4,128)} %param.23) | copy-start | bytes 12292
  9.2 20.5 %copy-start.8 = (f32[512]{0:T(512)S(1)}, f32[512]{0:T(512)}, u32[]{:S(2)}) copy-start(f32[512]{0:T(512)} %param.22) | copy-start | bytes 6148
  9.2 20.5 %copy-start.9 = (f32[256]{0:T(256)S(1)}, f32[256]{0:T(256)}, u32[]{:S(2)}) copy-start(f32[256]{0:T(256)} %param.24) | copy-start | bytes 3076
  9.2 20.7 %copy-start.14 = (f32[8]{0:T(128)S(1)}, f32[8]{0:T(128)}, u32[]{:S(2)}) copy-start(f32[8]{0:T(128)} %param.26) | copy-start | bytes 100
  10.1 17.9 %all-to-all-start = ((bf16[16,8,1408]{2,0,1:T(8,128)(2,1)}), bf16[16,8,1408]{2,0,1:T(8,128)(2,1)S(1)}, u32[]{:S(2)}, u32[]{:S(2)}) async-start(bf16[16,8,1408]{2,0,1:T(8,128)(2,1)} %concatenate.43), calls=%async_computation | async-start | bytes 720896 | tf_op jit(solution)/shard_map/all_to_all | solution.py:246
  18.2 58.7 %all-gather.6.cloned.1.call-start = ((), (), s32[]{:S(2)}) async-start(), calls=%async_computation.2 | async-start | bytes 8355840 | tf_op jit(solution)/shard_map/all_gather | solution.py:25
  28.8 155.9 %all-gather.4.cloned.1.call-start = ((), (), s32[]{:S(2)}) async-start(), calls=%async_computation.1 | async-start | bytes 4456448 | tf_op jit(solution)/shard_map/all_gather | solution.py:25
  30.1 52.8 %copy-start.10 = (f32[8]{0:T(128)S(1)}, f32[8]{0:T(128)}, u32[]{:S(2)}) copy-start(f32[8]{0:T(128)} %param.25) | copy-start | bytes 100
  82.9 8.7 %copy-start.2 = (bf16[512,1408]{0,1:T(8,128)(2,1)}, bf16[512,1408]{0,1:T(8,128)(2,1)S(1)}, u32[]{:S(2)}) copy-start(bf16[512,1408]{0,1:T(8,128)(2,1)S(1)} %get-tuple-element.43) | copy-start | bytes 4325380
  83.6 5.9 %collective-permute-start = (bf16[3,768]{0,1:T(8,128)(2,1)S(1)}, bf16[3,768]{0,1:T(8,128)(2,1)S(1)}, u32[]{:S(2)}, u32[]{:S(2)}) collective-permute-start(bf16[3,768]{0,1:T(8,128)(2,1)S(1)} %slice.150), channel_id=1, source_target_pairs={{0,8},{8,16},{16,24},{24,32},{32,40},{40,48},{48,56},{56,64},{64,7... | collective-permute-start | bytes 13832 | tf_op jit(solution)/shard_map/ppermute | solution.py:21
  93.8 17.5 %copy-start.15 = (s32[32]{0:T(128)S(1)}, s32[32]{0:T(128)}, u32[]{:S(2)}) copy-start(s32[32]{0:T(128)} %param.31) | copy-start | bytes 388
  116.1 1.7 copy-start.1
  116.1 1.7 copy-start.11
  119.0 2.2 %copy-start.12 = (f32[512]{0:T(512)S(1)}, f32[512]{0:T(512)}, u32[]{:S(2)}) copy-start(f32[512]{0:T(512)} %param.28) | copy-start | bytes 6148
Sparse Core Ops, SparseCore 0:
  28.9 47.9 all-gather.5
  111.4 73.2 all-gather.3

commit v19 on v18

--- a/solution.py
+++ b/solution.py
@@ -111,24 +111,24 @@
         pl.semaphore_signal(barrier, inc=1, device_id={SEQ: peer}, device_id_type=pl.DeviceIdType.MESH)
     pl.semaphore_wait(barrier, count - 1)
     distances = [1]
-    while distances[-1] * 2 < count:
-        distances.append(distances[-1] * 2)
-    rounds = [1] + distances
-
-    def links(r, target):
+    while distances[-1] * 4 < count:
+        distances.append(distances[-1] * 4)
+    rounds = [(1, [1])] + [(d, [1, 2, 3]) for d in distances]
+
+    def links(r, k, target):
         state = pltpu.make_async_remote_copy(
             src_ref=send_s.at[r],
-            dst_ref=recv_s.at[r],
-            send_sem=send_sem.at[0, r],
-            recv_sem=recv_sem.at[0, r],
+            dst_ref=recv_s.at[r, k],
+            send_sem=send_sem.at[0, r, k],
+            recv_sem=recv_sem.at[0, r, k],
             device_id={SEQ: target},
             device_id_type=pl.DeviceIdType.MESH,
         )
         gate = pltpu.make_async_remote_copy(
             src_ref=send_g.at[r],
-            dst_ref=recv_g.at[r],
-            send_sem=send_sem.at[1, r],
-            recv_sem=recv_sem.at[1, r],
+            dst_ref=recv_g.at[r, k],
+            send_sem=send_sem.at[1, r, k],
+            recv_sem=recv_sem.at[1, r, k],
             device_id={SEQ: target},
             device_id_type=pl.DeviceIdType.MESH,
         )
@@ -136,39 +136,40 @@
 
     acc_s[...] = jnp.zeros_like(acc_s)
     acc_g[...] = jnp.ones_like(acc_g)
-    for r, dist in enumerate(rounds):
+    for r, (dist, steps) in enumerate(rounds):
         if r == 0:
             send_s[0] = mine_ref[:, :width, :].astype(send_s.dtype)
             send_g[0] = mine_ref[:, width : width + 8, :]
         else:
             send_s[r] = acc_s[...].astype(send_s.dtype)
             send_g[r] = acc_g[...]
-
-        @pl.when(me + dist < count)
-        def _():
-            state, gate = links(r, me + dist)
-            state.start()
-            gate.start()
-
-        @pl.when(me >= dist)
-        def _():
-            state, gate = links(r, me - dist)
-            state.wait_recv()
-            gate.wait_recv()
-            if r == 0:
-                acc_s[...] = recv_s[0].astype(jnp.float32)
-                acc_g[...] = recv_g[0]
-            else:
-                mine_gate = acc_g[...][:, 0:1, :]
-                acc_s[...] = mine_gate * recv_s[r].astype(jnp.float32) + acc_s[...]
-                acc_g[...] = mine_gate * recv_g[r]
-
-    for r, dist in enumerate(rounds):
-        @pl.when(me + dist < count)
-        def _():
-            state, gate = links(r, me + dist)
-            state.wait_send()
-            gate.wait_send()
+        for k in steps:
+            @pl.when(me + k * dist < count)
+            def _():
+                state, gate = links(r, k - 1, me + k * dist)
+                state.start()
+                gate.start()
+        for k in steps:
+            @pl.when(me >= k * dist)
+            def _():
+                state, gate = links(r, k - 1, me - k * dist)
+                state.wait_recv()
+                gate.wait_recv()
+                if r == 0:
+                    acc_s[...] = recv_s[0, 0].astype(jnp.float32)
+                    acc_g[...] = recv_g[0, 0]
+                else:
+                    mine_gate = acc_g[...][:, 0:1, :]
+                    acc_s[...] = mine_gate * recv_s[r, k - 1].astype(jnp.float32) + acc_s[...]
+                    acc_g[...] = mine_gate * recv_g[r, k - 1]
+
+    for r, (dist, steps) in enumerate(rounds):
+        for k in steps:
+            @pl.when(me + k * dist < count)
+            def _():
+                state, gate = links(r, k - 1, me + k * dist)
+                state.wait_send()
+                gate.wait_send()
     out_ref[...] = acc_s[...]
 
 
@@ -176,8 +177,10 @@
     count = lax.axis_size(SEQ)
     heads, rows, lanes = mine.shape
     steps = 1
-    while (1 << (steps - 1)) < count:
+    span = 1
+    while span < count:
         steps += 1
+        span *= 4
     return pl.pallas_call(
         functools.partial(scan_kernel, count, width),
         out_shape=jax.ShapeDtypeStruct((heads, width, lanes), jnp.float32),
@@ -188,10 +191,10 @@
             pltpu.VMEM((heads, 8, lanes), jnp.float32),
             pltpu.VMEM((steps, heads, width, lanes), jnp.bfloat16),
             pltpu.VMEM((steps, heads, 8, lanes), jnp.float32),
-            pltpu.VMEM((steps, heads, width, lanes), jnp.bfloat16),
-            pltpu.VMEM((steps, heads, 8, lanes), jnp.float32),
-            pltpu.SemaphoreType.DMA((2, steps)),
-            pltpu.SemaphoreType.DMA((2, steps)),
+            pltpu.VMEM((steps, 3, heads, width, lanes), jnp.bfloat16),
+            pltpu.VMEM((steps, 3, heads, 8, lanes), jnp.float32),
+            pltpu.SemaphoreType.DMA((2, steps, 3)),
+            pltpu.SemaphoreType.DMA((2, steps, 3)),
         ],
         compiler_params=pltpu.CompilerParams(collective_id=1, has_side_effects=True),
     )(mine)

time: 194 us -> 194 us (level)
    pallas_call x1, Pallas kernels: 42.2 us -> 38.6 us  [scatter_sum(): pl.pallas_call(functools.partial(scatter_sum_kernel, count, rows), out_sh...]
  transfers between devices with their start and end apart: 4 -> 4, of which waited for: 4 -> 4; matrix products, arithmetic and copies ran while one was open for 8% -> 8% of each run, Pallas kernels for 22% -> 20%
where the time goes in v19:
time: 194 us; the launch traced here: 193 us
  waiting for transfers between devices  74.6 us (38%)
  Pallas kernels  55.2 us (28%)
  between operations  18.2 us (9%)
  matrix products  14.1 us (7%)
  other arithmetic  13.6 us (7%)
  starting transfers between devices  11.5 us (6%)
  local copies, waits for them, and re-layouts  6.14 us (3%)
    all_gather x2, waiting for transfers between devices, gather_seq(): return lax.all_gather(x, SEQ, axis=0, tiled=False)  62.6 us
    pallas_call x1, Pallas kernels, scatter_sum(): pl.pallas_call(functools.partial(scatter_sum_kernel, count, rows), out_sh...  38.6 us
    pallas_call x1, Pallas kernels, carry_in(): pl.pallas_call(functools.partial(scan_kernel, count, width), out_shape=ja...  16.6 us
    all_to_all x1, waiting for transfers between devices, on_device(): lax.all_to_all(packed, 'tp', split_axis=1, concat_axis=0, tiled=True)  9.56 us
    all_to_all x1, starting transfers between devices, on_device(): lax.all_to_all(packed, 'tp', split_axis=1, concat_axis=0, tiled=True)  8.16 us
    dot_general x1, matrix products, on_device(): jnp.dot(tokens, gathered[:, :width], preferred_element_type=jnp.float32)  5.9 us
    dot_general x1, matrix products, on_device(): lax.dot_general(scaled, gathered[:, width:], (((1,), (1,)), ((), ())), pr...  4.7 us
  transfers between devices with their start and end apart: 4, of which 4 were waited for; matrix products, arithmetic and copies ran while one was open for 8% of the time, Pallas kernels for 20%

profile of v19, /device:TPU:1, one launch (start us, length us, event | category | flops | bytes accessed | tf_op | source)
XLA Modules:
  0.0 193.4 jit_solution(4475808673283908137)
XLA Ops:
  7.2 1.2 convert_element_type.81
  8.5 0.2 copy.118
  8.7 0.2 reshape.225
  8.9 0.1 copy.81
  9.0 0.1 copy.82
  9.2 0.8 concatenate.43
  10.1 8.2 %all-to-all-start = ((bf16[16,8,1408]{2,0,1:T(8,128)(2,1)}), bf16[16,8,1408]{2,0,1:T(8,128)(2,1)S(1)}, u32[]{:S(2)}, u32[]{:S(2)}) async-start(bf16[16,8,1408]{2,0,1:T(8,128)(2,1)} %concatenate.43), calls=%async_computation | async-start | bytes 720896 | tf_op jit(solution)/shard_map/all_to_all | solution.py:249
  18.3 0.1 copy.83
  18.4 9.6 %all-to-all-done = bf16[16,8,1408]{2,0,1:T(8,128)(2,1)S(1)} async-done(((bf16[16,8,1408]{2,0,1:T(8,128)(2,1)}), bf16[16,8,1408]{2,0,1:T(8,128)(2,1)S(1)}, u32[]{:S(2)}, u32[]{:S(2)}) %all-to-all-start) | async-done | bytes 360480 | tf_op jit(solution)/shard_map/all_to_all | solution.py:249
  27.9 0.8 pad_maximum_fusion.1
  28.9 0.1 select_reduce_fusion
  29.2 0.2 fusion.41
  29.3 0.1 copy.88
  29.4 0.2 slice_reduce_fusion.5
  29.7 0.2 compare_reduce_fusion
  30.1 46.8 %all-gather.6.cloned.1.call-done = bf16[2048,1920]{1,0:T(8,128)(2,1)} async-done(((bf16[128,1920]{1,0:T(8,128)(2,1)}), bf16[2048,1920]{1,0:T(8,128)(2,1)}) %all-gather.6.cloned.1.call-update) | async-done | bytes 7864336 | tf_op jit(solution)/shard_map/all_gather | solution.py:25
  77.0 5.9 %fusion.47 = (bf16[512,1408]{0,1:T(8,128)(2,1)S(1)}, f32[512,1408]{0,1:T(8,128)S(1)}) fusion(bf16[512,2048]{1,0:T(8,128)(2,1)S(1)} %copy-done, bf16[2048,1920]{1,0:T(8,128)(2,1)} %all-gather.6.cloned.1.call-done), kind=kOutput, calls=%fused_computation.109 | convolution fusion | flops 2953510912 | bytes 12189696 | tf_op jit(solution)/shard_map/dot_general | solution.py:255
  82.9 0.1 compare_select_fusion
  83.0 0.2 fusion.31
  83.2 0.2 slice_reduce_fusion
  83.5 0.1 slice.150
  83.6 3.3 %collective-permute-start = (bf16[3,768]{0,1:T(8,128)(2,1)S(1)}, bf16[3,768]{0,1:T(8,128)(2,1)S(1)}, u32[]{:S(2)}, u32[]{:S(2)}) collective-permute-start(bf16[3,768]{0,1:T(8,128)(2,1)S(1)} %slice.150), channel_id=1, source_target_pairs={{0,8},{8,16},{16,24},{24,32},{32,40},{40,48},{48,56},{56,64},{64,7... | collective-permute-start | bytes 13832 | tf_op jit(solution)/shard_map/ppermute | solution.py:21
  87.0 2.4 %collective-permute-done = bf16[3,768]{0,1:T(8,128)(2,1)S(1)} collective-permute-done((bf16[3,768]{0,1:T(8,128)(2,1)S(1)}, bf16[3,768]{0,1:T(8,128)(2,1)S(1)}, u32[]{:S(2)}, u32[]{:S(2)}) %collective-permute-start) | collective-permute-done | bytes 4640 | tf_op jit(solution)/shard_map/ppermute | solution.py:21
  89.5 2.1 %multiply_convert_fusion.3 = bf16[512,768]{0,1:T(8,128)(2,1)S(1)} fusion(bf16[512,768]{0,1:T(8,128)(2,1)S(1)} %slice.151, bf16[3,768]{0,1:T(8,128)(2,1)S(1)} %collective-permute-done, f32[768]{0:T(1024)S(1)} %get-tuple-element.19, f32[768]{0:T(1024)S(1)} %get-tuple-element.20, f32[768]{0:T(1024)S(1)} %get-tuple-element.21, f32[768]{0:T(1024)S(1)} %get-tuple-element.18, ...), kind=kLoop, calls=%fused_computation.14 | loop fusion | flops 11403264 | bytes 1594368 | tf_op jit(solution)/shard_map/convert_element_type | solution.py:279
  91.7 0.1 reshape.228
  91.8 0.1 copy.89
  92.0 1.0 fusion.20
  93.0 0.8 slice_bitcast_fusion.1
  93.8 0.1 bitcast_add_fusion
  94.0 0.7 select_maximum_fusion.mine_ref
  94.7 16.6 %shard_map.158 = f32[8,64,128]{2,1,0:T(8,128)} custom-call(f32[8,72,128]{2,1,0:T(8,128)} %select_maximum_fusion.mine_ref), custom_call_target="tpu_custom_call" | custom-call | tf_op jit(solution)/shard_map/pallas_call | solution.py:184
  111.3 1.9 fusion.25
  113.3 0.6 fusion.46
  117.5 0.2 compare_and_fusion
  117.7 0.3 fusion.33
  118.0 1.7 fusion.13
  119.7 0.4 fusion.15
  120.1 0.8 copy.93
  121.0 1.4 multiply_reduce_fusion
  122.4 0.1 reshape.233
  122.5 0.6 pad_bitcast_fusion.q_ref
  123.2 4.7 %convolution_convert_fusion.x_ref = bf16[512,2048]{1,0:T(8,128)(2,1)} fusion(bf16[2048,1920]{1,0:T(8,128)(2,1)} %all-gather.6.cloned.1.call-done, f32[512]{0:T(512)S(1)} %copy-done.12, f32[512,512]{0,1:T(8,128)S(1)} %bitcast.75, bf16[512,1408]{0,1:T(8,128)(2,1)} %copy-done.2), kind=kOutput, calls=%fused_computation.4 | convolution fusion | flops 1076887552 | bytes 5769216 | tf_op jit(solution)/shard_map/dot_general | solution.py:369
  127.9 38.6 %shard_map.159 = (f32[64,2048]{1,0:T(8,128)}, f32[8,128]{1,0:T(8,128)}) custom-call(bf16[512,2048]{1,0:T(8,128)(2,1)} %convolution_convert_fusion.x_ref, f32[64,128]{1,0:T(8,128)} %pad_bitcast_fusion.q_ref), custom_call_target="tpu_custom_call" | custom-call | tf_op jit(solution)/shard_map/pallas_call | solution.py:88
  166.5 0.7 rsqrt_bitcast_fusion
  167.2 1.8 multiply_convert_fusion.9
  169.0 15.7 %all-gather.4.cloned.1.call-done = bf16[16,2,8,64,128]{4,3,2,1,0:T(8,128)(2,1)} async-done(((bf16[1,2,8,64,128]{4,3,2,1,0:T(8,128)(2,1)}), bf16[16,2,8,64,128]{4,3,2,1,0:T(8,128)(2,1)}) %all-gather.4.cloned.1.call-update) | async-done | bytes 4194320 | tf_op jit(solution)/shard_map/all_gather | solution.py:25
  184.7 1.0 constant_dynamic-slice_fusion.1
  185.7 0.8 maximum_convert_fusion
  (66 shorter events, 1.3 us)
Async XLA Ops:
  7.2 69.8 %copy-start = (bf16[512,2048]{1,0:T(8,128)(2,1)S(1)}, bf16[512,2048]{1,0:T(8,128)(2,1)}, u32[]{:S(2)}) copy-start(bf16[512,2048]{1,0:T(8,128)(2,1)} %param.17) | copy-start | bytes 6291460
  7.2 1.7 copy-start.4
  7.2 1.7 copy-start.5
  8.4 9.9 %copy-start.3 = (f32[512,128]{1,0:T(8,128)S(1)}, f32[512,128]{1,0:T(8,128)}, u32[]{:S(2)}) copy-start(f32[512,128]{1,0:T(8,128)} %param.29) | copy-start | bytes 786436
  9.2 19.7 %copy-start.13 = (s32[8]{0:T(128)S(1)}, s32[8]{0:T(128)}, u32[]{:S(2)}) copy-start(s32[8]{0:T(128)} %param.30) | copy-start | bytes 100
  9.2 20.5 %copy-start.6 = (f32[4,512]{1,0:T(4,128)S(1)}, f32[4,512]{1,0:T(4,128)}, u32[]{:S(2)}) copy-start(f32[4,512]{1,0:T(4,128)} %param.21) | copy-start | bytes 24580
  9.2 20.5 %copy-start.7 = (f32[4,256]{1,0:T(4,128)S(1)}, f32[4,256]{1,0:T(4,128)}, u32[]{:S(2)}) copy-start(f32[4,256]{1,0:T(4,128)} %param.23) | copy-start | bytes 12292
  9.2 20.5 %copy-start.8 = (f32[512]{0:T(512)S(1)}, f32[512]{0:T(512)}, u32[]{:S(2)}) copy-start(f32[512]{0:T(512)} %param.22) | copy-start | bytes 6148
  9.2 20.5 %copy-start.9 = (f32[256]{0:T(256)S(1)}, f32[256]{0:T(256)}, u32[]{:S(2)}) copy-start(f32[256]{0:T(256)} %param.24) | copy-start | bytes 3076
  9.2 20.7 %copy-start.14 = (f32[8]{0:T(128)S(1)}, f32[8]{0:T(128)}, u32[]{:S(2)}) copy-start(f32[8]{0:T(128)} %param.26) | copy-start | bytes 100
  10.1 17.9 %all-to-all-start = ((bf16[16,8,1408]{2,0,1:T(8,128)(2,1)}), bf16[16,8,1408]{2,0,1:T(8,128)(2,1)S(1)}, u32[]{:S(2)}, u32[]{:S(2)}) async-start(bf16[16,8,1408]{2,0,1:T(8,128)(2,1)} %concatenate.43), calls=%async_computation | async-start | bytes 720896 | tf_op jit(solution)/shard_map/all_to_all | solution.py:249
  18.2 58.7 %all-gather.6.cloned.1.call-start = ((), (), s32[]{:S(2)}) async-start(), calls=%async_computation.2 | async-start | bytes 8355840 | tf_op jit(solution)/shard_map/all_gather | solution.py:25
  28.8 156.0 %all-gather.4.cloned.1.call-start = ((), (), s32[]{:S(2)}) async-start(), calls=%async_computation.1 | async-start | bytes 4456448 | tf_op jit(solution)/shard_map/all_gather | solution.py:25
  30.1 52.8 %copy-start.10 = (f32[8]{0:T(128)S(1)}, f32[8]{0:T(128)}, u32[]{:S(2)}) copy-start(f32[8]{0:T(128)} %param.25) | copy-start | bytes 100
  82.9 8.7 %copy-start.2 = (bf16[512,1408]{0,1:T(8,128)(2,1)}, bf16[512,1408]{0,1:T(8,128)(2,1)S(1)}, u32[]{:S(2)}) copy-start(bf16[512,1408]{0,1:T(8,128)(2,1)S(1)} %get-tuple-element.43) | copy-start | bytes 4325380
  83.6 5.9 %collective-permute-start = (bf16[3,768]{0,1:T(8,128)(2,1)S(1)}, bf16[3,768]{0,1:T(8,128)(2,1)S(1)}, u32[]{:S(2)}, u32[]{:S(2)}) collective-permute-start(bf16[3,768]{0,1:T(8,128)(2,1)S(1)} %slice.150), channel_id=1, source_target_pairs={{0,8},{8,16},{16,24},{24,32},{32,40},{40,48},{48,56},{56,64},{64,7... | collective-permute-start | bytes 13832 | tf_op jit(solution)/shard_map/ppermute | solution.py:21
  93.8 19.4 %copy-start.15 = (s32[32]{0:T(128)S(1)}, s32[32]{0:T(128)}, u32[]{:S(2)}) copy-start(s32[32]{0:T(128)} %param.31) | copy-start | bytes 388
  118.0 1.7 copy-start.1
  118.0 1.7 copy-start.11
  121.0 2.2 %copy-start.12 = (f32[512]{0:T(512)S(1)}, f32[512]{0:T(512)}, u32[]{:S(2)}) copy-start(f32[512]{0:T(512)} %param.28) | copy-start | bytes 6148
Sparse Core Ops, SparseCore 0:
  28.9 47.9 all-gather.5
  113.3 71.3 all-gather.3

commit v20 on v18

--- a/solution.py
+++ b/solution.py
@@ -103,7 +103,7 @@
     )(x, q)
 
 
-def scan_kernel(count, width, mine_ref, out_ref, acc_s, acc_g, send_s, send_g, recv_s, recv_g, send_sem, recv_sem):
+def scan_kernel(count, width, mine_ref, out_ref, acc_s, acc_g, send_s, recv_s, send_sem, recv_sem):
     me = lax.axis_index(SEQ)
     barrier = pltpu.get_barrier_semaphore()
     for d in range(1, count):
@@ -116,7 +116,7 @@
     rounds = [1] + distances
 
     def links(r, target):
-        state = pltpu.make_async_remote_copy(
+        return pltpu.make_async_remote_copy(
             src_ref=send_s.at[r],
             dst_ref=recv_s.at[r],
             send_sem=send_sem.at[0, r],
@@ -124,51 +124,48 @@
             device_id={SEQ: target},
             device_id_type=pl.DeviceIdType.MESH,
         )
-        gate = pltpu.make_async_remote_copy(
-            src_ref=send_g.at[r],
-            dst_ref=recv_g.at[r],
-            send_sem=send_sem.at[1, r],
-            recv_sem=recv_sem.at[1, r],
-            device_id={SEQ: target},
-            device_id_type=pl.DeviceIdType.MESH,
-        )
-        return state, gate
-
+
+    tail_row = lax.broadcasted_iota(jnp.int32, (acc_s.shape[0], 16, acc_s.shape[2]), 1)
+
+    def pack(state, gate):
+        hi = gate.astype(jnp.bfloat16).astype(jnp.float32)
+        lo = (gate - hi).astype(jnp.bfloat16).astype(jnp.float32)
+        tail = jnp.where(tail_row == 0, hi, jnp.where(tail_row == 1, lo, 0.0))
+        send_s[r_now[0], :, :width, :] = state.astype(send_s.dtype)
+        send_s[r_now[0], :, width : width + 16, :] = tail.astype(send_s.dtype)
+
+    r_now = [0]
     acc_s[...] = jnp.zeros_like(acc_s)
     acc_g[...] = jnp.ones_like(acc_g)
     for r, dist in enumerate(rounds):
+        r_now[0] = r
         if r == 0:
-            send_s[0] = mine_ref[:, :width, :].astype(send_s.dtype)
-            send_g[0] = mine_ref[:, width : width + 8, :]
+            pack(mine_ref[:, :width, :], mine_ref[:, width : width + 8, :][:, 0:1, :])
         else:
-            send_s[r] = acc_s[...].astype(send_s.dtype)
-            send_g[r] = acc_g[...]
+            pack(acc_s[...], acc_g[...][:, 0:1, :])
 
         @pl.when(me + dist < count)
         def _():
-            state, gate = links(r, me + dist)
-            state.start()
-            gate.start()
+            links(r, me + dist).start()
 
         @pl.when(me >= dist)
         def _():
-            state, gate = links(r, me - dist)
-            state.wait_recv()
-            gate.wait_recv()
+            links(r, me - dist).wait_recv()
+            tail = recv_s[r, :, width : width + 16, :].astype(jnp.float32)
+            came_gate = tail[:, 0:1, :] + tail[:, 1:2, :]
+            came_state = recv_s[r, :, :width, :].astype(jnp.float32)
             if r == 0:
-                acc_s[...] = recv_s[0].astype(jnp.float32)
-                acc_g[...] = recv_g[0]
+                acc_s[...] = came_state
+                acc_g[...] = jnp.broadcast_to(came_gate, acc_g.shape)
             else:
                 mine_gate = acc_g[...][:, 0:1, :]
-                acc_s[...] = mine_gate * recv_s[r].astype(jnp.float32) + acc_s[...]
-                acc_g[...] = mine_gate * recv_g[r]
+                acc_s[...] = mine_gate * came_state + acc_s[...]
+                acc_g[...] = jnp.broadcast_to(mine_gate * came_gate, acc_g.shape)
 
     for r, dist in enumerate(rounds):
         @pl.when(me + dist < count)
         def _():
-            state, gate = links(r, me + dist)
-            state.wait_send()
-            gate.wait_send()
+            links(r, me + dist).wait_send()
     out_ref[...] = acc_s[...]
 
 
@@ -186,12 +183,10 @@
         scratch_shapes=[
             pltpu.VMEM((heads, width, lanes), jnp.float32),
             pltpu.VMEM((heads, 8, lanes), jnp.float32),
-            pltpu.VMEM((steps, heads, width, lanes), jnp.bfloat16),
-            pltpu.VMEM((steps, heads, 8, lanes), jnp.float32),
-            pltpu.VMEM((steps, heads, width, lanes), jnp.bfloat16),
-            pltpu.VMEM((steps, heads, 8, lanes), jnp.float32),
-            pltpu.SemaphoreType.DMA((2, steps)),
-            pltpu.SemaphoreType.DMA((2, steps)),
+            pltpu.VMEM((steps, heads, width + 16, lanes), jnp.bfloat16),
+            pltpu.VMEM((steps, heads, width + 16, lanes), jnp.bfloat16),
+            pltpu.SemaphoreType.DMA((1, steps)),
+            pltpu.SemaphoreType.DMA((1, steps)),
         ],
         compiler_params=pltpu.CompilerParams(collective_id=1, has_side_effects=True),
     )(mine)

time: 194 us -> 194 us (level)
  no operation moved by 1% of the time
where the time goes in v20:
time: 194 us; the launch traced here: 193 us
  waiting for transfers between devices  72.9 us (38%)
  Pallas kernels  56.7 us (29%)
  between operations  18.2 us (9%)
  matrix products  14.1 us (7%)
  other arithmetic  13.6 us (7%)
  starting transfers between devices  11.5 us (6%)
  local copies, waits for them, and re-layouts  6.14 us (3%)
    all_gather x2, waiting for transfers between devices, gather_seq(): return lax.all_gather(x, SEQ, axis=0, tiled=False)  60.9 us
    pallas_call x1, Pallas kernels, scatter_sum(): pl.pallas_call(functools.partial(scatter_sum_kernel, count, rows), out_sh...  42.1 us
    pallas_call x1, Pallas kernels, carry_in(): pl.pallas_call(functools.partial(scan_kernel, count, width), out_shape=ja...  14.6 us
    all_to_all x1, waiting for transfers between devices, on_device(): lax.all_to_all(packed, 'tp', split_axis=1, concat_axis=0, tiled=True)  9.56 us
    all_to_all x1, starting transfers between devices, on_device(): lax.all_to_all(packed, 'tp', split_axis=1, concat_axis=0, tiled=True)  8.16 us
    dot_general x1, matrix products, on_device(): jnp.dot(tokens, gathered[:, :width], preferred_element_type=jnp.float32)  5.9 us
    dot_general x1, matrix products, on_device(): lax.dot_general(scaled, gathered[:, width:], (((1,), (1,)), ((), ())), pr...  4.7 us
  transfers between devices with their start and end apart: 4, of which 4 were waited for; matrix products, arithmetic and copies ran while one was open for 8% of the time, Pallas kernels for 22%

profile of v20, /device:TPU:1, one launch (start us, length us, event | category | flops | bytes accessed | tf_op | source)
XLA Modules:
  0.0 193.3 jit_solution(8432267071801160757)
XLA Ops:
  7.2 1.2 convert_element_type.81
  8.5 0.2 copy.118
  8.7 0.2 reshape.225
  8.9 0.1 copy.81
  9.0 0.1 copy.82
  9.2 0.8 concatenate.43
  10.1 8.2 %all-to-all-start = ((bf16[16,8,1408]{2,0,1:T(8,128)(2,1)}), bf16[16,8,1408]{2,0,1:T(8,128)(2,1)S(1)}, u32[]{:S(2)}, u32[]{:S(2)}) async-start(bf16[16,8,1408]{2,0,1:T(8,128)(2,1)} %concatenate.43), calls=%async_computation | async-start | bytes 720896 | tf_op jit(solution)/shard_map/all_to_all | solution.py:241
  18.3 0.1 copy.83
  18.4 9.6 %all-to-all-done = bf16[16,8,1408]{2,0,1:T(8,128)(2,1)S(1)} async-done(((bf16[16,8,1408]{2,0,1:T(8,128)(2,1)}), bf16[16,8,1408]{2,0,1:T(8,128)(2,1)S(1)}, u32[]{:S(2)}, u32[]{:S(2)}) %all-to-all-start) | async-done | bytes 360480 | tf_op jit(solution)/shard_map/all_to_all | solution.py:241
  27.9 0.8 pad_maximum_fusion.1
  28.9 0.1 select_reduce_fusion
  29.2 0.2 fusion.41
  29.3 0.1 copy.88
  29.4 0.2 slice_reduce_fusion.5
  29.7 0.2 compare_reduce_fusion
  30.1 46.8 %all-gather.6.cloned.1.call-done = bf16[2048,1920]{1,0:T(8,128)(2,1)} async-done(((bf16[128,1920]{1,0:T(8,128)(2,1)}), bf16[2048,1920]{1,0:T(8,128)(2,1)}) %all-gather.6.cloned.1.call-update) | async-done | bytes 7864336 | tf_op jit(solution)/shard_map/all_gather | solution.py:25
  77.0 5.9 %fusion.47 = (bf16[512,1408]{0,1:T(8,128)(2,1)S(1)}, f32[512,1408]{0,1:T(8,128)S(1)}) fusion(bf16[512,2048]{1,0:T(8,128)(2,1)S(1)} %copy-done, bf16[2048,1920]{1,0:T(8,128)(2,1)} %all-gather.6.cloned.1.call-done), kind=kOutput, calls=%fused_computation.109 | convolution fusion | flops 2953510912 | bytes 12189696 | tf_op jit(solution)/shard_map/dot_general | solution.py:247
  82.9 0.1 compare_select_fusion
  83.0 0.2 fusion.31
  83.2 0.2 slice_reduce_fusion
  83.5 0.1 slice.150
  83.6 3.3 %collective-permute-start = (bf16[3,768]{0,1:T(8,128)(2,1)S(1)}, bf16[3,768]{0,1:T(8,128)(2,1)S(1)}, u32[]{:S(2)}, u32[]{:S(2)}) collective-permute-start(bf16[3,768]{0,1:T(8,128)(2,1)S(1)} %slice.150), channel_id=1, source_target_pairs={{0,8},{8,16},{16,24},{24,32},{32,40},{40,48},{48,56},{56,64},{64,7... | collective-permute-start | bytes 13832 | tf_op jit(solution)/shard_map/ppermute | solution.py:21
  87.0 2.4 %collective-permute-done = bf16[3,768]{0,1:T(8,128)(2,1)S(1)} collective-permute-done((bf16[3,768]{0,1:T(8,128)(2,1)S(1)}, bf16[3,768]{0,1:T(8,128)(2,1)S(1)}, u32[]{:S(2)}, u32[]{:S(2)}) %collective-permute-start) | collective-permute-done | bytes 4640 | tf_op jit(solution)/shard_map/ppermute | solution.py:21
  89.5 2.1 %multiply_convert_fusion.3 = bf16[512,768]{0,1:T(8,128)(2,1)S(1)} fusion(bf16[512,768]{0,1:T(8,128)(2,1)S(1)} %slice.151, bf16[3,768]{0,1:T(8,128)(2,1)S(1)} %collective-permute-done, f32[768]{0:T(1024)S(1)} %get-tuple-element.19, f32[768]{0:T(1024)S(1)} %get-tuple-element.20, f32[768]{0:T(1024)S(1)} %get-tuple-element.21, f32[768]{0:T(1024)S(1)} %get-tuple-element.18, ...), kind=kLoop, calls=%fused_computation.14 | loop fusion | flops 11403264 | bytes 1594368 | tf_op jit(solution)/shard_map/convert_element_type | solution.py:271
  91.7 0.1 reshape.228
  91.8 0.1 copy.89
  92.0 1.0 fusion.20
  93.0 0.8 slice_bitcast_fusion.1
  93.8 0.1 bitcast_add_fusion
  94.0 0.7 select_maximum_fusion.mine_ref
  94.7 14.6 %shard_map.158 = f32[8,64,128]{2,1,0:T(8,128)} custom-call(f32[8,72,128]{2,1,0:T(8,128)} %select_maximum_fusion.mine_ref), custom_call_target="tpu_custom_call" | custom-call | tf_op jit(solution)/shard_map/pallas_call | solution.py:178
  109.3 1.9 fusion.25
  111.3 0.6 fusion.46
  115.6 0.2 compare_and_fusion
  115.8 0.3 fusion.33
  116.1 1.7 fusion.13
  117.8 0.4 fusion.15
  118.1 0.8 copy.93
  119.1 1.4 multiply_reduce_fusion
  120.5 0.1 reshape.233
  120.5 0.6 pad_bitcast_fusion.q_ref
  121.2 4.7 %convolution_convert_fusion.x_ref = bf16[512,2048]{1,0:T(8,128)(2,1)} fusion(bf16[2048,1920]{1,0:T(8,128)(2,1)} %all-gather.6.cloned.1.call-done, f32[512]{0:T(512)S(1)} %copy-done.12, f32[512,512]{0,1:T(8,128)S(1)} %bitcast.75, bf16[512,1408]{0,1:T(8,128)(2,1)} %copy-done.2), kind=kOutput, calls=%fused_computation.4 | convolution fusion | flops 1076887552 | bytes 5769216 | tf_op jit(solution)/shard_map/dot_general | solution.py:361
  125.9 42.1 %shard_map.159 = (f32[64,2048]{1,0:T(8,128)}, f32[8,128]{1,0:T(8,128)}) custom-call(bf16[512,2048]{1,0:T(8,128)(2,1)} %convolution_convert_fusion.x_ref, f32[64,128]{1,0:T(8,128)} %pad_bitcast_fusion.q_ref), custom_call_target="tpu_custom_call" | custom-call | tf_op jit(solution)/shard_map/pallas_call | solution.py:88
  168.0 0.7 rsqrt_bitcast_fusion
  168.7 1.9 multiply_convert_fusion.9
  170.5 14.1 %all-gather.4.cloned.1.call-done = bf16[16,2,8,64,128]{4,3,2,1,0:T(8,128)(2,1)} async-done(((bf16[1,2,8,64,128]{4,3,2,1,0:T(8,128)(2,1)}), bf16[16,2,8,64,128]{4,3,2,1,0:T(8,128)(2,1)}) %all-gather.4.cloned.1.call-update) | async-done | bytes 4194320 | tf_op jit(solution)/shard_map/all_gather | solution.py:25
  184.6 1.0 constant_dynamic-slice_fusion.1
  185.6 0.8 maximum_convert_fusion
  (66 shorter events, 1.3 us)
Async XLA Ops:
  7.2 69.8 %copy-start = (bf16[512,2048]{1,0:T(8,128)(2,1)S(1)}, bf16[512,2048]{1,0:T(8,128)(2,1)}, u32[]{:S(2)}) copy-start(bf16[512,2048]{1,0:T(8,128)(2,1)} %param.17) | copy-start | bytes 6291460
  7.2 1.7 copy-start.4
  7.2 1.7 copy-start.5
  8.4 9.9 %copy-start.3 = (f32[512,128]{1,0:T(8,128)S(1)}, f32[512,128]{1,0:T(8,128)}, u32[]{:S(2)}) copy-start(f32[512,128]{1,0:T(8,128)} %param.29) | copy-start | bytes 786436
  9.2 19.7 %copy-start.13 = (s32[8]{0:T(128)S(1)}, s32[8]{0:T(128)}, u32[]{:S(2)}) copy-start(s32[8]{0:T(128)} %param.30) | copy-start | bytes 100
  9.2 20.5 %copy-start.6 = (f32[4,512]{1,0:T(4,128)S(1)}, f32[4,512]{1,0:T(4,128)}, u32[]{:S(2)}) copy-start(f32[4,512]{1,0:T(4,128)} %param.21) | copy-start | bytes 24580
  9.2 20.5 %copy-start.7 = (f32[4,256]{1,0:T(4,128)S(1)}, f32[4,256]{1,0:T(4,128)}, u32[]{:S(2)}) copy-start(f32[4,256]{1,0:T(4,128)} %param.23) | copy-start | bytes 12292
  9.2 20.5 %copy-start.8 = (f32[512]{0:T(512)S(1)}, f32[512]{0:T(512)}, u32[]{:S(2)}) copy-start(f32[512]{0:T(512)} %param.22) | copy-start | bytes 6148
  9.2 20.5 %copy-start.9 = (f32[256]{0:T(256)S(1)}, f32[256]{0:T(256)}, u32[]{:S(2)}) copy-start(f32[256]{0:T(256)} %param.24) | copy-start | bytes 3076
  9.2 20.7 %copy-start.14 = (f32[8]{0:T(128)S(1)}, f32[8]{0:T(128)}, u32[]{:S(2)}) copy-start(f32[8]{0:T(128)} %param.26) | copy-start | bytes 100
  10.1 17.9 %all-to-all-start = ((bf16[16,8,1408]{2,0,1:T(8,128)(2,1)}), bf16[16,8,1408]{2,0,1:T(8,128)(2,1)S(1)}, u32[]{:S(2)}, u32[]{:S(2)}) async-start(bf16[16,8,1408]{2,0,1:T(8,128)(2,1)} %concatenate.43), calls=%async_computation | async-start | bytes 720896 | tf_op jit(solution)/shard_map/all_to_all | solution.py:241
  18.2 58.7 %all-gather.6.cloned.1.call-start = ((), (), s32[]{:S(2)}) async-start(), calls=%async_computation.2 | async-start | bytes 8355840 | tf_op jit(solution)/shard_map/all_gather | solution.py:25
  28.8 155.8 %all-gather.4.cloned.1.call-start = ((), (), s32[]{:S(2)}) async-start(), calls=%async_computation.1 | async-start | bytes 4456448 | tf_op jit(solution)/shard_map/all_gather | solution.py:25
  30.1 52.8 %copy-start.10 = (f32[8]{0:T(128)S(1)}, f32[8]{0:T(128)}, u32[]{:S(2)}) copy-start(f32[8]{0:T(128)} %param.25) | copy-start | bytes 100
  82.9 8.7 %copy-start.2 = (bf16[512,1408]{0,1:T(8,128)(2,1)}, bf16[512,1408]{0,1:T(8,128)(2,1)S(1)}, u32[]{:S(2)}) copy-start(bf16[512,1408]{0,1:T(8,128)(2,1)S(1)} %get-tuple-element.43) | copy-start | bytes 4325380
  83.6 5.9 %collective-permute-start = (bf16[3,768]{0,1:T(8,128)(2,1)S(1)}, bf16[3,768]{0,1:T(8,128)(2,1)S(1)}, u32[]{:S(2)}, u32[]{:S(2)}) collective-permute-start(bf16[3,768]{0,1:T(8,128)(2,1)S(1)} %slice.150), channel_id=1, source_target_pairs={{0,8},{8,16},{16,24},{24,32},{32,40},{40,48},{48,56},{56,64},{64,7... | collective-permute-start | bytes 13832 | tf_op jit(solution)/shard_map/ppermute | solution.py:21
  93.8 17.4 %copy-start.15 = (s32[32]{0:T(128)S(1)}, s32[32]{0:T(128)}, u32[]{:S(2)}) copy-start(s32[32]{0:T(128)} %param.31) | copy-start | bytes 388
  116.0 1.7 copy-start.1
  116.0 1.7 copy-start.11
  119.0 2.2 %copy-start.12 = (f32[512]{0:T(512)S(1)}, f32[512]{0:T(512)}, u32[]{:S(2)}) copy-start(f32[512]{0:T(512)} %param.28) | copy-start | bytes 6148
Sparse Core Ops, SparseCore 0:
  28.9 47.9 all-gather.5
  111.3 73.2 all-gather.3
